TPU v7x, 32 devices: a whole 2x2x4 slice. The times are simulated.
32 devices in a mesh: lon: 8 (over y, x, core), depth: 4 (over z).
Axes of the slice: x: 2, y: 2, z: 4, core: 2. Of those that a mesh axis runs over, the one named last changes fastest.
Arguments:
- innovations: float32 [5, 256, 128, 256], P(None, 'depth', 'lon'), may hold values from -6 to 6
- courant: float32 [3, 256, 128, 256], P(None, 'depth', 'lon'), may hold values from -0.3 to 0.3
- diffusivity: float32 [256, 128, 256], P('depth', 'lon'), may hold values from 0.05 to 0.12
- sea_bricks: int32 [256, 8, 128], P('depth', 'lon'), may hold values 0 or 1
- tile_ranks: int32 [8, 8], P('lon'), may hold values from 16 to 128
- row_factors: bfloat16 [8, 8, 4096, 128], P('lon', None, None, 'depth'), may hold values from -0.09375 to 0.09375
- column_factors: bfloat16 [8, 8, 4096, 128], P('lon', None, None, 'depth'), may hold values from -0.25 to 0.25
Outputs:
- initial_adjoint: float32 [256, 128, 256], P('depth', 'lon')
- gradient: float32 [256, 128, 256], P('depth', 'lon')
All inputs are finite; a program needn't handle non-finite values. No bound on the sum of `sea_bricks` on one device may be relied on, other than what follows from the above.
Results may differ from a plain program's by a relative error of at most 0.0041.
Values may be sent and summed in bfloat16 or wider, within the bound.
No kernel may reach another device: no remote copies, remote signals or barrier semaphores. Data moves between devices by JAX's collectives and lax.ppermute only.
A program may use at most 64 MiB of HBM per device.

v0:
```python
import functools
import jax
import jax.numpy as jnp
from jax import lax
from jax.experimental import pallas as pl
from jax.experimental.pallas import tpu as pltpu
from jax.sharding import PartitionSpec as P

UNROLL = 3
LANES = 128
GRANT = 4 << 20
VMEM = pl.BlockSpec(memory_space=pltpu.VMEM)


def from_behind(value, axis, steps):
    count = lax.axis_size(axis)
    initial, last = (max(0, -steps), min(count, count - steps))
    return lax.ppermute(value, axis, [(source, source + steps) for source in range(initial, last)])


def shifted(block, axis, distance):
    devices = range(lax.axis_size(axis))
    if distance % len(devices) == 0:
        return block
    route = [((i - distance) % len(devices), i) for i in devices]
    return lax.ppermute(block, axis, route)


def swapped(block, axis, mask):
    return lax.ppermute(block, axis, [(i, i ^ mask) for i in range(lax.axis_size(axis))])


def halo_table(depth):
    order, at = {}, 0
    for name, extent in (
        [(("innov", k), k) for k in range(depth, 0, -1)]
        + [("diff", depth), ("c0", depth), ("c1", depth - 1), ("c2", depth - 1)]
    ):
        for distance in range(1, extent + 1):
            order[name, distance] = at
            at += 1
    order["sea"] = at
    return order, at + 1


def pack_kernel(table, innov_lo, innov_hi, cour_lo, cour_hi, diff_lo, diff_hi, sea_lo, sea_hi, down, up):
    depth = diff_lo.shape[0]

    def fill(out, innov, cour, diff, sea, level):
        for key, at in table.items():
            if key == "sea":
                rows = [sea[level(d)] for d in range(1, depth + 1)]
                rows.append(jnp.zeros((out.shape[1] - depth, out.shape[2]), jnp.float32))
                value = jnp.concatenate(rows, 0)
            else:
                name, distance = key
                z = level(distance)
                if name == "diff":
                    value = diff[z]
                elif name == "c0":
                    value = cour[0, z]
                elif name == "c1":
                    value = cour[1, z]
                elif name == "c2":
                    value = cour[2, z]
                else:
                    value = innov[name[1], z]
            out[at] = value.astype(jnp.bfloat16)

    fill(down, innov_hi, cour_hi, diff_hi, sea_hi, lambda d: depth - d)
    fill(up, innov_lo, cour_lo, diff_lo, sea_lo, lambda d: d - 1)


def first_kernel(table, innov, cour, diff, sea, before, after, sea_ext, east_gain, west_gain, to_east, to_west):
    steps = innov.shape[0] - 1
    levels, lon_cells, lat_cells = diff.shape
    last = lon_cells - 1

    def put(at, sea_row, diff_a, diff_b, cour_a, cour_b, innov_a, innov_b):
        sea_ext[at] = sea_row
        low_row, high_row = sea_row * innov_a, sea_row * innov_b
        west = diff_a + 0.5 * cour_a
        east = diff_b - 0.5 * cour_b
        west_gain[at], east_gain[at] = west, east
        to_west[at], to_east[at] = west * low_row, east * high_row

    for halo, where in ((before, lambda d: steps - d), (after, lambda d: steps + levels + d - 1)):
        sea_rows = halo[table["sea"]].astype(jnp.float32)
        for d in range(1, steps + 1):
            sea_row = sea_rows[d - 1 : d]
            at = where(d)
            if d == steps:
                zero = jnp.zeros((1, lat_cells), jnp.float32)
                sea_ext[at] = sea_row
                west_gain[at], east_gain[at], to_west[at], to_east[at] = zero, zero, zero, zero
            else:
                dd = halo[table["diff", d]].astype(jnp.float32)
                cc = halo[table["c1", d]].astype(jnp.float32)
                ii = halo[table[("innov", steps), d]].astype(jnp.float32)
                put(at, sea_row, dd[:1], dd[last:], cc[:1], cc[last:], ii[:1], ii[last:])

    def one(z, carry):
        edge = lambda ref: (ref[z, :1], ref[z, last:])
        put(z + steps, sea[z], *edge(diff), *edge(cour.at[1]), *edge(innov.at[steps]))
        return carry

    lax.fori_loop(0, levels, one, 0, unroll=4)


def step_kernel(table, step, innov, cour, diff, sea_ext, before, after, low, high, *rest):
    steps = innov.shape[0] - 1
    levels, lon_cells, lat_cells = diff.shape
    if step > 1:
        lam, rest = rest[0], rest[1:]
    out, out_low, out_high = rest
    last = lon_cells - 1
    x_at = lax.broadcasted_iota(jnp.int32, (lon_cells, lat_cells), 0)
    y_at = lax.broadcasted_iota(jnp.int32, (lon_cells, lat_cells), 1)
    first_x, last_x = x_at == 0, x_at == last
    first_y, last_y = y_at == 0, y_at == lat_cells - 1
    reach = steps - step

    def halo_level(halo, d, name):
        return halo[table[name, d]].astype(jnp.float32)

    def state(at, innovation):
        if step == 1:
            return sea_ext[at] * innovation
        value = jnp.where(first_x, low[at], lam[at])
        return jnp.where(last_x, high[at], value)

    def finish(at, acc, up_flux):
        value = sea_ext[at] * (acc + up_flux)
        out[at] = value
        out_low[at] = value[:1]
        out_high[at] = value[last:]

    def depth_terms(a, d, c):
        spread, drift = d * a, c * (0.5 * a)
        return spread - drift, spread + drift

    def level(a, d, c0, c1, c2, innovation):
        half = 0.5 * a
        spread = d * a
        drift = c0 * half
        plus0, minus0 = spread - drift, spread + drift
        drift = c1 * half
        plus1, minus1 = spread - drift, spread + drift
        drift = c2 * half
        plus2, minus2 = spread - drift, spread + drift
        acc = a - 6.0 * spread + innovation
        acc = acc + jnp.where(first_x, 0.0, pltpu.roll(plus1, 1, 0))
        acc = acc + jnp.where(last_x, 0.0, pltpu.roll(minus1, lon_cells - 1, 0))
        acc = acc + jnp.where(first_y, 0.0, pltpu.roll(plus2, 1, 1))
        acc = acc + jnp.where(last_y, 0.0, pltpu.roll(minus2, lat_cells - 1, 1))
        return acc, plus0, minus0

    def halo_full(halo, d, at):
        a = state(at, halo_level(halo, d, ("innov", steps)))
        return level(
            a,
            halo_level(halo, d, "diff"),
            halo_level(halo, d, "c0"),
            halo_level(halo, d, "c1"),
            halo_level(halo, d, "c2"),
            halo_level(halo, d, ("innov", steps - step)),
        )

    def halo_edge(halo, d, at):
        a = state(at, halo_level(halo, d, ("innov", steps)))
        return depth_terms(a, halo_level(halo, d, "diff"), halo_level(halo, d, "c0"))

    down_flux, _ = halo_edge(before, reach + 1, steps - reach - 1)
    acc = None
    for d in range(reach, 0, -1):
        at = steps - d
        value, plus0, minus0 = halo_full(before, d, at)
        if acc is not None:
            finish(at - 1, acc, minus0)
        acc, down_flux = value + down_flux, plus0

    def own(z):
        a = state(z + steps, innov[steps, z])
        return level(a, diff[z], cour[0, z], cour[1, z], cour[2, z], innov[steps - step, z])

    value, plus0, minus0 = own(0)
    if acc is not None:
        finish(steps - 1, acc, minus0)
    carry = (value + down_flux, plus0)

    def one(z, carry):
        acc, down_flux = carry
        value, plus0, minus0 = own(z)
        finish(z + steps - 1, acc, minus0)
        return value + down_flux, plus0

    head = (levels - 1) % UNROLL
    for z in range(1, 1 + head):
        carry = one(z, carry)

    def several(i, carry):
        for u in range(UNROLL):
            carry = one(1 + head + i * UNROLL + u, carry)
        return carry

    acc, down_flux = lax.fori_loop(0, (levels - 1) // UNROLL, several, carry)
    at = steps + levels - 1
    for d in range(1, reach + 1):
        value, plus0, minus0 = halo_full(after, d, at + d)
        finish(at + d - 1, acc, minus0)
        acc, down_flux = value + down_flux, plus0
    _, up_flux = halo_edge(after, reach + 1, at + reach + 1)
    finish(at + reach, acc, up_flux)


def last_kernel(side, lam, low, high, out, mine, other, *rows):
    levels, lon_cells, lat_cells = out.shape
    steps = (lam.shape[0] - levels) // 2
    x_at = lax.broadcasted_iota(jnp.int32, (lon_cells, lat_cells), 0)
    first_x, last_x = x_at == 0, x_at == lon_cells - 1

    def one(z, carry):
        value = jnp.where(first_x, low[z + steps], lam[z + steps])
        value = jnp.where(last_x, high[z + steps], value)
        out[z] = value
        for c, lanes in enumerate(rows):
            at = pl.multiple_of(z * lon_cells, lon_cells)
            lanes[pl.ds(at, lon_cells), :] = value[:, c * LANES : (c + 1) * LANES]
        return carry

    lax.fori_loop(0, levels, one, 0, unroll=4)
    half = lon_cells // 2
    for part, start in ((mine, side[0] * half), (other, (1 - side[0]) * half)):
        for x in range(half):
            for c, lanes in enumerate(rows):
                picked = lanes[pl.ds(start + x, levels, stride=lon_cells), :]
                at = x * lat_cells + c * LANES
                part[:, at : at + LANES] = picked.astype(jnp.bfloat16)


def face_kernel(sea_ext, out_low, out_high, west, east, west_gain, east_gain, low, high, to_west, to_east):
    low_rows = out_low[...] + sea_ext[...] * west[...]
    high_rows = out_high[...] + sea_ext[...] * east[...]
    low[...], high[...] = low_rows, high_rows
    to_west[...], to_east[...] = west_gain[...] * low_rows, east_gain[...] * high_rows


def sweep(innovations, courant, diffusivity, sea, side):
    levels, lon_cells, lat_cells = diffusivity.shape
    steps = innovations.shape[0] - 1
    table, layers = halo_table(steps)
    f32, bf16 = jnp.float32, jnp.bfloat16
    end = levels // steps - 1

    def edges(shape, axis):
        block = list(shape)
        block[axis] = steps
        at = lambda index: lambda i: tuple(index if a == axis else 0 for a in range(len(shape)))
        return [pl.BlockSpec(tuple(block), at(index)) for index in (0, end)]

    message = jax.ShapeDtypeStruct((layers, lon_cells, lat_cells), bf16)
    down, up = pl.pallas_call(
        functools.partial(pack_kernel, table),
        grid=(1,),
        in_specs=edges(innovations.shape, 1)
        + edges(courant.shape, 1)
        + edges(diffusivity.shape, 0)
        + edges(sea.shape, 0),
        out_shape=[message, message],
        out_specs=[VMEM, VMEM],
        compiler_params=pltpu.CompilerParams(vmem_limit_bytes=GRANT),
        cost_estimate=pl.CostEstimate(flops=0, bytes_accessed=1 << 20, transcendentals=0),
    )(innovations, innovations, courant, courant, diffusivity, diffusivity, sea, sea)
    before = from_behind(down, "depth", 1)
    after = from_behind(up, "depth", -1)
    row = jax.ShapeDtypeStruct((levels + 2 * steps, 1, lat_cells), f32)
    cells = jax.ShapeDtypeStruct((levels + 2 * steps, lon_cells, lat_cells), f32)
    inputs = (innovations, courant, diffusivity)
    sea_ext, east_gain, west_gain, to_east, to_west = pl.pallas_call(
        functools.partial(first_kernel, table),
        in_specs=[VMEM] * 6,
        out_shape=[row] * 5,
        out_specs=[VMEM] * 5,
        compiler_params=pltpu.CompilerParams(vmem_limit_bytes=GRANT),
        cost_estimate=pl.CostEstimate(flops=0, bytes_accessed=1 << 20, transcendentals=0),
    )(*inputs, sea, before, after)
    lam = ()
    low = high = sea_ext
    for step in range(1, steps + 1):
        west = shifted(to_east, "lon", 1)
        east = shifted(to_west, "lon", -1)
        state = (low, high) + lam
        out, out_low, out_high = pl.pallas_call(
            functools.partial(step_kernel, table, step),
            in_specs=[VMEM] * (6 + len(state)),
            out_shape=[cells, row, row],
            out_specs=[VMEM] * 3,
            compiler_params=pltpu.CompilerParams(vmem_limit_bytes=GRANT),
        cost_estimate=pl.CostEstimate(flops=40 * levels * lon_cells * lat_cells, bytes_accessed=9 << 20, transcendentals=0),
        )(*inputs, sea_ext, before, after, *state)
        low, high, to_west, to_east = pl.pallas_call(
            face_kernel,
            in_specs=[VMEM] * 7,
            out_shape=[row] * 4,
            out_specs=[VMEM] * 4,
            compiler_params=pltpu.CompilerParams(vmem_limit_bytes=GRANT),
            cost_estimate=pl.CostEstimate(flops=0, bytes_accessed=1 << 19, transcendentals=0),
        )(sea_ext, out_low, out_high, west, east, west_gain, east_gain)
        lam = (out,)
    half = jax.ShapeDtypeStruct((levels, lon_cells * lat_cells // 2), bf16)
    return pl.pallas_call(
        last_kernel,
        in_specs=[pl.BlockSpec(memory_space=pltpu.SMEM)] + [VMEM] * 3,
        out_shape=[jax.ShapeDtypeStruct((levels, lon_cells, lat_cells), f32), half, half],
        out_specs=[VMEM] * 3,
        scratch_shapes=[pltpu.VMEM((levels * lon_cells, LANES), f32)] * (lat_cells // LANES),
        compiler_params=pltpu.CompilerParams(vmem_limit_bytes=GRANT),
        cost_estimate=pl.CostEstimate(flops=0, bytes_accessed=3 << 20, transcendentals=0),
    )(side.reshape(1), out, low, high)


def per_device(
    innovations, courant, diffusivity, sea_bricks, tile_ranks, row_factors, column_factors
):
    levels_here, lon_cells, lat_cells = diffusivity.shape
    tile_cols = lon_cells * lat_cells
    half = tile_cols // 2
    blocks_row = tile_ranks.shape[1]
    count = lax.axis_size("depth")
    me = lax.axis_index("depth")
    side = me % 2
    left = row_factors[0].transpose(0, 2, 1)
    right = column_factors[0].transpose(0, 2, 1)
    width = left.shape[1]

    def split(array, axis):
        mine = lax.dynamic_slice_in_dim(array, side * half, half, axis)
        other = lax.dynamic_slice_in_dim(array, (1 - side) * half, half, axis)
        return mine, other

    left_mine, left_other = split(left, 2)
    right_mine, right_other = split(right, 2)

    sea = sea_bricks.astype(jnp.float32)
    sea = jnp.broadcast_to(sea[:, :, :, None], (levels_here, 1, lat_cells // 2, 2)).reshape(
        levels_here, 1, lat_cells
    )
    lam, lam_mine, lam_other = sweep(innovations, courant, diffusivity, sea, side)
    left_pair = swapped(left_other, "depth", 1)
    right_pair = swapped(right_other, "depth", 1)
    blocks = [lam_mine]
    for mask in range(1, count):
        blocks.append(swapped(lam_other if mask % 2 else lam_mine, "depth", mask))
    partial = [
        [
            jnp.einsum("zt,krt->krz", block, factor, preferred_element_type=jnp.float32)
            for factor in (left_mine, left_pair)
        ]
        for block in blocks
    ]
    sent = jnp.concatenate(
        [jnp.stack([partial[s ^ 1][1], partial[s ^ 1][0]], 1) for s in range(count)], 3
    ).astype(jnp.bfloat16)
    kept = jnp.concatenate([jnp.stack(partial[s], 1) for s in range(count)], 3)
    coeff = kept + swapped(sent, "depth", 1).astype(jnp.float32)
    ranks = tile_ranks[0]
    owner = jnp.stack([me, me ^ 1])
    columns = owner[:, None] * width + jnp.arange(width, dtype=jnp.int32)[None, :]
    keep = columns[None] < ranks[:, None, None]
    coeff = jnp.where(keep[:, :, :, None], coeff, 0.0).astype(jnp.bfloat16)
    received = jnp.stack(
        [shifted(coeff[k], "lon", k - blocks_row // 2) for k in range(blocks_row)], 0
    )
    sums = [
        jnp.einsum("krz,krt->zt", levels[:, 0], right_mine, preferred_element_type=jnp.float32)
        + jnp.einsum("krz,krt->zt", levels[:, 1], right_pair, preferred_element_type=jnp.float32)
        for levels in jnp.split(received, count, 3)
    ]
    arrived = [
        swapped(sums[mask].astype(jnp.bfloat16), "depth", mask) for mask in range(1, count)
    ]
    grad_mine = sums[0]
    for mask in range(2, count, 2):
        grad_mine = grad_mine + arrived[mask - 1].astype(jnp.float32)
    grad_other = arrived[0].astype(jnp.float32)
    for mask in range(3, count, 2):
        grad_other = grad_other + arrived[mask - 1].astype(jnp.float32)
    low = jnp.where(side == 0, grad_mine, grad_other)
    high = jnp.where(side == 0, grad_other, grad_mine)
    gradient = jnp.concatenate([low, high], 1)
    return (lam, gradient.reshape(levels_here, lon_cells, lat_cells))


def solution(mesh):
    placed = (
        P(None, "depth", "lon", None),
        P(None, "depth", "lon", None),
        P("depth", "lon", None),
        P("depth", "lon", None),
        P("lon", None),
        P("lon", None, None, "depth"),
        P("lon", None, None, "depth"),
    )
    return jax.shard_map(
        per_device,
        mesh=mesh,
        in_specs=placed,
        out_specs=(P("depth", "lon", None), P("depth", "lon", None)),
        check_vma=False,
    )
```

profile of v0, /device:TPU:6, one launch (start us, length us, event | category | flops | bytes accessed | tf_op | source)
XLA Modules:
  0.0 166.2 jit_solution(9872417756730289916)
XLA Ops:
  1.8 2.5 %copy-done.1 = f32[5,64,16,256]{3,2,1,0:T(8,128)S(1)} copy-done((f32[5,64,16,256]{3,2,1,0:T(8,128)S(1)}, f32[5,64,16,256]{3,2,1,0:T(8,128)}, u32[]{:S(2)}) %copy-start.1) | copy-done | bytes 5242904
  4.3 1.9 %copy-done.4 = f32[3,64,16,256]{3,2,1,0:T(8,128)S(1)} copy-done((f32[3,64,16,256]{3,2,1,0:T(8,128)S(1)}, f32[3,64,16,256]{3,2,1,0:T(8,128)}, u32[]{:S(2)}) %copy-start.4) | copy-done | bytes 3145752
  7.5 3.5 %collective-permute-start = (bf16[25,16,256]{2,1,0:T(8,128)(2,1)S(1)}, bf16[25,16,256]{2,1,0:T(8,128)(2,1)S(1)}, u32[]{:S(2)}, u32[]{:S(2)}) collective-permute-start(bf16[25,16,256]{2,1,0:T(8,128)(2,1)S(1)} %get-tuple-element.38), channel_id=1, source_target_pairs={{0,1},{1,2},{2,3},{4,5},{5,6},{6,7},{8,9},{9,10},{10,11},{12,13},{... | collective-permute-start | bytes 614408 | tf_op jit(solution)/shard_map/ppermute | solution.py:18
  12.3 3.0 %collective-permute-done.before = bf16[25,16,256]{2,1,0:T(8,128)(2,1)S(1)} collective-permute-done((bf16[25,16,256]{2,1,0:T(8,128)(2,1)S(1)}, bf16[25,16,256]{2,1,0:T(8,128)(2,1)S(1)}, u32[]{:S(2)}, u32[]{:S(2)}) %collective-permute-start) | collective-permute-done | bytes 204832 | tf_op jit(solution)/shard_map/ppermute | solution.py:18
  15.3 4.1 %collective-permute-done.1.after = bf16[25,16,256]{2,1,0:T(8,128)(2,1)S(1)} collective-permute-done((bf16[25,16,256]{2,1,0:T(8,128)(2,1)S(1)}, bf16[25,16,256]{2,1,0:T(8,128)(2,1)S(1)}, u32[]{:S(2)}, u32[]{:S(2)}) %collective-permute-start.1) | collective-permute-done | bytes 204832 | tf_op jit(solution)/shard_map/ppermute | solution.py:18
  21.5 2.4 %shard_map.88 = (f32[72,16,256]{2,1,0:T(8,128)S(1)}, f32[72,1,256]{2,1,0:T(1,128)S(1)}, f32[72,1,256]{2,1,0:T(1,128)S(1)}) custom-call(f32[5,64,16,256]{3,2,1,0:T(8,128)S(1)} %copy-done.1, f32[3,64,16,256]{3,2,1,0:T(8,128)S(1)} %copy-done.4, f32[64,16,256]{2,1,0:T(8,128)S(1)} %copy-done.7, f32[72,1,256]{2,1,0:T(1,128)S(1)} %get-tuple-element.40.sea_ext.low.high, ...), custom_call_target="tpu_custom_call" | custom-call | flops 10485760 | bytes 9437184 | tf_op jit(solution)/shard_map/pallas_call | solution.py:293
  26.0 2.4 %shard_map.90 = (f32[72,16,256]{2,1,0:T(8,128)S(1)}, f32[72,1,256]{2,1,0:T(1,128)S(1)}, f32[72,1,256]{2,1,0:T(1,128)S(1)}) custom-call(f32[5,64,16,256]{3,2,1,0:T(8,128)S(1)} %bitcast.209, f32[3,64,16,256]{3,2,1,0:T(8,128)S(1)} %copy-done.4, f32[64,16,256]{2,1,0:T(8,128)S(1)} %copy-done.7, f32[72,1,256]{2,1,0:T(1,128)S(1)} %get-tuple-element.40.sea_ext.low.high, ...), custom_call_target="tpu_custom_call" | custom-call | flops 10485760 | bytes 9437184 | tf_op jit(solution)/shard_map/pallas_call | solution.py:293
  33.2 2.5 %copy-done.2 = f32[5,64,16,256]{3,2,1,0:T(8,128)S(1)} copy-done((f32[5,64,16,256]{3,2,1,0:T(8,128)S(1)}, f32[5,64,16,256]{3,2,1,0:T(8,128)}, u32[]{:S(2)}) %copy-start.2) | copy-done | bytes 5242904
  41.6 2.4 %shard_map.92 = (f32[72,16,256]{2,1,0:T(8,128)S(1)}, f32[72,1,256]{2,1,0:T(1,128)S(1)}, f32[72,1,256]{2,1,0:T(1,128)S(1)}) custom-call(f32[5,64,16,256]{3,2,1,0:T(8,128)S(1)} %copy-done.2, f32[3,64,16,256]{3,2,1,0:T(8,128)S(1)} %copy-done.5, f32[64,16,256]{2,1,0:T(8,128)S(1)} %copy-done.8, f32[72,1,256]{2,1,0:T(1,128)S(1)} %get-tuple-element.40.sea_ext.low.high, ...), custom_call_target="tpu_custom_call" | custom-call | flops 10485760 | bytes 9437184 | tf_op jit(solution)/shard_map/pallas_call | solution.py:293
  52.3 2.5 %copy-done.3 = f32[5,64,16,256]{3,2,1,0:T(8,128)S(1)} copy-done((f32[5,64,16,256]{3,2,1,0:T(8,128)S(1)}, f32[5,64,16,256]{3,2,1,0:T(8,128)}, u32[]{:S(2)}) %copy-start.3) | copy-done | bytes 5242904
  60.7 2.3 %shard_map.94 = (f32[72,16,256]{2,1,0:T(8,128)S(1)}, f32[72,1,256]{2,1,0:T(1,128)S(1)}, f32[72,1,256]{2,1,0:T(1,128)S(1)}) custom-call(f32[5,64,16,256]{3,2,1,0:T(8,128)S(1)} %copy-done.3, f32[3,64,16,256]{3,2,1,0:T(8,128)S(1)} %copy-done.6, f32[64,16,256]{2,1,0:T(8,128)S(1)} %copy-done.8, f32[72,1,256]{2,1,0:T(1,128)S(1)} %get-tuple-element.40.sea_ext.low.high, ...), custom_call_target="tpu_custom_call" | custom-call | flops 10485760 | bytes 9437184 | tf_op jit(solution)/shard_map/pallas_call | solution.py:293
  65.9 2.5 %collective-permute-start.13 = (bf16[64,2048]{1,0:T(8,128)(2,1)S(1)}, bf16[64,2048]{1,0:T(8,128)(2,1)S(1)}, u32[]{:S(2)}, u32[]{:S(2)}) collective-permute-start(bf16[64,2048]{1,0:T(8,128)(2,1)S(1)} %get-tuple-element.73), channel_id=1, source_target_pairs={{0,3},{1,2},{2,1},{3,0},{4,7},{5,6},{6,5},{7,4},{8,11},{9,10},{10,... | collective-permute-start | bytes 786440 | tf_op jit(solution)/shard_map/ppermute | solution.py:30
  68.4 1.9 %collective-permute-start.12 = (bf16[64,2048]{1,0:T(8,128)(2,1)S(1)}, bf16[64,2048]{1,0:T(8,128)(2,1)S(1)}, u32[]{:S(2)}, u32[]{:S(2)}) collective-permute-start(bf16[64,2048]{1,0:T(8,128)(2,1)S(1)} %get-tuple-element.72), channel_id=1, source_target_pairs={{0,2},{1,3},{2,0},{3,1},{4,6},{5,7},{6,4},{7,5},{8,10},{9,11},{10,... | collective-permute-start | bytes 786440 | tf_op jit(solution)/shard_map/ppermute | solution.py:30
  72.0 12.2 %collective-permute-done.13 = bf16[64,2048]{1,0:T(8,128)(2,1)S(1)} collective-permute-done((bf16[64,2048]{1,0:T(8,128)(2,1)S(1)}, bf16[64,2048]{1,0:T(8,128)(2,1)S(1)}, u32[]{:S(2)}, u32[]{:S(2)}) %collective-permute-start.13) | collective-permute-done | bytes 262176 | tf_op jit(solution)/shard_map/ppermute | solution.py:30
  85.8 6.5 %collective-permute-done.12 = bf16[64,2048]{1,0:T(8,128)(2,1)S(1)} collective-permute-done((bf16[64,2048]{1,0:T(8,128)(2,1)S(1)}, bf16[64,2048]{1,0:T(8,128)(2,1)S(1)}, u32[]{:S(2)}, u32[]{:S(2)}) %collective-permute-start.12) | collective-permute-done | bytes 262176 | tf_op jit(solution)/shard_map/ppermute | solution.py:30
  100.5 3.1 %collective-permute-start.14 = (bf16[8,2,32,256]{3,2,0,1:T(8,128)(2,1)S(1)}, bf16[8,2,32,256]{3,2,0,1:T(8,128)(2,1)S(1)}, u32[]{:S(2)}, u32[]{:S(2)}) collective-permute-start(bf16[8,2,32,256]{3,2,0,1:T(8,128)(2,1)S(1)} %maximum_maximum_fusion), channel_id=1, source_target_pairs={{0,1},{1,0},{2,3},{3,2},{4,5},{5,4},{6,7},{7,6},{8,9},{9,8},{10,11... | collective-permute-start | bytes 786440 | tf_op jit(solution)/shard_map/ppermute | solution.py:30
  103.8 6.7 %collective-permute-done.14 = bf16[8,2,32,256]{3,2,0,1:T(8,128)(2,1)S(1)} collective-permute-done((bf16[8,2,32,256]{3,2,0,1:T(8,128)(2,1)S(1)}, bf16[8,2,32,256]{3,2,0,1:T(8,128)(2,1)S(1)}, u32[]{:S(2)}, u32[]{:S(2)}) %collective-permute-start.14) | collective-permute-done | bytes 262176 | tf_op jit(solution)/shard_map/ppermute | solution.py:30
  111.2 2.4 %collective-permute-start.22 = (bf16[8,32,2048]{2,1,0:T(8,128)(2,1)S(1)}, bf16[8,32,2048]{2,1,0:T(8,128)(2,1)S(1)}, u32[]{:S(2)}, u32[]{:S(2)}) collective-permute-start(bf16[8,32,2048]{2,1,0:T(8,128)(2,1)S(1)} %dynamic-slice_bitcast_fusion), channel_id=1, source_target_pairs={{0,1},{1,0},{2,3},{3,2},{4,5},{5,4},{6,7},{7,6},{8,9},{9,8},{10,11... | collective-permute-start | bytes 3145736 | tf_op jit(solution)/shard_map/ppermute | solution.py:30
  113.6 2.5 %collective-permute-start.18 = (bf16[2,32,256]{2,1,0:T(8,128)(2,1)S(1)}, bf16[2,32,256]{2,1,0:T(8,128)(2,1)S(1)}, u32[]{:S(2)}, u32[]{:S(2)}) collective-permute-start(bf16[2,32,256]{2,1,0:T(8,128)(2,1)S(1)} %get-tuple-element.78), channel_id=1, source_target_pairs={{4,0},{8,4},{12,8},{16,12},{20,16},{24,20},{28,24},{0,28},{5,1},{9... | collective-permute-start | bytes 98312 | tf_op jit(solution)/shard_map/ppermute | solution.py:26
  123.2 13.5 %collective-permute-done.22 = bf16[8,32,2048]{2,1,0:T(8,128)(2,1)S(1)} collective-permute-done((bf16[8,32,2048]{2,1,0:T(8,128)(2,1)S(1)}, bf16[8,32,2048]{2,1,0:T(8,128)(2,1)S(1)}, u32[]{:S(2)}, u32[]{:S(2)}) %collective-permute-start.22) | collective-permute-done | bytes 1048608 | tf_op jit(solution)/shard_map/ppermute | solution.py:30
  142.1 2.3 %collective-permute-start.23 = (bf16[64,2048]{1,0:T(8,128)(2,1)}, bf16[64,2048]{1,0:T(8,128)(2,1)}, u32[]{:S(2)}, u32[]{:S(2)}) collective-permute-start(bf16[64,2048]{1,0:T(8,128)(2,1)} %fusion.5), channel_id=1, source_target_pairs={{0,2},{1,3},{2,0},{3,1},{4,6},{5,7},{6,4},{7,5},{8,10},{9,11},{10,... | collective-permute-start | bytes 786440 | tf_op jit(solution)/shard_map/ppermute | solution.py:30
  144.7 4.5 %collective-permute-done.25 = bf16[64,2048]{1,0:T(8,128)(2,1)} collective-permute-done((bf16[64,2048]{1,0:T(8,128)(2,1)}, bf16[64,2048]{1,0:T(8,128)(2,1)}, u32[]{:S(2)}, u32[]{:S(2)}) %collective-permute-start.25) | collective-permute-done | bytes 262176 | tf_op jit(solution)/shard_map/ppermute | solution.py:30
  149.2 4.7 %collective-permute-done.24 = bf16[64,2048]{1,0:T(8,128)(2,1)} collective-permute-done((bf16[64,2048]{1,0:T(8,128)(2,1)}, bf16[64,2048]{1,0:T(8,128)(2,1)}, u32[]{:S(2)}, u32[]{:S(2)}) %collective-permute-start.24) | collective-permute-done | bytes 262176 | tf_op jit(solution)/shard_map/ppermute | solution.py:30
  153.9 9.5 %collective-permute-done.23 = bf16[64,2048]{1,0:T(8,128)(2,1)} collective-permute-done((bf16[64,2048]{1,0:T(8,128)(2,1)}, bf16[64,2048]{1,0:T(8,128)(2,1)}, u32[]{:S(2)}, u32[]{:S(2)}) %collective-permute-start.23) | collective-permute-done | bytes 262176 | tf_op jit(solution)/shard_map/ppermute | solution.py:30
  (142 shorter events, 63.5 us)
Async XLA Ops:
  7.5 7.8 %collective-permute-start = (bf16[25,16,256]{2,1,0:T(8,128)(2,1)S(1)}, bf16[25,16,256]{2,1,0:T(8,128)(2,1)S(1)}, u32[]{:S(2)}, u32[]{:S(2)}) collective-permute-start(bf16[25,16,256]{2,1,0:T(8,128)(2,1)S(1)} %get-tuple-element.38), channel_id=1, source_target_pairs={{0,1},{1,2},{2,3},{4,5},{5,6},{6,7},{8,9},{9,10},{10,11},{12,13},{... | collective-permute-start | bytes 614408 | tf_op jit(solution)/shard_map/ppermute | solution.py:18
  11.0 8.4 %collective-permute-start.1 = (bf16[25,16,256]{2,1,0:T(8,128)(2,1)S(1)}, bf16[25,16,256]{2,1,0:T(8,128)(2,1)S(1)}, u32[]{:S(2)}, u32[]{:S(2)}) collective-permute-start(bf16[25,16,256]{2,1,0:T(8,128)(2,1)S(1)} %get-tuple-element.39), channel_id=1, source_target_pairs={{1,0},{2,1},{3,2},{5,4},{6,5},{7,6},{9,8},{10,9},{11,10},{13,12},{... | collective-permute-start | bytes 614408 | tf_op jit(solution)/shard_map/ppermute | solution.py:18
  19.7 4.2 %collective-permute-start.2 = (f32[72,1,256]{2,1,0:T(1,128)S(1)}, f32[72,1,256]{2,1,0:T(1,128)S(1)}, u32[]{:S(2)}, u32[]{:S(2)}) collective-permute-start(f32[72,1,256]{2,1,0:T(1,128)S(1)} %get-tuple-element.43), channel_id=1, source_target_pairs={{28,0},{0,4},{4,8},{8,12},{12,16},{16,20},{20,24},{24,28},{29,1},{... | collective-permute-start | bytes 221192 | tf_op jit(solution)/shard_map/ppermute | solution.py:26
  19.8 4.2 %collective-permute-start.3 = (f32[72,1,256]{2,1,0:T(1,128)S(1)}, f32[72,1,256]{2,1,0:T(1,128)S(1)}, u32[]{:S(2)}, u32[]{:S(2)}) collective-permute-start(f32[72,1,256]{2,1,0:T(1,128)S(1)} %get-tuple-element.44), channel_id=1, source_target_pairs={{4,0},{8,4},{12,8},{16,12},{20,16},{24,20},{28,24},{0,28},{5,1},{9... | collective-permute-start | bytes 221192 | tf_op jit(solution)/shard_map/ppermute | solution.py:26
  24.1 5.3 %collective-permute-start.4 = (f32[72,1,256]{2,1,0:T(1,128)S(1)}, f32[72,1,256]{2,1,0:T(1,128)S(1)}, u32[]{:S(2)}, u32[]{:S(2)}) collective-permute-start(f32[72,1,256]{2,1,0:T(1,128)S(1)} %get-tuple-element.52), channel_id=1, source_target_pairs={{28,0},{0,4},{4,8},{8,12},{12,16},{16,20},{20,24},{24,28},{29,1},{... | collective-permute-start | bytes 221192 | tf_op jit(solution)/shard_map/ppermute | solution.py:26
  31.5 13.5 %collective-permute-start.6 = (f32[72,1,256]{2,1,0:T(1,128)}, f32[72,1,256]{2,1,0:T(1,128)}, u32[]{:S(2)}, u32[]{:S(2)}) collective-permute-start(f32[72,1,256]{2,1,0:T(1,128)} %get-tuple-element.59), channel_id=1, source_target_pairs={{28,0},{0,4},{4,8},{8,12},{12,16},{16,20},{20,24},{24,28},{29,1},{... | collective-permute-start | bytes 221192 | tf_op jit(solution)/shard_map/ppermute | solution.py:26
  32.4 12.6 %collective-permute-start.7 = (f32[72,1,256]{2,1,0:T(1,128)}, f32[72,1,256]{2,1,0:T(1,128)}, u32[]{:S(2)}, u32[]{:S(2)}) collective-permute-start(f32[72,1,256]{2,1,0:T(1,128)} %get-tuple-element.60), channel_id=1, source_target_pairs={{4,0},{8,4},{12,8},{16,12},{20,16},{24,20},{28,24},{0,28},{5,1},{9... | collective-permute-start | bytes 221192 | tf_op jit(solution)/shard_map/ppermute | solution.py:26
  47.9 15.0 %collective-permute-start.8 = (f32[72,1,256]{2,1,0:T(1,128)}, f32[72,1,256]{2,1,0:T(1,128)}, u32[]{:S(2)}, u32[]{:S(2)}) collective-permute-start(f32[72,1,256]{2,1,0:T(1,128)} %get-tuple-element.67), channel_id=1, source_target_pairs={{28,0},{0,4},{4,8},{8,12},{12,16},{16,20},{20,24},{24,28},{29,1},{... | collective-permute-start | bytes 221192 | tf_op jit(solution)/shard_map/ppermute | solution.py:26
  48.6 14.4 %collective-permute-start.9 = (f32[72,1,256]{2,1,0:T(1,128)}, f32[72,1,256]{2,1,0:T(1,128)}, u32[]{:S(2)}, u32[]{:S(2)}) collective-permute-start(f32[72,1,256]{2,1,0:T(1,128)} %get-tuple-element.68), channel_id=1, source_target_pairs={{4,0},{8,4},{12,8},{16,12},{20,16},{24,20},{28,24},{0,28},{5,1},{9... | collective-permute-start | bytes 221192 | tf_op jit(solution)/shard_map/ppermute | solution.py:26
  50.7 42.9 %collective-permute-start.10 = (bf16[8,32,2048]{2,1,0:T(8,128)(2,1)}, bf16[8,32,2048]{2,1,0:T(8,128)(2,1)}, u32[]{:S(2)}, u32[]{:S(2)}) collective-permute-start(bf16[8,32,2048]{2,1,0:T(8,128)(2,1)} %dynamic-slice_bitcast_fusion.1), channel_id=1, source_target_pairs={{0,1},{1,0},{2,3},{3,2},{4,5},{5,4},{6,7},{7,6},{8,9},{9,8},{10,11... | collective-permute-start | bytes 3145736 | tf_op jit(solution)/shard_map/ppermute | solution.py:30
  65.9 18.3 %collective-permute-start.13 = (bf16[64,2048]{1,0:T(8,128)(2,1)S(1)}, bf16[64,2048]{1,0:T(8,128)(2,1)S(1)}, u32[]{:S(2)}, u32[]{:S(2)}) collective-permute-start(bf16[64,2048]{1,0:T(8,128)(2,1)S(1)} %get-tuple-element.73), channel_id=1, source_target_pairs={{0,3},{1,2},{2,1},{3,0},{4,7},{5,6},{6,5},{7,4},{8,11},{9,10},{10,... | collective-permute-start | bytes 786440 | tf_op jit(solution)/shard_map/ppermute | solution.py:30
  68.4 24.8 %collective-permute-start.11 = (bf16[64,2048]{1,0:T(8,128)(2,1)S(1)}, bf16[64,2048]{1,0:T(8,128)(2,1)S(1)}, u32[]{:S(2)}, u32[]{:S(2)}) collective-permute-start(bf16[64,2048]{1,0:T(8,128)(2,1)S(1)} %get-tuple-element.73), channel_id=1, source_target_pairs={{0,1},{1,0},{2,3},{3,2},{4,5},{5,4},{6,7},{7,6},{8,9},{9,8},{10,11... | collective-permute-start | bytes 786440 | tf_op jit(solution)/shard_map/ppermute | solution.py:30
  68.4 23.9 %collective-permute-start.12 = (bf16[64,2048]{1,0:T(8,128)(2,1)S(1)}, bf16[64,2048]{1,0:T(8,128)(2,1)S(1)}, u32[]{:S(2)}, u32[]{:S(2)}) collective-permute-start(bf16[64,2048]{1,0:T(8,128)(2,1)S(1)} %get-tuple-element.72), channel_id=1, source_target_pairs={{0,2},{1,3},{2,0},{3,1},{4,6},{5,7},{6,4},{7,5},{8,10},{9,11},{10,... | collective-permute-start | bytes 786440 | tf_op jit(solution)/shard_map/ppermute | solution.py:30
  100.5 10.0 %collective-permute-start.14 = (bf16[8,2,32,256]{3,2,0,1:T(8,128)(2,1)S(1)}, bf16[8,2,32,256]{3,2,0,1:T(8,128)(2,1)S(1)}, u32[]{:S(2)}, u32[]{:S(2)}) collective-permute-start(bf16[8,2,32,256]{3,2,0,1:T(8,128)(2,1)S(1)} %maximum_maximum_fusion), channel_id=1, source_target_pairs={{0,1},{1,0},{2,3},{3,2},{4,5},{5,4},{6,7},{7,6},{8,9},{9,8},{10,11... | collective-permute-start | bytes 786440 | tf_op jit(solution)/shard_map/ppermute | solution.py:30
  110.9 5.2 %collective-permute-start.15 = (bf16[2,32,256]{2,1,0:T(8,128)(2,1)S(1)}, bf16[2,32,256]{2,1,0:T(8,128)(2,1)S(1)}, u32[]{:S(2)}, u32[]{:S(2)}) collective-permute-start(bf16[2,32,256]{2,1,0:T(8,128)(2,1)S(1)} %get-tuple-element.81), channel_id=1, source_target_pairs={{16,0},{20,4},{24,8},{28,12},{0,16},{4,20},{8,24},{12,28},{17,1},{... | collective-permute-start | bytes 98312 | tf_op jit(solution)/shard_map/ppermute | solution.py:26
  111.2 25.5 %collective-permute-start.22 = (bf16[8,32,2048]{2,1,0:T(8,128)(2,1)S(1)}, bf16[8,32,2048]{2,1,0:T(8,128)(2,1)S(1)}, u32[]{:S(2)}, u32[]{:S(2)}) collective-permute-start(bf16[8,32,2048]{2,1,0:T(8,128)(2,1)S(1)} %dynamic-slice_bitcast_fusion), channel_id=1, source_target_pairs={{0,1},{1,0},{2,3},{3,2},{4,5},{5,4},{6,7},{7,6},{8,9},{9,8},{10,11... | collective-permute-start | bytes 3145736 | tf_op jit(solution)/shard_map/ppermute | solution.py:30
  113.6 4.2 %collective-permute-start.16 = (bf16[2,32,256]{2,1,0:T(8,128)(2,1)S(1)}, bf16[2,32,256]{2,1,0:T(8,128)(2,1)S(1)}, u32[]{:S(2)}, u32[]{:S(2)}) collective-permute-start(bf16[2,32,256]{2,1,0:T(8,128)(2,1)S(1)} %get-tuple-element.80), channel_id=1, source_target_pairs={{12,0},{16,4},{20,8},{24,12},{28,16},{0,20},{4,24},{8,28},{13,1},{... | collective-permute-start | bytes 98312 | tf_op jit(solution)/shard_map/ppermute | solution.py:26
  113.6 5.2 %collective-permute-start.17 = (bf16[2,32,256]{2,1,0:T(8,128)(2,1)S(1)}, bf16[2,32,256]{2,1,0:T(8,128)(2,1)S(1)}, u32[]{:S(2)}, u32[]{:S(2)}) collective-permute-start(bf16[2,32,256]{2,1,0:T(8,128)(2,1)S(1)} %get-tuple-element.79), channel_id=1, source_target_pairs={{8,0},{12,4},{16,8},{20,12},{24,16},{28,20},{0,24},{4,28},{9,1},{1... | collective-permute-start | bytes 98312 | tf_op jit(solution)/shard_map/ppermute | solution.py:26
  113.6 6.8 %collective-permute-start.18 = (bf16[2,32,256]{2,1,0:T(8,128)(2,1)S(1)}, bf16[2,32,256]{2,1,0:T(8,128)(2,1)S(1)}, u32[]{:S(2)}, u32[]{:S(2)}) collective-permute-start(bf16[2,32,256]{2,1,0:T(8,128)(2,1)S(1)} %get-tuple-element.78), channel_id=1, source_target_pairs={{4,0},{8,4},{12,8},{16,12},{20,16},{24,20},{28,24},{0,28},{5,1},{9... | collective-permute-start | bytes 98312 | tf_op jit(solution)/shard_map/ppermute | solution.py:26
  116.1 4.3 %collective-permute-start.19 = (bf16[2,32,256]{2,1,0:T(8,128)(2,1)S(1)}, bf16[2,32,256]{2,1,0:T(8,128)(2,1)S(1)}, u32[]{:S(2)}, u32[]{:S(2)}) collective-permute-start(bf16[2,32,256]{2,1,0:T(8,128)(2,1)S(1)} %get-tuple-element.77), channel_id=1, source_target_pairs={{28,0},{0,4},{4,8},{8,12},{12,16},{16,20},{20,24},{24,28},{29,1},{... | collective-permute-start | bytes 98312 | tf_op jit(solution)/shard_map/ppermute | solution.py:26
  117.8 4.3 %collective-permute-start.20 = (bf16[2,32,256]{2,1,0:T(8,128)(2,1)S(1)}, bf16[2,32,256]{2,1,0:T(8,128)(2,1)S(1)}, u32[]{:S(2)}, u32[]{:S(2)}) collective-permute-start(bf16[2,32,256]{2,1,0:T(8,128)(2,1)S(1)} %get-tuple-element.82), channel_id=1, source_target_pairs={{24,0},{28,4},{0,8},{4,12},{8,16},{12,20},{16,24},{20,28},{25,1},{... | collective-permute-start | bytes 98312 | tf_op jit(solution)/shard_map/ppermute | solution.py:26
  137.9 11.3 %collective-permute-start.25 = (bf16[64,2048]{1,0:T(8,128)(2,1)}, bf16[64,2048]{1,0:T(8,128)(2,1)}, u32[]{:S(2)}, u32[]{:S(2)}) collective-permute-start(bf16[64,2048]{1,0:T(8,128)(2,1)} %fusion.7), channel_id=1, source_target_pairs={{0,3},{1,2},{2,1},{3,0},{4,7},{5,6},{6,5},{7,4},{8,11},{9,10},{10,... | collective-permute-start | bytes 786440 | tf_op jit(solution)/shard_map/ppermute | solution.py:30
  140.3 13.7 %collective-permute-start.24 = (bf16[64,2048]{1,0:T(8,128)(2,1)}, bf16[64,2048]{1,0:T(8,128)(2,1)}, u32[]{:S(2)}, u32[]{:S(2)}) collective-permute-start(bf16[64,2048]{1,0:T(8,128)(2,1)} %fusion.6), channel_id=1, source_target_pairs={{0,1},{1,0},{2,3},{3,2},{4,5},{5,4},{6,7},{7,6},{8,9},{9,8},{10,11... | collective-permute-start | bytes 786440 | tf_op jit(solution)/shard_map/ppermute | solution.py:30
  142.1 21.2 %collective-permute-start.23 = (bf16[64,2048]{1,0:T(8,128)(2,1)}, bf16[64,2048]{1,0:T(8,128)(2,1)}, u32[]{:S(2)}, u32[]{:S(2)}) collective-permute-start(bf16[64,2048]{1,0:T(8,128)(2,1)} %fusion.5), channel_id=1, source_target_pairs={{0,2},{1,3},{2,0},{3,1},{4,6},{5,7},{6,4},{7,5},{8,10},{9,11},{10,... | collective-permute-start | bytes 786440 | tf_op jit(solution)/shard_map/ppermute | solution.py:30
  (34 other events, 221.8 us)
where the time goes:
time: 167 us; the launch traced here: 166 us
  waiting for transfers between devices  68.6 us (41%)
  starting transfers between devices  33.1 us (20%)
  local copies, waits for them, and re-layouts  29.6 us (18%)
  matrix products  16.8 us (10%)
  Pallas kernels  15.3 us (9%)
  other arithmetic  1.76 us (1%)
    ppermute x9, waiting for transfers between devices, swapped(): lax.ppermute(block, axis, [(i, i ^ mask) for i in range(lax.axis_size(axi...  58.1 us
    unnamed x72, local copies, waits for them, and re-layouts  28.2 us
    ppermute x9, starting transfers between devices, swapped(): lax.ppermute(block, axis, [(i, i ^ mask) for i in range(lax.axis_size(axi...  15.9 us
    ppermute x15, starting transfers between devices, shifted(): return lax.ppermute(block, axis, route)  12.4 us
    dot_general x8, matrix products, per_device(): jnp.einsum('zt,krt->krz', block, factor, preferred_element_type=jnp.float32)  10.7 us
    pallas_call x4, Pallas kernels, sweep(): pl.pallas_call(functools.partial(step_kernel, table, step), in_specs=[VME...  9.42 us
    ppermute x2, waiting for transfers between devices, from_behind(): lax.ppermute(value, axis, [(source, source + steps) for source in range(i...  7.13 us
    ppermute x2, starting transfers between devices, from_behind(): lax.ppermute(value, axis, [(source, source + steps) for source in range(i...  4.78 us
  transfers between devices with their start and end apart: 26, of which 12 were waited for; matrix products, arithmetic and copies ran while one was open for 5% of the time, Pallas kernels for 7%

commit v1 on v0

--- a/solution.py
+++ b/solution.py
@@ -10,6 +10,8 @@
 LANES = 128
 GRANT = 4 << 20
 VMEM = pl.BlockSpec(memory_space=pltpu.VMEM)
+SMEM = pl.BlockSpec(memory_space=pltpu.SMEM)
+ANY = pl.BlockSpec(memory_space=pl.ANY)
 
 
 def from_behind(value, axis, steps):
@@ -43,7 +45,9 @@
     return order, at + 1
 
 
-def pack_kernel(table, innov_lo, innov_hi, cour_lo, cour_hi, diff_lo, diff_hi, sea_lo, sea_hi, down, up):
+def pack_kernel(table, place, innov_lo, innov_hi, cour_lo, cour_hi, diff_lo, diff_hi, sea_lo, sea_hi, down, up, placed):
+    for n in range(place.shape[0]):
+        placed[n] = place[n]
     depth = diff_lo.shape[0]
 
     def fill(out, innov, cour, diff, sea, level):
@@ -213,7 +217,7 @@
     finish(at + reach, acc, up_flux)
 
 
-def last_kernel(side, lam, low, high, out, mine, other, *rows):
+def last_kernel(place, lam, low, high, out, mine, other, *rows):
     levels, lon_cells, lat_cells = out.shape
     steps = (lam.shape[0] - levels) // 2
     x_at = lax.broadcasted_iota(jnp.int32, (lon_cells, lat_cells), 0)
@@ -230,7 +234,7 @@
 
     lax.fori_loop(0, levels, one, 0, unroll=4)
     half = lon_cells // 2
-    for part, start in ((mine, side[0] * half), (other, (1 - side[0]) * half)):
+    for part, start in ((mine, place[1] * half), (other, (1 - place[1]) * half)):
         for x in range(half):
             for c, lanes in enumerate(rows):
                 picked = lanes[pl.ds(start + x, levels, stride=lon_cells), :]
@@ -245,11 +249,11 @@
     to_west[...], to_east[...] = west_gain[...] * low_rows, east_gain[...] * high_rows
 
 
-def sweep(innovations, courant, diffusivity, sea, side):
+def pack(innovations, courant, diffusivity, sea, place):
     levels, lon_cells, lat_cells = diffusivity.shape
     steps = innovations.shape[0] - 1
     table, layers = halo_table(steps)
-    f32, bf16 = jnp.float32, jnp.bfloat16
+    bf16 = jnp.bfloat16
     end = levels // steps - 1
 
     def edges(shape, axis):
@@ -259,18 +263,27 @@
         return [pl.BlockSpec(tuple(block), at(index)) for index in (0, end)]
 
     message = jax.ShapeDtypeStruct((layers, lon_cells, lat_cells), bf16)
-    down, up = pl.pallas_call(
+    down, up, place = pl.pallas_call(
         functools.partial(pack_kernel, table),
         grid=(1,),
-        in_specs=edges(innovations.shape, 1)
+        in_specs=[SMEM]
+        + edges(innovations.shape, 1)
         + edges(courant.shape, 1)
         + edges(diffusivity.shape, 0)
         + edges(sea.shape, 0),
-        out_shape=[message, message],
-        out_specs=[VMEM, VMEM],
+        out_shape=[message, message, jax.ShapeDtypeStruct(place.shape, place.dtype)],
+        out_specs=[VMEM, VMEM, SMEM],
         compiler_params=pltpu.CompilerParams(vmem_limit_bytes=GRANT),
         cost_estimate=pl.CostEstimate(flops=0, bytes_accessed=1 << 20, transcendentals=0),
-    )(innovations, innovations, courant, courant, diffusivity, diffusivity, sea, sea)
+    )(place, innovations, innovations, courant, courant, diffusivity, diffusivity, sea, sea)
+    return down, up, place
+
+
+def sweep(innovations, courant, diffusivity, sea, down, up, place):
+    levels, lon_cells, lat_cells = diffusivity.shape
+    steps = innovations.shape[0] - 1
+    table, _ = halo_table(steps)
+    f32, bf16 = jnp.float32, jnp.bfloat16
     before = from_behind(down, "depth", 1)
     after = from_behind(up, "depth", -1)
     row = jax.ShapeDtypeStruct((levels + 2 * steps, 1, lat_cells), f32)
@@ -310,85 +323,207 @@
     half = jax.ShapeDtypeStruct((levels, lon_cells * lat_cells // 2), bf16)
     return pl.pallas_call(
         last_kernel,
-        in_specs=[pl.BlockSpec(memory_space=pltpu.SMEM)] + [VMEM] * 3,
+        in_specs=[SMEM] + [VMEM] * 3,
         out_shape=[jax.ShapeDtypeStruct((levels, lon_cells, lat_cells), f32), half, half],
         out_specs=[VMEM] * 3,
         scratch_shapes=[pltpu.VMEM((levels * lon_cells, LANES), f32)] * (lat_cells // LANES),
         compiler_params=pltpu.CompilerParams(vmem_limit_bytes=GRANT),
         cost_estimate=pl.CostEstimate(flops=0, bytes_accessed=3 << 20, transcendentals=0),
-    )(side.reshape(1), out, low, high)
+    )(place, out, low, high)
+
+
+def halves_kernel(place, left, right, left_mine, left_other, right_mine, right_other, *scratch):
+    half = left_mine.shape[2]
+    side = place[1]
+    vmem, sems = scratch
+    jobs = []
+    for source, mine, other in ((left, left_mine, left_other), (right, right_mine, right_other)):
+        jobs.append((source, other, 1 - side))
+        jobs.append((source, mine, side))
+    loads, stores = [], []
+    for n, (source, target, which) in enumerate(jobs):
+        window = source.at[0, :, :, pl.ds(pl.multiple_of(which * half, half), half)]
+        loads.append(pltpu.make_async_copy(window, vmem.at[n], sems.at[n]))
+        loads[-1].start()
+        stores.append(pltpu.make_async_copy(vmem.at[n], target, sems.at[len(jobs) + n]))
+    for load, store in zip(loads, stores):
+        load.wait()
+        store.start()
+    for store in stores:
+        store.wait()
+
+
+def against(a, b):
+    return lax.dot_general(a, b, (((1,), (1,)), ((), ())), preferred_element_type=jnp.float32)
+
+
+def rows_kernel(left_mine, left_pair, first, second, kept, sent):
+    for c, factor in enumerate((left_mine, left_pair)):
+        parts = [against(factor[...], block[...]) for block in (first, second)]
+        kept[c] = jnp.concatenate(parts, 1)
+        sent[1 - c] = jnp.concatenate(parts[::-1], 1).astype(jnp.bfloat16)
+
+
+def mask_kernel(slots, place, ranks, kept, arrived, *out):
+    rows = kept.shape[1] // slots
+    for c in range(2):
+        owner = place[0] if c == 0 else place[0] + 1 - 2 * place[1]
+        for k in range(slots):
+            at = slice(k * rows, (k + 1) * rows)
+            value = kept[c, at, :] + arrived[c, at, :].astype(jnp.float32)
+            row = lax.broadcasted_iota(jnp.int32, value.shape, 0) + owner * rows
+            value = jnp.where(row < ranks[0, k], value, 0.0).astype(jnp.bfloat16)
+            if len(out) > 1:
+                out[k][c] = value
+            else:
+                count = out[0].shape[0]
+                out[0][lax.rem(place[2] + (k - slots // 2 + count), count), c] = value
+
+
+def columns_kernel(slots, wide, place, right_mine, right_pair, *rest):
+    received, out = rest[:-2], rest[-2:]
+    count = received[0].shape[0]
+    total = None
+    for c, factor in enumerate((right_mine, right_pair)):
+        for k in range(slots):
+            if len(received) > 1:
+                coeff = received[k][c]
+            else:
+                coeff = received[0][lax.rem(place[2] + (count + slots // 2 - k), count), c]
+            coeffs = [coeff] if k == 0 and c == 0 else coeffs + [coeff]
+    stacked = jnp.concatenate(coeffs, 0)
+    rows = right_mine.shape[0]
+    lead = (((0,), (0,)), ((), ()))
+    for at in range(0, right_mine.shape[1], wide):
+        lanes = slice(at, at + wide)
+        total = lax.dot_general(stacked[:rows], right_mine[:, lanes], lead, preferred_element_type=jnp.float32)
+        total = total + lax.dot_general(stacked[rows:], right_pair[:, lanes], lead, preferred_element_type=jnp.float32)
+        levels = out[0].shape[0]
+        out[0][:, lanes] = total[:levels].astype(out[0].dtype)
+        out[1][:, lanes] = total[levels:].astype(out[1].dtype)
+
+
+def join_kernel(place, own, arrived1, arrived2, arrived3, out, *rows):
+    levels, lon_cells, lat_cells = out.shape
+    half = lon_cells // 2
+    f32 = jnp.float32
+    for x in range(half):
+        for c, lanes in enumerate(rows):
+            at = x * lat_cells + c * LANES
+            cols = slice(at, at + LANES)
+            mine = own[:, cols] + arrived2[:, cols].astype(f32)
+            other = arrived1[:, cols].astype(f32) + arrived3[:, cols].astype(f32)
+            lanes[pl.ds(place[1] * half + x, levels, stride=lon_cells), :] = mine
+            lanes[pl.ds((1 - place[1]) * half + x, levels, stride=lon_cells), :] = other
+
+    def one(z, carry):
+        at = pl.multiple_of(z * lon_cells, lon_cells)
+        for c, lanes in enumerate(rows):
+            out[z, :, c * LANES : (c + 1) * LANES] = lanes[pl.ds(at, lon_cells), :]
+        return carry
+
+    lax.fori_loop(0, levels, one, 0, unroll=4)
+
+
+def call(kernel, operands, in_specs, outs, grant=GRANT, flops=0, moved=1 << 20, scratch=()):
+    return pl.pallas_call(
+        kernel,
+        in_specs=in_specs,
+        out_shape=[jax.ShapeDtypeStruct(*o[:2]) for o in outs],
+        out_specs=[o[2] if len(o) > 2 else VMEM for o in outs],
+        scratch_shapes=list(scratch),
+        compiler_params=pltpu.CompilerParams(vmem_limit_bytes=grant),
+        cost_estimate=pl.CostEstimate(flops=flops, bytes_accessed=moved, transcendentals=0),
+    )(*operands)
 
 
 def per_device(
     innovations, courant, diffusivity, sea_bricks, tile_ranks, row_factors, column_factors
 ):
-    levels_here, lon_cells, lat_cells = diffusivity.shape
+    levels, lon_cells, lat_cells = diffusivity.shape
     tile_cols = lon_cells * lat_cells
     half = tile_cols // 2
-    blocks_row = tile_ranks.shape[1]
+    slots = tile_ranks.shape[1]
     count = lax.axis_size("depth")
+    lon_count = lax.axis_size("lon")
+    f32, bf16 = jnp.float32, jnp.bfloat16
     me = lax.axis_index("depth")
-    side = me % 2
-    left = row_factors[0].transpose(0, 2, 1)
-    right = column_factors[0].transpose(0, 2, 1)
-    width = left.shape[1]
-
-    def split(array, axis):
-        mine = lax.dynamic_slice_in_dim(array, side * half, half, axis)
-        other = lax.dynamic_slice_in_dim(array, (1 - side) * half, half, axis)
-        return mine, other
-
-    left_mine, left_other = split(left, 2)
-    right_mine, right_other = split(right, 2)
-
-    sea = sea_bricks.astype(jnp.float32)
-    sea = jnp.broadcast_to(sea[:, :, :, None], (levels_here, 1, lat_cells // 2, 2)).reshape(
-        levels_here, 1, lat_cells
+    place = jnp.stack([me, me % 2, lax.axis_index("lon")]).astype(jnp.int32)
+    left = row_factors.transpose(0, 1, 3, 2)
+    right = column_factors.transpose(0, 1, 3, 2)
+    width = left.shape[2]
+    rows = slots * width
+
+    sea = sea_bricks.astype(f32)
+    sea = jnp.broadcast_to(sea[:, :, :, None], (levels, 1, lat_cells // 2, 2)).reshape(levels, 1, lat_cells)
+    down, up, place = pack(innovations, courant, diffusivity, sea, place)
+    part = (slots, width, half)
+    left_mine, left_other, right_mine, right_other = call(
+        halves_kernel,
+        (place, left, right),
+        [SMEM, ANY, ANY],
+        [(part, bf16, ANY)] * 4,
+        grant=8 << 20,
+        moved=8 << 20,
+        scratch=[pltpu.VMEM((4, slots, width, half), bf16), pltpu.SemaphoreType.DMA((8,))],
     )
-    lam, lam_mine, lam_other = sweep(innovations, courant, diffusivity, sea, side)
     left_pair = swapped(left_other, "depth", 1)
     right_pair = swapped(right_other, "depth", 1)
-    blocks = [lam_mine]
-    for mask in range(1, count):
-        blocks.append(swapped(lam_other if mask % 2 else lam_mine, "depth", mask))
-    partial = [
-        [
-            jnp.einsum("zt,krt->krz", block, factor, preferred_element_type=jnp.float32)
-            for factor in (left_mine, left_pair)
-        ]
-        for block in blocks
-    ]
-    sent = jnp.concatenate(
-        [jnp.stack([partial[s ^ 1][1], partial[s ^ 1][0]], 1) for s in range(count)], 3
-    ).astype(jnp.bfloat16)
-    kept = jnp.concatenate([jnp.stack(partial[s], 1) for s in range(count)], 3)
-    coeff = kept + swapped(sent, "depth", 1).astype(jnp.float32)
-    ranks = tile_ranks[0]
-    owner = jnp.stack([me, me ^ 1])
-    columns = owner[:, None] * width + jnp.arange(width, dtype=jnp.int32)[None, :]
-    keep = columns[None] < ranks[:, None, None]
-    coeff = jnp.where(keep[:, :, :, None], coeff, 0.0).astype(jnp.bfloat16)
-    received = jnp.stack(
-        [shifted(coeff[k], "lon", k - blocks_row // 2) for k in range(blocks_row)], 0
+    lam, lam_mine, lam_other = sweep(innovations, courant, diffusivity, sea, down, up, place)
+    left_mine, left_pair, right_mine, right_pair = (
+        a.reshape(rows, half) for a in (left_mine, left_pair, right_mine, right_pair)
     )
-    sums = [
-        jnp.einsum("krz,krt->zt", levels[:, 0], right_mine, preferred_element_type=jnp.float32)
-        + jnp.einsum("krz,krt->zt", levels[:, 1], right_pair, preferred_element_type=jnp.float32)
-        for levels in jnp.split(received, count, 3)
-    ]
-    arrived = [
-        swapped(sums[mask].astype(jnp.bfloat16), "depth", mask) for mask in range(1, count)
-    ]
-    grad_mine = sums[0]
-    for mask in range(2, count, 2):
-        grad_mine = grad_mine + arrived[mask - 1].astype(jnp.float32)
-    grad_other = arrived[0].astype(jnp.float32)
-    for mask in range(3, count, 2):
-        grad_other = grad_other + arrived[mask - 1].astype(jnp.float32)
-    low = jnp.where(side == 0, grad_mine, grad_other)
-    high = jnp.where(side == 0, grad_other, grad_mine)
-    gradient = jnp.concatenate([low, high], 1)
-    return (lam, gradient.reshape(levels_here, lon_cells, lat_cells))
+    blocks = {0: lam_mine}
+    for mask in [1] + list(range(count - 1, 1, -1)):
+        blocks[mask] = swapped(lam_other if mask % 2 else lam_mine, "depth", mask)
+    arrived, own = {}, None
+    for stage in range(0, count, 2):
+        pair = (2, rows, 2 * levels)
+        kept, sent = call(
+            rows_kernel,
+            (left_mine, left_pair, blocks[stage], blocks[stage + 1]),
+            [VMEM] * 4,
+            [(pair, f32), (pair, bf16)],
+            flops=8 * rows * half * levels,
+            moved=3 << 20,
+        )
+        other = swapped(sent, "depth", 1)
+        grouped = lon_count == slots
+        slot = (2, width, 2 * levels)
+        outs = [((lon_count,) + slot, bf16)] if grouped else [(slot, bf16)] * slots
+        coeff = call(
+            functools.partial(mask_kernel, slots),
+            (place, tile_ranks, kept, other),
+            [SMEM, SMEM, VMEM, VMEM],
+            outs,
+        )
+        if grouped:
+            received = [lax.all_to_all(coeff[0], "lon", 0, 0, tiled=True)]
+        else:
+            received = [shifted(coeff[k], "lon", k - slots // 2) for k in range(slots)]
+        block = (levels, half)
+        first, second = call(
+            functools.partial(columns_kernel, slots, 4 * LANES),
+            (place, right_mine, right_pair, *received),
+            [SMEM] + [VMEM] * (2 + len(received)),
+            [(block, bf16 if stage else f32), (block, bf16)],
+            flops=8 * rows * half * levels,
+            moved=3 << 20,
+        )
+        if stage:
+            arrived[stage] = swapped(first, "depth", stage)
+        else:
+            own = first
+        arrived[stage + 1] = swapped(second, "depth", stage + 1)
+    (gradient,) = call(
+        join_kernel,
+        (place, own, *(arrived[mask] for mask in range(1, count))),
+        [SMEM] + [VMEM] * count,
+        [((levels, lon_cells, lat_cells), f32)],
+        scratch=[pltpu.VMEM((levels * lon_cells, LANES), f32)] * (lat_cells // LANES),
+        moved=4 << 20,
+    )
+    return (lam, gradient)
 
 
 def solution(mesh):

time: 167 us -> 143 us (0.86)
  the two profiles are of different devices: /device:TPU:6 before, /device:TPU:0 now
where the time goes in v1:
time: 143 us; the launch traced here: 140 us
  waiting for transfers between devices  65.7 us (46%)
  starting transfers between devices  40.6 us (28%)
  Pallas kernels  25.5 us (18%)
  local copies, waits for them, and re-layouts  6.91 us (5%)
    ppermute x10, waiting for transfers between devices, swapped(): lax.ppermute(block, axis, [(i, i ^ mask) for i in range(lax.axis_size(axi...  35.7 us
    ppermute x2, waiting for transfers between devices, from_behind(): lax.ppermute(value, axis, [(source, source + steps) for source in range(i...  21.3 us
    ppermute x10, starting transfers between devices, swapped(): lax.ppermute(block, axis, [(i, i ^ mask) for i in range(lax.axis_size(axi...  19.8 us
    pallas_call x8, Pallas kernels, call(): pl.pallas_call(kernel, in_specs=in_specs, out_shape=[jax.ShapeDtypeStruct...  11.5 us
    ppermute x8, starting transfers between devices, shifted(): return lax.ppermute(block, axis, route)  10.8 us
    pallas_call x4, Pallas kernels, sweep(): pl.pallas_call(functools.partial(step_kernel, table, step), in_specs=[VME...  9.55 us
    all_to_all x2, waiting for transfers between devices, per_device(): received = [lax.all_to_all(coeff[0], 'lon', 0, 0, tiled=True)]  8.48 us
    all_to_all x2, starting transfers between devices, per_device(): received = [lax.all_to_all(coeff[0], 'lon', 0, 0, tiled=True)]  6.74 us
  transfers between devices with their start and end apart: 22, of which 9 were waited for; matrix products, arithmetic and copies ran while one was open for 0% of the time, Pallas kernels for 14%

profile of v1, /device:TPU:0, one launch (start us, length us, event | category | flops | bytes accessed | tf_op | source)
XLA Modules:
  0.0 140.5 jit_solution(12055273984581951729)
XLA Ops:
  1.8 2.5 %copy-done = f32[5,64,16,256]{3,2,1,0:T(8,128)S(1)} copy-done((f32[5,64,16,256]{3,2,1,0:T(8,128)S(1)}, f32[5,64,16,256]{3,2,1,0:T(8,128)}, u32[]{:S(2)}) %copy-start) | copy-done | bytes 5242904
  4.2 1.9 %copy-done.2 = f32[3,64,16,256]{3,2,1,0:T(8,128)S(1)} copy-done((f32[3,64,16,256]{3,2,1,0:T(8,128)S(1)}, f32[3,64,16,256]{3,2,1,0:T(8,128)}, u32[]{:S(2)}) %copy-start.2) | copy-done | bytes 3145752
  9.6 2.2 %shard_map.97 = (bf16[8,32,2048]{2,1,0:T(8,128)(2,1)S(1)}, bf16[8,32,2048]{2,1,0:T(8,128)(2,1)S(1)}, bf16[8,32,2048]{2,1,0:T(8,128)(2,1)S(1)}, bf16[8,32,2048]{2,1,0:T(8,128)(2,1)}) custom-call(s32[3]{0:T(128)S(1)} %get-tuple-element.51.place, bf16[1,8,32,4096]{3,2,1,0:T(8,128)(2,1)S(1)} %bitcast.19, bf16[1,8,32,4096]{3,2,1,0:T(8,128)(2,1)S(1)} %bitcast.20), custom_call_target="tpu_custom_call" | custom-call | bytes 8388608 | tf_op jit(solution)/shard_map/pallas_call | solution.py:429
  11.8 3.1 %collective-permute-start.11 = (bf16[8,32,2048]{2,1,0:T(8,128)(2,1)S(1)}, bf16[8,32,2048]{2,1,0:T(8,128)(2,1)S(1)}, u32[]{:S(2)}, u32[]{:S(2)}) collective-permute-start(bf16[8,32,2048]{2,1,0:T(8,128)(2,1)S(1)} %get-tuple-element.89), channel_id=1, source_target_pairs={{0,1},{1,0},{2,3},{3,2},{4,5},{5,4},{6,7},{7,6},{8,9},{9,8},{10,11... | collective-permute-start | bytes 3145736 | tf_op jit(solution)/shard_map/ppermute | solution.py:32
  14.9 1.9 %collective-permute-start = (bf16[25,16,256]{2,1,0:T(8,128)(2,1)S(1)}, bf16[25,16,256]{2,1,0:T(8,128)(2,1)S(1)}, u32[]{:S(2)}, u32[]{:S(2)}) collective-permute-start(bf16[25,16,256]{2,1,0:T(8,128)(2,1)S(1)} %get-tuple-element.52), channel_id=1, source_target_pairs={{0,1},{1,2},{2,3},{4,5},{5,6},{6,7},{8,9},{9,10},{10,11},{12,13},{... | collective-permute-start | bytes 614408 | tf_op jit(solution)/shard_map/ppermute | solution.py:20
  18.1 3.8 %collective-permute-start.10 = (bf16[8,32,2048]{2,1,0:T(8,128)(2,1)}, bf16[8,32,2048]{2,1,0:T(8,128)(2,1)S(1)}, u32[]{:S(2)}, u32[]{:S(2)}) collective-permute-start(bf16[8,32,2048]{2,1,0:T(8,128)(2,1)} %get-tuple-element.87), channel_id=1, source_target_pairs={{0,1},{1,0},{2,3},{3,2},{4,5},{5,4},{6,7},{7,6},{8,9},{9,8},{10,11... | collective-permute-start | bytes 3145736 | tf_op jit(solution)/shard_map/ppermute | solution.py:32
  21.9 20.9 %collective-permute-done.before = bf16[25,16,256]{2,1,0:T(8,128)(2,1)S(1)} collective-permute-done((bf16[25,16,256]{2,1,0:T(8,128)(2,1)S(1)}, bf16[25,16,256]{2,1,0:T(8,128)(2,1)S(1)}, u32[]{:S(2)}, u32[]{:S(2)}) %collective-permute-start) | collective-permute-done | bytes 204832 | tf_op jit(solution)/shard_map/ppermute | solution.py:20
  43.7 2.6 %collective-permute-start.3 = (f32[72,1,256]{2,1,0:T(1,128)S(1)}, f32[72,1,256]{2,1,0:T(1,128)S(1)}, u32[]{:S(2)}, u32[]{:S(2)}) collective-permute-start(f32[72,1,256]{2,1,0:T(1,128)S(1)} %get-tuple-element.58), channel_id=1, source_target_pairs={{4,0},{8,4},{12,8},{16,12},{20,16},{24,20},{28,24},{0,28},{5,1},{9... | collective-permute-start | bytes 221192 | tf_op jit(solution)/shard_map/ppermute | solution.py:28
  46.3 2.4 %shard_map.88 = (f32[72,16,256]{2,1,0:T(8,128)S(1)}, f32[72,1,256]{2,1,0:T(1,128)S(1)}, f32[72,1,256]{2,1,0:T(1,128)S(1)}) custom-call(f32[5,64,16,256]{3,2,1,0:T(8,128)S(1)} %copy-done.1, f32[3,64,16,256]{3,2,1,0:T(8,128)S(1)} %copy-done.3, f32[64,16,256]{2,1,0:T(8,128)S(1)} %copy-done.5, f32[72,1,256]{2,1,0:T(1,128)S(1)} %get-tuple-element.54.sea_ext.low.high, ...), custom_call_target="tpu_custom_call" | custom-call | flops 10485760 | bytes 9437184 | tf_op jit(solution)/shard_map/pallas_call | solution.py:306
  51.6 2.4 %shard_map.90 = (f32[72,16,256]{2,1,0:T(8,128)S(1)}, f32[72,1,256]{2,1,0:T(1,128)S(1)}, f32[72,1,256]{2,1,0:T(1,128)S(1)}) custom-call(f32[5,64,16,256]{3,2,1,0:T(8,128)S(1)} %copy-done.1, f32[3,64,16,256]{3,2,1,0:T(8,128)S(1)} %copy-done.3, f32[64,16,256]{2,1,0:T(8,128)S(1)} %copy-done.5, f32[72,1,256]{2,1,0:T(1,128)S(1)} %get-tuple-element.54.sea_ext.low.high, ...), custom_call_target="tpu_custom_call" | custom-call | flops 10485760 | bytes 9437184 | tf_op jit(solution)/shard_map/pallas_call | solution.py:306
  56.9 2.4 %shard_map.92 = (f32[72,16,256]{2,1,0:T(8,128)S(1)}, f32[72,1,256]{2,1,0:T(1,128)S(1)}, f32[72,1,256]{2,1,0:T(1,128)S(1)}) custom-call(f32[5,64,16,256]{3,2,1,0:T(8,128)S(1)} %copy-done.1, f32[3,64,16,256]{3,2,1,0:T(8,128)S(1)} %copy-done.3, f32[64,16,256]{2,1,0:T(8,128)S(1)} %copy-done.5, f32[72,1,256]{2,1,0:T(1,128)S(1)} %get-tuple-element.54.sea_ext.low.high, ...), custom_call_target="tpu_custom_call" | custom-call | flops 10485760 | bytes 9437184 | tf_op jit(solution)/shard_map/pallas_call | solution.py:306
  62.2 2.3 %shard_map.94 = (f32[72,16,256]{2,1,0:T(8,128)S(1)}, f32[72,1,256]{2,1,0:T(1,128)S(1)}, f32[72,1,256]{2,1,0:T(1,128)S(1)}) custom-call(f32[5,64,16,256]{3,2,1,0:T(8,128)S(1)} %copy-done.1, f32[3,64,16,256]{3,2,1,0:T(8,128)S(1)} %copy-done.3, f32[64,16,256]{2,1,0:T(8,128)S(1)} %copy-done.5, f32[72,1,256]{2,1,0:T(1,128)S(1)} %get-tuple-element.54.sea_ext.low.high, ...), custom_call_target="tpu_custom_call" | custom-call | flops 10485760 | bytes 9437184 | tf_op jit(solution)/shard_map/pallas_call | solution.py:306
  65.6 1.7 %shard_map.96 = (f32[64,16,256]{2,1,0:T(8,128)}, bf16[64,2048]{1,0:T(8,128)(2,1)S(1)}, bf16[64,2048]{1,0:T(8,128)(2,1)S(1)}) custom-call(s32[3]{0:T(128)S(1)} %get-tuple-element.51.place, f32[72,16,256]{2,1,0:T(8,128)S(1)} %get-tuple-element.78.lam, f32[72,1,256]{2,1,0:T(1,128)S(1)} %get-tuple-element.83.low, f32[72,1,256]{2,1,0:T(1,128)S(1)} %get-tuple-element.84.high), custom_call_target="tpu_custom_call" | custom-call | bytes 3145728 | tf_op jit(solution)/shard_map/pallas_call | solution.py:324
  67.3 2.3 %collective-permute-start.12 = (bf16[64,2048]{1,0:T(8,128)(2,1)S(1)}, bf16[64,2048]{1,0:T(8,128)(2,1)S(1)}, u32[]{:S(2)}, u32[]{:S(2)}) collective-permute-start(bf16[64,2048]{1,0:T(8,128)(2,1)S(1)} %get-tuple-element.91), channel_id=1, source_target_pairs={{0,1},{1,0},{2,3},{3,2},{4,5},{5,4},{6,7},{7,6},{8,9},{9,8},{10,11... | collective-permute-start | bytes 786440 | tf_op jit(solution)/shard_map/ppermute | solution.py:32
  69.6 2.6 %collective-permute-start.15 = (bf16[64,2048]{1,0:T(8,128)(2,1)S(1)}, bf16[64,2048]{1,0:T(8,128)(2,1)S(1)}, u32[]{:S(2)}, u32[]{:S(2)}) collective-permute-start(bf16[64,2048]{1,0:T(8,128)(2,1)S(1)} %get-tuple-element.90.first), channel_id=1, source_target_pairs={{0,2},{1,3},{2,0},{3,1},{4,6},{5,7},{6,4},{7,5},{8,10},{9,11},{10,... | collective-permute-start | bytes 786440 | tf_op jit(solution)/shard_map/ppermute | solution.py:32
  72.2 9.3 %collective-permute-done.12.second = bf16[64,2048]{1,0:T(8,128)(2,1)S(1)} collective-permute-done((bf16[64,2048]{1,0:T(8,128)(2,1)S(1)}, bf16[64,2048]{1,0:T(8,128)(2,1)S(1)}, u32[]{:S(2)}, u32[]{:S(2)}) %collective-permute-start.12) | collective-permute-done | bytes 262176 | tf_op jit(solution)/shard_map/ppermute | solution.py:32
  82.8 8.1 %collective-permute-done.15.first = bf16[64,2048]{1,0:T(8,128)(2,1)S(1)} collective-permute-done((bf16[64,2048]{1,0:T(8,128)(2,1)S(1)}, bf16[64,2048]{1,0:T(8,128)(2,1)S(1)}, u32[]{:S(2)}, u32[]{:S(2)}) %collective-permute-start.15) | collective-permute-done | bytes 262176 | tf_op jit(solution)/shard_map/ppermute | solution.py:32
  92.2 5.2 %collective-permute-start.17 = (bf16[2,256,128]{2,1,0:T(8,128)(2,1)S(1)}, bf16[2,256,128]{2,1,0:T(8,128)(2,1)S(1)}, u32[]{:S(2)}, u32[]{:S(2)}) collective-permute-start(bf16[2,256,128]{2,1,0:T(8,128)(2,1)S(1)} %get-tuple-element.97), channel_id=1, source_target_pairs={{0,1},{1,0},{2,3},{3,2},{4,5},{5,4},{6,7},{7,6},{8,9},{9,8},{10,11... | collective-permute-start | bytes 393224 | tf_op jit(solution)/shard_map/ppermute | solution.py:32
  98.7 3.4 %all-to-all-start = ((bf16[8,2,32,128]{3,2,1,0:T(8,128)(2,1)}), bf16[8,2,32,128]{3,2,1,0:T(8,128)(2,1)S(1)}, u32[]{:S(2)}, u32[]{:S(2)}) async-start(bf16[8,2,32,128]{3,2,1,0:T(8,128)(2,1)} %shard_map.99), calls=%async_computation | async-start | bytes 262144 | tf_op jit(solution)/shard_map/all_to_all | solution.py:501
  103.3 4.2 %all-to-all-done.rest_0_ = bf16[8,2,32,128]{3,2,1,0:T(8,128)(2,1)S(1)} async-done(((bf16[8,2,32,128]{3,2,1,0:T(8,128)(2,1)}), bf16[8,2,32,128]{3,2,1,0:T(8,128)(2,1)S(1)}, u32[]{:S(2)}, u32[]{:S(2)}) %all-to-all-start) | async-done | bytes 131104 | tf_op jit(solution)/shard_map/all_to_all | solution.py:501
  107.5 3.4 %all-to-all-start.1 = ((bf16[8,2,32,128]{3,2,1,0:T(8,128)(2,1)}), bf16[8,2,32,128]{3,2,1,0:T(8,128)(2,1)S(1)}, u32[]{:S(2)}, u32[]{:S(2)}) async-start(bf16[8,2,32,128]{3,2,1,0:T(8,128)(2,1)} %shard_map.102), calls=%async_computation.1 | async-start | bytes 262144 | tf_op jit(solution)/shard_map/all_to_all | solution.py:501
  112.0 4.3 %all-to-all-done.1.rest_0_ = bf16[8,2,32,128]{3,2,1,0:T(8,128)(2,1)S(1)} async-done(((bf16[8,2,32,128]{3,2,1,0:T(8,128)(2,1)}), bf16[8,2,32,128]{3,2,1,0:T(8,128)(2,1)S(1)}, u32[]{:S(2)}, u32[]{:S(2)}) %all-to-all-start.1) | async-done | bytes 131104 | tf_op jit(solution)/shard_map/all_to_all | solution.py:501
  121.3 17.0 %collective-permute-done.18.arrived2 = bf16[64,2048]{1,0:T(8,128)(2,1)S(1)} collective-permute-done((bf16[64,2048]{1,0:T(8,128)(2,1)S(1)}, bf16[64,2048]{1,0:T(8,128)(2,1)S(1)}, u32[]{:S(2)}, u32[]{:S(2)}) %collective-permute-start.18) | collective-permute-done | bytes 262176 | tf_op jit(solution)/shard_map/ppermute | solution.py:32
  138.3 2.2 %shard_map.104 = f32[64,16,256]{2,1,0:T(8,128)} custom-call(s32[3]{0:T(128)S(1)} %get-tuple-element.51.place, f32[64,2048]{1,0:T(8,128)S(1)} %get-tuple-element.94.own, bf16[64,2048]{1,0:T(8,128)(2,1)S(1)} %collective-permute-done.14.arrived1, bf16[64,2048]{1,0:T(8,128)(2,1)S(1)} %collective-permute-done.18.arrived2, ...), custom_call_target="tpu_custom_call" | custom-call | bytes 4194304 | tf_op jit(solution)/shard_map/pallas_call | solution.py:429
  (62 shorter events, 27.5 us)
Async XLA Ops:
  7.4 35.9 %copy-start.1 = (f32[5,64,16,256]{3,2,1,0:T(8,128)S(1)}, f32[5,64,16,256]{3,2,1,0:T(8,128)}, u32[]{:S(2)}) copy-start(f32[5,64,16,256]{3,2,1,0:T(8,128)} %innov.9) | copy-start | bytes 15728644
  9.6 33.7 %copy-start.5 = (f32[64,16,256]{2,1,0:T(8,128)S(1)}, f32[64,16,256]{2,1,0:T(8,128)}, u32[]{:S(2)}) copy-start(f32[64,16,256]{2,1,0:T(8,128)} %diff.9) | copy-start | bytes 3145732
  11.8 69.6 %collective-permute-start.11 = (bf16[8,32,2048]{2,1,0:T(8,128)(2,1)S(1)}, bf16[8,32,2048]{2,1,0:T(8,128)(2,1)S(1)}, u32[]{:S(2)}, u32[]{:S(2)}) collective-permute-start(bf16[8,32,2048]{2,1,0:T(8,128)(2,1)S(1)} %get-tuple-element.89), channel_id=1, source_target_pairs={{0,1},{1,0},{2,3},{3,2},{4,5},{5,4},{6,7},{7,6},{8,9},{9,8},{10,11... | collective-permute-start | bytes 3145736 | tf_op jit(solution)/shard_map/ppermute | solution.py:32
  14.9 27.9 %collective-permute-start = (bf16[25,16,256]{2,1,0:T(8,128)(2,1)S(1)}, bf16[25,16,256]{2,1,0:T(8,128)(2,1)S(1)}, u32[]{:S(2)}, u32[]{:S(2)}) collective-permute-start(bf16[25,16,256]{2,1,0:T(8,128)(2,1)S(1)} %get-tuple-element.52), channel_id=1, source_target_pairs={{0,1},{1,2},{2,3},{4,5},{5,6},{6,7},{8,9},{9,10},{10,11},{12,13},{... | collective-permute-start | bytes 614408 | tf_op jit(solution)/shard_map/ppermute | solution.py:20
  16.8 26.5 %collective-permute-start.1 = (bf16[25,16,256]{2,1,0:T(8,128)(2,1)S(1)}, bf16[25,16,256]{2,1,0:T(8,128)(2,1)S(1)}, u32[]{:S(2)}, u32[]{:S(2)}) collective-permute-start(bf16[25,16,256]{2,1,0:T(8,128)(2,1)S(1)} %get-tuple-element.53), channel_id=1, source_target_pairs={{1,0},{2,1},{3,2},{5,4},{6,5},{7,6},{9,8},{10,9},{11,10},{13,12},{... | collective-permute-start | bytes 614408 | tf_op jit(solution)/shard_map/ppermute | solution.py:20
  18.1 92.8 %collective-permute-start.10 = (bf16[8,32,2048]{2,1,0:T(8,128)(2,1)}, bf16[8,32,2048]{2,1,0:T(8,128)(2,1)S(1)}, u32[]{:S(2)}, u32[]{:S(2)}) collective-permute-start(bf16[8,32,2048]{2,1,0:T(8,128)(2,1)} %get-tuple-element.87), channel_id=1, source_target_pairs={{0,1},{1,0},{2,3},{3,2},{4,5},{5,4},{6,7},{7,6},{8,9},{9,8},{10,11... | collective-permute-start | bytes 3145736 | tf_op jit(solution)/shard_map/ppermute | solution.py:32
  43.6 5.1 %collective-permute-start.2 = (f32[72,1,256]{2,1,0:T(1,128)S(1)}, f32[72,1,256]{2,1,0:T(1,128)S(1)}, u32[]{:S(2)}, u32[]{:S(2)}) collective-permute-start(f32[72,1,256]{2,1,0:T(1,128)S(1)} %get-tuple-element.57), channel_id=1, source_target_pairs={{28,0},{0,4},{4,8},{8,12},{12,16},{16,20},{20,24},{24,28},{29,1},{... | collective-permute-start | bytes 221192 | tf_op jit(solution)/shard_map/ppermute | solution.py:28
  43.7 5.1 %collective-permute-start.3 = (f32[72,1,256]{2,1,0:T(1,128)S(1)}, f32[72,1,256]{2,1,0:T(1,128)S(1)}, u32[]{:S(2)}, u32[]{:S(2)}) collective-permute-start(f32[72,1,256]{2,1,0:T(1,128)S(1)} %get-tuple-element.58), channel_id=1, source_target_pairs={{4,0},{8,4},{12,8},{16,12},{20,16},{24,20},{28,24},{0,28},{5,1},{9... | collective-permute-start | bytes 221192 | tf_op jit(solution)/shard_map/ppermute | solution.py:28
  48.9 5.1 %collective-permute-start.4 = (f32[72,1,256]{2,1,0:T(1,128)S(1)}, f32[72,1,256]{2,1,0:T(1,128)S(1)}, u32[]{:S(2)}, u32[]{:S(2)}) collective-permute-start(f32[72,1,256]{2,1,0:T(1,128)S(1)} %get-tuple-element.66), channel_id=1, source_target_pairs={{28,0},{0,4},{4,8},{8,12},{12,16},{16,20},{20,24},{24,28},{29,1},{... | collective-permute-start | bytes 221192 | tf_op jit(solution)/shard_map/ppermute | solution.py:28
  50.0 4.0 %collective-permute-start.5 = (f32[72,1,256]{2,1,0:T(1,128)S(1)}, f32[72,1,256]{2,1,0:T(1,128)S(1)}, u32[]{:S(2)}, u32[]{:S(2)}) collective-permute-start(f32[72,1,256]{2,1,0:T(1,128)S(1)} %get-tuple-element.67), channel_id=1, source_target_pairs={{4,0},{8,4},{12,8},{16,12},{20,16},{24,20},{28,24},{0,28},{5,1},{9... | collective-permute-start | bytes 221192 | tf_op jit(solution)/shard_map/ppermute | solution.py:28
  54.2 5.1 %collective-permute-start.6 = (f32[72,1,256]{2,1,0:T(1,128)S(1)}, f32[72,1,256]{2,1,0:T(1,128)S(1)}, u32[]{:S(2)}, u32[]{:S(2)}) collective-permute-start(f32[72,1,256]{2,1,0:T(1,128)S(1)} %get-tuple-element.73), channel_id=1, source_target_pairs={{28,0},{0,4},{4,8},{8,12},{12,16},{16,20},{20,24},{24,28},{29,1},{... | collective-permute-start | bytes 221192 | tf_op jit(solution)/shard_map/ppermute | solution.py:28
  55.3 4.1 %collective-permute-start.7 = (f32[72,1,256]{2,1,0:T(1,128)S(1)}, f32[72,1,256]{2,1,0:T(1,128)S(1)}, u32[]{:S(2)}, u32[]{:S(2)}) collective-permute-start(f32[72,1,256]{2,1,0:T(1,128)S(1)} %get-tuple-element.74), channel_id=1, source_target_pairs={{4,0},{8,4},{12,8},{16,12},{20,16},{24,20},{28,24},{0,28},{5,1},{9... | collective-permute-start | bytes 221192 | tf_op jit(solution)/shard_map/ppermute | solution.py:28
  59.5 5.2 %collective-permute-start.8 = (f32[72,1,256]{2,1,0:T(1,128)S(1)}, f32[72,1,256]{2,1,0:T(1,128)S(1)}, u32[]{:S(2)}, u32[]{:S(2)}) collective-permute-start(f32[72,1,256]{2,1,0:T(1,128)S(1)} %get-tuple-element.81), channel_id=1, source_target_pairs={{28,0},{0,4},{4,8},{8,12},{12,16},{16,20},{20,24},{24,28},{29,1},{... | collective-permute-start | bytes 221192 | tf_op jit(solution)/shard_map/ppermute | solution.py:28
  60.7 4.1 %collective-permute-start.9 = (f32[72,1,256]{2,1,0:T(1,128)S(1)}, f32[72,1,256]{2,1,0:T(1,128)S(1)}, u32[]{:S(2)}, u32[]{:S(2)}) collective-permute-start(f32[72,1,256]{2,1,0:T(1,128)S(1)} %get-tuple-element.82), channel_id=1, source_target_pairs={{4,0},{8,4},{12,8},{16,12},{20,16},{24,20},{28,24},{0,28},{5,1},{9... | collective-permute-start | bytes 221192 | tf_op jit(solution)/shard_map/ppermute | solution.py:28
  67.3 14.2 %collective-permute-start.12 = (bf16[64,2048]{1,0:T(8,128)(2,1)S(1)}, bf16[64,2048]{1,0:T(8,128)(2,1)S(1)}, u32[]{:S(2)}, u32[]{:S(2)}) collective-permute-start(bf16[64,2048]{1,0:T(8,128)(2,1)S(1)} %get-tuple-element.91), channel_id=1, source_target_pairs={{0,1},{1,0},{2,3},{3,2},{4,5},{5,4},{6,7},{7,6},{8,9},{9,8},{10,11... | collective-permute-start | bytes 786440 | tf_op jit(solution)/shard_map/ppermute | solution.py:32
  69.6 21.4 %collective-permute-start.15 = (bf16[64,2048]{1,0:T(8,128)(2,1)S(1)}, bf16[64,2048]{1,0:T(8,128)(2,1)S(1)}, u32[]{:S(2)}, u32[]{:S(2)}) collective-permute-start(bf16[64,2048]{1,0:T(8,128)(2,1)S(1)} %get-tuple-element.90.first), channel_id=1, source_target_pairs={{0,2},{1,3},{2,0},{3,1},{4,6},{5,7},{6,4},{7,5},{8,10},{9,11},{10,... | collective-permute-start | bytes 786440 | tf_op jit(solution)/shard_map/ppermute | solution.py:32
  72.2 18.8 %collective-permute-start.16 = (bf16[64,2048]{1,0:T(8,128)(2,1)S(1)}, bf16[64,2048]{1,0:T(8,128)(2,1)S(1)}, u32[]{:S(2)}, u32[]{:S(2)}) collective-permute-start(bf16[64,2048]{1,0:T(8,128)(2,1)S(1)} %get-tuple-element.91), channel_id=1, source_target_pairs={{0,3},{1,2},{2,1},{3,0},{4,7},{5,6},{6,5},{7,4},{8,11},{9,10},{10,... | collective-permute-start | bytes 786440 | tf_op jit(solution)/shard_map/ppermute | solution.py:32
  82.7 14.7 %collective-permute-start.13 = (bf16[2,256,128]{2,1,0:T(8,128)(2,1)S(1)}, bf16[2,256,128]{2,1,0:T(8,128)(2,1)S(1)}, u32[]{:S(2)}, u32[]{:S(2)}) collective-permute-start(bf16[2,256,128]{2,1,0:T(8,128)(2,1)S(1)} %get-tuple-element.93), channel_id=1, source_target_pairs={{0,1},{1,0},{2,3},{3,2},{4,5},{5,4},{6,7},{7,6},{8,9},{9,8},{10,11... | collective-permute-start | bytes 393224 | tf_op jit(solution)/shard_map/ppermute | solution.py:32
  92.2 9.9 %collective-permute-start.17 = (bf16[2,256,128]{2,1,0:T(8,128)(2,1)S(1)}, bf16[2,256,128]{2,1,0:T(8,128)(2,1)S(1)}, u32[]{:S(2)}, u32[]{:S(2)}) collective-permute-start(bf16[2,256,128]{2,1,0:T(8,128)(2,1)S(1)} %get-tuple-element.97), channel_id=1, source_target_pairs={{0,1},{1,0},{2,3},{3,2},{4,5},{5,4},{6,7},{7,6},{8,9},{9,8},{10,11... | collective-permute-start | bytes 393224 | tf_op jit(solution)/shard_map/ppermute | solution.py:32
  98.7 8.8 %all-to-all-start = ((bf16[8,2,32,128]{3,2,1,0:T(8,128)(2,1)}), bf16[8,2,32,128]{3,2,1,0:T(8,128)(2,1)S(1)}, u32[]{:S(2)}, u32[]{:S(2)}) async-start(bf16[8,2,32,128]{3,2,1,0:T(8,128)(2,1)} %shard_map.99), calls=%async_computation | async-start | bytes 262144 | tf_op jit(solution)/shard_map/all_to_all | solution.py:501
  107.5 8.8 %all-to-all-start.1 = ((bf16[8,2,32,128]{3,2,1,0:T(8,128)(2,1)}), bf16[8,2,32,128]{3,2,1,0:T(8,128)(2,1)S(1)}, u32[]{:S(2)}, u32[]{:S(2)}) async-start(bf16[8,2,32,128]{3,2,1,0:T(8,128)(2,1)} %shard_map.102), calls=%async_computation.1 | async-start | bytes 262144 | tf_op jit(solution)/shard_map/all_to_all | solution.py:501
  111.9 9.4 %collective-permute-start.14 = (bf16[64,2048]{1,0:T(8,128)(2,1)S(1)}, bf16[64,2048]{1,0:T(8,128)(2,1)S(1)}, u32[]{:S(2)}, u32[]{:S(2)}) collective-permute-start(bf16[64,2048]{1,0:T(8,128)(2,1)S(1)} %get-tuple-element.95), channel_id=1, source_target_pairs={{0,1},{1,0},{2,3},{3,2},{4,5},{5,4},{6,7},{7,6},{8,9},{9,8},{10,11... | collective-permute-start | bytes 786440 | tf_op jit(solution)/shard_map/ppermute | solution.py:32
  117.4 20.9 %collective-permute-start.18 = (bf16[64,2048]{1,0:T(8,128)(2,1)S(1)}, bf16[64,2048]{1,0:T(8,128)(2,1)S(1)}, u32[]{:S(2)}, u32[]{:S(2)}) collective-permute-start(bf16[64,2048]{1,0:T(8,128)(2,1)S(1)} %get-tuple-element.98), channel_id=1, source_target_pairs={{0,2},{1,3},{2,0},{3,1},{4,6},{5,7},{6,4},{7,5},{8,10},{9,11},{10,... | collective-permute-start | bytes 786440 | tf_op jit(solution)/shard_map/ppermute | solution.py:32
  118.5 19.8 %collective-permute-start.19 = (bf16[64,2048]{1,0:T(8,128)(2,1)S(1)}, bf16[64,2048]{1,0:T(8,128)(2,1)S(1)}, u32[]{:S(2)}, u32[]{:S(2)}) collective-permute-start(bf16[64,2048]{1,0:T(8,128)(2,1)S(1)} %get-tuple-element.99), channel_id=1, source_target_pairs={{0,3},{1,2},{2,1},{3,0},{4,7},{5,6},{6,5},{7,4},{8,11},{9,10},{10,... | collective-permute-start | bytes 786440 | tf_op jit(solution)/shard_map/ppermute | solution.py:32
  (7 other events, 59.2 us)

commit v2 on v1

--- a/solution.py
+++ b/solution.py
@@ -8,6 +8,7 @@
 
 UNROLL = 3
 LANES = 128
+PARTS = 4
 GRANT = 4 << 20
 VMEM = pl.BlockSpec(memory_space=pltpu.VMEM)
 SMEM = pl.BlockSpec(memory_space=pltpu.SMEM)
@@ -45,10 +46,21 @@
     return order, at + 1
 
 
-def pack_kernel(table, place, innov_lo, innov_hi, cour_lo, cour_hi, diff_lo, diff_hi, sea_lo, sea_hi, down, up, placed):
+def pack_kernel(table, place, bricks, innov_lo, innov_hi, cour_lo, cour_hi, diff_lo, diff_hi, down, up, sea, placed, rows):
     for n in range(place.shape[0]):
         placed[n] = place[n]
     depth = diff_lo.shape[0]
+    levels, _, count = bricks.shape
+    lat_cells = sea.shape[2]
+    for z in range(levels):
+        rows[z : z + 1] = bricks[z].astype(jnp.float32)
+    brick_at = lax.broadcasted_iota(jnp.int32, (count, lat_cells), 0)
+    cell_at = lax.broadcasted_iota(jnp.int32, (count, lat_cells), 1)
+    inside = (brick_at == cell_at // (lat_cells // count)).astype(jnp.bfloat16)
+    wide = jnp.dot(rows[...].astype(jnp.bfloat16), inside, preferred_element_type=jnp.float32)
+    for z in range(levels):
+        sea[z] = wide[z : z + 1]
+    sea_lo, sea_hi = sea, sea.at[pl.ds(levels - depth, depth)]
 
     def fill(out, innov, cour, diff, sea, level):
         for key, at in table.items():
@@ -217,15 +229,17 @@
     finish(at + reach, acc, up_flux)
 
 
-def last_kernel(place, lam, low, high, out, mine, other, *rows):
+def last_kernel(place, lam, sea_ext, out_low, out_high, west, east, out, mine, other, *rows):
     levels, lon_cells, lat_cells = out.shape
     steps = (lam.shape[0] - levels) // 2
     x_at = lax.broadcasted_iota(jnp.int32, (lon_cells, lat_cells), 0)
     first_x, last_x = x_at == 0, x_at == lon_cells - 1
 
     def one(z, carry):
-        value = jnp.where(first_x, low[z + steps], lam[z + steps])
-        value = jnp.where(last_x, high[z + steps], value)
+        at = z + steps
+        low = out_low[at] + sea_ext[at] * west[at]
+        high = out_high[at] + sea_ext[at] * east[at]
+        value = jnp.where(last_x, high, jnp.where(first_x, low, lam[at]))
         out[z] = value
         for c, lanes in enumerate(rows):
             at = pl.multiple_of(z * lon_cells, lon_cells)
@@ -249,11 +263,11 @@
     to_west[...], to_east[...] = west_gain[...] * low_rows, east_gain[...] * high_rows
 
 
-def pack(innovations, courant, diffusivity, sea, place):
+def pack(innovations, courant, diffusivity, bricks, place):
     levels, lon_cells, lat_cells = diffusivity.shape
     steps = innovations.shape[0] - 1
     table, layers = halo_table(steps)
-    bf16 = jnp.bfloat16
+    f32, bf16 = jnp.float32, jnp.bfloat16
     end = levels // steps - 1
 
     def edges(shape, axis):
@@ -263,20 +277,19 @@
         return [pl.BlockSpec(tuple(block), at(index)) for index in (0, end)]
 
     message = jax.ShapeDtypeStruct((layers, lon_cells, lat_cells), bf16)
-    down, up, place = pl.pallas_call(
+    down, up, sea, place = pl.pallas_call(
         functools.partial(pack_kernel, table),
         grid=(1,),
-        in_specs=[SMEM]
+        in_specs=[SMEM, VMEM]
         + edges(innovations.shape, 1)
         + edges(courant.shape, 1)
-        + edges(diffusivity.shape, 0)
-        + edges(sea.shape, 0),
-        out_shape=[message, message, jax.ShapeDtypeStruct(place.shape, place.dtype)],
-        out_specs=[VMEM, VMEM, SMEM],
-        compiler_params=pltpu.CompilerParams(vmem_limit_bytes=GRANT),
+        + edges(diffusivity.shape, 0),
+        out_shape=[message, message, jax.ShapeDtypeStruct((levels, 1, lat_cells), f32), jax.ShapeDtypeStruct(place.shape, place.dtype)],
+        out_specs=[VMEM, VMEM, VMEM, SMEM],
+        scratch_shapes=[pltpu.VMEM((levels, bricks.shape[2]), f32)],
         cost_estimate=pl.CostEstimate(flops=0, bytes_accessed=1 << 20, transcendentals=0),
-    )(place, innovations, innovations, courant, courant, diffusivity, diffusivity, sea, sea)
-    return down, up, place
+    )(place, bricks, innovations, innovations, courant, courant, diffusivity, diffusivity)
+    return down, up, sea, place
 
 
 def sweep(innovations, courant, diffusivity, sea, down, up, place):
@@ -309,8 +322,10 @@
             out_shape=[cells, row, row],
             out_specs=[VMEM] * 3,
             compiler_params=pltpu.CompilerParams(vmem_limit_bytes=GRANT),
-        cost_estimate=pl.CostEstimate(flops=40 * levels * lon_cells * lat_cells, bytes_accessed=9 << 20, transcendentals=0),
+            cost_estimate=pl.CostEstimate(flops=40 * levels * lon_cells * lat_cells, bytes_accessed=9 << 20, transcendentals=0),
         )(*inputs, sea_ext, before, after, *state)
+        if step == steps:
+            break
         low, high, to_west, to_east = pl.pallas_call(
             face_kernel,
             in_specs=[VMEM] * 7,
@@ -323,32 +338,37 @@
     half = jax.ShapeDtypeStruct((levels, lon_cells * lat_cells // 2), bf16)
     return pl.pallas_call(
         last_kernel,
-        in_specs=[SMEM] + [VMEM] * 3,
+        in_specs=[SMEM] + [VMEM] * 6,
         out_shape=[jax.ShapeDtypeStruct((levels, lon_cells, lat_cells), f32), half, half],
         out_specs=[VMEM] * 3,
         scratch_shapes=[pltpu.VMEM((levels * lon_cells, LANES), f32)] * (lat_cells // LANES),
         compiler_params=pltpu.CompilerParams(vmem_limit_bytes=GRANT),
         cost_estimate=pl.CostEstimate(flops=0, bytes_accessed=3 << 20, transcendentals=0),
-    )(place, out, low, high)
-
-
-def halves_kernel(place, left, right, left_mine, left_other, right_mine, right_other, *scratch):
+    )(place, out, sea_ext, out_low, out_high, west, east)
+
+
+def halves_kernel(place, left, right, left_mine, right_mine, left_other, *rest):
+    right_other, (vmem, sems) = rest[:-2], rest[-2:]
     half = left_mine.shape[2]
     side = place[1]
-    vmem, sems = scratch
-    jobs = []
-    for source, mine, other in ((left, left_mine, left_other), (right, right_mine, right_other)):
-        jobs.append((source, other, 1 - side))
-        jobs.append((source, mine, side))
+    jobs = [
+        (left, 1 - side, [left_other]),
+        (right, 1 - side, right_other),
+        (left, side, [left_mine]),
+        (right, side, [right_mine]),
+    ]
     loads, stores = [], []
-    for n, (source, target, which) in enumerate(jobs):
+    for n, (source, which, targets) in enumerate(jobs):
         window = source.at[0, :, :, pl.ds(pl.multiple_of(which * half, half), half)]
         loads.append(pltpu.make_async_copy(window, vmem.at[n], sems.at[n]))
         loads[-1].start()
-        stores.append(pltpu.make_async_copy(vmem.at[n], target, sems.at[len(jobs) + n]))
-    for load, store in zip(loads, stores):
-        load.wait()
-        store.start()
+    for n, (source, which, targets) in enumerate(jobs):
+        loads[n].wait()
+        size = vmem.shape[1] // len(targets)
+        for q, target in enumerate(targets):
+            piece = vmem.at[n, pl.ds(q * size, size)]
+            stores.append(pltpu.make_async_copy(piece, target, sems.at[len(jobs) + len(stores)]))
+            stores[-1].start()
     for store in stores:
         store.wait()
 
@@ -380,11 +400,11 @@
                 out[0][lax.rem(place[2] + (k - slots // 2 + count), count), c] = value
 
 
-def columns_kernel(slots, wide, place, right_mine, right_pair, *rest):
-    received, out = rest[:-2], rest[-2:]
+def columns_kernel(slots, wide, place, right_mine, *rest):
+    right_pair, received, out = rest[:PARTS], rest[PARTS:-2], rest[-2:]
     count = received[0].shape[0]
     total = None
-    for c, factor in enumerate((right_mine, right_pair)):
+    for c in range(2):
         for k in range(slots):
             if len(received) > 1:
                 coeff = received[k][c]
@@ -397,7 +417,8 @@
     for at in range(0, right_mine.shape[1], wide):
         lanes = slice(at, at + wide)
         total = lax.dot_general(stacked[:rows], right_mine[:, lanes], lead, preferred_element_type=jnp.float32)
-        total = total + lax.dot_general(stacked[rows:], right_pair[:, lanes], lead, preferred_element_type=jnp.float32)
+        pair = jnp.concatenate([piece[:, lanes] for piece in right_pair], 0)
+        total = total + lax.dot_general(stacked[rows:], pair, lead, preferred_element_type=jnp.float32)
         levels = out[0].shape[0]
         out[0][:, lanes] = total[:levels].astype(out[0].dtype)
         out[1][:, lanes] = total[levels:].astype(out[1].dtype)
@@ -454,25 +475,24 @@
     width = left.shape[2]
     rows = slots * width
 
-    sea = sea_bricks.astype(f32)
-    sea = jnp.broadcast_to(sea[:, :, :, None], (levels, 1, lat_cells // 2, 2)).reshape(levels, 1, lat_cells)
-    down, up, place = pack(innovations, courant, diffusivity, sea, place)
+    down, up, sea, place = pack(innovations, courant, diffusivity, sea_bricks, place)
     part = (slots, width, half)
-    left_mine, left_other, right_mine, right_other = call(
+    piece = (slots // PARTS, width, half)
+    left_mine, right_mine, left_other, *right_other = call(
         halves_kernel,
         (place, left, right),
         [SMEM, ANY, ANY],
-        [(part, bf16, ANY)] * 4,
+        [(part, bf16, ANY)] * 3 + [(piece, bf16, ANY)] * PARTS,
         grant=8 << 20,
         moved=8 << 20,
-        scratch=[pltpu.VMEM((4, slots, width, half), bf16), pltpu.SemaphoreType.DMA((8,))],
+        scratch=[pltpu.VMEM((4, slots, width, half), bf16), pltpu.SemaphoreType.DMA((7 + PARTS,))],
     )
     left_pair = swapped(left_other, "depth", 1)
-    right_pair = swapped(right_other, "depth", 1)
+    right_pair = []
+    for part in range(PARTS):
+        right_pair.append(swapped(right_other[part], "depth", 1).reshape(rows // PARTS, half))
     lam, lam_mine, lam_other = sweep(innovations, courant, diffusivity, sea, down, up, place)
-    left_mine, left_pair, right_mine, right_pair = (
-        a.reshape(rows, half) for a in (left_mine, left_pair, right_mine, right_pair)
-    )
+    left_mine, left_pair, right_mine = (a.reshape(rows, half) for a in (left_mine, left_pair, right_mine))
     blocks = {0: lam_mine}
     for mask in [1] + list(range(count - 1, 1, -1)):
         blocks[mask] = swapped(lam_other if mask % 2 else lam_mine, "depth", mask)
@@ -504,8 +524,8 @@
         block = (levels, half)
         first, second = call(
             functools.partial(columns_kernel, slots, 4 * LANES),
-            (place, right_mine, right_pair, *received),
-            [SMEM] + [VMEM] * (2 + len(received)),
+            (place, right_mine, *right_pair, *received),
+            [SMEM] + [VMEM] * (1 + PARTS + len(received)),
             [(block, bf16 if stage else f32), (block, bf16)],
             flops=8 * rows * half * levels,
             moved=3 << 20,

time: 143 us -> 153 us (1.070)
  waiting for transfers between devices: 65.7 us -> 78.8 us
  starting transfers between devices: 40.6 us -> 38.3 us
    ppermute x10 -> x13, waiting for transfers between devices: 35.7 us -> 49.8 us  [swapped(): lax.ppermute(block, axis, [(i, i ^ mask) for i in range(lax.axis_size(axi...]
    all_to_all x2, waiting for transfers between devices: 8.48 us -> 4.29 us  [per_device(): received = [lax.all_to_all(coeff[0], 'lon', 0, 0, tiled=True)]]
    ppermute x2, waiting for transfers between devices: 21.3 us -> 24.3 us  [from_behind(): lax.ppermute(value, axis, [(source, source + steps) for source in range(i...]
    ppermute x10 -> x13, starting transfers between devices: 19.8 us -> 17.6 us  [swapped(): lax.ppermute(block, axis, [(i, i ^ mask) for i in range(lax.axis_size(axi...]
    unnamed x18 -> x22, local copies, waits for them, and re-layouts: 6.68 us -> 5.57 us
  transfers between devices with their start and end apart: 22 -> 25, of which waited for: 9 -> 10; matrix products, arithmetic and copies ran while one was open for 0% -> 0% of each run, Pallas kernels for 14% -> 13%
where the time goes in v2:
time: 153 us; the launch traced here: 150 us
  waiting for transfers between devices  78.8 us (52%)
  starting transfers between devices  38.3 us (25%)
  Pallas kernels  25.7 us (17%)
  local copies, waits for them, and re-layouts  5.57 us (4%)
    ppermute x13, waiting for transfers between devices, swapped(): lax.ppermute(block, axis, [(i, i ^ mask) for i in range(lax.axis_size(axi...  49.8 us
    ppermute x2, waiting for transfers between devices, from_behind(): lax.ppermute(value, axis, [(source, source + steps) for source in range(i...  24.3 us
    ppermute x13, starting transfers between devices, swapped(): lax.ppermute(block, axis, [(i, i ^ mask) for i in range(lax.axis_size(axi...  17.6 us
    pallas_call x8, Pallas kernels, call(): pl.pallas_call(kernel, in_specs=in_specs, out_shape=[jax.ShapeDtypeStruct...  11.3 us
    ppermute x8, starting transfers between devices, shifted(): return lax.ppermute(block, axis, route)  10.8 us
    pallas_call x4, Pallas kernels, sweep(): pl.pallas_call(functools.partial(step_kernel, table, step), in_specs=[VME...  9.51 us
    all_to_all x2, starting transfers between devices, per_device(): received = [lax.all_to_all(coeff[0], 'lon', 0, 0, tiled=True)]  6.74 us
    unnamed x22, local copies, waits for them, and re-layouts  5.57 us
  transfers between devices with their start and end apart: 25, of which 10 were waited for; matrix products, arithmetic and copies ran while one was open for 0% of the time, Pallas kernels for 13%

profile of v2, /device:TPU:0, one launch (start us, length us, event | category | flops | bytes accessed | tf_op | source)
XLA Modules:
  0.0 150.0 jit_solution(3503951458160486043)
XLA Ops:
  1.3 2.3 %shard_map.86 = (bf16[25,16,256]{2,1,0:T(8,128)(2,1)}, bf16[25,16,256]{2,1,0:T(8,128)(2,1)}, f32[64,1,256]{2,1,0:T(1,128)}, s32[3]{0:T(128)}) custom-call(s32[3]{0:T(128)} %pad_add_fusion.place, s32[64,1,128]{2,1,0:T(1,128)} %bricks.1, f32[5,64,16,256]{3,2,1,0:T(8,128)} %innov.9, f32[5,64,16,256]{3,2,1,0:T(8,128)} %innov.9, f32[3,64,16,256]{3,2,1,0:T(8,128)} %cour.9, ...), custom_call_target="tpu_custom_call" | custom-call | bytes 1048576 | tf_op jit(solution)/shard_map/pallas_call | solution.py:280
  7.8 3.1 %collective-permute-start.14 = (bf16[8,32,2048]{2,1,0:T(8,128)(2,1)S(1)}, bf16[8,32,2048]{2,1,0:T(8,128)(2,1)S(1)}, u32[]{:S(2)}, u32[]{:S(2)}) collective-permute-start(bf16[8,32,2048]{2,1,0:T(8,128)(2,1)S(1)} %get-tuple-element.93), channel_id=1, source_target_pairs={{0,1},{1,0},{2,3},{3,2},{4,5},{5,4},{6,7},{7,6},{8,9},{9,8},{10,11... | collective-permute-start | bytes 3145736 | tf_op jit(solution)/shard_map/ppermute | solution.py:33
  14.2 23.7 %collective-permute-done.before = bf16[25,16,256]{2,1,0:T(8,128)(2,1)S(1)} collective-permute-done((bf16[25,16,256]{2,1,0:T(8,128)(2,1)}, bf16[25,16,256]{2,1,0:T(8,128)(2,1)S(1)}, u32[]{:S(2)}, u32[]{:S(2)}) %collective-permute-start) | collective-permute-done | bytes 204832 | tf_op jit(solution)/shard_map/ppermute | solution.py:21
  38.5 2.5 %copy-done = f32[5,64,16,256]{3,2,1,0:T(8,128)S(1)} copy-done((f32[5,64,16,256]{3,2,1,0:T(8,128)S(1)}, f32[5,64,16,256]{3,2,1,0:T(8,128)}, u32[]{:S(2)}) %copy-start) | copy-done | bytes 5242904
  42.2 2.6 %collective-permute-start.3 = (f32[72,1,256]{2,1,0:T(1,128)S(1)}, f32[72,1,256]{2,1,0:T(1,128)S(1)}, u32[]{:S(2)}, u32[]{:S(2)}) collective-permute-start(f32[72,1,256]{2,1,0:T(1,128)S(1)} %get-tuple-element.61), channel_id=1, source_target_pairs={{4,0},{8,4},{12,8},{16,12},{20,16},{24,20},{28,24},{0,28},{5,1},{9... | collective-permute-start | bytes 221192 | tf_op jit(solution)/shard_map/ppermute | solution.py:29
  44.8 2.5 %shard_map.88 = (f32[72,16,256]{2,1,0:T(8,128)S(1)}, f32[72,1,256]{2,1,0:T(1,128)S(1)}, f32[72,1,256]{2,1,0:T(1,128)S(1)}) custom-call(f32[5,64,16,256]{3,2,1,0:T(8,128)S(1)} %copy-done, f32[3,64,16,256]{3,2,1,0:T(8,128)S(1)} %copy-done.1, f32[64,16,256]{2,1,0:T(8,128)S(1)} %copy-done.2, f32[72,1,256]{2,1,0:T(1,128)S(1)} %get-tuple-element.57.sea_ext.low.high, ...), custom_call_target="tpu_custom_call" | custom-call | flops 10485760 | bytes 9437184 | tf_op jit(solution)/shard_map/pallas_call | solution.py:319
  48.0 2.3 %collective-permute-start.5 = (f32[72,1,256]{2,1,0:T(1,128)S(1)}, f32[72,1,256]{2,1,0:T(1,128)S(1)}, u32[]{:S(2)}, u32[]{:S(2)}) collective-permute-start(f32[72,1,256]{2,1,0:T(1,128)S(1)} %get-tuple-element.70), channel_id=1, source_target_pairs={{4,0},{8,4},{12,8},{16,12},{20,16},{24,20},{28,24},{0,28},{5,1},{9... | collective-permute-start | bytes 221192 | tf_op jit(solution)/shard_map/ppermute | solution.py:29
  50.2 2.4 %shard_map.90 = (f32[72,16,256]{2,1,0:T(8,128)S(1)}, f32[72,1,256]{2,1,0:T(1,128)S(1)}, f32[72,1,256]{2,1,0:T(1,128)S(1)}) custom-call(f32[5,64,16,256]{3,2,1,0:T(8,128)S(1)} %bitcast.13, f32[3,64,16,256]{3,2,1,0:T(8,128)S(1)} %copy-done.1, f32[64,16,256]{2,1,0:T(8,128)S(1)} %copy-done.2, f32[72,1,256]{2,1,0:T(1,128)S(1)} %get-tuple-element.57.sea_ext.low.high, ...), custom_call_target="tpu_custom_call" | custom-call | flops 10485760 | bytes 9437184 | tf_op jit(solution)/shard_map/pallas_call | solution.py:319
  53.3 2.2 %collective-permute-start.7 = (f32[72,1,256]{2,1,0:T(1,128)S(1)}, f32[72,1,256]{2,1,0:T(1,128)S(1)}, u32[]{:S(2)}, u32[]{:S(2)}) collective-permute-start(f32[72,1,256]{2,1,0:T(1,128)S(1)} %get-tuple-element.77), channel_id=1, source_target_pairs={{4,0},{8,4},{12,8},{16,12},{20,16},{24,20},{28,24},{0,28},{5,1},{9... | collective-permute-start | bytes 221192 | tf_op jit(solution)/shard_map/ppermute | solution.py:29
  55.5 2.4 %shard_map.92 = (f32[72,16,256]{2,1,0:T(8,128)S(1)}, f32[72,1,256]{2,1,0:T(1,128)S(1)}, f32[72,1,256]{2,1,0:T(1,128)S(1)}) custom-call(f32[5,64,16,256]{3,2,1,0:T(8,128)S(1)} %bitcast.13, f32[3,64,16,256]{3,2,1,0:T(8,128)S(1)} %copy-done.1, f32[64,16,256]{2,1,0:T(8,128)S(1)} %copy-done.2, f32[72,1,256]{2,1,0:T(1,128)S(1)} %get-tuple-element.57.sea_ext.low.high, ...), custom_call_target="tpu_custom_call" | custom-call | flops 10485760 | bytes 9437184 | tf_op jit(solution)/shard_map/pallas_call | solution.py:319
  58.8 2.1 %collective-permute-start.9 = (f32[72,1,256]{2,1,0:T(1,128)S(1)}, f32[72,1,256]{2,1,0:T(1,128)S(1)}, u32[]{:S(2)}, u32[]{:S(2)}) collective-permute-start(f32[72,1,256]{2,1,0:T(1,128)S(1)} %get-tuple-element.85), channel_id=1, source_target_pairs={{4,0},{8,4},{12,8},{16,12},{20,16},{24,20},{28,24},{0,28},{5,1},{9... | collective-permute-start | bytes 221192 | tf_op jit(solution)/shard_map/ppermute | solution.py:29
  60.9 2.3 %shard_map.94 = (f32[72,16,256]{2,1,0:T(8,128)S(1)}, f32[72,1,256]{2,1,0:T(1,128)S(1)}, f32[72,1,256]{2,1,0:T(1,128)S(1)}) custom-call(f32[5,64,16,256]{3,2,1,0:T(8,128)S(1)} %bitcast.13, f32[3,64,16,256]{3,2,1,0:T(8,128)S(1)} %copy-done.1, f32[64,16,256]{2,1,0:T(8,128)S(1)} %copy-done.2, f32[72,1,256]{2,1,0:T(1,128)S(1)} %get-tuple-element.57.sea_ext.low.high, ...), custom_call_target="tpu_custom_call" | custom-call | flops 10485760 | bytes 9437184 | tf_op jit(solution)/shard_map/pallas_call | solution.py:319
  67.0 2.6 %collective-permute-start.18 = (bf16[64,2048]{1,0:T(8,128)(2,1)S(1)}, bf16[64,2048]{1,0:T(8,128)(2,1)S(1)}, u32[]{:S(2)}, u32[]{:S(2)}) collective-permute-start(bf16[64,2048]{1,0:T(8,128)(2,1)S(1)} %get-tuple-element.94.first), channel_id=1, source_target_pairs={{0,2},{1,3},{2,0},{3,1},{4,6},{5,7},{6,4},{7,5},{8,10},{9,11},{10,... | collective-permute-start | bytes 786440 | tf_op jit(solution)/shard_map/ppermute | solution.py:33
  69.7 9.7 %collective-permute-done.15.second = bf16[64,2048]{1,0:T(8,128)(2,1)S(1)} collective-permute-done((bf16[64,2048]{1,0:T(8,128)(2,1)S(1)}, bf16[64,2048]{1,0:T(8,128)(2,1)S(1)}, u32[]{:S(2)}, u32[]{:S(2)}) %collective-permute-start.15) | collective-permute-done | bytes 262176 | tf_op jit(solution)/shard_map/ppermute | solution.py:33
  80.8 2.0 %collective-permute-start.10 = (bf16[2,32,2048]{2,1,0:T(8,128)(2,1)}, bf16[2,32,2048]{2,1,0:T(8,128)(2,1)S(1)}, u32[]{:S(2)}, u32[]{:S(2)}) collective-permute-start(bf16[2,32,2048]{2,1,0:T(8,128)(2,1)} %get-tuple-element.88), channel_id=1, source_target_pairs={{0,1},{1,0},{2,3},{3,2},{4,5},{5,4},{6,7},{7,6},{8,9},{9,8},{10,11... | collective-permute-start | bytes 786440 | tf_op jit(solution)/shard_map/ppermute | solution.py:33
  82.9 5.6 %collective-permute-done.18.first = bf16[64,2048]{1,0:T(8,128)(2,1)S(1)} collective-permute-done((bf16[64,2048]{1,0:T(8,128)(2,1)S(1)}, bf16[64,2048]{1,0:T(8,128)(2,1)S(1)}, u32[]{:S(2)}, u32[]{:S(2)}) %collective-permute-start.18) | collective-permute-done | bytes 262176 | tf_op jit(solution)/shard_map/ppermute | solution.py:33
  88.4 5.5 %collective-permute-start.13 = (bf16[2,32,2048]{2,1,0:T(8,128)(2,1)S(1)}, bf16[2,32,2048]{2,1,0:T(8,128)(2,1)S(1)}, u32[]{:S(2)}, u32[]{:S(2)}) collective-permute-start(bf16[2,32,2048]{2,1,0:T(8,128)(2,1)S(1)} %get-tuple-element.91), channel_id=1, source_target_pairs={{0,1},{1,0},{2,3},{3,2},{4,5},{5,4},{6,7},{7,6},{8,9},{9,8},{10,11... | collective-permute-start | bytes 786440 | tf_op jit(solution)/shard_map/ppermute | solution.py:33
  96.5 3.4 %all-to-all-start = ((bf16[8,2,32,128]{3,2,1,0:T(8,128)(2,1)}), bf16[8,2,32,128]{3,2,1,0:T(8,128)(2,1)S(1)}, u32[]{:S(2)}, u32[]{:S(2)}) async-start(bf16[8,2,32,128]{3,2,1,0:T(8,128)(2,1)} %shard_map.98), calls=%async_computation | async-start | bytes 262144 | tf_op jit(solution)/shard_map/all_to_all | solution.py:521
  99.9 16.1 %collective-permute-done.20.arrived = bf16[2,256,128]{2,1,0:T(8,128)(2,1)S(1)} collective-permute-done((bf16[2,256,128]{2,1,0:T(8,128)(2,1)S(1)}, bf16[2,256,128]{2,1,0:T(8,128)(2,1)S(1)}, u32[]{:S(2)}, u32[]{:S(2)}) %collective-permute-start.20) | collective-permute-done | bytes 131104 | tf_op jit(solution)/shard_map/ppermute | solution.py:33
  117.3 3.4 %all-to-all-start.1 = ((bf16[8,2,32,128]{3,2,1,0:T(8,128)(2,1)}), bf16[8,2,32,128]{3,2,1,0:T(8,128)(2,1)S(1)}, u32[]{:S(2)}, u32[]{:S(2)}) async-start(bf16[8,2,32,128]{3,2,1,0:T(8,128)(2,1)} %shard_map.101), calls=%async_computation.1 | async-start | bytes 262144 | tf_op jit(solution)/shard_map/all_to_all | solution.py:521
  121.8 4.3 %all-to-all-done.1.rest_4_ = bf16[8,2,32,128]{3,2,1,0:T(8,128)(2,1)S(1)} async-done(((bf16[8,2,32,128]{3,2,1,0:T(8,128)(2,1)}), bf16[8,2,32,128]{3,2,1,0:T(8,128)(2,1)S(1)}, u32[]{:S(2)}, u32[]{:S(2)}) %all-to-all-start.1) | async-done | bytes 131104 | tf_op jit(solution)/shard_map/all_to_all | solution.py:521
  127.5 2.0 %collective-permute-start.22 = (bf16[64,2048]{1,0:T(8,128)(2,1)S(1)}, bf16[64,2048]{1,0:T(8,128)(2,1)S(1)}, u32[]{:S(2)}, u32[]{:S(2)}) collective-permute-start(bf16[64,2048]{1,0:T(8,128)(2,1)S(1)} %get-tuple-element.103), channel_id=1, source_target_pairs={{0,3},{1,2},{2,1},{3,0},{4,7},{5,6},{6,5},{7,4},{8,11},{9,10},{10,... | collective-permute-start | bytes 786440 | tf_op jit(solution)/shard_map/ppermute | solution.py:33
  130.9 16.9 %collective-permute-done.21.arrived2 = bf16[64,2048]{1,0:T(8,128)(2,1)S(1)} collective-permute-done((bf16[64,2048]{1,0:T(8,128)(2,1)S(1)}, bf16[64,2048]{1,0:T(8,128)(2,1)S(1)}, u32[]{:S(2)}, u32[]{:S(2)}) %collective-permute-start.21) | collective-permute-done | bytes 262176 | tf_op jit(solution)/shard_map/ppermute | solution.py:33
  147.8 2.2 %shard_map.103 = f32[64,16,256]{2,1,0:T(8,128)} custom-call(s32[3]{0:T(128)S(1)} %copy-done.7, f32[64,2048]{1,0:T(8,128)S(1)} %get-tuple-element.98.own, bf16[64,2048]{1,0:T(8,128)(2,1)S(1)} %collective-permute-done.17.arrived1, bf16[64,2048]{1,0:T(8,128)(2,1)S(1)} %collective-permute-done.21.arrived2, bf16[64,2048]{1,0:T(8,128)(2,1)S(1)} %collective-permute-done.22.arrived3), custom_call_target="tpu_custom_call" | custom-call | bytes 4194304 | tf_op jit(solution)/shard_map/pallas_call | solution.py:450
  (68 shorter events, 25.2 us)
Async XLA Ops:
  7.8 71.5 %collective-permute-start.14 = (bf16[8,32,2048]{2,1,0:T(8,128)(2,1)S(1)}, bf16[8,32,2048]{2,1,0:T(8,128)(2,1)S(1)}, u32[]{:S(2)}, u32[]{:S(2)}) collective-permute-start(bf16[8,32,2048]{2,1,0:T(8,128)(2,1)S(1)} %get-tuple-element.93), channel_id=1, source_target_pairs={{0,1},{1,0},{2,3},{3,2},{4,5},{5,4},{6,7},{7,6},{8,9},{9,8},{10,11... | collective-permute-start | bytes 3145736 | tf_op jit(solution)/shard_map/ppermute | solution.py:33
  10.9 26.9 %collective-permute-start = (bf16[25,16,256]{2,1,0:T(8,128)(2,1)}, bf16[25,16,256]{2,1,0:T(8,128)(2,1)S(1)}, u32[]{:S(2)}, u32[]{:S(2)}) collective-permute-start(bf16[25,16,256]{2,1,0:T(8,128)(2,1)} %get-tuple-element.55), channel_id=1, source_target_pairs={{0,1},{1,2},{2,3},{4,5},{5,6},{6,7},{8,9},{9,10},{10,11},{12,13},{... | collective-permute-start | bytes 614408 | tf_op jit(solution)/shard_map/ppermute | solution.py:21
  12.9 25.6 %collective-permute-start.1 = (bf16[25,16,256]{2,1,0:T(8,128)(2,1)}, bf16[25,16,256]{2,1,0:T(8,128)(2,1)S(1)}, u32[]{:S(2)}, u32[]{:S(2)}) collective-permute-start(bf16[25,16,256]{2,1,0:T(8,128)(2,1)} %get-tuple-element.56), channel_id=1, source_target_pairs={{1,0},{2,1},{3,2},{5,4},{6,5},{7,6},{9,8},{10,9},{11,10},{13,12},{... | collective-permute-start | bytes 614408 | tf_op jit(solution)/shard_map/ppermute | solution.py:21
  42.1 5.2 %collective-permute-start.2 = (f32[72,1,256]{2,1,0:T(1,128)S(1)}, f32[72,1,256]{2,1,0:T(1,128)S(1)}, u32[]{:S(2)}, u32[]{:S(2)}) collective-permute-start(f32[72,1,256]{2,1,0:T(1,128)S(1)} %get-tuple-element.60), channel_id=1, source_target_pairs={{28,0},{0,4},{4,8},{8,12},{12,16},{16,20},{20,24},{24,28},{29,1},{... | collective-permute-start | bytes 221192 | tf_op jit(solution)/shard_map/ppermute | solution.py:29
  42.2 5.2 %collective-permute-start.3 = (f32[72,1,256]{2,1,0:T(1,128)S(1)}, f32[72,1,256]{2,1,0:T(1,128)S(1)}, u32[]{:S(2)}, u32[]{:S(2)}) collective-permute-start(f32[72,1,256]{2,1,0:T(1,128)S(1)} %get-tuple-element.61), channel_id=1, source_target_pairs={{4,0},{8,4},{12,8},{16,12},{20,16},{24,20},{28,24},{0,28},{5,1},{9... | collective-permute-start | bytes 221192 | tf_op jit(solution)/shard_map/ppermute | solution.py:29
  47.5 5.1 %collective-permute-start.4 = (f32[72,1,256]{2,1,0:T(1,128)S(1)}, f32[72,1,256]{2,1,0:T(1,128)S(1)}, u32[]{:S(2)}, u32[]{:S(2)}) collective-permute-start(f32[72,1,256]{2,1,0:T(1,128)S(1)} %get-tuple-element.69), channel_id=1, source_target_pairs={{28,0},{0,4},{4,8},{8,12},{12,16},{16,20},{20,24},{24,28},{29,1},{... | collective-permute-start | bytes 221192 | tf_op jit(solution)/shard_map/ppermute | solution.py:29
  48.0 4.7 %collective-permute-start.5 = (f32[72,1,256]{2,1,0:T(1,128)S(1)}, f32[72,1,256]{2,1,0:T(1,128)S(1)}, u32[]{:S(2)}, u32[]{:S(2)}) collective-permute-start(f32[72,1,256]{2,1,0:T(1,128)S(1)} %get-tuple-element.70), channel_id=1, source_target_pairs={{4,0},{8,4},{12,8},{16,12},{20,16},{24,20},{28,24},{0,28},{5,1},{9... | collective-permute-start | bytes 221192 | tf_op jit(solution)/shard_map/ppermute | solution.py:29
  52.8 5.2 %collective-permute-start.6 = (f32[72,1,256]{2,1,0:T(1,128)S(1)}, f32[72,1,256]{2,1,0:T(1,128)S(1)}, u32[]{:S(2)}, u32[]{:S(2)}) collective-permute-start(f32[72,1,256]{2,1,0:T(1,128)S(1)} %get-tuple-element.76), channel_id=1, source_target_pairs={{28,0},{0,4},{4,8},{8,12},{12,16},{16,20},{20,24},{24,28},{29,1},{... | collective-permute-start | bytes 221192 | tf_op jit(solution)/shard_map/ppermute | solution.py:29
  53.3 4.7 %collective-permute-start.7 = (f32[72,1,256]{2,1,0:T(1,128)S(1)}, f32[72,1,256]{2,1,0:T(1,128)S(1)}, u32[]{:S(2)}, u32[]{:S(2)}) collective-permute-start(f32[72,1,256]{2,1,0:T(1,128)S(1)} %get-tuple-element.77), channel_id=1, source_target_pairs={{4,0},{8,4},{12,8},{16,12},{20,16},{24,20},{28,24},{0,28},{5,1},{9... | collective-permute-start | bytes 221192 | tf_op jit(solution)/shard_map/ppermute | solution.py:29
  58.2 5.3 %collective-permute-start.8 = (f32[72,1,256]{2,1,0:T(1,128)S(1)}, f32[72,1,256]{2,1,0:T(1,128)S(1)}, u32[]{:S(2)}, u32[]{:S(2)}) collective-permute-start(f32[72,1,256]{2,1,0:T(1,128)S(1)} %get-tuple-element.84), channel_id=1, source_target_pairs={{28,0},{0,4},{4,8},{8,12},{12,16},{16,20},{20,24},{24,28},{29,1},{... | collective-permute-start | bytes 221192 | tf_op jit(solution)/shard_map/ppermute | solution.py:29
  65.3 14.1 %collective-permute-start.15 = (bf16[64,2048]{1,0:T(8,128)(2,1)S(1)}, bf16[64,2048]{1,0:T(8,128)(2,1)S(1)}, u32[]{:S(2)}, u32[]{:S(2)}) collective-permute-start(bf16[64,2048]{1,0:T(8,128)(2,1)S(1)} %get-tuple-element.95), channel_id=1, source_target_pairs={{0,1},{1,0},{2,3},{3,2},{4,5},{5,4},{6,7},{7,6},{8,9},{9,8},{10,11... | collective-permute-start | bytes 786440 | tf_op jit(solution)/shard_map/ppermute | solution.py:33
  67.0 21.4 %collective-permute-start.18 = (bf16[64,2048]{1,0:T(8,128)(2,1)S(1)}, bf16[64,2048]{1,0:T(8,128)(2,1)S(1)}, u32[]{:S(2)}, u32[]{:S(2)}) collective-permute-start(bf16[64,2048]{1,0:T(8,128)(2,1)S(1)} %get-tuple-element.94.first), channel_id=1, source_target_pairs={{0,2},{1,3},{2,0},{3,1},{4,6},{5,7},{6,4},{7,5},{8,10},{9,11},{10,... | collective-permute-start | bytes 786440 | tf_op jit(solution)/shard_map/ppermute | solution.py:33
  69.6 18.8 %collective-permute-start.19 = (bf16[64,2048]{1,0:T(8,128)(2,1)S(1)}, bf16[64,2048]{1,0:T(8,128)(2,1)S(1)}, u32[]{:S(2)}, u32[]{:S(2)}) collective-permute-start(bf16[64,2048]{1,0:T(8,128)(2,1)S(1)} %get-tuple-element.95), channel_id=1, source_target_pairs={{0,3},{1,2},{2,1},{3,0},{4,7},{5,6},{6,5},{7,4},{8,11},{9,10},{10,... | collective-permute-start | bytes 786440 | tf_op jit(solution)/shard_map/ppermute | solution.py:33
  80.7 14.5 %collective-permute-start.16 = (bf16[2,256,128]{2,1,0:T(8,128)(2,1)S(1)}, bf16[2,256,128]{2,1,0:T(8,128)(2,1)S(1)}, u32[]{:S(2)}, u32[]{:S(2)}) collective-permute-start(bf16[2,256,128]{2,1,0:T(8,128)(2,1)S(1)} %get-tuple-element.97), channel_id=1, source_target_pairs={{0,1},{1,0},{2,3},{3,2},{4,5},{5,4},{6,7},{7,6},{8,9},{9,8},{10,11... | collective-permute-start | bytes 393224 | tf_op jit(solution)/shard_map/ppermute | solution.py:33
  80.8 39.9 %collective-permute-start.10 = (bf16[2,32,2048]{2,1,0:T(8,128)(2,1)}, bf16[2,32,2048]{2,1,0:T(8,128)(2,1)S(1)}, u32[]{:S(2)}, u32[]{:S(2)}) collective-permute-start(bf16[2,32,2048]{2,1,0:T(8,128)(2,1)} %get-tuple-element.88), channel_id=1, source_target_pairs={{0,1},{1,0},{2,3},{3,2},{4,5},{5,4},{6,7},{7,6},{8,9},{9,8},{10,11... | collective-permute-start | bytes 786440 | tf_op jit(solution)/shard_map/ppermute | solution.py:33
  82.8 37.9 %collective-permute-start.11 = (bf16[2,32,2048]{2,1,0:T(8,128)(2,1)}, bf16[2,32,2048]{2,1,0:T(8,128)(2,1)S(1)}, u32[]{:S(2)}, u32[]{:S(2)}) collective-permute-start(bf16[2,32,2048]{2,1,0:T(8,128)(2,1)} %get-tuple-element.89), channel_id=1, source_target_pairs={{0,1},{1,0},{2,3},{3,2},{4,5},{5,4},{6,7},{7,6},{8,9},{9,8},{10,11... | collective-permute-start | bytes 786440 | tf_op jit(solution)/shard_map/ppermute | solution.py:33
  88.4 32.3 %collective-permute-start.12 = (bf16[2,32,2048]{2,1,0:T(8,128)(2,1)}, bf16[2,32,2048]{2,1,0:T(8,128)(2,1)S(1)}, u32[]{:S(2)}, u32[]{:S(2)}) collective-permute-start(bf16[2,32,2048]{2,1,0:T(8,128)(2,1)} %get-tuple-element.90), channel_id=1, source_target_pairs={{0,1},{1,0},{2,3},{3,2},{4,5},{5,4},{6,7},{7,6},{8,9},{9,8},{10,11... | collective-permute-start | bytes 786440 | tf_op jit(solution)/shard_map/ppermute | solution.py:33
  88.4 32.3 %collective-permute-start.13 = (bf16[2,32,2048]{2,1,0:T(8,128)(2,1)S(1)}, bf16[2,32,2048]{2,1,0:T(8,128)(2,1)S(1)}, u32[]{:S(2)}, u32[]{:S(2)}) collective-permute-start(bf16[2,32,2048]{2,1,0:T(8,128)(2,1)S(1)} %get-tuple-element.91), channel_id=1, source_target_pairs={{0,1},{1,0},{2,3},{3,2},{4,5},{5,4},{6,7},{7,6},{8,9},{9,8},{10,11... | collective-permute-start | bytes 786440 | tf_op jit(solution)/shard_map/ppermute | solution.py:33
  95.2 20.9 %collective-permute-start.20 = (bf16[2,256,128]{2,1,0:T(8,128)(2,1)S(1)}, bf16[2,256,128]{2,1,0:T(8,128)(2,1)S(1)}, u32[]{:S(2)}, u32[]{:S(2)}) collective-permute-start(bf16[2,256,128]{2,1,0:T(8,128)(2,1)S(1)} %get-tuple-element.101), channel_id=1, source_target_pairs={{0,1},{1,0},{2,3},{3,2},{4,5},{5,4},{6,7},{7,6},{8,9},{9,8},{10,11... | collective-permute-start | bytes 393224 | tf_op jit(solution)/shard_map/ppermute | solution.py:33
  96.5 20.8 %all-to-all-start = ((bf16[8,2,32,128]{3,2,1,0:T(8,128)(2,1)}), bf16[8,2,32,128]{3,2,1,0:T(8,128)(2,1)S(1)}, u32[]{:S(2)}, u32[]{:S(2)}) async-start(bf16[8,2,32,128]{3,2,1,0:T(8,128)(2,1)} %shard_map.98), calls=%async_computation | async-start | bytes 262144 | tf_op jit(solution)/shard_map/all_to_all | solution.py:521
  117.3 8.8 %all-to-all-start.1 = ((bf16[8,2,32,128]{3,2,1,0:T(8,128)(2,1)}), bf16[8,2,32,128]{3,2,1,0:T(8,128)(2,1)S(1)}, u32[]{:S(2)}, u32[]{:S(2)}) async-start(bf16[8,2,32,128]{3,2,1,0:T(8,128)(2,1)} %shard_map.101), calls=%async_computation.1 | async-start | bytes 262144 | tf_op jit(solution)/shard_map/all_to_all | solution.py:521
  121.8 9.1 %collective-permute-start.17 = (bf16[64,2048]{1,0:T(8,128)(2,1)S(1)}, bf16[64,2048]{1,0:T(8,128)(2,1)S(1)}, u32[]{:S(2)}, u32[]{:S(2)}) collective-permute-start(bf16[64,2048]{1,0:T(8,128)(2,1)S(1)} %get-tuple-element.99), channel_id=1, source_target_pairs={{0,1},{1,0},{2,3},{3,2},{4,5},{5,4},{6,7},{7,6},{8,9},{9,8},{10,11... | collective-permute-start | bytes 786440 | tf_op jit(solution)/shard_map/ppermute | solution.py:33
  127.1 20.7 %collective-permute-start.21 = (bf16[64,2048]{1,0:T(8,128)(2,1)S(1)}, bf16[64,2048]{1,0:T(8,128)(2,1)S(1)}, u32[]{:S(2)}, u32[]{:S(2)}) collective-permute-start(bf16[64,2048]{1,0:T(8,128)(2,1)S(1)} %get-tuple-element.102), channel_id=1, source_target_pairs={{0,2},{1,3},{2,0},{3,1},{4,6},{5,7},{6,4},{7,5},{8,10},{9,11},{10,... | collective-permute-start | bytes 786440 | tf_op jit(solution)/shard_map/ppermute | solution.py:33
  127.5 20.3 %collective-permute-start.22 = (bf16[64,2048]{1,0:T(8,128)(2,1)S(1)}, bf16[64,2048]{1,0:T(8,128)(2,1)S(1)}, u32[]{:S(2)}, u32[]{:S(2)}) collective-permute-start(bf16[64,2048]{1,0:T(8,128)(2,1)S(1)} %get-tuple-element.103), channel_id=1, source_target_pairs={{0,3},{1,2},{2,1},{3,0},{4,7},{5,6},{6,5},{7,4},{8,11},{9,10},{10,... | collective-permute-start | bytes 786440 | tf_op jit(solution)/shard_map/ppermute | solution.py:33
  (12 other events, 107.2 us)

commit v3 on v2

--- a/solution.py
+++ b/solution.py
@@ -9,6 +9,7 @@
 UNROLL = 3
 LANES = 128
 PARTS = 4
+STAGES = 2
 GRANT = 4 << 20
 VMEM = pl.BlockSpec(memory_space=pltpu.VMEM)
 SMEM = pl.BlockSpec(memory_space=pltpu.SMEM)
@@ -46,9 +47,19 @@
     return order, at + 1
 
 
-def pack_kernel(table, place, bricks, innov_lo, innov_hi, cour_lo, cour_hi, diff_lo, diff_hi, down, up, sea, placed, rows):
-    for n in range(place.shape[0]):
-        placed[n] = place[n]
+def pack_kernel(table, axes, bricks, innov_lo, innov_hi, cour_lo, cour_hi, diff_lo, diff_hi, left, right, *rest):
+    down, up, sea, place, left_other, *right_other = rest[:-3]
+    rows, vmem, sems = rest[-3:]
+    me = lax.axis_index(axes[1])
+    side = lax.rem(me, 2)
+    place[0], place[1], place[2] = me, side, lax.axis_index(axes[0])
+    half = left_other.shape[2]
+    start = pl.multiple_of((1 - side) * half, half)
+    loads, stores = [], []
+    for n, source in enumerate((left, right)):
+        window = source.at[0, :, :, pl.ds(start, half)]
+        loads.append(pltpu.make_async_copy(window, vmem.at[n], sems.at[n]))
+        loads[-1].start()
     depth = diff_lo.shape[0]
     levels, _, count = bricks.shape
     lat_cells = sea.shape[2]
@@ -85,6 +96,24 @@
 
     fill(down, innov_hi, cour_hi, diff_hi, sea_hi, lambda d: depth - d)
     fill(up, innov_lo, cour_lo, diff_lo, sea_lo, lambda d: d - 1)
+    for n, targets in enumerate(([left_other], right_other)):
+        loads[n].wait()
+        size = vmem.shape[1] // len(targets)
+        for q, target in enumerate(targets):
+            piece = vmem.at[n, pl.ds(q * size, size)]
+            stores.append(pltpu.make_async_copy(piece, target, sems.at[2 + len(stores)]))
+            stores[-1].start()
+    for store in stores:
+        store.wait()
+
+
+def load_kernel(*refs):
+    count = len(refs) // 2
+    copies = [pltpu.make_async_copy(refs[n], refs[count + n], refs[-1].at[n]) for n in range(count)]
+    for copy in copies:
+        copy.start()
+    for copy in copies:
+        copy.wait()
 
 
 def first_kernel(table, innov, cour, diff, sea, before, after, sea_ext, east_gain, west_gain, to_east, to_west):
@@ -229,18 +258,13 @@
     finish(at + reach, acc, up_flux)
 
 
-def last_kernel(place, lam, sea_ext, out_low, out_high, west, east, out, mine, other, *rows):
-    levels, lon_cells, lat_cells = out.shape
-    steps = (lam.shape[0] - levels) // 2
-    x_at = lax.broadcasted_iota(jnp.int32, (lon_cells, lat_cells), 0)
-    first_x, last_x = x_at == 0, x_at == lon_cells - 1
+def lay_kernel(place, lam, mine, other, *rows):
+    levels = mine.shape[0]
+    total, lon_cells, lat_cells = lam.shape
+    steps = (total - levels) // 2
 
     def one(z, carry):
-        at = z + steps
-        low = out_low[at] + sea_ext[at] * west[at]
-        high = out_high[at] + sea_ext[at] * east[at]
-        value = jnp.where(last_x, high, jnp.where(first_x, low, lam[at]))
-        out[z] = value
+        value = lam[z + steps]
         for c, lanes in enumerate(rows):
             at = pl.multiple_of(z * lon_cells, lon_cells)
             lanes[pl.ds(at, lon_cells), :] = value[:, c * LANES : (c + 1) * LANES]
@@ -256,6 +280,44 @@
                 part[:, at : at + LANES] = picked.astype(jnp.bfloat16)
 
 
+def fix_kernel(place, sea_ext, out_low, out_high, west, east, mine_in, other_in, mine, other, low_rows, high_rows):
+    levels, half = mine.shape
+    lat_cells = low_rows.shape[1]
+    steps = (sea_ext.shape[0] - levels) // 2
+    for z in range(levels):
+        at = z + steps
+        low_rows[z : z + 1] = out_low[at] + sea_ext[at] * west[at]
+        high_rows[z : z + 1] = out_high[at] + sea_ext[at] * east[at]
+    low = low_rows[...].astype(jnp.bfloat16)
+    high = high_rows[...].astype(jnp.bfloat16)
+
+    @pl.when(place[1] == 0)
+    def _():
+        mine[:, :lat_cells] = low
+        other[:, half - lat_cells :] = high
+
+    @pl.when(place[1] != 0)
+    def _():
+        other[:, :lat_cells] = low
+        mine[:, half - lat_cells :] = high
+
+
+def emit_kernel(lam, sea_ext, out_low, out_high, west, east, out):
+    levels, lon_cells, lat_cells = out.shape
+    steps = (lam.shape[0] - levels) // 2
+    x_at = lax.broadcasted_iota(jnp.int32, (lon_cells, lat_cells), 0)
+    first_x, last_x = x_at == 0, x_at == lon_cells - 1
+
+    def one(z, carry):
+        at = z + steps
+        low = out_low[at] + sea_ext[at] * west[at]
+        high = out_high[at] + sea_ext[at] * east[at]
+        out[z] = jnp.where(last_x, high, jnp.where(first_x, low, lam[at]))
+        return carry
+
+    lax.fori_loop(0, levels, one, 0, unroll=4)
+
+
 def face_kernel(sea_ext, out_low, out_high, west, east, west_gain, east_gain, low, high, to_west, to_east):
     low_rows = out_low[...] + sea_ext[...] * west[...]
     high_rows = out_high[...] + sea_ext[...] * east[...]
@@ -263,7 +325,7 @@
     to_west[...], to_east[...] = west_gain[...] * low_rows, east_gain[...] * high_rows
 
 
-def pack(innovations, courant, diffusivity, bricks, place):
+def pack(innovations, courant, diffusivity, bricks, left, right):
     levels, lon_cells, lat_cells = diffusivity.shape
     steps = innovations.shape[0] - 1
     table, layers = halo_table(steps)
@@ -277,19 +339,33 @@
         return [pl.BlockSpec(tuple(block), at(index)) for index in (0, end)]
 
     message = jax.ShapeDtypeStruct((layers, lon_cells, lat_cells), bf16)
-    down, up, sea, place = pl.pallas_call(
-        functools.partial(pack_kernel, table),
+    _, slots, width, cols = left.shape
+    other = jax.ShapeDtypeStruct((slots, width, cols // 2), bf16)
+    piece = jax.ShapeDtypeStruct((slots // PARTS, width, cols // 2), bf16)
+    return pl.pallas_call(
+        functools.partial(pack_kernel, table, ("lon", "depth")),
         grid=(1,),
-        in_specs=[SMEM, VMEM]
+        in_specs=[VMEM]
         + edges(innovations.shape, 1)
         + edges(courant.shape, 1)
-        + edges(diffusivity.shape, 0),
-        out_shape=[message, message, jax.ShapeDtypeStruct((levels, 1, lat_cells), f32), jax.ShapeDtypeStruct(place.shape, place.dtype)],
-        out_specs=[VMEM, VMEM, VMEM, SMEM],
-        scratch_shapes=[pltpu.VMEM((levels, bricks.shape[2]), f32)],
+        + edges(diffusivity.shape, 0)
+        + [ANY, ANY],
+        out_shape=[
+            message,
+            message,
+            jax.ShapeDtypeStruct((levels, 1, lat_cells), f32),
+            jax.ShapeDtypeStruct((3,), jnp.int32),
+            other,
+        ]
+        + [piece] * PARTS,
+        out_specs=[VMEM, VMEM, VMEM, SMEM] + [ANY] * (1 + PARTS),
+        scratch_shapes=[
+            pltpu.VMEM((levels, bricks.shape[2]), f32),
+            pltpu.VMEM((2, slots, width, cols // 2), bf16),
+            pltpu.SemaphoreType.DMA((3 + PARTS,)),
+        ],
         cost_estimate=pl.CostEstimate(flops=0, bytes_accessed=1 << 20, transcendentals=0),
-    )(place, bricks, innovations, innovations, courant, courant, diffusivity, diffusivity)
-    return down, up, sea, place
+    )(bricks, innovations, innovations, courant, courant, diffusivity, diffusivity, left, right)
 
 
 def sweep(innovations, courant, diffusivity, sea, down, up, place):
@@ -302,6 +378,15 @@
     row = jax.ShapeDtypeStruct((levels + 2 * steps, 1, lat_cells), f32)
     cells = jax.ShapeDtypeStruct((levels + 2 * steps, lon_cells, lat_cells), f32)
     inputs = (innovations, courant, diffusivity)
+    inputs = call(
+        load_kernel,
+        inputs,
+        [ANY] * 3,
+        [(a.shape, a.dtype) for a in inputs],
+        grant=40 << 20,
+        moved=18 << 20,
+        scratch=[pltpu.SemaphoreType.DMA((3,))],
+    )
     sea_ext, east_gain, west_gain, to_east, to_west = pl.pallas_call(
         functools.partial(first_kernel, table),
         in_specs=[VMEM] * 6,
@@ -335,62 +420,58 @@
             cost_estimate=pl.CostEstimate(flops=0, bytes_accessed=1 << 19, transcendentals=0),
         )(sea_ext, out_low, out_high, west, east, west_gain, east_gain)
         lam = (out,)
-    half = jax.ShapeDtypeStruct((levels, lon_cells * lat_cells // 2), bf16)
-    return pl.pallas_call(
-        last_kernel,
-        in_specs=[SMEM] + [VMEM] * 6,
-        out_shape=[jax.ShapeDtypeStruct((levels, lon_cells, lat_cells), f32), half, half],
-        out_specs=[VMEM] * 3,
-        scratch_shapes=[pltpu.VMEM((levels * lon_cells, LANES), f32)] * (lat_cells // LANES),
-        compiler_params=pltpu.CompilerParams(vmem_limit_bytes=GRANT),
-        cost_estimate=pl.CostEstimate(flops=0, bytes_accessed=3 << 20, transcendentals=0),
-    )(place, out, sea_ext, out_low, out_high, west, east)
-
-
-def halves_kernel(place, left, right, left_mine, right_mine, left_other, *rest):
-    right_other, (vmem, sems) = rest[:-2], rest[-2:]
-    half = left_mine.shape[2]
-    side = place[1]
-    jobs = [
-        (left, 1 - side, [left_other]),
-        (right, 1 - side, right_other),
-        (left, side, [left_mine]),
-        (right, side, [right_mine]),
-    ]
-    loads, stores = [], []
-    for n, (source, which, targets) in enumerate(jobs):
-        window = source.at[0, :, :, pl.ds(pl.multiple_of(which * half, half), half)]
-        loads.append(pltpu.make_async_copy(window, vmem.at[n], sems.at[n]))
-        loads[-1].start()
-    for n, (source, which, targets) in enumerate(jobs):
-        loads[n].wait()
-        size = vmem.shape[1] // len(targets)
-        for q, target in enumerate(targets):
-            piece = vmem.at[n, pl.ds(q * size, size)]
-            stores.append(pltpu.make_async_copy(piece, target, sems.at[len(jobs) + len(stores)]))
-            stores[-1].start()
-    for store in stores:
-        store.wait()
+    half = (levels, lon_cells * lat_cells // 2)
+    mine, other = call(
+        lay_kernel,
+        (place, out),
+        [SMEM, VMEM],
+        [(half, bf16)] * 2,
+        scratch=[pltpu.VMEM((levels * lon_cells, LANES), f32)] * (lat_cells // LANES),
+        moved=3 << 20,
+    )
+    edge = (sea_ext, out_low, out_high, west, east)
+    mine, other = call(
+        fix_kernel,
+        (place, *edge, mine, other),
+        [SMEM] + [VMEM] * 7,
+        [(half, bf16)] * 2,
+        scratch=[pltpu.VMEM((levels, lat_cells), f32)] * 2,
+        aliases={6: 0, 7: 1},
+    )
+    (lam,) = call(
+        emit_kernel,
+        (out, *edge),
+        [VMEM] * 6,
+        [((levels, lon_cells, lat_cells), f32)],
+        moved=3 << 20,
+    )
+    return lam, mine, other
 
 
 def against(a, b):
     return lax.dot_general(a, b, (((1,), (1,)), ((), ())), preferred_element_type=jnp.float32)
 
 
-def rows_kernel(left_mine, left_pair, first, second, kept, sent):
-    for c, factor in enumerate((left_mine, left_pair)):
-        parts = [against(factor[...], block[...]) for block in (first, second)]
+def rows_kernel(place, left, left_pair, first, second, kept, sent):
+    half = left_pair.shape[1]
+    mine = left[:, pl.ds(pl.multiple_of(place[1] * half, half), half)]
+    for c, factor in enumerate((mine, left_pair[...])):
+        parts = [against(factor, block[...]) for block in (first, second)]
         kept[c] = jnp.concatenate(parts, 1)
         sent[1 - c] = jnp.concatenate(parts[::-1], 1).astype(jnp.bfloat16)
 
 
-def mask_kernel(slots, place, ranks, kept, arrived, *out):
-    rows = kept.shape[1] // slots
+def mask_kernel(slots, place, ranks, *rest):
+    stages = [rest[n : n + 2] for n in range(0, STAGES * 2, 2)]
+    out = rest[STAGES * 2 :]
+    rows = stages[0][0].shape[1] // slots
     for c in range(2):
         owner = place[0] if c == 0 else place[0] + 1 - 2 * place[1]
         for k in range(slots):
             at = slice(k * rows, (k + 1) * rows)
-            value = kept[c, at, :] + arrived[c, at, :].astype(jnp.float32)
+            value = jnp.concatenate(
+                [kept[c, at, :] + arrived[c, at, :].astype(jnp.float32) for kept, arrived in stages], 1
+            )
             row = lax.broadcasted_iota(jnp.int32, value.shape, 0) + owner * rows
             value = jnp.where(row < ranks[0, k], value, 0.0).astype(jnp.bfloat16)
             if len(out) > 1:
@@ -400,26 +481,28 @@
                 out[0][lax.rem(place[2] + (k - slots // 2 + count), count), c] = value
 
 
-def columns_kernel(slots, wide, place, right_mine, *rest):
+def columns_kernel(slots, wide, stage, place, right, *rest):
     right_pair, received, out = rest[:PARTS], rest[PARTS:-2], rest[-2:]
     count = received[0].shape[0]
-    total = None
+    levels, half = out[0].shape
+    picked = slice(stage * levels, (stage + 2) * levels)
+    coeffs = []
     for c in range(2):
         for k in range(slots):
             if len(received) > 1:
-                coeff = received[k][c]
+                coeffs.append(received[k][c, :, picked])
             else:
-                coeff = received[0][lax.rem(place[2] + (count + slots // 2 - k), count), c]
-            coeffs = [coeff] if k == 0 and c == 0 else coeffs + [coeff]
+                source = lax.rem(place[2] + (count + slots // 2 - k), count)
+                coeffs.append(received[0][source, c, :, picked])
     stacked = jnp.concatenate(coeffs, 0)
-    rows = right_mine.shape[0]
+    rows = right.shape[0]
     lead = (((0,), (0,)), ((), ()))
-    for at in range(0, right_mine.shape[1], wide):
+    for at in range(0, half, wide):
         lanes = slice(at, at + wide)
-        total = lax.dot_general(stacked[:rows], right_mine[:, lanes], lead, preferred_element_type=jnp.float32)
+        mine = right[:, pl.ds(pl.multiple_of(place[1] * half + at, LANES), wide)]
+        total = lax.dot_general(stacked[:rows], mine, lead, preferred_element_type=jnp.float32)
         pair = jnp.concatenate([piece[:, lanes] for piece in right_pair], 0)
         total = total + lax.dot_general(stacked[rows:], pair, lead, preferred_element_type=jnp.float32)
-        levels = out[0].shape[0]
         out[0][:, lanes] = total[:levels].astype(out[0].dtype)
         out[1][:, lanes] = total[levels:].astype(out[1].dtype)
 
@@ -446,13 +529,14 @@
     lax.fori_loop(0, levels, one, 0, unroll=4)
 
 
-def call(kernel, operands, in_specs, outs, grant=GRANT, flops=0, moved=1 << 20, scratch=()):
+def call(kernel, operands, in_specs, outs, grant=GRANT, flops=0, moved=1 << 20, scratch=(), aliases=None):
     return pl.pallas_call(
         kernel,
         in_specs=in_specs,
         out_shape=[jax.ShapeDtypeStruct(*o[:2]) for o in outs],
         out_specs=[o[2] if len(o) > 2 else VMEM for o in outs],
         scratch_shapes=list(scratch),
+        input_output_aliases=aliases or {},
         compiler_params=pltpu.CompilerParams(vmem_limit_bytes=grant),
         cost_estimate=pl.CostEstimate(flops=flops, bytes_accessed=moved, transcendentals=0),
     )(*operands)
@@ -468,73 +552,64 @@
     count = lax.axis_size("depth")
     lon_count = lax.axis_size("lon")
     f32, bf16 = jnp.float32, jnp.bfloat16
-    me = lax.axis_index("depth")
-    place = jnp.stack([me, me % 2, lax.axis_index("lon")]).astype(jnp.int32)
     left = row_factors.transpose(0, 1, 3, 2)
     right = column_factors.transpose(0, 1, 3, 2)
     width = left.shape[2]
     rows = slots * width
 
-    down, up, sea, place = pack(innovations, courant, diffusivity, sea_bricks, place)
-    part = (slots, width, half)
-    piece = (slots // PARTS, width, half)
-    left_mine, right_mine, left_other, *right_other = call(
-        halves_kernel,
-        (place, left, right),
-        [SMEM, ANY, ANY],
-        [(part, bf16, ANY)] * 3 + [(piece, bf16, ANY)] * PARTS,
-        grant=8 << 20,
-        moved=8 << 20,
-        scratch=[pltpu.VMEM((4, slots, width, half), bf16), pltpu.SemaphoreType.DMA((7 + PARTS,))],
+    down, up, sea, place, left_other, *right_other = pack(
+        innovations, courant, diffusivity, sea_bricks, left, right
     )
     left_pair = swapped(left_other, "depth", 1)
     right_pair = []
     for part in range(PARTS):
         right_pair.append(swapped(right_other[part], "depth", 1).reshape(rows // PARTS, half))
     lam, lam_mine, lam_other = sweep(innovations, courant, diffusivity, sea, down, up, place)
-    left_mine, left_pair, right_mine = (a.reshape(rows, half) for a in (left_mine, left_pair, right_mine))
+    left_pair = left_pair.reshape(rows, half)
+    left, right = left.reshape(rows, tile_cols), right.reshape(rows, tile_cols)
     blocks = {0: lam_mine}
     for mask in [1] + list(range(count - 1, 1, -1)):
         blocks[mask] = swapped(lam_other if mask % 2 else lam_mine, "depth", mask)
-    arrived, own = {}, None
+    sums = []
     for stage in range(0, count, 2):
         pair = (2, rows, 2 * levels)
         kept, sent = call(
             rows_kernel,
-            (left_mine, left_pair, blocks[stage], blocks[stage + 1]),
-            [VMEM] * 4,
+            (place, left, left_pair, blocks[stage], blocks[stage + 1]),
+            [SMEM] + [VMEM] * 4,
             [(pair, f32), (pair, bf16)],
             flops=8 * rows * half * levels,
             moved=3 << 20,
         )
-        other = swapped(sent, "depth", 1)
-        grouped = lon_count == slots
-        slot = (2, width, 2 * levels)
-        outs = [((lon_count,) + slot, bf16)] if grouped else [(slot, bf16)] * slots
-        coeff = call(
-            functools.partial(mask_kernel, slots),
-            (place, tile_ranks, kept, other),
-            [SMEM, SMEM, VMEM, VMEM],
-            outs,
-        )
-        if grouped:
-            received = [lax.all_to_all(coeff[0], "lon", 0, 0, tiled=True)]
-        else:
-            received = [shifted(coeff[k], "lon", k - slots // 2) for k in range(slots)]
-        block = (levels, half)
+        sums += [kept, swapped(sent, "depth", 1)]
+    grouped = lon_count == slots
+    slot = (2, width, count * levels)
+    coeff = call(
+        functools.partial(mask_kernel, slots),
+        (place, tile_ranks, *sums),
+        [SMEM, SMEM] + [VMEM] * len(sums),
+        [((lon_count,) + slot, bf16)] if grouped else [(slot, bf16)] * slots,
+    )
+    if grouped:
+        received = [lax.all_to_all(coeff[0], "lon", 0, 0, tiled=True)]
+    else:
+        received = [shifted(coeff[k], "lon", k - slots // 2) for k in range(slots)]
+    arrived, own = {}, None
+    block = (levels, half)
+    for stage in range(count - 2, -1, -2):
         first, second = call(
-            functools.partial(columns_kernel, slots, 4 * LANES),
-            (place, right_mine, *right_pair, *received),
+            functools.partial(columns_kernel, slots, 4 * LANES, stage),
+            (place, right, *right_pair, *received),
             [SMEM] + [VMEM] * (1 + PARTS + len(received)),
             [(block, bf16 if stage else f32), (block, bf16)],
             flops=8 * rows * half * levels,
             moved=3 << 20,
         )
+        arrived[stage + 1] = swapped(second, "depth", stage + 1)
         if stage:
             arrived[stage] = swapped(first, "depth", stage)
         else:
             own = first
-        arrived[stage + 1] = swapped(second, "depth", stage + 1)
     (gradient,) = call(
         join_kernel,
         (place, own, *(arrived[mask] for mask in range(1, count))),

time: 153 us -> 145 us (0.948); the launches traced: 150 us -> 145 us
  waiting for transfers between devices: 78.8 us -> 71.9 us
  Pallas kernels: 25.7 us -> 30.6 us
  local copies, waits for them, and re-layouts: 5.57 us -> 1.96 us
    all_to_all x2 -> x1, waiting for transfers between devices: 4.29 us -> 0.01 us  [per_device(): received = [lax.all_to_all(coeff[0], 'lon', 0, 0, tiled=True)]]
    pallas_call x8 -> x10, Pallas kernels: 11.3 us -> 15.4 us  [call(): pl.pallas_call(kernel, in_specs=in_specs, out_shape=[jax.ShapeDtypeStruct...]
    ppermute x13, starting transfers between devices: 17.6 us -> 21.3 us  [swapped(): lax.ppermute(block, axis, [(i, i ^ mask) for i in range(lax.axis_size(axi...]
    unnamed x22 -> x24, local copies, waits for them, and re-layouts: 5.57 us -> 1.96 us
    ppermute x2, waiting for transfers between devices: 24.3 us -> 20.7 us  [from_behind(): lax.ppermute(value, axis, [(source, source + steps) for source in range(i...]
    all_to_all x2 -> x1, starting transfers between devices: 6.74 us -> 4.06 us  [per_device(): received = [lax.all_to_all(coeff[0], 'lon', 0, 0, tiled=True)]]
    pallas_call x2 -> x1, Pallas kernels: 4.06 us -> 4.79 us  [pack(): pl.pallas_call(functools.partial(pack_kernel, table, ('lon', 'depth')), g...]
  transfers between devices with their start and end apart: 25 -> 24, of which waited for: 10 -> 11; matrix products, arithmetic and copies ran while one was open for 0% -> 0% of each run, Pallas kernels for 13% -> 15%
where the time goes in v3:
time: 145 us
  waiting for transfers between devices  71.9 us (50%)
  starting transfers between devices  39.3 us (27%)
  Pallas kernels  30.6 us (21%)
  local copies, waits for them, and re-layouts  1.96 us (1%)
    ppermute x13, waiting for transfers between devices, swapped(): lax.ppermute(block, axis, [(i, i ^ mask) for i in range(lax.axis_size(axi...  50.9 us
    ppermute x13, starting transfers between devices, swapped(): lax.ppermute(block, axis, [(i, i ^ mask) for i in range(lax.axis_size(axi...  21.3 us
    ppermute x2, waiting for transfers between devices, from_behind(): lax.ppermute(value, axis, [(source, source + steps) for source in range(i...  20.7 us
    pallas_call x10, Pallas kernels, call(): pl.pallas_call(kernel, in_specs=in_specs, out_shape=[jax.ShapeDtypeStruct...  15.4 us
    ppermute x8, starting transfers between devices, shifted(): return lax.ppermute(block, axis, route)  10.8 us
    pallas_call x4, Pallas kernels, sweep(): pl.pallas_call(functools.partial(step_kernel, table, step), in_specs=[VME...  9.55 us
    pallas_call x1, Pallas kernels, pack(): pl.pallas_call(functools.partial(pack_kernel, table, ('lon', 'depth')), g...  4.79 us
    all_to_all x1, starting transfers between devices, per_device(): received = [lax.all_to_all(coeff[0], 'lon', 0, 0, tiled=True)]  4.06 us
  transfers between devices with their start and end apart: 24, of which 11 were waited for; matrix products, arithmetic and copies ran while one was open for 0% of the time, Pallas kernels for 15%

profile of v3, /device:TPU:0, one launch (start us, length us, event | category | flops | bytes accessed | tf_op | source)
XLA Modules:
  0.0 144.7 jit_solution(5465618969972000073)
XLA Ops:
  0.6 4.8 %shard_map.87 = (bf16[25,16,256]{2,1,0:T(8,128)(2,1)}, bf16[25,16,256]{2,1,0:T(8,128)(2,1)}, f32[64,1,256]{2,1,0:T(1,128)}, s32[3]{0:T(128)}, bf16[8,32,2048]{2,...) custom-call(s32[64,1,128]{2,1,0:T(1,128)} %bricks.1, ...), custom_call_target="tpu_custom_call" | custom-call | bytes 1048576 | tf_op jit(solution)/shard_map/pallas_call | solution.py:345
  5.4 3.1 %collective-permute-start.14 = (bf16[8,32,2048]{2,1,0:T(8,128)(2,1)}, bf16[8,32,2048]{2,1,0:T(8,128)(2,1)S(1)}, u32[]{:S(2)}, u32[]{:S(2)}) collective-permute-start(bf16[8,32,2048]{2,1,0:T(8,128)(2,1)} %get-tuple-element.95), channel_id=1, source_target_pairs={{0,1},{1,0},{2,3},{3,2},{4,5},{5,4},{6,7},{7,6},{8,9},{9,8},{10,11... | collective-permute-start | bytes 3145736 | tf_op jit(solution)/shard_map/ppermute | solution.py:34
  13.0 2.5 %shard_map.86 = (f32[5,64,16,256]{3,2,1,0:T(8,128)S(1)}, f32[3,64,16,256]{3,2,1,0:T(8,128)S(1)}, f32[64,16,256]{2,1,0:T(8,128)S(1)}) custom-call(f32[5,64,16,256]{3,2,1,0:T(8,128)} %innov_hi.1, f32[3,64,16,256]{3,2,1,0:T(8,128)S(1)} %copy-done, f32[64,16,256]{2,1,0:T(8,128)S(1)} %copy-done.3), custom_call_target="tpu_custom_call" | custom-call | bytes 18874368 | tf_op jit(solution)/shard_map/pallas_call | solution.py:533
  15.6 20.1 %collective-permute-done.before = bf16[25,16,256]{2,1,0:T(8,128)(2,1)S(1)} collective-permute-done((bf16[25,16,256]{2,1,0:T(8,128)(2,1)}, bf16[25,16,256]{2,1,0:T(8,128)(2,1)S(1)}, u32[]{:S(2)}, u32[]{:S(2)}) %collective-permute-start) | collective-permute-done | bytes 204832 | tf_op jit(solution)/shard_map/ppermute | solution.py:22
  36.7 2.6 %collective-permute-start.3 = (f32[72,1,256]{2,1,0:T(1,128)S(1)}, f32[72,1,256]{2,1,0:T(1,128)S(1)}, u32[]{:S(2)}, u32[]{:S(2)}) collective-permute-start(f32[72,1,256]{2,1,0:T(1,128)S(1)} %get-tuple-element.65), channel_id=1, source_target_pairs={{4,0},{8,4},{12,8},{16,12},{20,16},{24,20},{28,24},{0,28},{5,1},{9... | collective-permute-start | bytes 221192 | tf_op jit(solution)/shard_map/ppermute | solution.py:30
  39.3 2.4 %shard_map.89 = (f32[72,16,256]{2,1,0:T(8,128)S(1)}, f32[72,1,256]{2,1,0:T(1,128)S(1)}, f32[72,1,256]{2,1,0:T(1,128)S(1)}) custom-call(f32[5,64,16,256]{3,2,1,0:T(8,128)S(1)} %get-tuple-element.55.innov, f32[3,64,16,256]{3,2,1,0:T(8,128)S(1)} %get-tuple-element.56.cour, f32[64,16,256]{2,1,0:T(8,128)S(1)} %get-tuple-element.57.diff, ...), custom_call_target="tpu_custom_call" | custom-call | flops 10485760 | bytes 9437184 | tf_op jit(solution)/shard_map/pallas_call | solution.py:404
  42.4 2.2 %collective-permute-start.5 = (f32[72,1,256]{2,1,0:T(1,128)S(1)}, f32[72,1,256]{2,1,0:T(1,128)S(1)}, u32[]{:S(2)}, u32[]{:S(2)}) collective-permute-start(f32[72,1,256]{2,1,0:T(1,128)S(1)} %get-tuple-element.74), channel_id=1, source_target_pairs={{4,0},{8,4},{12,8},{16,12},{20,16},{24,20},{28,24},{0,28},{5,1},{9... | collective-permute-start | bytes 221192 | tf_op jit(solution)/shard_map/ppermute | solution.py:30
  44.6 2.4 %shard_map.91 = (f32[72,16,256]{2,1,0:T(8,128)S(1)}, f32[72,1,256]{2,1,0:T(1,128)S(1)}, f32[72,1,256]{2,1,0:T(1,128)S(1)}) custom-call(f32[5,64,16,256]{3,2,1,0:T(8,128)S(1)} %get-tuple-element.55.innov, f32[3,64,16,256]{3,2,1,0:T(8,128)S(1)} %get-tuple-element.56.cour, f32[64,16,256]{2,1,0:T(8,128)S(1)} %get-tuple-element.57.diff, ...), custom_call_target="tpu_custom_call" | custom-call | flops 10485760 | bytes 9437184 | tf_op jit(solution)/shard_map/pallas_call | solution.py:404
  47.7 2.2 %collective-permute-start.7 = (f32[72,1,256]{2,1,0:T(1,128)S(1)}, f32[72,1,256]{2,1,0:T(1,128)S(1)}, u32[]{:S(2)}, u32[]{:S(2)}) collective-permute-start(f32[72,1,256]{2,1,0:T(1,128)S(1)} %get-tuple-element.81), channel_id=1, source_target_pairs={{4,0},{8,4},{12,8},{16,12},{20,16},{24,20},{28,24},{0,28},{5,1},{9... | collective-permute-start | bytes 221192 | tf_op jit(solution)/shard_map/ppermute | solution.py:30
  50.0 2.4 %shard_map.93 = (f32[72,16,256]{2,1,0:T(8,128)S(1)}, f32[72,1,256]{2,1,0:T(1,128)S(1)}, f32[72,1,256]{2,1,0:T(1,128)S(1)}) custom-call(f32[5,64,16,256]{3,2,1,0:T(8,128)S(1)} %get-tuple-element.55.innov, f32[3,64,16,256]{3,2,1,0:T(8,128)S(1)} %get-tuple-element.56.cour, f32[64,16,256]{2,1,0:T(8,128)S(1)} %get-tuple-element.57.diff, ...), custom_call_target="tpu_custom_call" | custom-call | flops 10485760 | bytes 9437184 | tf_op jit(solution)/shard_map/pallas_call | solution.py:404
  53.1 2.3 %collective-permute-start.9 = (f32[72,1,256]{2,1,0:T(1,128)S(1)}, f32[72,1,256]{2,1,0:T(1,128)S(1)}, u32[]{:S(2)}, u32[]{:S(2)}) collective-permute-start(f32[72,1,256]{2,1,0:T(1,128)S(1)} %get-tuple-element.89), channel_id=1, source_target_pairs={{4,0},{8,4},{12,8},{16,12},{20,16},{24,20},{28,24},{0,28},{5,1},{9... | collective-permute-start | bytes 221192 | tf_op jit(solution)/shard_map/ppermute | solution.py:30
  55.4 2.4 %shard_map.95 = (f32[72,16,256]{2,1,0:T(8,128)S(1)}, f32[72,1,256]{2,1,0:T(1,128)S(1)}, f32[72,1,256]{2,1,0:T(1,128)S(1)}) custom-call(f32[5,64,16,256]{3,2,1,0:T(8,128)S(1)} %get-tuple-element.55.innov, f32[3,64,16,256]{3,2,1,0:T(8,128)S(1)} %get-tuple-element.56.cour, f32[64,16,256]{2,1,0:T(8,128)S(1)} %get-tuple-element.57.diff, ...), custom_call_target="tpu_custom_call" | custom-call | flops 10485760 | bytes 9437184 | tf_op jit(solution)/shard_map/pallas_call | solution.py:404
  59.5 2.8 %collective-permute-start.17 = (bf16[64,2048]{1,0:T(8,128)(2,1)S(1)}, bf16[64,2048]{1,0:T(8,128)(2,1)S(1)}, u32[]{:S(2)}, u32[]{:S(2)}) collective-permute-start(bf16[64,2048]{1,0:T(8,128)(2,1)S(1)} %get-tuple-element.98.first), channel_id=1, source_target_pairs={{0,2},{1,3},{2,0},{3,1},{4,6},{5,7},{6,4},{7,5},{8,10},{9,11},{10,... | collective-permute-start | bytes 786440 | tf_op jit(solution)/shard_map/ppermute | solution.py:34
  63.9 16.7 %collective-permute-done.17.first = bf16[64,2048]{1,0:T(8,128)(2,1)S(1)} collective-permute-done((bf16[64,2048]{1,0:T(8,128)(2,1)S(1)}, bf16[64,2048]{1,0:T(8,128)(2,1)S(1)}, u32[]{:S(2)}, u32[]{:S(2)}) %collective-permute-start.17) | collective-permute-done | bytes 262176 | tf_op jit(solution)/shard_map/ppermute | solution.py:34
  82.5 5.2 %collective-permute-start.19 = (bf16[2,256,128]{2,1,0:T(8,128)(2,1)S(1)}, bf16[2,256,128]{2,1,0:T(8,128)(2,1)S(1)}, u32[]{:S(2)}, u32[]{:S(2)}) collective-permute-start(bf16[2,256,128]{2,1,0:T(8,128)(2,1)S(1)} %get-tuple-element.103), channel_id=1, source_target_pairs={{0,1},{1,0},{2,3},{3,2},{4,5},{5,4},{6,7},{7,6},{8,9},{9,8},{10,11... | collective-permute-start | bytes 393224 | tf_op jit(solution)/shard_map/ppermute | solution.py:34
  94.1 2.0 %collective-permute-done.16.rest_1_ = bf16[2,256,128]{2,1,0:T(8,128)(2,1)S(1)} collective-permute-done((bf16[2,256,128]{2,1,0:T(8,128)(2,1)S(1)}, bf16[2,256,128]{2,1,0:T(8,128)(2,1)S(1)}, u32[]{:S(2)}, u32[]{:S(2)}) %collective-permute-start.16) | collective-permute-done | bytes 131104 | tf_op jit(solution)/shard_map/ppermute | solution.py:34
  97.4 4.1 %all-to-all-start = ((bf16[8,2,32,256]{3,2,1,0:T(8,128)(2,1)}), bf16[8,2,32,256]{3,2,1,0:T(8,128)(2,1)}, u32[]{:S(2)}, u32[]{:S(2)}) async-start(bf16[8,2,32,256]{3,2,1,0:T(8,128)(2,1)} %copy-done.4), calls=%async_computation | async-start | bytes 524288 | tf_op jit(solution)/shard_map/all_to_all | solution.py:594
  101.8 5.6 %collective-permute-done.11 = bf16[2,32,2048]{2,1,0:T(8,128)(2,1)} collective-permute-done((bf16[2,32,2048]{2,1,0:T(8,128)(2,1)}, bf16[2,32,2048]{2,1,0:T(8,128)(2,1)}, u32[]{:S(2)}, u32[]{:S(2)}) %collective-permute-start.11) | collective-permute-done | bytes 262176 | tf_op jit(solution)/shard_map/ppermute | solution.py:34
  107.4 5.6 %collective-permute-done.12 = bf16[2,32,2048]{2,1,0:T(8,128)(2,1)} collective-permute-done((bf16[2,32,2048]{2,1,0:T(8,128)(2,1)}, bf16[2,32,2048]{2,1,0:T(8,128)(2,1)}, u32[]{:S(2)}, u32[]{:S(2)}) %collective-permute-start.12) | collective-permute-done | bytes 262176 | tf_op jit(solution)/shard_map/ppermute | solution.py:34
  113.0 4.4 %collective-permute-done.13 = bf16[2,32,2048]{2,1,0:T(8,128)(2,1)} collective-permute-done((bf16[2,32,2048]{2,1,0:T(8,128)(2,1)}, bf16[2,32,2048]{2,1,0:T(8,128)(2,1)}, u32[]{:S(2)}, u32[]{:S(2)}) %collective-permute-start.13) | collective-permute-done | bytes 262176 | tf_op jit(solution)/shard_map/ppermute | solution.py:34
  119.2 3.2 %collective-permute-start.21 = (bf16[64,2048]{1,0:T(8,128)(2,1)S(1)}, bf16[64,2048]{1,0:T(8,128)(2,1)S(1)}, u32[]{:S(2)}, u32[]{:S(2)}) collective-permute-start(bf16[64,2048]{1,0:T(8,128)(2,1)S(1)} %get-tuple-element.106), channel_id=1, source_target_pairs={{0,2},{1,3},{2,0},{3,1},{4,6},{5,7},{6,4},{7,5},{8,10},{9,11},{10,... | collective-permute-start | bytes 786440 | tf_op jit(solution)/shard_map/ppermute | solution.py:34
  126.2 13.4 %collective-permute-done.21.arrived2 = bf16[64,2048]{1,0:T(8,128)(2,1)S(1)} collective-permute-done((bf16[64,2048]{1,0:T(8,128)(2,1)S(1)}, bf16[64,2048]{1,0:T(8,128)(2,1)S(1)}, u32[]{:S(2)}, u32[]{:S(2)}) %collective-permute-start.21) | collective-permute-done | bytes 262176 | tf_op jit(solution)/shard_map/ppermute | solution.py:34
  139.6 2.9 %collective-permute-done.20.arrived1 = bf16[64,2048]{1,0:T(8,128)(2,1)S(1)} collective-permute-done((bf16[64,2048]{1,0:T(8,128)(2,1)S(1)}, bf16[64,2048]{1,0:T(8,128)(2,1)S(1)}, u32[]{:S(2)}, u32[]{:S(2)}) %collective-permute-start.20) | collective-permute-done | bytes 262176 | tf_op jit(solution)/shard_map/ppermute | solution.py:34
  142.5 2.2 %shard_map.104 = f32[64,16,256]{2,1,0:T(8,128)} custom-call(s32[3]{0:T(128)S(1)} %copy-done.10, f32[64,2048]{1,0:T(8,128)S(1)} %get-tuple-element.104.own, bf16[64,2048]{1,0:T(8,128)(2,1)S(1)} %collective-permute-done.20.arrived1, bf16[64,2048]{1,0:T(8,128)(2,1)S(1)} %collective-permute-done.21.arrived2, bf16[64,2048]{1,0:T(8,128)(2,1)S(1)} %collective-permute-done.22.arrived3), custom_call_target="tpu_custom_call" | custom-call | bytes 4194304 | tf_op jit(solution)/shard_map/pallas_call | solution.py:533
  (67 shorter events, 26.3 us)
Async XLA Ops:
  5.4 75.2 %collective-permute-start.14 = (bf16[8,32,2048]{2,1,0:T(8,128)(2,1)}, bf16[8,32,2048]{2,1,0:T(8,128)(2,1)S(1)}, u32[]{:S(2)}, u32[]{:S(2)}) collective-permute-start(bf16[8,32,2048]{2,1,0:T(8,128)(2,1)} %get-tuple-element.95), channel_id=1, source_target_pairs={{0,1},{1,0},{2,3},{3,2},{4,5},{5,4},{6,7},{7,6},{8,9},{9,8},{10,11... | collective-permute-start | bytes 3145736 | tf_op jit(solution)/shard_map/ppermute | solution.py:34
  8.6 27.1 %collective-permute-start = (bf16[25,16,256]{2,1,0:T(8,128)(2,1)}, bf16[25,16,256]{2,1,0:T(8,128)(2,1)S(1)}, u32[]{:S(2)}, u32[]{:S(2)}) collective-permute-start(bf16[25,16,256]{2,1,0:T(8,128)(2,1)} %get-tuple-element.59), channel_id=1, source_target_pairs={{0,1},{1,2},{2,3},{4,5},{5,6},{6,7},{8,9},{9,10},{10,11},{12,13},{... | collective-permute-start | bytes 614408 | tf_op jit(solution)/shard_map/ppermute | solution.py:22
  10.5 25.8 %collective-permute-start.1 = (bf16[25,16,256]{2,1,0:T(8,128)(2,1)}, bf16[25,16,256]{2,1,0:T(8,128)(2,1)S(1)}, u32[]{:S(2)}, u32[]{:S(2)}) collective-permute-start(bf16[25,16,256]{2,1,0:T(8,128)(2,1)} %get-tuple-element.60), channel_id=1, source_target_pairs={{1,0},{2,1},{3,2},{5,4},{6,5},{7,6},{9,8},{10,9},{11,10},{13,12},{... | collective-permute-start | bytes 614408 | tf_op jit(solution)/shard_map/ppermute | solution.py:22
  36.6 5.1 %collective-permute-start.2 = (f32[72,1,256]{2,1,0:T(1,128)S(1)}, f32[72,1,256]{2,1,0:T(1,128)S(1)}, u32[]{:S(2)}, u32[]{:S(2)}) collective-permute-start(f32[72,1,256]{2,1,0:T(1,128)S(1)} %get-tuple-element.64), channel_id=1, source_target_pairs={{28,0},{0,4},{4,8},{8,12},{12,16},{16,20},{20,24},{24,28},{29,1},{... | collective-permute-start | bytes 221192 | tf_op jit(solution)/shard_map/ppermute | solution.py:30
  36.7 5.1 %collective-permute-start.3 = (f32[72,1,256]{2,1,0:T(1,128)S(1)}, f32[72,1,256]{2,1,0:T(1,128)S(1)}, u32[]{:S(2)}, u32[]{:S(2)}) collective-permute-start(f32[72,1,256]{2,1,0:T(1,128)S(1)} %get-tuple-element.65), channel_id=1, source_target_pairs={{4,0},{8,4},{12,8},{16,12},{20,16},{24,20},{28,24},{0,28},{5,1},{9... | collective-permute-start | bytes 221192 | tf_op jit(solution)/shard_map/ppermute | solution.py:30
  41.9 5.1 %collective-permute-start.4 = (f32[72,1,256]{2,1,0:T(1,128)S(1)}, f32[72,1,256]{2,1,0:T(1,128)S(1)}, u32[]{:S(2)}, u32[]{:S(2)}) collective-permute-start(f32[72,1,256]{2,1,0:T(1,128)S(1)} %get-tuple-element.73), channel_id=1, source_target_pairs={{28,0},{0,4},{4,8},{8,12},{12,16},{16,20},{20,24},{24,28},{29,1},{... | collective-permute-start | bytes 221192 | tf_op jit(solution)/shard_map/ppermute | solution.py:30
  42.4 4.6 %collective-permute-start.5 = (f32[72,1,256]{2,1,0:T(1,128)S(1)}, f32[72,1,256]{2,1,0:T(1,128)S(1)}, u32[]{:S(2)}, u32[]{:S(2)}) collective-permute-start(f32[72,1,256]{2,1,0:T(1,128)S(1)} %get-tuple-element.74), channel_id=1, source_target_pairs={{4,0},{8,4},{12,8},{16,12},{20,16},{24,20},{28,24},{0,28},{5,1},{9... | collective-permute-start | bytes 221192 | tf_op jit(solution)/shard_map/ppermute | solution.py:30
  47.3 5.3 %collective-permute-start.6 = (f32[72,1,256]{2,1,0:T(1,128)S(1)}, f32[72,1,256]{2,1,0:T(1,128)S(1)}, u32[]{:S(2)}, u32[]{:S(2)}) collective-permute-start(f32[72,1,256]{2,1,0:T(1,128)S(1)} %get-tuple-element.80), channel_id=1, source_target_pairs={{28,0},{0,4},{4,8},{8,12},{12,16},{16,20},{20,24},{24,28},{29,1},{... | collective-permute-start | bytes 221192 | tf_op jit(solution)/shard_map/ppermute | solution.py:30
  47.7 4.8 %collective-permute-start.7 = (f32[72,1,256]{2,1,0:T(1,128)S(1)}, f32[72,1,256]{2,1,0:T(1,128)S(1)}, u32[]{:S(2)}, u32[]{:S(2)}) collective-permute-start(f32[72,1,256]{2,1,0:T(1,128)S(1)} %get-tuple-element.81), channel_id=1, source_target_pairs={{4,0},{8,4},{12,8},{16,12},{20,16},{24,20},{28,24},{0,28},{5,1},{9... | collective-permute-start | bytes 221192 | tf_op jit(solution)/shard_map/ppermute | solution.py:30
  52.7 6.1 %collective-permute-start.8 = (f32[72,1,256]{2,1,0:T(1,128)S(1)}, f32[72,1,256]{2,1,0:T(1,128)S(1)}, u32[]{:S(2)}, u32[]{:S(2)}) collective-permute-start(f32[72,1,256]{2,1,0:T(1,128)S(1)} %get-tuple-element.88), channel_id=1, source_target_pairs={{28,0},{0,4},{4,8},{8,12},{12,16},{16,20},{20,24},{24,28},{29,1},{... | collective-permute-start | bytes 221192 | tf_op jit(solution)/shard_map/ppermute | solution.py:30
  53.1 5.7 %collective-permute-start.9 = (f32[72,1,256]{2,1,0:T(1,128)S(1)}, f32[72,1,256]{2,1,0:T(1,128)S(1)}, u32[]{:S(2)}, u32[]{:S(2)}) collective-permute-start(f32[72,1,256]{2,1,0:T(1,128)S(1)} %get-tuple-element.89), channel_id=1, source_target_pairs={{4,0},{8,4},{12,8},{16,12},{20,16},{24,20},{28,24},{0,28},{5,1},{9... | collective-permute-start | bytes 221192 | tf_op jit(solution)/shard_map/ppermute | solution.py:30
  59.5 21.1 %collective-permute-start.17 = (bf16[64,2048]{1,0:T(8,128)(2,1)S(1)}, bf16[64,2048]{1,0:T(8,128)(2,1)S(1)}, u32[]{:S(2)}, u32[]{:S(2)}) collective-permute-start(bf16[64,2048]{1,0:T(8,128)(2,1)S(1)} %get-tuple-element.98.first), channel_id=1, source_target_pairs={{0,2},{1,3},{2,0},{3,1},{4,6},{5,7},{6,4},{7,5},{8,10},{9,11},{10,... | collective-permute-start | bytes 786440 | tf_op jit(solution)/shard_map/ppermute | solution.py:34
  62.3 18.3 %collective-permute-start.18 = (bf16[64,2048]{1,0:T(8,128)(2,1)S(1)}, bf16[64,2048]{1,0:T(8,128)(2,1)S(1)}, u32[]{:S(2)}, u32[]{:S(2)}) collective-permute-start(bf16[64,2048]{1,0:T(8,128)(2,1)S(1)} %get-tuple-element.99), channel_id=1, source_target_pairs={{0,3},{1,2},{2,1},{3,0},{4,7},{5,6},{6,5},{7,4},{8,11},{9,10},{10,... | collective-permute-start | bytes 786440 | tf_op jit(solution)/shard_map/ppermute | solution.py:34
  63.7 24.1 %collective-permute-start.15 = (bf16[64,2048]{1,0:T(8,128)(2,1)S(1)}, bf16[64,2048]{1,0:T(8,128)(2,1)S(1)}, u32[]{:S(2)}, u32[]{:S(2)}) collective-permute-start(bf16[64,2048]{1,0:T(8,128)(2,1)S(1)} %get-tuple-element.99), channel_id=1, source_target_pairs={{0,1},{1,0},{2,3},{3,2},{4,5},{5,4},{6,7},{7,6},{8,9},{9,8},{10,11... | collective-permute-start | bytes 786440 | tf_op jit(solution)/shard_map/ppermute | solution.py:34
  82.5 11.2 %collective-permute-start.19 = (bf16[2,256,128]{2,1,0:T(8,128)(2,1)S(1)}, bf16[2,256,128]{2,1,0:T(8,128)(2,1)S(1)}, u32[]{:S(2)}, u32[]{:S(2)}) collective-permute-start(bf16[2,256,128]{2,1,0:T(8,128)(2,1)S(1)} %get-tuple-element.103), channel_id=1, source_target_pairs={{0,1},{1,0},{2,3},{3,2},{4,5},{5,4},{6,7},{7,6},{8,9},{9,8},{10,11... | collective-permute-start | bytes 393224 | tf_op jit(solution)/shard_map/ppermute | solution.py:34
  89.6 6.4 %collective-permute-start.16 = (bf16[2,256,128]{2,1,0:T(8,128)(2,1)S(1)}, bf16[2,256,128]{2,1,0:T(8,128)(2,1)S(1)}, u32[]{:S(2)}, u32[]{:S(2)}) collective-permute-start(bf16[2,256,128]{2,1,0:T(8,128)(2,1)S(1)} %get-tuple-element.101), channel_id=1, source_target_pairs={{0,1},{1,0},{2,3},{3,2},{4,5},{5,4},{6,7},{7,6},{8,9},{9,8},{10,11... | collective-permute-start | bytes 393224 | tf_op jit(solution)/shard_map/ppermute | solution.py:34
  89.7 12.1 %collective-permute-start.10 = (bf16[2,32,2048]{2,1,0:T(8,128)(2,1)}, bf16[2,32,2048]{2,1,0:T(8,128)(2,1)}, u32[]{:S(2)}, u32[]{:S(2)}) collective-permute-start(bf16[2,32,2048]{2,1,0:T(8,128)(2,1)} %get-tuple-element.91), channel_id=1, source_target_pairs={{0,1},{1,0},{2,3},{3,2},{4,5},{5,4},{6,7},{7,6},{8,9},{9,8},{10,11... | collective-permute-start | bytes 786440 | tf_op jit(solution)/shard_map/ppermute | solution.py:34
  91.7 15.7 %collective-permute-start.11 = (bf16[2,32,2048]{2,1,0:T(8,128)(2,1)}, bf16[2,32,2048]{2,1,0:T(8,128)(2,1)}, u32[]{:S(2)}, u32[]{:S(2)}) collective-permute-start(bf16[2,32,2048]{2,1,0:T(8,128)(2,1)} %get-tuple-element.92), channel_id=1, source_target_pairs={{0,1},{1,0},{2,3},{3,2},{4,5},{5,4},{6,7},{7,6},{8,9},{9,8},{10,11... | collective-permute-start | bytes 786440 | tf_op jit(solution)/shard_map/ppermute | solution.py:34
  91.8 21.2 %collective-permute-start.12 = (bf16[2,32,2048]{2,1,0:T(8,128)(2,1)}, bf16[2,32,2048]{2,1,0:T(8,128)(2,1)}, u32[]{:S(2)}, u32[]{:S(2)}) collective-permute-start(bf16[2,32,2048]{2,1,0:T(8,128)(2,1)} %get-tuple-element.93), channel_id=1, source_target_pairs={{0,1},{1,0},{2,3},{3,2},{4,5},{5,4},{6,7},{7,6},{8,9},{9,8},{10,11... | collective-permute-start | bytes 786440 | tf_op jit(solution)/shard_map/ppermute | solution.py:34
  93.8 23.7 %collective-permute-start.13 = (bf16[2,32,2048]{2,1,0:T(8,128)(2,1)}, bf16[2,32,2048]{2,1,0:T(8,128)(2,1)}, u32[]{:S(2)}, u32[]{:S(2)}) collective-permute-start(bf16[2,32,2048]{2,1,0:T(8,128)(2,1)} %get-tuple-element.94), channel_id=1, source_target_pairs={{0,1},{1,0},{2,3},{3,2},{4,5},{5,4},{6,7},{7,6},{8,9},{9,8},{10,11... | collective-permute-start | bytes 786440 | tf_op jit(solution)/shard_map/ppermute | solution.py:34
  97.4 20.0 %all-to-all-start = ((bf16[8,2,32,256]{3,2,1,0:T(8,128)(2,1)}), bf16[8,2,32,256]{3,2,1,0:T(8,128)(2,1)}, u32[]{:S(2)}, u32[]{:S(2)}) async-start(bf16[8,2,32,256]{3,2,1,0:T(8,128)(2,1)} %copy-done.4), calls=%async_computation | async-start | bytes 524288 | tf_op jit(solution)/shard_map/all_to_all | solution.py:594
  119.2 20.4 %collective-permute-start.21 = (bf16[64,2048]{1,0:T(8,128)(2,1)S(1)}, bf16[64,2048]{1,0:T(8,128)(2,1)S(1)}, u32[]{:S(2)}, u32[]{:S(2)}) collective-permute-start(bf16[64,2048]{1,0:T(8,128)(2,1)S(1)} %get-tuple-element.106), channel_id=1, source_target_pairs={{0,2},{1,3},{2,0},{3,1},{4,6},{5,7},{6,4},{7,5},{8,10},{9,11},{10,... | collective-permute-start | bytes 786440 | tf_op jit(solution)/shard_map/ppermute | solution.py:34
  122.3 17.3 %collective-permute-start.22 = (bf16[64,2048]{1,0:T(8,128)(2,1)S(1)}, bf16[64,2048]{1,0:T(8,128)(2,1)S(1)}, u32[]{:S(2)}, u32[]{:S(2)}) collective-permute-start(bf16[64,2048]{1,0:T(8,128)(2,1)S(1)} %get-tuple-element.107), channel_id=1, source_target_pairs={{0,3},{1,2},{2,1},{3,0},{4,7},{5,6},{6,5},{7,4},{8,11},{9,10},{10,... | collective-permute-start | bytes 786440 | tf_op jit(solution)/shard_map/ppermute | solution.py:34
  124.6 17.9 %collective-permute-start.20 = (bf16[64,2048]{1,0:T(8,128)(2,1)S(1)}, bf16[64,2048]{1,0:T(8,128)(2,1)S(1)}, u32[]{:S(2)}, u32[]{:S(2)}) collective-permute-start(bf16[64,2048]{1,0:T(8,128)(2,1)S(1)} %get-tuple-element.105), channel_id=1, source_target_pairs={{0,1},{1,0},{2,3},{3,2},{4,5},{5,4},{6,7},{7,6},{8,9},{9,8},{10,11... | collective-permute-start | bytes 786440 | tf_op jit(solution)/shard_map/ppermute | solution.py:34
  (12 other events, 173.6 us)

commit v4 on v3

--- a/solution.py
+++ b/solution.py
@@ -6,10 +6,12 @@
 from jax.experimental.pallas import tpu as pltpu
 from jax.sharding import PartitionSpec as P
 
-UNROLL = 3
+UNROLL = 9
 LANES = 128
 PARTS = 4
 STAGES = 2
+LANE_TILES = 2
+HALVES = 2
 GRANT = 4 << 20
 VMEM = pl.BlockSpec(memory_space=pltpu.VMEM)
 SMEM = pl.BlockSpec(memory_space=pltpu.SMEM)
@@ -47,19 +49,14 @@
     return order, at + 1
 
 
-def pack_kernel(table, axes, bricks, innov_lo, innov_hi, cour_lo, cour_hi, diff_lo, diff_hi, left, right, *rest):
-    down, up, sea, place, left_other, *right_other = rest[:-3]
-    rows, vmem, sems = rest[-3:]
+def pack_kernel(table, axes, bricks, innov_lo, innov_hi, cour_lo, cour_hi, diff_lo, diff_hi, left, down, up, sea, place, left_other, rows, vmem, sems):
     me = lax.axis_index(axes[1])
     side = lax.rem(me, 2)
     place[0], place[1], place[2] = me, side, lax.axis_index(axes[0])
     half = left_other.shape[2]
     start = pl.multiple_of((1 - side) * half, half)
-    loads, stores = [], []
-    for n, source in enumerate((left, right)):
-        window = source.at[0, :, :, pl.ds(start, half)]
-        loads.append(pltpu.make_async_copy(window, vmem.at[n], sems.at[n]))
-        loads[-1].start()
+    load = pltpu.make_async_copy(left.at[0, :, :, pl.ds(start, half)], vmem, sems.at[0])
+    load.start()
     depth = diff_lo.shape[0]
     levels, _, count = bricks.shape
     lat_cells = sea.shape[2]
@@ -94,15 +91,27 @@
                     value = innov[name[1], z]
             out[at] = value.astype(jnp.bfloat16)
 
+    load.wait()
+    store = pltpu.make_async_copy(vmem, left_other, sems.at[1])
+    store.start()
     fill(down, innov_hi, cour_hi, diff_hi, sea_hi, lambda d: depth - d)
     fill(up, innov_lo, cour_lo, diff_lo, sea_lo, lambda d: d - 1)
-    for n, targets in enumerate(([left_other], right_other)):
-        loads[n].wait()
-        size = vmem.shape[1] // len(targets)
-        for q, target in enumerate(targets):
-            piece = vmem.at[n, pl.ds(q * size, size)]
-            stores.append(pltpu.make_async_copy(piece, target, sems.at[2 + len(stores)]))
-            stores[-1].start()
+    store.wait()
+
+
+def halves_kernel(place, right, *rest):
+    targets, (vmem, sems) = rest[:-2], rest[-2:]
+    wide = targets[0].shape[2]
+    start = (1 - place[1]) * wide * len(targets)
+    loads, stores = [], []
+    for n, target in enumerate(targets):
+        window = pl.ds(pl.multiple_of(start + n * wide, wide), wide)
+        loads.append(pltpu.make_async_copy(right.at[0, :, :, window], vmem.at[n], sems.at[n]))
+        loads[-1].start()
+        stores.append(pltpu.make_async_copy(vmem.at[n], target, sems.at[len(targets) + n]))
+    for load, store in zip(loads, stores):
+        load.wait()
+        store.start()
     for store in stores:
         store.wait()
 
@@ -325,7 +334,7 @@
     to_west[...], to_east[...] = west_gain[...] * low_rows, east_gain[...] * high_rows
 
 
-def pack(innovations, courant, diffusivity, bricks, left, right):
+def pack(innovations, courant, diffusivity, bricks, left):
     levels, lon_cells, lat_cells = diffusivity.shape
     steps = innovations.shape[0] - 1
     table, layers = halo_table(steps)
@@ -341,7 +350,6 @@
     message = jax.ShapeDtypeStruct((layers, lon_cells, lat_cells), bf16)
     _, slots, width, cols = left.shape
     other = jax.ShapeDtypeStruct((slots, width, cols // 2), bf16)
-    piece = jax.ShapeDtypeStruct((slots // PARTS, width, cols // 2), bf16)
     return pl.pallas_call(
         functools.partial(pack_kernel, table, ("lon", "depth")),
         grid=(1,),
@@ -349,23 +357,22 @@
         + edges(innovations.shape, 1)
         + edges(courant.shape, 1)
         + edges(diffusivity.shape, 0)
-        + [ANY, ANY],
+        + [ANY],
         out_shape=[
             message,
             message,
             jax.ShapeDtypeStruct((levels, 1, lat_cells), f32),
             jax.ShapeDtypeStruct((3,), jnp.int32),
             other,
-        ]
-        + [piece] * PARTS,
-        out_specs=[VMEM, VMEM, VMEM, SMEM] + [ANY] * (1 + PARTS),
+        ],
+        out_specs=[VMEM, VMEM, VMEM, SMEM, ANY],
         scratch_shapes=[
             pltpu.VMEM((levels, bricks.shape[2]), f32),
-            pltpu.VMEM((2, slots, width, cols // 2), bf16),
-            pltpu.SemaphoreType.DMA((3 + PARTS,)),
+            pltpu.VMEM((slots, width, cols // 2), bf16),
+            pltpu.SemaphoreType.DMA((2,)),
         ],
         cost_estimate=pl.CostEstimate(flops=0, bytes_accessed=1 << 20, transcendentals=0),
-    )(bricks, innovations, innovations, courant, courant, diffusivity, diffusivity, left, right)
+    )(bricks, innovations, innovations, courant, courant, diffusivity, diffusivity, left)
 
 
 def sweep(innovations, courant, diffusivity, sea, down, up, place):
@@ -452,13 +459,21 @@
     return lax.dot_general(a, b, (((1,), (1,)), ((), ())), preferred_element_type=jnp.float32)
 
 
-def rows_kernel(place, left, left_pair, first, second, kept, sent):
+def rows_kernel(wide, place, left, left_pair, first, second, kept, sent):
     half = left_pair.shape[1]
-    mine = left[:, pl.ds(pl.multiple_of(place[1] * half, half), half)]
-    for c, factor in enumerate((mine, left_pair[...])):
-        parts = [against(factor, block[...]) for block in (first, second)]
-        kept[c] = jnp.concatenate(parts, 1)
-        sent[1 - c] = jnp.concatenate(parts[::-1], 1).astype(jnp.bfloat16)
+    levels = first.shape[0]
+    sums = [None, None]
+    for at in range(0, half, wide):
+        lanes = slice(at, at + wide)
+        mine = left[:, pl.ds(pl.multiple_of(place[1] * half + at, LANES), wide)]
+        both = jnp.concatenate([first[:, lanes], second[:, lanes]], 0)
+        for c, factor in enumerate((mine, left_pair[:, lanes])):
+            term = against(factor, both)
+            sums[c] = term if at == 0 else sums[c] + term
+    for c in range(2):
+        kept[c] = sums[c]
+        other_order = [sums[c][:, levels:], sums[c][:, :levels]]
+        sent[1 - c] = jnp.concatenate(other_order, 1).astype(jnp.bfloat16)
 
 
 def mask_kernel(slots, place, ranks, *rest):
@@ -481,10 +496,13 @@
                 out[0][lax.rem(place[2] + (k - slots // 2 + count), count), c] = value
 
 
-def columns_kernel(slots, wide, stage, place, right, *rest):
-    right_pair, received, out = rest[:PARTS], rest[PARTS:-2], rest[-2:]
+def columns_kernel(slots, stage, start, place, right, *rest):
+    pieces = PARTS // HALVES
+    right_pair, received, out = rest[:pieces], rest[pieces:-2], rest[-2:]
     count = received[0].shape[0]
-    levels, half = out[0].shape
+    levels = out[0].shape[0]
+    wide = right_pair[0].shape[1]
+    half = wide * PARTS
     picked = slice(stage * levels, (stage + 2) * levels)
     coeffs = []
     for c in range(2):
@@ -497,36 +515,42 @@
     stacked = jnp.concatenate(coeffs, 0)
     rows = right.shape[0]
     lead = (((0,), (0,)), ((), ()))
-    for at in range(0, half, wide):
-        lanes = slice(at, at + wide)
-        mine = right[:, pl.ds(pl.multiple_of(place[1] * half + at, LANES), wide)]
+    for n, piece in enumerate(right_pair):
+        lanes = slice(n * wide, (n + 1) * wide)
+        mine = right[:, pl.ds(pl.multiple_of(place[1] * half + start + n * wide, LANES), wide)]
         total = lax.dot_general(stacked[:rows], mine, lead, preferred_element_type=jnp.float32)
-        pair = jnp.concatenate([piece[:, lanes] for piece in right_pair], 0)
-        total = total + lax.dot_general(stacked[rows:], pair, lead, preferred_element_type=jnp.float32)
+        total = total + lax.dot_general(stacked[rows:], piece[...], lead, preferred_element_type=jnp.float32)
         out[0][:, lanes] = total[:levels].astype(out[0].dtype)
         out[1][:, lanes] = total[levels:].astype(out[1].dtype)
 
 
-def join_kernel(place, own, arrived1, arrived2, arrived3, out, *rows):
-    levels, lon_cells, lat_cells = out.shape
-    half = lon_cells // 2
+def join_kernel(flip, place, *rest):
+    ones, twos = rest[:HALVES], rest[HALVES : 2 * HALVES]
+    out, slab, sem, *rows = rest[-(3 + LANE_TILES) :]
+    levels, half, lat_cells = slab.shape
     f32 = jnp.float32
+    each = half // HALVES
     for x in range(half):
         for c, lanes in enumerate(rows):
-            at = x * lat_cells + c * LANES
+            at = (x % each) * lat_cells + c * LANES
             cols = slice(at, at + LANES)
-            mine = own[:, cols] + arrived2[:, cols].astype(f32)
-            other = arrived1[:, cols].astype(f32) + arrived3[:, cols].astype(f32)
-            lanes[pl.ds(place[1] * half + x, levels, stride=lon_cells), :] = mine
-            lanes[pl.ds((1 - place[1]) * half + x, levels, stride=lon_cells), :] = other
-
-    def one(z, carry):
-        at = pl.multiple_of(z * lon_cells, lon_cells)
-        for c, lanes in enumerate(rows):
-            out[z, :, c * LANES : (c + 1) * LANES] = lanes[pl.ds(at, lon_cells), :]
-        return carry
-
-    lax.fori_loop(0, levels, one, 0, unroll=4)
+            value = ones[x // each][:, cols].astype(f32) + twos[x // each][:, cols].astype(f32)
+            lanes[pl.ds(x, levels, stride=half), :] = value
+    side = 1 - place[1] if flip else place[1]
+    start = pl.multiple_of(side * half, half)
+    parts = 4
+    size = levels // parts
+    copies = []
+    for part in range(parts):
+        for z in range(part * size, (part + 1) * size):
+            for c, lanes in enumerate(rows):
+                slab[z, :, c * LANES : (c + 1) * LANES] = lanes[z * half : (z + 1) * half, :]
+        here = pl.ds(part * size, size)
+        target = out.at[here, pl.ds(start, half)]
+        copies.append(pltpu.make_async_copy(slab.at[here], target, sem.at[part]))
+        copies[-1].start()
+    for copy in copies:
+        copy.wait()
 
 
 def call(kernel, operands, in_specs, outs, grant=GRANT, flops=0, moved=1 << 20, scratch=(), aliases=None):
@@ -557,24 +581,30 @@
     width = left.shape[2]
     rows = slots * width
 
-    down, up, sea, place, left_other, *right_other = pack(
-        innovations, courant, diffusivity, sea_bricks, left, right
+    down, up, sea, place, left_other = pack(innovations, courant, diffusivity, sea_bricks, left)
+    right_other = call(
+        halves_kernel,
+        (place, right),
+        [SMEM, ANY],
+        [((slots, width, half // PARTS), bf16, ANY)] * PARTS,
+        moved=4 << 20,
+        scratch=[pltpu.VMEM((PARTS, slots, width, half // PARTS), bf16), pltpu.SemaphoreType.DMA((2 * PARTS,))],
     )
     left_pair = swapped(left_other, "depth", 1)
     right_pair = []
     for part in range(PARTS):
-        right_pair.append(swapped(right_other[part], "depth", 1).reshape(rows // PARTS, half))
+        right_pair.append(swapped(right_other[part], "depth", 1).reshape(rows, half // PARTS))
     lam, lam_mine, lam_other = sweep(innovations, courant, diffusivity, sea, down, up, place)
     left_pair = left_pair.reshape(rows, half)
     left, right = left.reshape(rows, tile_cols), right.reshape(rows, tile_cols)
     blocks = {0: lam_mine}
-    for mask in [1] + list(range(count - 1, 1, -1)):
+    for mask in range(count - 1, 0, -1):
         blocks[mask] = swapped(lam_other if mask % 2 else lam_mine, "depth", mask)
     sums = []
     for stage in range(0, count, 2):
         pair = (2, rows, 2 * levels)
         kept, sent = call(
-            rows_kernel,
+            functools.partial(rows_kernel, 4 * LANES),
             (place, left, left_pair, blocks[stage], blocks[stage + 1]),
             [SMEM] + [VMEM] * 4,
             [(pair, f32), (pair, bf16)],
@@ -594,29 +624,44 @@
         received = [lax.all_to_all(coeff[0], "lon", 0, 0, tiled=True)]
     else:
         received = [shifted(coeff[k], "lon", k - slots // 2) for k in range(slots)]
-    arrived, own = {}, None
-    block = (levels, half)
-    for stage in range(count - 2, -1, -2):
-        first, second = call(
-            functools.partial(columns_kernel, slots, 4 * LANES, stage),
-            (place, right, *right_pair, *received),
-            [SMEM] + [VMEM] * (1 + PARTS + len(received)),
-            [(block, bf16 if stage else f32), (block, bf16)],
-            flops=8 * rows * half * levels,
-            moved=3 << 20,
-        )
-        arrived[stage + 1] = swapped(second, "depth", stage + 1)
-        if stage:
-            arrived[stage] = swapped(first, "depth", stage)
-        else:
-            own = first
+    arrived = {mask: [] for mask in range(count)}
+    block = (levels, half // HALVES)
+    pieces = PARTS // HALVES
+    for part in range(HALVES):
+        for stage in range(count - 2, -1, -2):
+            first, second = call(
+                functools.partial(columns_kernel, slots, stage, part * (half // HALVES)),
+                (place, right, *right_pair[part * pieces : (part + 1) * pieces], *received),
+                [SMEM] + [VMEM] * (1 + pieces + len(received)),
+                [(block, bf16 if stage else f32), (block, bf16)],
+                flops=8 * rows * half * levels // HALVES,
+                moved=2 << 20,
+            )
+            arrived[stage + 1].append(swapped(second, "depth", stage + 1))
+            if stage:
+                first = swapped(first, "depth", stage)
+            arrived[stage].append(first)
+    scratch = [
+        pltpu.VMEM((levels, lon_cells // 2, lat_cells), f32),
+        pltpu.SemaphoreType.DMA((4,)),
+    ] + [pltpu.VMEM((levels * lon_cells // 2, LANES), f32)] * LANE_TILES
+    whole = [((levels, lon_cells, lat_cells), f32, ANY)]
     (gradient,) = call(
-        join_kernel,
-        (place, own, *(arrived[mask] for mask in range(1, count))),
-        [SMEM] + [VMEM] * count,
-        [((levels, lon_cells, lat_cells), f32)],
-        scratch=[pltpu.VMEM((levels * lon_cells, LANES), f32)] * (lat_cells // LANES),
-        moved=4 << 20,
+        functools.partial(join_kernel, True),
+        (place, *arrived[1], *arrived[3]),
+        [SMEM] + [VMEM] * (2 * HALVES),
+        whole,
+        scratch=scratch,
+        moved=2 << 20,
+    )
+    (gradient,) = call(
+        functools.partial(join_kernel, False),
+        (place, *arrived[0], *arrived[2], gradient),
+        [SMEM] + [VMEM] * (2 * HALVES) + [ANY],
+        whole,
+        scratch=scratch,
+        moved=2 << 20,
+        aliases={1 + 2 * HALVES: 0},
     )
     return (lam, gradient)
 

time: 145 us -> 139 us (0.959)
  waiting for transfers between devices: 71.9 us -> 59 us
  starting transfers between devices: 39.3 us -> 47.3 us
  Pallas kernels: 30.6 us -> 28.7 us
    ppermute x13 -> x16, waiting for transfers between devices: 50.9 us -> 36.1 us  [swapped(): lax.ppermute(block, axis, [(i, i ^ mask) for i in range(lax.axis_size(axi...]
    ppermute x13 -> x16, starting transfers between devices: 21.3 us -> 29.5 us  [swapped(): lax.ppermute(block, axis, [(i, i ^ mask) for i in range(lax.axis_size(axi...]
    pallas_call x4, Pallas kernels: 9.55 us -> 6 us  [sweep(): pl.pallas_call(functools.partial(step_kernel, table, step), in_specs=[VME...]
    pallas_call x10 -> x14, Pallas kernels: 15.4 us -> 17.5 us  [call(): pl.pallas_call(kernel, in_specs=in_specs, out_shape=[jax.ShapeDtypeStruct...]
    unnamed x24 -> x34, local copies, waits for them, and re-layouts: 1.96 us -> 2.95 us
  transfers between devices with their start and end apart: 24 -> 27, of which waited for: 11 -> 15; matrix products, arithmetic and copies ran while one was open for 0% -> 0% of each run, Pallas kernels for 15% -> 16%
where the time goes in v4:
time: 139 us
  waiting for transfers between devices  59 us (42%)
  starting transfers between devices  47.3 us (34%)
  Pallas kernels  28.7 us (21%)
  local copies, waits for them, and re-layouts  2.95 us (2%)
    ppermute x16, waiting for transfers between devices, swapped(): lax.ppermute(block, axis, [(i, i ^ mask) for i in range(lax.axis_size(axi...  36.1 us
    ppermute x16, starting transfers between devices, swapped(): lax.ppermute(block, axis, [(i, i ^ mask) for i in range(lax.axis_size(axi...  29.5 us
    ppermute x2, waiting for transfers between devices, from_behind(): lax.ppermute(value, axis, [(source, source + steps) for source in range(i...  20.7 us
    pallas_call x14, Pallas kernels, call(): pl.pallas_call(kernel, in_specs=in_specs, out_shape=[jax.ShapeDtypeStruct...  17.5 us
    ppermute x8, starting transfers between devices, shifted(): return lax.ppermute(block, axis, route)  11 us
    pallas_call x4, Pallas kernels, sweep(): pl.pallas_call(functools.partial(step_kernel, table, step), in_specs=[VME...  6 us
    pallas_call x1, Pallas kernels, pack(): pl.pallas_call(functools.partial(pack_kernel, table, ('lon', 'depth')), g...  4.38 us
    all_to_all x1, starting transfers between devices, per_device(): received = [lax.all_to_all(coeff[0], 'lon', 0, 0, tiled=True)]  3.59 us
  transfers between devices with their start and end apart: 27, of which 15 were waited for; matrix products, arithmetic and copies ran while one was open for 0% of the time, Pallas kernels for 16%

profile of v4, /device:TPU:0, one launch (start us, length us, event | category | flops | bytes accessed | tf_op | source)
XLA Modules:
  0.0 138.9 jit_solution(12505726429648792866)
XLA Ops:
  0.6 4.4 %shard_map.87 = (bf16[25,16,256]{2,1,0:T(8,128)(2,1)}, bf16[25,16,256]{2,1,0:T(8,128)(2,1)}, f32[64,1,256]{2,1,0:T(1,128)}, s32[3]{0:T(128)}, bf16[8,32,2048]{2,1,0:T(8,128)(2,1)}) custom-call(s32[64,1,128]{2,1,0:T(1,128)} %bricks.1, f32[5,64,16,256]{3,2,1,0:T(8,128)} %innov_hi.1, f32[5,64,16,256]{3,2,1,0:T(8,128)} %innov_hi.1, f32[3,64,16,256]{3,2,1,0:T(8,128)} %cour_hi.1, ...), custom_call_target="tpu_custom_call" | custom-call | bytes 1048576 | tf_op jit(solution)/shard_map/pallas_call | solution.py:353
  5.0 3.1 %collective-permute-start.12 = (bf16[8,32,2048]{2,1,0:T(8,128)(2,1)}, bf16[8,32,2048]{2,1,0:T(8,128)(2,1)S(1)}, u32[]{:S(2)}, u32[]{:S(2)}) collective-permute-start(bf16[8,32,2048]{2,1,0:T(8,128)(2,1)} %get-tuple-element.97), channel_id=1, source_target_pairs={{0,1},{1,0},{2,3},{3,2},{4,5},{5,4},{6,7},{7,6},{8,9},{9,8},{10,11... | collective-permute-start | bytes 3145736 | tf_op jit(solution)/shard_map/ppermute | solution.py:36
  8.1 1.9 %collective-permute-start = (bf16[25,16,256]{2,1,0:T(8,128)(2,1)}, bf16[25,16,256]{2,1,0:T(8,128)(2,1)S(1)}, u32[]{:S(2)}, u32[]{:S(2)}) collective-permute-start(bf16[25,16,256]{2,1,0:T(8,128)(2,1)} %get-tuple-element.63), channel_id=1, source_target_pairs={{0,1},{1,2},{2,3},{4,5},{5,6},{6,7},{8,9},{9,10},{10,11},{12,13},{... | collective-permute-start | bytes 614408 | tf_op jit(solution)/shard_map/ppermute | solution.py:24
  12.6 2.5 %shard_map.86 = (f32[5,64,16,256]{3,2,1,0:T(8,128)S(1)}, f32[3,64,16,256]{3,2,1,0:T(8,128)S(1)}, f32[64,16,256]{2,1,0:T(8,128)S(1)}) custom-call(f32[5,64,16,256]{3,2,1,0:T(8,128)} %innov_hi.1, f32[3,64,16,256]{3,2,1,0:T(8,128)S(1)} %copy-done.1, f32[64,16,256]{2,1,0:T(8,128)S(1)} %copy-done.3), custom_call_target="tpu_custom_call" | custom-call | bytes 18874368 | tf_op jit(solution)/shard_map/pallas_call | solution.py:557
  15.2 20.1 %collective-permute-done.before = bf16[25,16,256]{2,1,0:T(8,128)(2,1)S(1)} collective-permute-done((bf16[25,16,256]{2,1,0:T(8,128)(2,1)}, bf16[25,16,256]{2,1,0:T(8,128)(2,1)S(1)}, u32[]{:S(2)}, u32[]{:S(2)}) %collective-permute-start) | collective-permute-done | bytes 204832 | tf_op jit(solution)/shard_map/ppermute | solution.py:24
  36.3 2.6 %collective-permute-start.3 = (f32[72,1,256]{2,1,0:T(1,128)S(1)}, f32[72,1,256]{2,1,0:T(1,128)S(1)}, u32[]{:S(2)}, u32[]{:S(2)}) collective-permute-start(f32[72,1,256]{2,1,0:T(1,128)S(1)} %get-tuple-element.69), channel_id=1, source_target_pairs={{4,0},{8,4},{12,8},{16,12},{20,16},{24,20},{28,24},{0,28},{5,1},{9... | collective-permute-start | bytes 221192 | tf_op jit(solution)/shard_map/ppermute | solution.py:32
  42.0 1.8 %collective-permute-start.5 = (f32[72,1,256]{2,1,0:T(1,128)S(1)}, f32[72,1,256]{2,1,0:T(1,128)S(1)}, u32[]{:S(2)}, u32[]{:S(2)}) collective-permute-start(f32[72,1,256]{2,1,0:T(1,128)S(1)} %get-tuple-element.78), channel_id=1, source_target_pairs={{4,0},{8,4},{12,8},{16,12},{20,16},{24,20},{28,24},{0,28},{5,1},{9... | collective-permute-start | bytes 221192 | tf_op jit(solution)/shard_map/ppermute | solution.py:32
  46.9 1.9 %collective-permute-start.7 = (f32[72,1,256]{2,1,0:T(1,128)S(1)}, f32[72,1,256]{2,1,0:T(1,128)S(1)}, u32[]{:S(2)}, u32[]{:S(2)}) collective-permute-start(f32[72,1,256]{2,1,0:T(1,128)S(1)} %get-tuple-element.85), channel_id=1, source_target_pairs={{4,0},{8,4},{12,8},{16,12},{20,16},{24,20},{28,24},{0,28},{5,1},{9... | collective-permute-start | bytes 221192 | tf_op jit(solution)/shard_map/ppermute | solution.py:32
  51.9 1.9 %collective-permute-start.9 = (f32[72,1,256]{2,1,0:T(1,128)S(1)}, f32[72,1,256]{2,1,0:T(1,128)S(1)}, u32[]{:S(2)}, u32[]{:S(2)}) collective-permute-start(f32[72,1,256]{2,1,0:T(1,128)S(1)} %get-tuple-element.93), channel_id=1, source_target_pairs={{4,0},{8,4},{12,8},{16,12},{20,16},{24,20},{28,24},{0,28},{5,1},{9... | collective-permute-start | bytes 221192 | tf_op jit(solution)/shard_map/ppermute | solution.py:32
  58.1 2.8 %collective-permute-start.15 = (bf16[64,2048]{1,0:T(8,128)(2,1)S(1)}, bf16[64,2048]{1,0:T(8,128)(2,1)S(1)}, u32[]{:S(2)}, u32[]{:S(2)}) collective-permute-start(bf16[64,2048]{1,0:T(8,128)(2,1)S(1)} %get-tuple-element.100.first), channel_id=1, source_target_pairs={{0,2},{1,3},{2,0},{3,1},{4,6},{5,7},{6,4},{7,5},{8,10},{9,11},{10,... | collective-permute-start | bytes 786440 | tf_op jit(solution)/shard_map/ppermute | solution.py:36
  62.5 16.5 %collective-permute-done.15.first = bf16[64,2048]{1,0:T(8,128)(2,1)S(1)} collective-permute-done((bf16[64,2048]{1,0:T(8,128)(2,1)S(1)}, bf16[64,2048]{1,0:T(8,128)(2,1)S(1)}, u32[]{:S(2)}, u32[]{:S(2)}) %collective-permute-start.15) | collective-permute-done | bytes 262176 | tf_op jit(solution)/shard_map/ppermute | solution.py:36
  80.4 5.2 %collective-permute-start.17 = (bf16[2,256,128]{2,1,0:T(8,128)(2,1)S(1)}, bf16[2,256,128]{2,1,0:T(8,128)(2,1)S(1)}, u32[]{:S(2)}, u32[]{:S(2)}) collective-permute-start(bf16[2,256,128]{2,1,0:T(8,128)(2,1)S(1)} %get-tuple-element.105), channel_id=1, source_target_pairs={{0,1},{1,0},{2,3},{3,2},{4,5},{5,4},{6,7},{7,6},{8,9},{9,8},{10,11... | collective-permute-start | bytes 393224 | tf_op jit(solution)/shard_map/ppermute | solution.py:36
  88.6 2.1 %collective-permute-start.19 = (bf16[8,32,512]{2,1,0:T(8,128)(2,1)}, bf16[8,32,512]{2,1,0:T(8,128)(2,1)S(1)}, u32[]{:S(2)}, u32[]{:S(2)}) collective-permute-start(bf16[8,32,512]{2,1,0:T(8,128)(2,1)} %get-tuple-element.108), channel_id=1, source_target_pairs={{0,1},{1,0},{2,3},{3,2},{4,5},{5,4},{6,7},{7,6},{8,9},{9,8},{10,11... | collective-permute-start | bytes 786440 | tf_op jit(solution)/shard_map/ppermute | solution.py:36
  90.8 2.3 %collective-permute-done.14.rest_1_ = bf16[2,256,128]{2,1,0:T(8,128)(2,1)S(1)} collective-permute-done((bf16[2,256,128]{2,1,0:T(8,128)(2,1)S(1)}, bf16[2,256,128]{2,1,0:T(8,128)(2,1)S(1)}, u32[]{:S(2)}, u32[]{:S(2)}) %collective-permute-start.14) | collective-permute-done | bytes 131104 | tf_op jit(solution)/shard_map/ppermute | solution.py:36
  94.4 3.6 %all-to-all-start = ((bf16[8,2,32,256]{3,2,1,0:T(8,128)(2,1)}), bf16[8,2,32,256]{3,2,1,0:T(8,128)(2,1)S(1)}, u32[]{:S(2)}, u32[]{:S(2)}) async-start(bf16[8,2,32,256]{3,2,1,0:T(8,128)(2,1)} %shard_map.102), calls=%async_computation | async-start | bytes 524288 | tf_op jit(solution)/shard_map/all_to_all | solution.py:624
  98.0 1.6 %collective-permute-start.10 = (bf16[8,32,512]{2,1,0:T(8,128)(2,1)}, bf16[8,32,512]{2,1,0:T(8,128)(2,1)S(1)}, u32[]{:S(2)}, u32[]{:S(2)}) collective-permute-start(bf16[8,32,512]{2,1,0:T(8,128)(2,1)} %get-tuple-element.95), channel_id=1, source_target_pairs={{0,1},{1,0},{2,3},{3,2},{4,5},{5,4},{6,7},{7,6},{8,9},{9,8},{10,11... | collective-permute-start | bytes 786440 | tf_op jit(solution)/shard_map/ppermute | solution.py:36
  100.0 4.3 %collective-permute-done.18 = bf16[8,32,512]{2,1,0:T(8,128)(2,1)S(1)} collective-permute-done((bf16[8,32,512]{2,1,0:T(8,128)(2,1)}, bf16[8,32,512]{2,1,0:T(8,128)(2,1)S(1)}, u32[]{:S(2)}, u32[]{:S(2)}) %collective-permute-start.18) | collective-permute-done | bytes 262176 | tf_op jit(solution)/shard_map/ppermute | solution.py:36
  106.4 3.4 %collective-permute-start.25 = (bf16[64,1024]{1,0:T(8,128)(2,1)S(1)}, bf16[64,1024]{1,0:T(8,128)(2,1)S(1)}, u32[]{:S(2)}, u32[]{:S(2)}) collective-permute-start(bf16[64,1024]{1,0:T(8,128)(2,1)S(1)} %get-tuple-element.115), channel_id=1, source_target_pairs={{0,3},{1,2},{2,1},{3,0},{4,7},{5,6},{6,5},{7,4},{8,11},{9,10},{10,... | collective-permute-start | bytes 393224 | tf_op jit(solution)/shard_map/ppermute | solution.py:36
  109.9 4.9 %collective-permute-done.11 = bf16[8,32,512]{2,1,0:T(8,128)(2,1)S(1)} collective-permute-done((bf16[8,32,512]{2,1,0:T(8,128)(2,1)}, bf16[8,32,512]{2,1,0:T(8,128)(2,1)S(1)}, u32[]{:S(2)}, u32[]{:S(2)}) %collective-permute-start.11) | collective-permute-done | bytes 262176 | tf_op jit(solution)/shard_map/ppermute | solution.py:36
  115.7 4.0 %collective-permute-start.24 = (bf16[64,1024]{1,0:T(8,128)(2,1)S(1)}, bf16[64,1024]{1,0:T(8,128)(2,1)S(1)}, u32[]{:S(2)}, u32[]{:S(2)}) collective-permute-start(bf16[64,1024]{1,0:T(8,128)(2,1)S(1)} %get-tuple-element.114), channel_id=1, source_target_pairs={{0,3},{1,2},{2,1},{3,0},{4,7},{5,6},{6,5},{7,4},{8,11},{9,10},{10,... | collective-permute-start | bytes 393224 | tf_op jit(solution)/shard_map/ppermute | solution.py:36
  124.0 2.6 %collective-permute-start.20 = (bf16[64,1024]{1,0:T(8,128)(2,1)S(1)}, bf16[64,1024]{1,0:T(8,128)(2,1)S(1)}, u32[]{:S(2)}, u32[]{:S(2)}) collective-permute-start(bf16[64,1024]{1,0:T(8,128)(2,1)S(1)} %get-tuple-element.110), channel_id=1, source_target_pairs={{0,2},{1,3},{2,0},{3,1},{4,6},{5,7},{6,4},{7,5},{8,10},{9,11},{10,... | collective-permute-start | bytes 393224 | tf_op jit(solution)/shard_map/ppermute | solution.py:36
  127.8 2.2 %collective-permute-done.23.rest_1_ = bf16[64,1024]{1,0:T(8,128)(2,1)S(1)} collective-permute-done((bf16[64,1024]{1,0:T(8,128)(2,1)S(1)}, bf16[64,1024]{1,0:T(8,128)(2,1)S(1)}, u32[]{:S(2)}, u32[]{:S(2)}) %collective-permute-start.23) | collective-permute-done | bytes 131104 | tf_op jit(solution)/shard_map/ppermute | solution.py:36
  130.0 1.9 %collective-permute-done.22.rest_0_ = bf16[64,1024]{1,0:T(8,128)(2,1)S(1)} collective-permute-done((bf16[64,1024]{1,0:T(8,128)(2,1)S(1)}, bf16[64,1024]{1,0:T(8,128)(2,1)S(1)}, u32[]{:S(2)}, u32[]{:S(2)}) %collective-permute-start.22) | collective-permute-done | bytes 131104 | tf_op jit(solution)/shard_map/ppermute | solution.py:36
  133.4 2.5 %collective-permute-done.21.rest_3_ = bf16[64,1024]{1,0:T(8,128)(2,1)S(1)} collective-permute-done((bf16[64,1024]{1,0:T(8,128)(2,1)S(1)}, bf16[64,1024]{1,0:T(8,128)(2,1)S(1)}, u32[]{:S(2)}, u32[]{:S(2)}) %collective-permute-start.21) | collective-permute-done | bytes 131104 | tf_op jit(solution)/shard_map/ppermute | solution.py:36
  (87 shorter events, 37.7 us)
Async XLA Ops:
  5.0 74.0 %collective-permute-start.12 = (bf16[8,32,2048]{2,1,0:T(8,128)(2,1)}, bf16[8,32,2048]{2,1,0:T(8,128)(2,1)S(1)}, u32[]{:S(2)}, u32[]{:S(2)}) collective-permute-start(bf16[8,32,2048]{2,1,0:T(8,128)(2,1)} %get-tuple-element.97), channel_id=1, source_target_pairs={{0,1},{1,0},{2,3},{3,2},{4,5},{5,4},{6,7},{7,6},{8,9},{9,8},{10,11... | collective-permute-start | bytes 3145736 | tf_op jit(solution)/shard_map/ppermute | solution.py:36
  8.1 27.1 %collective-permute-start = (bf16[25,16,256]{2,1,0:T(8,128)(2,1)}, bf16[25,16,256]{2,1,0:T(8,128)(2,1)S(1)}, u32[]{:S(2)}, u32[]{:S(2)}) collective-permute-start(bf16[25,16,256]{2,1,0:T(8,128)(2,1)} %get-tuple-element.63), channel_id=1, source_target_pairs={{0,1},{1,2},{2,3},{4,5},{5,6},{6,7},{8,9},{9,10},{10,11},{12,13},{... | collective-permute-start | bytes 614408 | tf_op jit(solution)/shard_map/ppermute | solution.py:24
  10.1 25.8 %collective-permute-start.1 = (bf16[25,16,256]{2,1,0:T(8,128)(2,1)}, bf16[25,16,256]{2,1,0:T(8,128)(2,1)S(1)}, u32[]{:S(2)}, u32[]{:S(2)}) collective-permute-start(bf16[25,16,256]{2,1,0:T(8,128)(2,1)} %get-tuple-element.64), channel_id=1, source_target_pairs={{1,0},{2,1},{3,2},{5,4},{6,5},{7,6},{9,8},{10,9},{11,10},{13,12},{... | collective-permute-start | bytes 614408 | tf_op jit(solution)/shard_map/ppermute | solution.py:24
  36.2 4.7 %collective-permute-start.2 = (f32[72,1,256]{2,1,0:T(1,128)S(1)}, f32[72,1,256]{2,1,0:T(1,128)S(1)}, u32[]{:S(2)}, u32[]{:S(2)}) collective-permute-start(f32[72,1,256]{2,1,0:T(1,128)S(1)} %get-tuple-element.68), channel_id=1, source_target_pairs={{28,0},{0,4},{4,8},{8,12},{12,16},{16,20},{20,24},{24,28},{29,1},{... | collective-permute-start | bytes 221192 | tf_op jit(solution)/shard_map/ppermute | solution.py:32
  41.1 4.7 %collective-permute-start.4 = (f32[72,1,256]{2,1,0:T(1,128)S(1)}, f32[72,1,256]{2,1,0:T(1,128)S(1)}, u32[]{:S(2)}, u32[]{:S(2)}) collective-permute-start(f32[72,1,256]{2,1,0:T(1,128)S(1)} %get-tuple-element.77), channel_id=1, source_target_pairs={{28,0},{0,4},{4,8},{8,12},{12,16},{16,20},{20,24},{24,28},{29,1},{... | collective-permute-start | bytes 221192 | tf_op jit(solution)/shard_map/ppermute | solution.py:32
  46.0 4.9 %collective-permute-start.6 = (f32[72,1,256]{2,1,0:T(1,128)S(1)}, f32[72,1,256]{2,1,0:T(1,128)S(1)}, u32[]{:S(2)}, u32[]{:S(2)}) collective-permute-start(f32[72,1,256]{2,1,0:T(1,128)S(1)} %get-tuple-element.84), channel_id=1, source_target_pairs={{28,0},{0,4},{4,8},{8,12},{12,16},{16,20},{20,24},{24,28},{29,1},{... | collective-permute-start | bytes 221192 | tf_op jit(solution)/shard_map/ppermute | solution.py:32
  51.1 6.3 %collective-permute-start.8 = (f32[72,1,256]{2,1,0:T(1,128)S(1)}, f32[72,1,256]{2,1,0:T(1,128)S(1)}, u32[]{:S(2)}, u32[]{:S(2)}) collective-permute-start(f32[72,1,256]{2,1,0:T(1,128)S(1)} %get-tuple-element.92), channel_id=1, source_target_pairs={{28,0},{0,4},{4,8},{8,12},{12,16},{16,20},{20,24},{24,28},{29,1},{... | collective-permute-start | bytes 221192 | tf_op jit(solution)/shard_map/ppermute | solution.py:32
  51.9 5.5 %collective-permute-start.9 = (f32[72,1,256]{2,1,0:T(1,128)S(1)}, f32[72,1,256]{2,1,0:T(1,128)S(1)}, u32[]{:S(2)}, u32[]{:S(2)}) collective-permute-start(f32[72,1,256]{2,1,0:T(1,128)S(1)} %get-tuple-element.93), channel_id=1, source_target_pairs={{4,0},{8,4},{12,8},{16,12},{20,16},{24,20},{28,24},{0,28},{5,1},{9... | collective-permute-start | bytes 221192 | tf_op jit(solution)/shard_map/ppermute | solution.py:32
  58.1 20.9 %collective-permute-start.15 = (bf16[64,2048]{1,0:T(8,128)(2,1)S(1)}, bf16[64,2048]{1,0:T(8,128)(2,1)S(1)}, u32[]{:S(2)}, u32[]{:S(2)}) collective-permute-start(bf16[64,2048]{1,0:T(8,128)(2,1)S(1)} %get-tuple-element.100.first), channel_id=1, source_target_pairs={{0,2},{1,3},{2,0},{3,1},{4,6},{5,7},{6,4},{7,5},{8,10},{9,11},{10,... | collective-permute-start | bytes 786440 | tf_op jit(solution)/shard_map/ppermute | solution.py:36
  60.9 18.1 %collective-permute-start.16 = (bf16[64,2048]{1,0:T(8,128)(2,1)S(1)}, bf16[64,2048]{1,0:T(8,128)(2,1)S(1)}, u32[]{:S(2)}, u32[]{:S(2)}) collective-permute-start(bf16[64,2048]{1,0:T(8,128)(2,1)S(1)} %get-tuple-element.101), channel_id=1, source_target_pairs={{0,3},{1,2},{2,1},{3,0},{4,7},{5,6},{6,5},{7,4},{8,11},{9,10},{10,... | collective-permute-start | bytes 786440 | tf_op jit(solution)/shard_map/ppermute | solution.py:36
  62.2 23.4 %collective-permute-start.13 = (bf16[64,2048]{1,0:T(8,128)(2,1)S(1)}, bf16[64,2048]{1,0:T(8,128)(2,1)S(1)}, u32[]{:S(2)}, u32[]{:S(2)}) collective-permute-start(bf16[64,2048]{1,0:T(8,128)(2,1)S(1)} %get-tuple-element.101), channel_id=1, source_target_pairs={{0,1},{1,0},{2,3},{3,2},{4,5},{5,4},{6,7},{7,6},{8,9},{9,8},{10,11... | collective-permute-start | bytes 786440 | tf_op jit(solution)/shard_map/ppermute | solution.py:36
  80.4 10.4 %collective-permute-start.17 = (bf16[2,256,128]{2,1,0:T(8,128)(2,1)S(1)}, bf16[2,256,128]{2,1,0:T(8,128)(2,1)S(1)}, u32[]{:S(2)}, u32[]{:S(2)}) collective-permute-start(bf16[2,256,128]{2,1,0:T(8,128)(2,1)S(1)} %get-tuple-element.105), channel_id=1, source_target_pairs={{0,1},{1,0},{2,3},{3,2},{4,5},{5,4},{6,7},{7,6},{8,9},{9,8},{10,11... | collective-permute-start | bytes 393224 | tf_op jit(solution)/shard_map/ppermute | solution.py:36
  86.9 6.1 %collective-permute-start.14 = (bf16[2,256,128]{2,1,0:T(8,128)(2,1)S(1)}, bf16[2,256,128]{2,1,0:T(8,128)(2,1)S(1)}, u32[]{:S(2)}, u32[]{:S(2)}) collective-permute-start(bf16[2,256,128]{2,1,0:T(8,128)(2,1)S(1)} %get-tuple-element.103), channel_id=1, source_target_pairs={{0,1},{1,0},{2,3},{3,2},{4,5},{5,4},{6,7},{7,6},{8,9},{9,8},{10,11... | collective-permute-start | bytes 393224 | tf_op jit(solution)/shard_map/ppermute | solution.py:36
  88.6 11.4 %collective-permute-start.19 = (bf16[8,32,512]{2,1,0:T(8,128)(2,1)}, bf16[8,32,512]{2,1,0:T(8,128)(2,1)S(1)}, u32[]{:S(2)}, u32[]{:S(2)}) collective-permute-start(bf16[8,32,512]{2,1,0:T(8,128)(2,1)} %get-tuple-element.108), channel_id=1, source_target_pairs={{0,1},{1,0},{2,3},{3,2},{4,5},{5,4},{6,7},{7,6},{8,9},{9,8},{10,11... | collective-permute-start | bytes 786440 | tf_op jit(solution)/shard_map/ppermute | solution.py:36
  90.7 13.6 %collective-permute-start.18 = (bf16[8,32,512]{2,1,0:T(8,128)(2,1)}, bf16[8,32,512]{2,1,0:T(8,128)(2,1)S(1)}, u32[]{:S(2)}, u32[]{:S(2)}) collective-permute-start(bf16[8,32,512]{2,1,0:T(8,128)(2,1)} %get-tuple-element.107), channel_id=1, source_target_pairs={{0,1},{1,0},{2,3},{3,2},{4,5},{5,4},{6,7},{7,6},{8,9},{9,8},{10,11... | collective-permute-start | bytes 786440 | tf_op jit(solution)/shard_map/ppermute | solution.py:36
  94.4 10.5 %all-to-all-start = ((bf16[8,2,32,256]{3,2,1,0:T(8,128)(2,1)}), bf16[8,2,32,256]{3,2,1,0:T(8,128)(2,1)S(1)}, u32[]{:S(2)}, u32[]{:S(2)}) async-start(bf16[8,2,32,256]{3,2,1,0:T(8,128)(2,1)} %shard_map.102), calls=%async_computation | async-start | bytes 524288 | tf_op jit(solution)/shard_map/all_to_all | solution.py:624
  98.0 11.9 %collective-permute-start.10 = (bf16[8,32,512]{2,1,0:T(8,128)(2,1)}, bf16[8,32,512]{2,1,0:T(8,128)(2,1)S(1)}, u32[]{:S(2)}, u32[]{:S(2)}) collective-permute-start(bf16[8,32,512]{2,1,0:T(8,128)(2,1)} %get-tuple-element.95), channel_id=1, source_target_pairs={{0,1},{1,0},{2,3},{3,2},{4,5},{5,4},{6,7},{7,6},{8,9},{9,8},{10,11... | collective-permute-start | bytes 786440 | tf_op jit(solution)/shard_map/ppermute | solution.py:36
  99.6 15.2 %collective-permute-start.11 = (bf16[8,32,512]{2,1,0:T(8,128)(2,1)}, bf16[8,32,512]{2,1,0:T(8,128)(2,1)S(1)}, u32[]{:S(2)}, u32[]{:S(2)}) collective-permute-start(bf16[8,32,512]{2,1,0:T(8,128)(2,1)} %copy-done.16), channel_id=1, source_target_pairs={{0,1},{1,0},{2,3},{3,2},{4,5},{5,4},{6,7},{7,6},{8,9},{9,8},{10,11... | collective-permute-start | bytes 786440 | tf_op jit(solution)/shard_map/ppermute | solution.py:36
  106.4 17.7 %collective-permute-start.25 = (bf16[64,1024]{1,0:T(8,128)(2,1)S(1)}, bf16[64,1024]{1,0:T(8,128)(2,1)S(1)}, u32[]{:S(2)}, u32[]{:S(2)}) collective-permute-start(bf16[64,1024]{1,0:T(8,128)(2,1)S(1)} %get-tuple-element.115), channel_id=1, source_target_pairs={{0,3},{1,2},{2,1},{3,0},{4,7},{5,6},{6,5},{7,4},{8,11},{9,10},{10,... | collective-permute-start | bytes 393224 | tf_op jit(solution)/shard_map/ppermute | solution.py:36
  115.7 12.1 %collective-permute-start.24 = (bf16[64,1024]{1,0:T(8,128)(2,1)S(1)}, bf16[64,1024]{1,0:T(8,128)(2,1)S(1)}, u32[]{:S(2)}, u32[]{:S(2)}) collective-permute-start(bf16[64,1024]{1,0:T(8,128)(2,1)S(1)} %get-tuple-element.114), channel_id=1, source_target_pairs={{0,3},{1,2},{2,1},{3,0},{4,7},{5,6},{6,5},{7,4},{8,11},{9,10},{10,... | collective-permute-start | bytes 393224 | tf_op jit(solution)/shard_map/ppermute | solution.py:36
  120.6 9.3 %collective-permute-start.23 = (bf16[64,1024]{1,0:T(8,128)(2,1)S(1)}, bf16[64,1024]{1,0:T(8,128)(2,1)S(1)}, u32[]{:S(2)}, u32[]{:S(2)}) collective-permute-start(bf16[64,1024]{1,0:T(8,128)(2,1)S(1)} %get-tuple-element.113), channel_id=1, source_target_pairs={{0,1},{1,0},{2,3},{3,2},{4,5},{5,4},{6,7},{7,6},{8,9},{9,8},{10,11... | collective-permute-start | bytes 393224 | tf_op jit(solution)/shard_map/ppermute | solution.py:36
  122.5 9.4 %collective-permute-start.22 = (bf16[64,1024]{1,0:T(8,128)(2,1)S(1)}, bf16[64,1024]{1,0:T(8,128)(2,1)S(1)}, u32[]{:S(2)}, u32[]{:S(2)}) collective-permute-start(bf16[64,1024]{1,0:T(8,128)(2,1)S(1)} %get-tuple-element.112), channel_id=1, source_target_pairs={{0,1},{1,0},{2,3},{3,2},{4,5},{5,4},{6,7},{7,6},{8,9},{9,8},{10,11... | collective-permute-start | bytes 393224 | tf_op jit(solution)/shard_map/ppermute | solution.py:36
  123.7 12.3 %collective-permute-start.21 = (bf16[64,1024]{1,0:T(8,128)(2,1)S(1)}, bf16[64,1024]{1,0:T(8,128)(2,1)S(1)}, u32[]{:S(2)}, u32[]{:S(2)}) collective-permute-start(bf16[64,1024]{1,0:T(8,128)(2,1)S(1)} %get-tuple-element.111), channel_id=1, source_target_pairs={{0,2},{1,3},{2,0},{3,1},{4,6},{5,7},{6,4},{7,5},{8,10},{9,11},{10,... | collective-permute-start | bytes 393224 | tf_op jit(solution)/shard_map/ppermute | solution.py:36
  124.0 13.3 %collective-permute-start.20 = (bf16[64,1024]{1,0:T(8,128)(2,1)S(1)}, bf16[64,1024]{1,0:T(8,128)(2,1)S(1)}, u32[]{:S(2)}, u32[]{:S(2)}) collective-permute-start(bf16[64,1024]{1,0:T(8,128)(2,1)S(1)} %get-tuple-element.110), channel_id=1, source_target_pairs={{0,2},{1,3},{2,0},{3,1},{4,6},{5,7},{6,4},{7,5},{8,10},{9,11},{10,... | collective-permute-start | bytes 393224 | tf_op jit(solution)/shard_map/ppermute | solution.py:36
  (20 other events, 196.9 us)

commit v5 on v4

--- a/solution.py
+++ b/solution.py
@@ -9,6 +9,7 @@
 UNROLL = 9
 LANES = 128
 PARTS = 4
+LOAD_GRANT = 40 << 20
 STAGES = 2
 LANE_TILES = 2
 HALVES = 2
@@ -39,14 +40,18 @@
 def halo_table(depth):
     order, at = {}, 0
     for name, extent in (
-        [(("innov", k), k) for k in range(depth, 0, -1)]
-        + [("diff", depth), ("c0", depth), ("c1", depth - 1), ("c2", depth - 1)]
+        [(("innov", k), min(k, depth - 1)) for k in range(depth, 0, -1)]
+        + [("diff", depth - 1), ("c0", depth - 1), ("c1", depth - 1), ("c2", depth - 1)]
     ):
         for distance in range(1, extent + 1):
             order[name, distance] = at
             at += 1
-    order["sea"] = at
-    return order, at + 1
+    order["sea"], order["flux"] = at, at + 1
+    return order, at + 2
+
+
+def row(ref, at):
+    return ref[pl.ds(at, 1), :]
 
 
 def pack_kernel(table, axes, bricks, innov_lo, innov_hi, cour_lo, cour_hi, diff_lo, diff_hi, left, down, up, sea, place, left_other, rows, vmem, sems):
@@ -54,28 +59,31 @@
     side = lax.rem(me, 2)
     place[0], place[1], place[2] = me, side, lax.axis_index(axes[0])
     half = left_other.shape[2]
-    start = pl.multiple_of((1 - side) * half, half)
-    load = pltpu.make_async_copy(left.at[0, :, :, pl.ds(start, half)], vmem, sems.at[0])
+    window = pl.ds(pl.multiple_of((1 - side) * half, half), half)
+    load = pltpu.make_async_copy(left.at[0, :, :, window], vmem, sems.at[0])
     load.start()
     depth = diff_lo.shape[0]
     levels, _, count = bricks.shape
-    lat_cells = sea.shape[2]
+    lat_cells = sea.shape[1]
     for z in range(levels):
         rows[z : z + 1] = bricks[z].astype(jnp.float32)
     brick_at = lax.broadcasted_iota(jnp.int32, (count, lat_cells), 0)
     cell_at = lax.broadcasted_iota(jnp.int32, (count, lat_cells), 1)
     inside = (brick_at == cell_at // (lat_cells // count)).astype(jnp.bfloat16)
     wide = jnp.dot(rows[...].astype(jnp.bfloat16), inside, preferred_element_type=jnp.float32)
-    for z in range(levels):
-        sea[z] = wide[z : z + 1]
-    sea_lo, sea_hi = sea, sea.at[pl.ds(levels - depth, depth)]
-
-    def fill(out, innov, cour, diff, sea, level):
+    sea[...] = wide
+    sea_lo, sea_hi = wide[:depth], wide[levels - depth :]
+
+    def fill(out, innov, cour, diff, sea, level, sign):
         for key, at in table.items():
             if key == "sea":
-                rows = [sea[level(d)] for d in range(1, depth + 1)]
+                rows = [sea[level(d) : level(d) + 1] for d in range(1, depth + 1)]
                 rows.append(jnp.zeros((out.shape[1] - depth, out.shape[2]), jnp.float32))
                 value = jnp.concatenate(rows, 0)
+            elif key == "flux":
+                z = level(depth)
+                gain = diff[z] + (0.5 * sign) * cour[0, z]
+                value = gain * (sea[z : z + 1] * innov[innov.shape[0] - 1, z])
             else:
                 name, distance = key
                 z = level(distance)
@@ -91,12 +99,21 @@
                     value = innov[name[1], z]
             out[at] = value.astype(jnp.bfloat16)
 
+    fill(down, innov_hi, cour_hi, diff_hi, sea_hi, lambda d: depth - d, -1.0)
     load.wait()
     store = pltpu.make_async_copy(vmem, left_other, sems.at[1])
     store.start()
-    fill(down, innov_hi, cour_hi, diff_hi, sea_hi, lambda d: depth - d)
-    fill(up, innov_lo, cour_lo, diff_lo, sea_lo, lambda d: d - 1)
+    fill(up, innov_lo, cour_lo, diff_lo, sea_lo, lambda d: d - 1, 1.0)
     store.wait()
+
+
+def load_kernel(*refs):
+    count = len(refs) // 2
+    copies = [pltpu.make_async_copy(refs[n], refs[count + n], refs[-1].at[n]) for n in range(count)]
+    for copy in copies:
+        copy.start()
+    for copy in copies:
+        copy.wait()
 
 
 def halves_kernel(place, right, *rest):
@@ -116,27 +133,19 @@
         store.wait()
 
 
-def load_kernel(*refs):
-    count = len(refs) // 2
-    copies = [pltpu.make_async_copy(refs[n], refs[count + n], refs[-1].at[n]) for n in range(count)]
-    for copy in copies:
-        copy.start()
-    for copy in copies:
-        copy.wait()
-
-
-def first_kernel(table, innov, cour, diff, sea, before, after, sea_ext, east_gain, west_gain, to_east, to_west):
+def first_kernel(table, innov, cour, diff, sea, before, after, sea_ext, east_gain, west_gain, to_east, to_west, east_rows, west_rows):
     steps = innov.shape[0] - 1
     levels, lon_cells, lat_cells = diff.shape
     last = lon_cells - 1
 
     def put(at, sea_row, diff_a, diff_b, cour_a, cour_b, innov_a, innov_b):
-        sea_ext[at] = sea_row
+        here = pl.ds(at, 1)
+        sea_ext[here, :] = sea_row
         low_row, high_row = sea_row * innov_a, sea_row * innov_b
         west = diff_a + 0.5 * cour_a
         east = diff_b - 0.5 * cour_b
-        west_gain[at], east_gain[at] = west, east
-        to_west[at], to_east[at] = west * low_row, east * high_row
+        west_gain[here, :], east_gain[here, :] = west, east
+        west_rows[here, :], east_rows[here, :] = west * low_row, east * high_row
 
     for halo, where in ((before, lambda d: steps - d), (after, lambda d: steps + levels + d - 1)):
         sea_rows = halo[table["sea"]].astype(jnp.float32)
@@ -145,8 +154,8 @@
             at = where(d)
             if d == steps:
                 zero = jnp.zeros((1, lat_cells), jnp.float32)
-                sea_ext[at] = sea_row
-                west_gain[at], east_gain[at], to_west[at], to_east[at] = zero, zero, zero, zero
+                for ref in (sea_ext, west_gain, east_gain, west_rows, east_rows):
+                    ref[pl.ds(at, 1), :] = zero
             else:
                 dd = halo[table["diff", d]].astype(jnp.float32)
                 cc = halo[table["c1", d]].astype(jnp.float32)
@@ -155,10 +164,12 @@
 
     def one(z, carry):
         edge = lambda ref: (ref[z, :1], ref[z, last:])
-        put(z + steps, sea[z], *edge(diff), *edge(cour.at[1]), *edge(innov.at[steps]))
+        put(z + steps, row(sea, z), *edge(diff), *edge(cour.at[1]), *edge(innov.at[steps]))
         return carry
 
     lax.fori_loop(0, levels, one, 0, unroll=4)
+    to_west[...] = west_rows[...].astype(jnp.bfloat16)
+    to_east[...] = east_rows[...].astype(jnp.bfloat16)
 
 
 def step_kernel(table, step, innov, cour, diff, sea_ext, before, after, low, high, *rest):
@@ -179,15 +190,15 @@
 
     def state(at, innovation):
         if step == 1:
-            return sea_ext[at] * innovation
-        value = jnp.where(first_x, low[at], lam[at])
-        return jnp.where(last_x, high[at], value)
+            return row(sea_ext, at) * innovation
+        value = jnp.where(first_x, row(low, at), lam[at])
+        return jnp.where(last_x, row(high, at), value)
 
     def finish(at, acc, up_flux):
-        value = sea_ext[at] * (acc + up_flux)
+        value = row(sea_ext, at) * (acc + up_flux)
         out[at] = value
-        out_low[at] = value[:1]
-        out_high[at] = value[last:]
+        out_low[pl.ds(at, 1), :] = value[:1]
+        out_high[pl.ds(at, 1), :] = value[last:]
 
     def depth_terms(a, d, c):
         spread, drift = d * a, c * (0.5 * a)
@@ -209,8 +220,11 @@
         acc = acc + jnp.where(last_y, 0.0, pltpu.roll(minus2, lat_cells - 1, 1))
         return acc, plus0, minus0
 
+    def halo_start(halo, d, at):
+        return state(at, halo_level(halo, d, ("innov", steps)) if step == 1 else None)
+
     def halo_full(halo, d, at):
-        a = state(at, halo_level(halo, d, ("innov", steps)))
+        a = halo_start(halo, d, at)
         return level(
             a,
             halo_level(halo, d, "diff"),
@@ -221,7 +235,10 @@
         )
 
     def halo_edge(halo, d, at):
-        a = state(at, halo_level(halo, d, ("innov", steps)))
+        if step == 1:
+            flux = halo[table["flux"]].astype(jnp.float32)
+            return flux, flux
+        a = halo_start(halo, d, at)
         return depth_terms(a, halo_level(halo, d, "diff"), halo_level(halo, d, "c0"))
 
     down_flux, _ = halo_edge(before, reach + 1, steps - reach - 1)
@@ -234,7 +251,7 @@
         acc, down_flux = value + down_flux, plus0
 
     def own(z):
-        a = state(z + steps, innov[steps, z])
+        a = state(z + steps, innov[steps, z] if step == 1 else None)
         return level(a, diff[z], cour[0, z], cour[1, z], cour[2, z], innov[steps - step, z])
 
     value, plus0, minus0 = own(0)
@@ -289,29 +306,27 @@
                 part[:, at : at + LANES] = picked.astype(jnp.bfloat16)
 
 
-def fix_kernel(place, sea_ext, out_low, out_high, west, east, mine_in, other_in, mine, other, low_rows, high_rows):
+def fix_kernel(place, sea_ext, out_low, out_high, west, east, mine_in, other_in, mine, other, low, high):
     levels, half = mine.shape
-    lat_cells = low_rows.shape[1]
+    lat_cells = low.shape[1]
     steps = (sea_ext.shape[0] - levels) // 2
-    for z in range(levels):
-        at = z + steps
-        low_rows[z : z + 1] = out_low[at] + sea_ext[at] * west[at]
-        high_rows[z : z + 1] = out_high[at] + sea_ext[at] * east[at]
-    low = low_rows[...].astype(jnp.bfloat16)
-    high = high_rows[...].astype(jnp.bfloat16)
+    low[...] = out_low[...] + sea_ext[...] * west[...].astype(jnp.float32)
+    high[...] = out_high[...] + sea_ext[...] * east[...].astype(jnp.float32)
+    low_rows = low[steps : steps + levels, :].astype(jnp.bfloat16)
+    high_rows = high[steps : steps + levels, :].astype(jnp.bfloat16)
 
     @pl.when(place[1] == 0)
     def _():
-        mine[:, :lat_cells] = low
-        other[:, half - lat_cells :] = high
+        mine[:, :lat_cells] = low_rows
+        other[:, half - lat_cells :] = high_rows
 
     @pl.when(place[1] != 0)
     def _():
-        other[:, :lat_cells] = low
-        mine[:, half - lat_cells :] = high
-
-
-def emit_kernel(lam, sea_ext, out_low, out_high, west, east, out):
+        other[:, :lat_cells] = low_rows
+        mine[:, half - lat_cells :] = high_rows
+
+
+def emit_kernel(lam, low, high, out):
     levels, lon_cells, lat_cells = out.shape
     steps = (lam.shape[0] - levels) // 2
     x_at = lax.broadcasted_iota(jnp.int32, (lon_cells, lat_cells), 0)
@@ -319,19 +334,18 @@
 
     def one(z, carry):
         at = z + steps
-        low = out_low[at] + sea_ext[at] * west[at]
-        high = out_high[at] + sea_ext[at] * east[at]
-        out[z] = jnp.where(last_x, high, jnp.where(first_x, low, lam[at]))
+        out[z] = jnp.where(last_x, row(high, at), jnp.where(first_x, row(low, at), lam[at]))
         return carry
 
     lax.fori_loop(0, levels, one, 0, unroll=4)
 
 
 def face_kernel(sea_ext, out_low, out_high, west, east, west_gain, east_gain, low, high, to_west, to_east):
-    low_rows = out_low[...] + sea_ext[...] * west[...]
-    high_rows = out_high[...] + sea_ext[...] * east[...]
+    low_rows = out_low[...] + sea_ext[...] * west[...].astype(jnp.float32)
+    high_rows = out_high[...] + sea_ext[...] * east[...].astype(jnp.float32)
     low[...], high[...] = low_rows, high_rows
-    to_west[...], to_east[...] = west_gain[...] * low_rows, east_gain[...] * high_rows
+    to_west[...] = (west_gain[...] * low_rows).astype(jnp.bfloat16)
+    to_east[...] = (east_gain[...] * high_rows).astype(jnp.bfloat16)
 
 
 def pack(innovations, courant, diffusivity, bricks, left):
@@ -361,7 +375,7 @@
         out_shape=[
             message,
             message,
-            jax.ShapeDtypeStruct((levels, 1, lat_cells), f32),
+            jax.ShapeDtypeStruct((levels, lat_cells), f32),
             jax.ShapeDtypeStruct((3,), jnp.int32),
             other,
         ],
@@ -375,30 +389,21 @@
     )(bricks, innovations, innovations, courant, courant, diffusivity, diffusivity, left)
 
 
-def sweep(innovations, courant, diffusivity, sea, down, up, place):
-    levels, lon_cells, lat_cells = diffusivity.shape
-    steps = innovations.shape[0] - 1
+def sweep(inputs, sea, before, after, place):
+    levels, lon_cells, lat_cells = inputs[2].shape
+    steps = inputs[0].shape[0] - 1
     table, _ = halo_table(steps)
     f32, bf16 = jnp.float32, jnp.bfloat16
-    before = from_behind(down, "depth", 1)
-    after = from_behind(up, "depth", -1)
-    row = jax.ShapeDtypeStruct((levels + 2 * steps, 1, lat_cells), f32)
+    extended = (levels + 2 * steps, lat_cells)
+    row_of = jax.ShapeDtypeStruct(extended, f32)
+    sent_row = jax.ShapeDtypeStruct(extended, bf16)
     cells = jax.ShapeDtypeStruct((levels + 2 * steps, lon_cells, lat_cells), f32)
-    inputs = (innovations, courant, diffusivity)
-    inputs = call(
-        load_kernel,
-        inputs,
-        [ANY] * 3,
-        [(a.shape, a.dtype) for a in inputs],
-        grant=40 << 20,
-        moved=18 << 20,
-        scratch=[pltpu.SemaphoreType.DMA((3,))],
-    )
     sea_ext, east_gain, west_gain, to_east, to_west = pl.pallas_call(
         functools.partial(first_kernel, table),
         in_specs=[VMEM] * 6,
-        out_shape=[row] * 5,
+        out_shape=[row_of] * 3 + [sent_row] * 2,
         out_specs=[VMEM] * 5,
+        scratch_shapes=[pltpu.VMEM(extended, f32)] * 2,
         compiler_params=pltpu.CompilerParams(vmem_limit_bytes=GRANT),
         cost_estimate=pl.CostEstimate(flops=0, bytes_accessed=1 << 20, transcendentals=0),
     )(*inputs, sea, before, after)
@@ -411,7 +416,7 @@
         out, out_low, out_high = pl.pallas_call(
             functools.partial(step_kernel, table, step),
             in_specs=[VMEM] * (6 + len(state)),
-            out_shape=[cells, row, row],
+            out_shape=[cells, row_of, row_of],
             out_specs=[VMEM] * 3,
             compiler_params=pltpu.CompilerParams(vmem_limit_bytes=GRANT),
             cost_estimate=pl.CostEstimate(flops=40 * levels * lon_cells * lat_cells, bytes_accessed=9 << 20, transcendentals=0),
@@ -421,7 +426,7 @@
         low, high, to_west, to_east = pl.pallas_call(
             face_kernel,
             in_specs=[VMEM] * 7,
-            out_shape=[row] * 4,
+            out_shape=[row_of] * 2 + [sent_row] * 2,
             out_specs=[VMEM] * 4,
             compiler_params=pltpu.CompilerParams(vmem_limit_bytes=GRANT),
             cost_estimate=pl.CostEstimate(flops=0, bytes_accessed=1 << 19, transcendentals=0),
@@ -437,18 +442,17 @@
         moved=3 << 20,
     )
     edge = (sea_ext, out_low, out_high, west, east)
-    mine, other = call(
+    mine, other, low, high = call(
         fix_kernel,
         (place, *edge, mine, other),
         [SMEM] + [VMEM] * 7,
-        [(half, bf16)] * 2,
-        scratch=[pltpu.VMEM((levels, lat_cells), f32)] * 2,
+        [(half, bf16)] * 2 + [(extended, f32)] * 2,
         aliases={6: 0, 7: 1},
     )
     (lam,) = call(
         emit_kernel,
-        (out, *edge),
-        [VMEM] * 6,
+        (out, low, high),
+        [VMEM] * 3,
         [((levels, lon_cells, lat_cells), f32)],
         moved=3 << 20,
     )
@@ -582,6 +586,18 @@
     rows = slots * width
 
     down, up, sea, place, left_other = pack(innovations, courant, diffusivity, sea_bricks, left)
+    before = from_behind(down, "depth", 1)
+    after = from_behind(up, "depth", -1)
+    inputs = (innovations, courant, diffusivity)
+    inputs = call(
+        load_kernel,
+        inputs,
+        [ANY] * 3,
+        [(a.shape, a.dtype) for a in inputs],
+        grant=LOAD_GRANT,
+        moved=18 << 20,
+        scratch=[pltpu.SemaphoreType.DMA((3,))],
+    )
     right_other = call(
         halves_kernel,
         (place, right),
@@ -594,7 +610,7 @@
     right_pair = []
     for part in range(PARTS):
         right_pair.append(swapped(right_other[part], "depth", 1).reshape(rows, half // PARTS))
-    lam, lam_mine, lam_other = sweep(innovations, courant, diffusivity, sea, down, up, place)
+    lam, lam_mine, lam_other = sweep(inputs, sea, before, after, place)
     left_pair = left_pair.reshape(rows, half)
     left, right = left.reshape(rows, tile_cols), right.reshape(rows, tile_cols)
     blocks = {0: lam_mine}

time: 139 us -> 137 us (0.986)
  waiting for transfers between devices: 59 us -> 56.7 us
    unnamed x34 -> x28, local copies, waits for them, and re-layouts: 2.95 us -> 1.97 us
  transfers between devices with their start and end apart: 27 -> 27, of which waited for: 15 -> 16; matrix products, arithmetic and copies ran while one was open for 0% -> 0% of each run, Pallas kernels for 16% -> 17%
where the time goes in v5:
time: 137 us; the launch traced here: 136 us
  waiting for transfers between devices  56.7 us (41%)
  starting transfers between devices  47.3 us (35%)
  Pallas kernels  29.5 us (22%)
  local copies, waits for them, and re-layouts  1.97 us (1%)
    ppermute x16, waiting for transfers between devices, swapped(): lax.ppermute(block, axis, [(i, i ^ mask) for i in range(lax.axis_size(axi...  35.7 us
    ppermute x16, starting transfers between devices, swapped(): lax.ppermute(block, axis, [(i, i ^ mask) for i in range(lax.axis_size(axi...  29.7 us
    ppermute x2, waiting for transfers between devices, from_behind(): lax.ppermute(value, axis, [(source, source + steps) for source in range(i...  20.4 us
    pallas_call x14, Pallas kernels, call(): pl.pallas_call(kernel, in_specs=in_specs, out_shape=[jax.ShapeDtypeStruct...  18.6 us
    ppermute x8, starting transfers between devices, shifted(): return lax.ppermute(block, axis, route)  11 us
    pallas_call x4, Pallas kernels, sweep(): pl.pallas_call(functools.partial(step_kernel, table, step), in_specs=[VME...  5.99 us
    pallas_call x1, Pallas kernels, pack(): pl.pallas_call(functools.partial(pack_kernel, table, ('lon', 'depth')), g...  4.35 us
    all_to_all x1, starting transfers between devices, per_device(): received = [lax.all_to_all(coeff[0], 'lon', 0, 0, tiled=True)]  3.41 us
  transfers between devices with their start and end apart: 27, of which 16 were waited for; matrix products, arithmetic and copies ran while one was open for 0% of the time, Pallas kernels for 17%

profile of v5, /device:TPU:0, one launch (start us, length us, event | category | flops | bytes accessed | tf_op | source)
XLA Modules:
  0.0 136.5 jit_solution(9032800077906815195)
XLA Ops:
  0.6 4.3 %shard_map.87 = (bf16[23,16,256]{2,1,0:T(8,128)(2,1)}, bf16[23,16,256]{2,1,0:T(8,128)(2,1)}, f32[64,256]{1,0:T(8,128)}, s32[3]{0:T(128)}, bf16[8,32,2048]{2,1,0:T(8,128)(2,1)}) custom-call(s32[64,1,128]{2,1,0:T(1,128)} %bricks.1, f32[5,64,16,256]{3,2,1,0:T(8,128)} %innov_hi.1, f32[5,64,16,256]{3,2,1,0:T(8,128)} %innov_hi.1, f32[3,64,16,256]{3,2,1,0:T(8,128)} %cour_hi.1, ...), custom_call_target="tpu_custom_call" | custom-call | bytes 1048576 | tf_op jit(solution)/shard_map/pallas_call | solution.py:367
  5.0 3.1 %collective-permute-start.12 = (bf16[8,32,2048]{2,1,0:T(8,128)(2,1)}, bf16[8,32,2048]{2,1,0:T(8,128)(2,1)S(1)}, u32[]{:S(2)}, u32[]{:S(2)}) collective-permute-start(bf16[8,32,2048]{2,1,0:T(8,128)(2,1)} %get-tuple-element.103), channel_id=1, source_target_pairs={{0,1},{1,0},{2,3},{3,2},{4,5},{5,4},{6,7},{7,6},{8,9},{9,8},{10,11... | collective-permute-start | bytes 3145736 | tf_op jit(solution)/shard_map/ppermute | solution.py:37
  8.1 1.9 %collective-permute-start = (bf16[23,16,256]{2,1,0:T(8,128)(2,1)}, bf16[23,16,256]{2,1,0:T(8,128)(2,1)S(1)}, u32[]{:S(2)}, u32[]{:S(2)}) collective-permute-start(bf16[23,16,256]{2,1,0:T(8,128)(2,1)} %get-tuple-element.65), channel_id=1, source_target_pairs={{0,1},{1,2},{2,3},{4,5},{5,6},{6,7},{8,9},{9,10},{10,11},{12,13},{... | collective-permute-start | bytes 565256 | tf_op jit(solution)/shard_map/ppermute | solution.py:25
  12.6 2.5 %shard_map.86 = (f32[5,64,16,256]{3,2,1,0:T(8,128)S(1)}, f32[3,64,16,256]{3,2,1,0:T(8,128)S(1)}, f32[64,16,256]{2,1,0:T(8,128)S(1)}) custom-call(f32[5,64,16,256]{3,2,1,0:T(8,128)} %innov_hi.1, f32[3,64,16,256]{3,2,1,0:T(8,128)S(1)} %copy-done.1, f32[64,16,256]{2,1,0:T(8,128)S(1)} %copy-done.3), custom_call_target="tpu_custom_call" | custom-call | bytes 18874368 | tf_op jit(solution)/shard_map/pallas_call | solution.py:561
  15.1 19.7 %collective-permute-done.before = bf16[23,16,256]{2,1,0:T(8,128)(2,1)S(1)} collective-permute-done((bf16[23,16,256]{2,1,0:T(8,128)(2,1)}, bf16[23,16,256]{2,1,0:T(8,128)(2,1)S(1)}, u32[]{:S(2)}, u32[]{:S(2)}) %collective-permute-start) | collective-permute-done | bytes 188448 | tf_op jit(solution)/shard_map/ppermute | solution.py:25
  36.0 2.6 %collective-permute-start.3 = (bf16[72,256]{1,0:T(8,128)(2,1)S(1)}, bf16[72,256]{1,0:T(8,128)(2,1)S(1)}, u32[]{:S(2)}, u32[]{:S(2)}) collective-permute-start(bf16[72,256]{1,0:T(8,128)(2,1)S(1)} %get-tuple-element.71), channel_id=1, source_target_pairs={{4,0},{8,4},{12,8},{16,12},{20,16},{24,20},{28,24},{0,28},{5,1},{9... | collective-permute-start | bytes 110600 | tf_op jit(solution)/shard_map/ppermute | solution.py:33
  41.3 1.8 %collective-permute-start.5 = (bf16[72,256]{1,0:T(8,128)(2,1)S(1)}, bf16[72,256]{1,0:T(8,128)(2,1)S(1)}, u32[]{:S(2)}, u32[]{:S(2)}) collective-permute-start(bf16[72,256]{1,0:T(8,128)(2,1)S(1)} %get-tuple-element.80), channel_id=1, source_target_pairs={{4,0},{8,4},{12,8},{16,12},{20,16},{24,20},{28,24},{0,28},{5,1},{9... | collective-permute-start | bytes 110600 | tf_op jit(solution)/shard_map/ppermute | solution.py:33
  43.1 1.6 %shard_map.91 = (f32[72,16,256]{2,1,0:T(8,128)S(1)}, f32[72,256]{1,0:T(8,128)S(1)}, f32[72,256]{1,0:T(8,128)S(1)}) custom-call(f32[5,64,16,256]{3,2,1,0:T(8,128)S(1)} %get-tuple-element.61.innov, f32[3,64,16,256]{3,2,1,0:T(8,128)S(1)} %get-tuple-element.62.cour, f32[64,16,256]{2,1,0:T(8,128)S(1)} %get-tuple-element.63.diff, ...), custom_call_target="tpu_custom_call" | custom-call | flops 10485760 | bytes 9437184 | tf_op jit(solution)/shard_map/pallas_call | solution.py:416
  45.5 2.0 %collective-permute-start.7 = (bf16[72,256]{1,0:T(8,128)(2,1)S(1)}, bf16[72,256]{1,0:T(8,128)(2,1)S(1)}, u32[]{:S(2)}, u32[]{:S(2)}) collective-permute-start(bf16[72,256]{1,0:T(8,128)(2,1)S(1)} %get-tuple-element.87), channel_id=1, source_target_pairs={{4,0},{8,4},{12,8},{16,12},{20,16},{24,20},{28,24},{0,28},{5,1},{9... | collective-permute-start | bytes 110600 | tf_op jit(solution)/shard_map/ppermute | solution.py:33
  50.0 2.0 %collective-permute-start.9 = (bf16[72,256]{1,0:T(8,128)(2,1)S(1)}, bf16[72,256]{1,0:T(8,128)(2,1)S(1)}, u32[]{:S(2)}, u32[]{:S(2)}) collective-permute-start(bf16[72,256]{1,0:T(8,128)(2,1)S(1)} %get-tuple-element.96), channel_id=1, source_target_pairs={{4,0},{8,4},{12,8},{16,12},{20,16},{24,20},{28,24},{0,28},{5,1},{9... | collective-permute-start | bytes 110600 | tf_op jit(solution)/shard_map/ppermute | solution.py:33
  55.1 2.8 %collective-permute-start.15 = (bf16[64,2048]{1,0:T(8,128)(2,1)S(1)}, bf16[64,2048]{1,0:T(8,128)(2,1)S(1)}, u32[]{:S(2)}, u32[]{:S(2)}) collective-permute-start(bf16[64,2048]{1,0:T(8,128)(2,1)S(1)} %get-tuple-element.104.first), channel_id=1, source_target_pairs={{0,2},{1,3},{2,0},{3,1},{4,6},{5,7},{6,4},{7,5},{8,10},{9,11},{10,... | collective-permute-start | bytes 786440 | tf_op jit(solution)/shard_map/ppermute | solution.py:37
  59.5 17.0 %collective-permute-done.15.first = bf16[64,2048]{1,0:T(8,128)(2,1)S(1)} collective-permute-done((bf16[64,2048]{1,0:T(8,128)(2,1)S(1)}, bf16[64,2048]{1,0:T(8,128)(2,1)S(1)}, u32[]{:S(2)}, u32[]{:S(2)}) %collective-permute-start.15) | collective-permute-done | bytes 262176 | tf_op jit(solution)/shard_map/ppermute | solution.py:37
  77.8 5.2 %collective-permute-start.17 = (bf16[2,256,128]{2,1,0:T(8,128)(2,1)S(1)}, bf16[2,256,128]{2,1,0:T(8,128)(2,1)S(1)}, u32[]{:S(2)}, u32[]{:S(2)}) collective-permute-start(bf16[2,256,128]{2,1,0:T(8,128)(2,1)S(1)} %get-tuple-element.109), channel_id=1, source_target_pairs={{0,1},{1,0},{2,3},{3,2},{4,5},{5,4},{6,7},{7,6},{8,9},{9,8},{10,11... | collective-permute-start | bytes 393224 | tf_op jit(solution)/shard_map/ppermute | solution.py:37
  86.1 2.1 %collective-permute-start.19 = (bf16[8,32,512]{2,1,0:T(8,128)(2,1)}, bf16[8,32,512]{2,1,0:T(8,128)(2,1)}, u32[]{:S(2)}, u32[]{:S(2)}) collective-permute-start(bf16[8,32,512]{2,1,0:T(8,128)(2,1)} %get-tuple-element.112), channel_id=1, source_target_pairs={{0,1},{1,0},{2,3},{3,2},{4,5},{5,4},{6,7},{7,6},{8,9},{9,8},{10,11... | collective-permute-start | bytes 786440 | tf_op jit(solution)/shard_map/ppermute | solution.py:37
  88.2 2.4 %collective-permute-done.14.rest_1_ = bf16[2,256,128]{2,1,0:T(8,128)(2,1)S(1)} collective-permute-done((bf16[2,256,128]{2,1,0:T(8,128)(2,1)S(1)}, bf16[2,256,128]{2,1,0:T(8,128)(2,1)S(1)}, u32[]{:S(2)}, u32[]{:S(2)}) %collective-permute-start.14) | collective-permute-done | bytes 131104 | tf_op jit(solution)/shard_map/ppermute | solution.py:37
  91.9 3.4 %all-to-all-start = ((bf16[8,2,32,256]{3,2,1,0:T(8,128)(2,1)}), bf16[8,2,32,256]{3,2,1,0:T(8,128)(2,1)S(1)}, u32[]{:S(2)}, u32[]{:S(2)}) async-start(bf16[8,2,32,256]{3,2,1,0:T(8,128)(2,1)} %copy-done.4), calls=%async_computation | async-start | bytes 524288 | tf_op jit(solution)/shard_map/all_to_all | solution.py:640
  95.3 1.7 %collective-permute-start.10 = (bf16[8,32,512]{2,1,0:T(8,128)(2,1)}, bf16[8,32,512]{2,1,0:T(8,128)(2,1)}, u32[]{:S(2)}, u32[]{:S(2)}) collective-permute-start(bf16[8,32,512]{2,1,0:T(8,128)(2,1)} %copy-done.13), channel_id=1, source_target_pairs={{0,1},{1,0},{2,3},{3,2},{4,5},{5,4},{6,7},{7,6},{8,9},{9,8},{10,11... | collective-permute-start | bytes 786440 | tf_op jit(solution)/shard_map/ppermute | solution.py:37
  97.4 4.5 %collective-permute-done.18 = bf16[8,32,512]{2,1,0:T(8,128)(2,1)} collective-permute-done((bf16[8,32,512]{2,1,0:T(8,128)(2,1)}, bf16[8,32,512]{2,1,0:T(8,128)(2,1)}, u32[]{:S(2)}, u32[]{:S(2)}) %collective-permute-start.18) | collective-permute-done | bytes 262176 | tf_op jit(solution)/shard_map/ppermute | solution.py:37
  103.6 3.4 %collective-permute-start.25 = (bf16[64,1024]{1,0:T(8,128)(2,1)S(1)}, bf16[64,1024]{1,0:T(8,128)(2,1)S(1)}, u32[]{:S(2)}, u32[]{:S(2)}) collective-permute-start(bf16[64,1024]{1,0:T(8,128)(2,1)S(1)} %get-tuple-element.119), channel_id=1, source_target_pairs={{0,3},{1,2},{2,1},{3,0},{4,7},{5,6},{6,5},{7,4},{8,11},{9,10},{10,... | collective-permute-start | bytes 393224 | tf_op jit(solution)/shard_map/ppermute | solution.py:37
  107.5 4.8 %collective-permute-done.11 = bf16[8,32,512]{2,1,0:T(8,128)(2,1)} collective-permute-done((bf16[8,32,512]{2,1,0:T(8,128)(2,1)}, bf16[8,32,512]{2,1,0:T(8,128)(2,1)}, u32[]{:S(2)}, u32[]{:S(2)}) %collective-permute-start.11) | collective-permute-done | bytes 262176 | tf_op jit(solution)/shard_map/ppermute | solution.py:37
  113.7 4.1 %collective-permute-start.24 = (bf16[64,1024]{1,0:T(8,128)(2,1)S(1)}, bf16[64,1024]{1,0:T(8,128)(2,1)S(1)}, u32[]{:S(2)}, u32[]{:S(2)}) collective-permute-start(bf16[64,1024]{1,0:T(8,128)(2,1)S(1)} %get-tuple-element.118), channel_id=1, source_target_pairs={{0,3},{1,2},{2,1},{3,0},{4,7},{5,6},{6,5},{7,4},{8,11},{9,10},{10,... | collective-permute-start | bytes 393224 | tf_op jit(solution)/shard_map/ppermute | solution.py:37
  123.1 2.6 %collective-permute-start.20 = (bf16[64,1024]{1,0:T(8,128)(2,1)S(1)}, bf16[64,1024]{1,0:T(8,128)(2,1)S(1)}, u32[]{:S(2)}, u32[]{:S(2)}) collective-permute-start(bf16[64,1024]{1,0:T(8,128)(2,1)S(1)} %get-tuple-element.114), channel_id=1, source_target_pairs={{0,2},{1,3},{2,0},{3,1},{4,6},{5,7},{6,4},{7,5},{8,10},{9,11},{10,... | collective-permute-start | bytes 393224 | tf_op jit(solution)/shard_map/ppermute | solution.py:37
  127.2 2.1 %collective-permute-done.22.rest_0_ = bf16[64,1024]{1,0:T(8,128)(2,1)S(1)} collective-permute-done((bf16[64,1024]{1,0:T(8,128)(2,1)S(1)}, bf16[64,1024]{1,0:T(8,128)(2,1)S(1)}, u32[]{:S(2)}, u32[]{:S(2)}) %collective-permute-start.22) | collective-permute-done | bytes 131104 | tf_op jit(solution)/shard_map/ppermute | solution.py:37
  130.7 2.9 %collective-permute-done.21.rest_3_ = bf16[64,1024]{1,0:T(8,128)(2,1)S(1)} collective-permute-done((bf16[64,1024]{1,0:T(8,128)(2,1)S(1)}, bf16[64,1024]{1,0:T(8,128)(2,1)S(1)}, u32[]{:S(2)}, u32[]{:S(2)}) %collective-permute-start.21) | collective-permute-done | bytes 131104 | tf_op jit(solution)/shard_map/ppermute | solution.py:37
  (81 shorter events, 34.9 us)
Async XLA Ops:
  5.0 71.5 %collective-permute-start.12 = (bf16[8,32,2048]{2,1,0:T(8,128)(2,1)}, bf16[8,32,2048]{2,1,0:T(8,128)(2,1)S(1)}, u32[]{:S(2)}, u32[]{:S(2)}) collective-permute-start(bf16[8,32,2048]{2,1,0:T(8,128)(2,1)} %get-tuple-element.103), channel_id=1, source_target_pairs={{0,1},{1,0},{2,3},{3,2},{4,5},{5,4},{6,7},{7,6},{8,9},{9,8},{10,11... | collective-permute-start | bytes 3145736 | tf_op jit(solution)/shard_map/ppermute | solution.py:37
  8.1 26.8 %collective-permute-start = (bf16[23,16,256]{2,1,0:T(8,128)(2,1)}, bf16[23,16,256]{2,1,0:T(8,128)(2,1)S(1)}, u32[]{:S(2)}, u32[]{:S(2)}) collective-permute-start(bf16[23,16,256]{2,1,0:T(8,128)(2,1)} %get-tuple-element.65), channel_id=1, source_target_pairs={{0,1},{1,2},{2,3},{4,5},{5,6},{6,7},{8,9},{9,10},{10,11},{12,13},{... | collective-permute-start | bytes 565256 | tf_op jit(solution)/shard_map/ppermute | solution.py:25
  10.0 25.5 %collective-permute-start.1 = (bf16[23,16,256]{2,1,0:T(8,128)(2,1)}, bf16[23,16,256]{2,1,0:T(8,128)(2,1)S(1)}, u32[]{:S(2)}, u32[]{:S(2)}) collective-permute-start(bf16[23,16,256]{2,1,0:T(8,128)(2,1)} %get-tuple-element.66), channel_id=1, source_target_pairs={{1,0},{2,1},{3,2},{5,4},{6,5},{7,6},{9,8},{10,9},{11,10},{13,12},{... | collective-permute-start | bytes 565256 | tf_op jit(solution)/shard_map/ppermute | solution.py:25
  36.0 4.3 %collective-permute-start.2 = (bf16[72,256]{1,0:T(8,128)(2,1)S(1)}, bf16[72,256]{1,0:T(8,128)(2,1)S(1)}, u32[]{:S(2)}, u32[]{:S(2)}) collective-permute-start(bf16[72,256]{1,0:T(8,128)(2,1)S(1)} %get-tuple-element.70), channel_id=1, source_target_pairs={{28,0},{0,4},{4,8},{8,12},{12,16},{16,20},{20,24},{24,28},{29,1},{... | collective-permute-start | bytes 110600 | tf_op jit(solution)/shard_map/ppermute | solution.py:33
  40.4 4.3 %collective-permute-start.4 = (bf16[72,256]{1,0:T(8,128)(2,1)S(1)}, bf16[72,256]{1,0:T(8,128)(2,1)S(1)}, u32[]{:S(2)}, u32[]{:S(2)}) collective-permute-start(bf16[72,256]{1,0:T(8,128)(2,1)S(1)} %get-tuple-element.79), channel_id=1, source_target_pairs={{28,0},{0,4},{4,8},{8,12},{12,16},{16,20},{20,24},{24,28},{29,1},{... | collective-permute-start | bytes 110600 | tf_op jit(solution)/shard_map/ppermute | solution.py:33
  44.8 4.3 %collective-permute-start.6 = (bf16[72,256]{1,0:T(8,128)(2,1)S(1)}, bf16[72,256]{1,0:T(8,128)(2,1)S(1)}, u32[]{:S(2)}, u32[]{:S(2)}) collective-permute-start(bf16[72,256]{1,0:T(8,128)(2,1)S(1)} %get-tuple-element.86), channel_id=1, source_target_pairs={{28,0},{0,4},{4,8},{8,12},{12,16},{16,20},{20,24},{24,28},{29,1},{... | collective-permute-start | bytes 110600 | tf_op jit(solution)/shard_map/ppermute | solution.py:33
  49.2 5.3 %collective-permute-start.8 = (bf16[72,256]{1,0:T(8,128)(2,1)S(1)}, bf16[72,256]{1,0:T(8,128)(2,1)S(1)}, u32[]{:S(2)}, u32[]{:S(2)}) collective-permute-start(bf16[72,256]{1,0:T(8,128)(2,1)S(1)} %get-tuple-element.95), channel_id=1, source_target_pairs={{28,0},{0,4},{4,8},{8,12},{12,16},{16,20},{20,24},{24,28},{29,1},{... | collective-permute-start | bytes 110600 | tf_op jit(solution)/shard_map/ppermute | solution.py:33
  50.0 4.5 %collective-permute-start.9 = (bf16[72,256]{1,0:T(8,128)(2,1)S(1)}, bf16[72,256]{1,0:T(8,128)(2,1)S(1)}, u32[]{:S(2)}, u32[]{:S(2)}) collective-permute-start(bf16[72,256]{1,0:T(8,128)(2,1)S(1)} %get-tuple-element.96), channel_id=1, source_target_pairs={{4,0},{8,4},{12,8},{16,12},{20,16},{24,20},{28,24},{0,28},{5,1},{9... | collective-permute-start | bytes 110600 | tf_op jit(solution)/shard_map/ppermute | solution.py:33
  55.1 21.4 %collective-permute-start.15 = (bf16[64,2048]{1,0:T(8,128)(2,1)S(1)}, bf16[64,2048]{1,0:T(8,128)(2,1)S(1)}, u32[]{:S(2)}, u32[]{:S(2)}) collective-permute-start(bf16[64,2048]{1,0:T(8,128)(2,1)S(1)} %get-tuple-element.104.first), channel_id=1, source_target_pairs={{0,2},{1,3},{2,0},{3,1},{4,6},{5,7},{6,4},{7,5},{8,10},{9,11},{10,... | collective-permute-start | bytes 786440 | tf_op jit(solution)/shard_map/ppermute | solution.py:37
  57.9 18.5 %collective-permute-start.16 = (bf16[64,2048]{1,0:T(8,128)(2,1)S(1)}, bf16[64,2048]{1,0:T(8,128)(2,1)S(1)}, u32[]{:S(2)}, u32[]{:S(2)}) collective-permute-start(bf16[64,2048]{1,0:T(8,128)(2,1)S(1)} %get-tuple-element.105), channel_id=1, source_target_pairs={{0,3},{1,2},{2,1},{3,0},{4,7},{5,6},{6,5},{7,4},{8,11},{9,10},{10,... | collective-permute-start | bytes 786440 | tf_op jit(solution)/shard_map/ppermute | solution.py:37
  59.3 23.8 %collective-permute-start.13 = (bf16[64,2048]{1,0:T(8,128)(2,1)S(1)}, bf16[64,2048]{1,0:T(8,128)(2,1)S(1)}, u32[]{:S(2)}, u32[]{:S(2)}) collective-permute-start(bf16[64,2048]{1,0:T(8,128)(2,1)S(1)} %get-tuple-element.105), channel_id=1, source_target_pairs={{0,1},{1,0},{2,3},{3,2},{4,5},{5,4},{6,7},{7,6},{8,9},{9,8},{10,11... | collective-permute-start | bytes 786440 | tf_op jit(solution)/shard_map/ppermute | solution.py:37
  77.8 10.4 %collective-permute-start.17 = (bf16[2,256,128]{2,1,0:T(8,128)(2,1)S(1)}, bf16[2,256,128]{2,1,0:T(8,128)(2,1)S(1)}, u32[]{:S(2)}, u32[]{:S(2)}) collective-permute-start(bf16[2,256,128]{2,1,0:T(8,128)(2,1)S(1)} %get-tuple-element.109), channel_id=1, source_target_pairs={{0,1},{1,0},{2,3},{3,2},{4,5},{5,4},{6,7},{7,6},{8,9},{9,8},{10,11... | collective-permute-start | bytes 393224 | tf_op jit(solution)/shard_map/ppermute | solution.py:37
  84.4 6.2 %collective-permute-start.14 = (bf16[2,256,128]{2,1,0:T(8,128)(2,1)S(1)}, bf16[2,256,128]{2,1,0:T(8,128)(2,1)S(1)}, u32[]{:S(2)}, u32[]{:S(2)}) collective-permute-start(bf16[2,256,128]{2,1,0:T(8,128)(2,1)S(1)} %get-tuple-element.107), channel_id=1, source_target_pairs={{0,1},{1,0},{2,3},{3,2},{4,5},{5,4},{6,7},{7,6},{8,9},{9,8},{10,11... | collective-permute-start | bytes 393224 | tf_op jit(solution)/shard_map/ppermute | solution.py:37
  86.1 11.4 %collective-permute-start.19 = (bf16[8,32,512]{2,1,0:T(8,128)(2,1)}, bf16[8,32,512]{2,1,0:T(8,128)(2,1)}, u32[]{:S(2)}, u32[]{:S(2)}) collective-permute-start(bf16[8,32,512]{2,1,0:T(8,128)(2,1)} %get-tuple-element.112), channel_id=1, source_target_pairs={{0,1},{1,0},{2,3},{3,2},{4,5},{5,4},{6,7},{7,6},{8,9},{9,8},{10,11... | collective-permute-start | bytes 786440 | tf_op jit(solution)/shard_map/ppermute | solution.py:37
  88.1 13.8 %collective-permute-start.18 = (bf16[8,32,512]{2,1,0:T(8,128)(2,1)}, bf16[8,32,512]{2,1,0:T(8,128)(2,1)}, u32[]{:S(2)}, u32[]{:S(2)}) collective-permute-start(bf16[8,32,512]{2,1,0:T(8,128)(2,1)} %get-tuple-element.111), channel_id=1, source_target_pairs={{0,1},{1,0},{2,3},{3,2},{4,5},{5,4},{6,7},{7,6},{8,9},{9,8},{10,11... | collective-permute-start | bytes 786440 | tf_op jit(solution)/shard_map/ppermute | solution.py:37
  91.9 10.3 %all-to-all-start = ((bf16[8,2,32,256]{3,2,1,0:T(8,128)(2,1)}), bf16[8,2,32,256]{3,2,1,0:T(8,128)(2,1)S(1)}, u32[]{:S(2)}, u32[]{:S(2)}) async-start(bf16[8,2,32,256]{3,2,1,0:T(8,128)(2,1)} %copy-done.4), calls=%async_computation | async-start | bytes 524288 | tf_op jit(solution)/shard_map/all_to_all | solution.py:640
  95.3 12.2 %collective-permute-start.10 = (bf16[8,32,512]{2,1,0:T(8,128)(2,1)}, bf16[8,32,512]{2,1,0:T(8,128)(2,1)}, u32[]{:S(2)}, u32[]{:S(2)}) collective-permute-start(bf16[8,32,512]{2,1,0:T(8,128)(2,1)} %copy-done.13), channel_id=1, source_target_pairs={{0,1},{1,0},{2,3},{3,2},{4,5},{5,4},{6,7},{7,6},{8,9},{9,8},{10,11... | collective-permute-start | bytes 786440 | tf_op jit(solution)/shard_map/ppermute | solution.py:37
  97.1 15.3 %collective-permute-start.11 = (bf16[8,32,512]{2,1,0:T(8,128)(2,1)}, bf16[8,32,512]{2,1,0:T(8,128)(2,1)}, u32[]{:S(2)}, u32[]{:S(2)}) collective-permute-start(bf16[8,32,512]{2,1,0:T(8,128)(2,1)} %copy-done.12), channel_id=1, source_target_pairs={{0,1},{1,0},{2,3},{3,2},{4,5},{5,4},{6,7},{7,6},{8,9},{9,8},{10,11... | collective-permute-start | bytes 786440 | tf_op jit(solution)/shard_map/ppermute | solution.py:37
  103.6 19.6 %collective-permute-start.25 = (bf16[64,1024]{1,0:T(8,128)(2,1)S(1)}, bf16[64,1024]{1,0:T(8,128)(2,1)S(1)}, u32[]{:S(2)}, u32[]{:S(2)}) collective-permute-start(bf16[64,1024]{1,0:T(8,128)(2,1)S(1)} %get-tuple-element.119), channel_id=1, source_target_pairs={{0,3},{1,2},{2,1},{3,0},{4,7},{5,6},{6,5},{7,4},{8,11},{9,10},{10,... | collective-permute-start | bytes 393224 | tf_op jit(solution)/shard_map/ppermute | solution.py:37
  113.7 13.2 %collective-permute-start.24 = (bf16[64,1024]{1,0:T(8,128)(2,1)S(1)}, bf16[64,1024]{1,0:T(8,128)(2,1)S(1)}, u32[]{:S(2)}, u32[]{:S(2)}) collective-permute-start(bf16[64,1024]{1,0:T(8,128)(2,1)S(1)} %get-tuple-element.118), channel_id=1, source_target_pairs={{0,3},{1,2},{2,1},{3,0},{4,7},{5,6},{6,5},{7,4},{8,11},{9,10},{10,... | collective-permute-start | bytes 393224 | tf_op jit(solution)/shard_map/ppermute | solution.py:37
  119.2 7.9 %collective-permute-start.23 = (bf16[64,1024]{1,0:T(8,128)(2,1)S(1)}, bf16[64,1024]{1,0:T(8,128)(2,1)S(1)}, u32[]{:S(2)}, u32[]{:S(2)}) collective-permute-start(bf16[64,1024]{1,0:T(8,128)(2,1)S(1)} %get-tuple-element.117), channel_id=1, source_target_pairs={{0,1},{1,0},{2,3},{3,2},{4,5},{5,4},{6,7},{7,6},{8,9},{9,8},{10,11... | collective-permute-start | bytes 393224 | tf_op jit(solution)/shard_map/ppermute | solution.py:37
  121.6 7.7 %collective-permute-start.22 = (bf16[64,1024]{1,0:T(8,128)(2,1)S(1)}, bf16[64,1024]{1,0:T(8,128)(2,1)S(1)}, u32[]{:S(2)}, u32[]{:S(2)}) collective-permute-start(bf16[64,1024]{1,0:T(8,128)(2,1)S(1)} %get-tuple-element.116), channel_id=1, source_target_pairs={{0,1},{1,0},{2,3},{3,2},{4,5},{5,4},{6,7},{7,6},{8,9},{9,8},{10,11... | collective-permute-start | bytes 393224 | tf_op jit(solution)/shard_map/ppermute | solution.py:37
  122.7 10.8 %collective-permute-start.21 = (bf16[64,1024]{1,0:T(8,128)(2,1)S(1)}, bf16[64,1024]{1,0:T(8,128)(2,1)S(1)}, u32[]{:S(2)}, u32[]{:S(2)}) collective-permute-start(bf16[64,1024]{1,0:T(8,128)(2,1)S(1)} %get-tuple-element.115), channel_id=1, source_target_pairs={{0,2},{1,3},{2,0},{3,1},{4,6},{5,7},{6,4},{7,5},{8,10},{9,11},{10,... | collective-permute-start | bytes 393224 | tf_op jit(solution)/shard_map/ppermute | solution.py:37
  123.1 11.9 %collective-permute-start.20 = (bf16[64,1024]{1,0:T(8,128)(2,1)S(1)}, bf16[64,1024]{1,0:T(8,128)(2,1)S(1)}, u32[]{:S(2)}, u32[]{:S(2)}) collective-permute-start(bf16[64,1024]{1,0:T(8,128)(2,1)S(1)} %get-tuple-element.114), channel_id=1, source_target_pairs={{0,2},{1,3},{2,0},{3,1},{4,6},{5,7},{6,4},{7,5},{8,10},{9,11},{10,... | collective-permute-start | bytes 393224 | tf_op jit(solution)/shard_map/ppermute | solution.py:37
  (17 other events, 166.4 us)

commit v6 on v5

--- a/solution.py
+++ b/solution.py
@@ -10,7 +10,7 @@
 LANES = 128
 PARTS = 4
 LOAD_GRANT = 40 << 20
-STAGES = 2
+WIDE_GRANT = 60 << 20
 LANE_TILES = 2
 HALVES = 2
 GRANT = 4 << 20
@@ -54,14 +54,9 @@
     return ref[pl.ds(at, 1), :]
 
 
-def pack_kernel(table, axes, bricks, innov_lo, innov_hi, cour_lo, cour_hi, diff_lo, diff_hi, left, down, up, sea, place, left_other, rows, vmem, sems):
+def pack_kernel(table, axes, bricks, innov_lo, innov_hi, cour_lo, cour_hi, diff_lo, diff_hi, down, up, sea, place, rows):
     me = lax.axis_index(axes[1])
-    side = lax.rem(me, 2)
-    place[0], place[1], place[2] = me, side, lax.axis_index(axes[0])
-    half = left_other.shape[2]
-    window = pl.ds(pl.multiple_of((1 - side) * half, half), half)
-    load = pltpu.make_async_copy(left.at[0, :, :, window], vmem, sems.at[0])
-    load.start()
+    place[0], place[1], place[2] = me, lax.rem(me, 2), lax.axis_index(axes[0])
     depth = diff_lo.shape[0]
     levels, _, count = bricks.shape
     lat_cells = sea.shape[1]
@@ -100,11 +95,7 @@
             out[at] = value.astype(jnp.bfloat16)
 
     fill(down, innov_hi, cour_hi, diff_hi, sea_hi, lambda d: depth - d, -1.0)
-    load.wait()
-    store = pltpu.make_async_copy(vmem, left_other, sems.at[1])
-    store.start()
     fill(up, innov_lo, cour_lo, diff_lo, sea_lo, lambda d: d - 1, 1.0)
-    store.wait()
 
 
 def load_kernel(*refs):
@@ -348,7 +339,7 @@
     to_east[...] = (east_gain[...] * high_rows).astype(jnp.bfloat16)
 
 
-def pack(innovations, courant, diffusivity, bricks, left):
+def pack(innovations, courant, diffusivity, bricks):
     levels, lon_cells, lat_cells = diffusivity.shape
     steps = innovations.shape[0] - 1
     table, layers = halo_table(steps)
@@ -362,31 +353,25 @@
         return [pl.BlockSpec(tuple(block), at(index)) for index in (0, end)]
 
     message = jax.ShapeDtypeStruct((layers, lon_cells, lat_cells), bf16)
-    _, slots, width, cols = left.shape
-    other = jax.ShapeDtypeStruct((slots, width, cols // 2), bf16)
     return pl.pallas_call(
         functools.partial(pack_kernel, table, ("lon", "depth")),
         grid=(1,),
         in_specs=[VMEM]
         + edges(innovations.shape, 1)
         + edges(courant.shape, 1)
-        + edges(diffusivity.shape, 0)
-        + [ANY],
+        + edges(diffusivity.shape, 0),
         out_shape=[
             message,
             message,
             jax.ShapeDtypeStruct((levels, lat_cells), f32),
             jax.ShapeDtypeStruct((3,), jnp.int32),
-            other,
         ],
-        out_specs=[VMEM, VMEM, VMEM, SMEM, ANY],
+        out_specs=[VMEM, VMEM, VMEM, SMEM],
         scratch_shapes=[
             pltpu.VMEM((levels, bricks.shape[2]), f32),
-            pltpu.VMEM((slots, width, cols // 2), bf16),
-            pltpu.SemaphoreType.DMA((2,)),
         ],
         cost_estimate=pl.CostEstimate(flops=0, bytes_accessed=1 << 20, transcendentals=0),
-    )(bricks, innovations, innovations, courant, courant, diffusivity, diffusivity, left)
+    )(bricks, innovations, innovations, courant, courant, diffusivity, diffusivity)
 
 
 def sweep(inputs, sea, before, after, place):
@@ -480,19 +465,15 @@
         sent[1 - c] = jnp.concatenate(other_order, 1).astype(jnp.bfloat16)
 
 
-def mask_kernel(slots, place, ranks, *rest):
-    stages = [rest[n : n + 2] for n in range(0, STAGES * 2, 2)]
-    out = rest[STAGES * 2 :]
-    rows = stages[0][0].shape[1] // slots
+def mask_kernel(slots, place, ranks, kept, arrived, *out):
+    rows = kept.shape[1] // slots
     for c in range(2):
         owner = place[0] if c == 0 else place[0] + 1 - 2 * place[1]
         for k in range(slots):
             at = slice(k * rows, (k + 1) * rows)
-            value = jnp.concatenate(
-                [kept[c, at, :] + arrived[c, at, :].astype(jnp.float32) for kept, arrived in stages], 1
-            )
-            row = lax.broadcasted_iota(jnp.int32, value.shape, 0) + owner * rows
-            value = jnp.where(row < ranks[0, k], value, 0.0).astype(jnp.bfloat16)
+            value = kept[c, at, :] + arrived[c, at, :].astype(jnp.float32)
+            row_at = lax.broadcasted_iota(jnp.int32, value.shape, 0) + owner * rows
+            value = jnp.where(row_at < ranks[0, k], value, 0.0).astype(jnp.bfloat16)
             if len(out) > 1:
                 out[k][c] = value
             else:
@@ -500,22 +481,21 @@
                 out[0][lax.rem(place[2] + (k - slots // 2 + count), count), c] = value
 
 
-def columns_kernel(slots, stage, start, place, right, *rest):
+def columns_kernel(slots, start, place, right, *rest):
     pieces = PARTS // HALVES
     right_pair, received, out = rest[:pieces], rest[pieces:-2], rest[-2:]
     count = received[0].shape[0]
     levels = out[0].shape[0]
     wide = right_pair[0].shape[1]
     half = wide * PARTS
-    picked = slice(stage * levels, (stage + 2) * levels)
     coeffs = []
     for c in range(2):
         for k in range(slots):
             if len(received) > 1:
-                coeffs.append(received[k][c, :, picked])
+                coeffs.append(received[k][c])
             else:
                 source = lax.rem(place[2] + (count + slots // 2 - k), count)
-                coeffs.append(received[0][source, c, :, picked])
+                coeffs.append(received[0][source, c])
     stacked = jnp.concatenate(coeffs, 0)
     rows = right.shape[0]
     lead = (((0,), (0,)), ((), ()))
@@ -585,7 +565,16 @@
     width = left.shape[2]
     rows = slots * width
 
-    down, up, sea, place, left_other = pack(innovations, courant, diffusivity, sea_bricks, left)
+    down, up, sea, place = pack(innovations, courant, diffusivity, sea_bricks)
+    (left_other,) = call(
+        halves_kernel,
+        (place, left),
+        [SMEM, ANY],
+        [((slots, width, half), bf16, ANY)],
+        grant=WIDE_GRANT,
+        moved=2 << 20,
+        scratch=[pltpu.VMEM((1, slots, width, half), bf16), pltpu.SemaphoreType.DMA((2,))],
+    )
     before = from_behind(down, "depth", 1)
     after = from_behind(up, "depth", -1)
     inputs = (innovations, courant, diffusivity)
@@ -616,7 +605,7 @@
     blocks = {0: lam_mine}
     for mask in range(count - 1, 0, -1):
         blocks[mask] = swapped(lam_other if mask % 2 else lam_mine, "depth", mask)
-    sums = []
+    sums = {}
     for stage in range(0, count, 2):
         pair = (2, rows, 2 * levels)
         kept, sent = call(
@@ -627,26 +616,26 @@
             flops=8 * rows * half * levels,
             moved=3 << 20,
         )
-        sums += [kept, swapped(sent, "depth", 1)]
+        sums[stage] = (kept, swapped(sent, "depth", 1))
     grouped = lon_count == slots
-    slot = (2, width, count * levels)
-    coeff = call(
-        functools.partial(mask_kernel, slots),
-        (place, tile_ranks, *sums),
-        [SMEM, SMEM] + [VMEM] * len(sums),
-        [((lon_count,) + slot, bf16)] if grouped else [(slot, bf16)] * slots,
-    )
-    if grouped:
-        received = [lax.all_to_all(coeff[0], "lon", 0, 0, tiled=True)]
-    else:
-        received = [shifted(coeff[k], "lon", k - slots // 2) for k in range(slots)]
+    slot = (2, width, 2 * levels)
     arrived = {mask: [] for mask in range(count)}
     block = (levels, half // HALVES)
     pieces = PARTS // HALVES
-    for part in range(HALVES):
-        for stage in range(count - 2, -1, -2):
+    for stage in range(count - 2, -1, -2):
+        coeff = call(
+            functools.partial(mask_kernel, slots),
+            (place, tile_ranks, *sums[stage]),
+            [SMEM, SMEM, VMEM, VMEM],
+            [((lon_count,) + slot, bf16)] if grouped else [(slot, bf16)] * slots,
+        )
+        if grouped:
+            received = [lax.all_to_all(coeff[0], "lon", 0, 0, tiled=True)]
+        else:
+            received = [shifted(coeff[k], "lon", k - slots // 2) for k in range(slots)]
+        for part in range(HALVES):
             first, second = call(
-                functools.partial(columns_kernel, slots, stage, part * (half // HALVES)),
+                functools.partial(columns_kernel, slots, part * (half // HALVES)),
                 (place, right, *right_pair[part * pieces : (part + 1) * pieces], *received),
                 [SMEM] + [VMEM] * (1 + pieces + len(received)),
                 [(block, bf16 if stage else f32), (block, bf16)],

time: 137 us -> 151 us (1.10)
  waiting for transfers between devices: 56.7 us -> 62.4 us
  Pallas kernels: 29.5 us -> 34.4 us
  local copies, waits for them, and re-layouts: 1.97 us -> 4.89 us
    pallas_call x14 -> x16, Pallas kernels: 18.6 us -> 25.5 us  [call(): pl.pallas_call(kernel, in_specs=in_specs, out_shape=[jax.ShapeDtypeStruct...]
    ppermute x16, waiting for transfers between devices: 35.7 us -> 41.9 us  [swapped(): lax.ppermute(block, axis, [(i, i ^ mask) for i in range(lax.axis_size(axi...]
    all_to_all x1 -> x2, starting transfers between devices: 3.41 us -> 6.74 us  [per_device(): received = [lax.all_to_all(coeff[0], 'lon', 0, 0, tiled=True)]]
    ppermute x16, starting transfers between devices: 29.7 us -> 26.7 us  [swapped(): lax.ppermute(block, axis, [(i, i ^ mask) for i in range(lax.axis_size(axi...]
    unnamed x28 -> x36, local copies, waits for them, and re-layouts: 1.97 us -> 4.89 us
    pallas_call x1, Pallas kernels: 4.35 us -> 2.14 us  [pack(): pl.pallas_call(functools.partial(pack_kernel, table, ('lon', 'depth')), g...]
  transfers between devices with their start and end apart: 27 -> 28, of which waited for: 16 -> 8; matrix products, arithmetic and copies ran while one was open for 0% -> 0% of each run, Pallas kernels for 17% -> 18%
where the time goes in v6:
time: 151 us; the launch traced here: 150 us
  waiting for transfers between devices  62.4 us (41%)
  starting transfers between devices  47.7 us (32%)
  Pallas kernels  34.4 us (23%)
  local copies, waits for them, and re-layouts  4.89 us (3%)
    ppermute x16, waiting for transfers between devices, swapped(): lax.ppermute(block, axis, [(i, i ^ mask) for i in range(lax.axis_size(axi...  41.9 us
    ppermute x16, starting transfers between devices, swapped(): lax.ppermute(block, axis, [(i, i ^ mask) for i in range(lax.axis_size(axi...  26.7 us
    pallas_call x16, Pallas kernels, call(): pl.pallas_call(kernel, in_specs=in_specs, out_shape=[jax.ShapeDtypeStruct...  25.5 us
    ppermute x2, waiting for transfers between devices, from_behind(): lax.ppermute(value, axis, [(source, source + steps) for source in range(i...  20.4 us
    ppermute x8, starting transfers between devices, shifted(): return lax.ppermute(block, axis, route)  11 us
    all_to_all x2, starting transfers between devices, per_device(): received = [lax.all_to_all(coeff[0], 'lon', 0, 0, tiled=True)]  6.74 us
    pallas_call x4, Pallas kernels, sweep(): pl.pallas_call(functools.partial(step_kernel, table, step), in_specs=[VME...  6.23 us
    unnamed x36, local copies, waits for them, and re-layouts  4.89 us
  transfers between devices with their start and end apart: 28, of which 8 were waited for; matrix products, arithmetic and copies ran while one was open for 0% of the time, Pallas kernels for 18%

profile of v6, /device:TPU:0, one launch (start us, length us, event | category | flops | bytes accessed | tf_op | source)
XLA Modules:
  0.0 150.4 jit_solution(6777535969786790166)
XLA Ops:
  0.6 2.1 %shard_map.87 = (bf16[23,16,256]{2,1,0:T(8,128)(2,1)}, bf16[23,16,256]{2,1,0:T(8,128)(2,1)}, f32[64,256]{1,0:T(8,128)}, s32[3]{0:T(128)}) custom-call(s32[64,1,128]{2,1,0:T(1,128)} %bricks.1, f32[5,64,16,256]{3,2,1,0:T(8,128)} %innov_hi.1, f32[5,64,16,256]{3,2,1,0:T(8,128)} %innov_hi.1, f32[3,64,16,256]{3,2,1,0:T(8,128)} %cour_hi.1, ...), custom_call_target="tpu_custom_call" | custom-call | bytes 1048576 | tf_op jit(solution)/shard_map/pallas_call | solution.py:356
  2.8 3.1 %shard_map.100 = bf16[8,32,2048]{2,1,0:T(8,128)(2,1)} custom-call(s32[3]{0:T(128)} %get-tuple-element.91.place, bf16[1,8,32,4096]{3,2,1,0:T(8,128)(2,1)} %bitcast.16), custom_call_target="tpu_custom_call" | custom-call | bytes 2097152 | tf_op jit(solution)/shard_map/pallas_call | solution.py:541
  5.9 3.1 %collective-permute-start.12 = (bf16[8,32,2048]{2,1,0:T(8,128)(2,1)}, bf16[8,32,2048]{2,1,0:T(8,128)(2,1)S(1)}, u32[]{:S(2)}, u32[]{:S(2)}) collective-permute-start(bf16[8,32,2048]{2,1,0:T(8,128)(2,1)} %shard_map.100), channel_id=1, source_target_pairs={{0,1},{1,0},{2,3},{3,2},{4,5},{5,4},{6,7},{7,6},{8,9},{9,8},{10,11... | collective-permute-start | bytes 3145736 | tf_op jit(solution)/shard_map/ppermute | solution.py:37
  13.5 2.5 %shard_map.86 = (f32[5,64,16,256]{3,2,1,0:T(8,128)S(1)}, f32[3,64,16,256]{3,2,1,0:T(8,128)S(1)}, f32[64,16,256]{2,1,0:T(8,128)S(1)}) custom-call(f32[5,64,16,256]{3,2,1,0:T(8,128)} %innov_hi.1, f32[3,64,16,256]{3,2,1,0:T(8,128)S(1)} %copy-done.1, f32[64,16,256]{2,1,0:T(8,128)S(1)} %copy-done.3), custom_call_target="tpu_custom_call" | custom-call | bytes 18874368 | tf_op jit(solution)/shard_map/pallas_call | solution.py:541
  16.1 19.7 %collective-permute-done.before = bf16[23,16,256]{2,1,0:T(8,128)(2,1)S(1)} collective-permute-done((bf16[23,16,256]{2,1,0:T(8,128)(2,1)}, bf16[23,16,256]{2,1,0:T(8,128)(2,1)S(1)}, u32[]{:S(2)}, u32[]{:S(2)}) %collective-permute-start) | collective-permute-done | bytes 188448 | tf_op jit(solution)/shard_map/ppermute | solution.py:25
  37.0 2.6 %collective-permute-start.3 = (bf16[72,256]{1,0:T(8,128)(2,1)S(1)}, bf16[72,256]{1,0:T(8,128)(2,1)S(1)}, u32[]{:S(2)}, u32[]{:S(2)}) collective-permute-start(bf16[72,256]{1,0:T(8,128)(2,1)S(1)} %get-tuple-element.70), channel_id=1, source_target_pairs={{4,0},{8,4},{12,8},{16,12},{20,16},{24,20},{28,24},{0,28},{5,1},{9... | collective-permute-start | bytes 110600 | tf_op jit(solution)/shard_map/ppermute | solution.py:33
  46.5 2.0 %collective-permute-start.7 = (bf16[72,256]{1,0:T(8,128)(2,1)S(1)}, bf16[72,256]{1,0:T(8,128)(2,1)S(1)}, u32[]{:S(2)}, u32[]{:S(2)}) collective-permute-start(bf16[72,256]{1,0:T(8,128)(2,1)S(1)} %get-tuple-element.86), channel_id=1, source_target_pairs={{4,0},{8,4},{12,8},{16,12},{20,16},{24,20},{28,24},{0,28},{5,1},{9... | collective-permute-start | bytes 110600 | tf_op jit(solution)/shard_map/ppermute | solution.py:33
  50.9 2.0 %collective-permute-start.9 = (bf16[72,256]{1,0:T(8,128)(2,1)S(1)}, bf16[72,256]{1,0:T(8,128)(2,1)S(1)}, u32[]{:S(2)}, u32[]{:S(2)}) collective-permute-start(bf16[72,256]{1,0:T(8,128)(2,1)S(1)} %get-tuple-element.95), channel_id=1, source_target_pairs={{4,0},{8,4},{12,8},{16,12},{20,16},{24,20},{28,24},{0,28},{5,1},{9... | collective-permute-start | bytes 110600 | tf_op jit(solution)/shard_map/ppermute | solution.py:33
  56.1 2.8 %collective-permute-start.17 = (bf16[64,2048]{1,0:T(8,128)(2,1)S(1)}, bf16[64,2048]{1,0:T(8,128)(2,1)S(1)}, u32[]{:S(2)}, u32[]{:S(2)}) collective-permute-start(bf16[64,2048]{1,0:T(8,128)(2,1)S(1)} %get-tuple-element.102.first), channel_id=1, source_target_pairs={{0,2},{1,3},{2,0},{3,1},{4,6},{5,7},{6,4},{7,5},{8,10},{9,11},{10,... | collective-permute-start | bytes 786440 | tf_op jit(solution)/shard_map/ppermute | solution.py:37
  60.5 16.9 %collective-permute-done.17.first = bf16[64,2048]{1,0:T(8,128)(2,1)S(1)} collective-permute-done((bf16[64,2048]{1,0:T(8,128)(2,1)S(1)}, bf16[64,2048]{1,0:T(8,128)(2,1)S(1)}, u32[]{:S(2)}, u32[]{:S(2)}) %collective-permute-start.17) | collective-permute-done | bytes 262176 | tf_op jit(solution)/shard_map/ppermute | solution.py:37
  78.8 5.2 %collective-permute-start.19 = (bf16[2,256,128]{2,1,0:T(8,128)(2,1)S(1)}, bf16[2,256,128]{2,1,0:T(8,128)(2,1)S(1)}, u32[]{:S(2)}, u32[]{:S(2)}) collective-permute-start(bf16[2,256,128]{2,1,0:T(8,128)(2,1)S(1)} %get-tuple-element.111), channel_id=1, source_target_pairs={{0,1},{1,0},{2,3},{3,2},{4,5},{5,4},{6,7},{7,6},{8,9},{9,8},{10,11... | collective-permute-start | bytes 393224 | tf_op jit(solution)/shard_map/ppermute | solution.py:37
  85.8 2.0 %collective-permute-start.16 = (bf16[8,32,512]{2,1,0:T(8,128)(2,1)}, bf16[8,32,512]{2,1,0:T(8,128)(2,1)}, u32[]{:S(2)}, u32[]{:S(2)}) collective-permute-start(bf16[8,32,512]{2,1,0:T(8,128)(2,1)} %get-tuple-element.108), channel_id=1, source_target_pairs={{0,1},{1,0},{2,3},{3,2},{4,5},{5,4},{6,7},{7,6},{8,9},{9,8},{10,11... | collective-permute-start | bytes 786440 | tf_op jit(solution)/shard_map/ppermute | solution.py:37
  89.8 2.0 %shard_map.101 = (f32[2,256,128]{2,1,0:T(8,128)S(1)}, bf16[2,256,128]{2,1,0:T(8,128)(2,1)}) custom-call(s32[3]{0:T(128)S(1)} %copy-done.7, bf16[256,4096]{1,0:T(8,128)(2,1)S(1)} %bitcast.18, bf16[256,2048]{1,0:T(8,128)(2,1)S(1)} %bitcast.20, bf16[64,2048]{1,0:T(8,128)(2,1)S(1)} %get-tuple-element.102.first, bf16[64,2048]{1,0:T(8,128)(2,1)S(1)} %collective-permute-done.13.second), custom_call_target="tpu_custom_call" | custom-call | flops 268435456 | bytes 3145728 | tf_op jit(solution)/shard_map/pallas_call | solution.py:541
  93.8 3.4 %all-to-all-start.1 = ((bf16[8,2,32,128]{3,2,1,0:T(8,128)(2,1)}), bf16[8,2,32,128]{3,2,1,0:T(8,128)(2,1)S(1)}, u32[]{:S(2)}, u32[]{:S(2)}) async-start(bf16[8,2,32,128]{3,2,1,0:T(8,128)(2,1)} %shard_map.106), calls=%async_computation.1 | async-start | bytes 262144 | tf_op jit(solution)/shard_map/all_to_all | solution.py:633
  97.2 16.4 %collective-permute-done.14.arrived = bf16[2,256,128]{2,1,0:T(8,128)(2,1)S(1)} collective-permute-done((bf16[2,256,128]{2,1,0:T(8,128)(2,1)}, bf16[2,256,128]{2,1,0:T(8,128)(2,1)S(1)}, u32[]{:S(2)}, u32[]{:S(2)}) %collective-permute-start.14) | collective-permute-done | bytes 131104 | tf_op jit(solution)/shard_map/ppermute | solution.py:37
  115.8 3.4 %all-to-all-start = ((bf16[8,2,32,128]{3,2,1,0:T(8,128)(2,1)}), bf16[8,2,32,128]{3,2,1,0:T(8,128)(2,1)S(1)}, u32[]{:S(2)}, u32[]{:S(2)}) async-start(bf16[8,2,32,128]{3,2,1,0:T(8,128)(2,1)} %copy-done.4), calls=%async_computation | async-start | bytes 262144 | tf_op jit(solution)/shard_map/all_to_all | solution.py:633
  119.2 2.0 %shard_map.108 = (bf16[64,1024]{1,0:T(8,128)(2,1)S(1)}, bf16[64,1024]{1,0:T(8,128)(2,1)}) custom-call(s32[3]{0:T(128)S(1)} %copy-done.7, bf16[256,4096]{1,0:T(8,128)(2,1)S(1)} %bitcast.12, bf16[256,512]{1,0:T(8,128)(2,1)} %bitcast.8.rest_0_, bf16[256,512]{1,0:T(8,128)(2,1)} %bitcast.9.rest_1_, bf16[8,2,32,128]{3,2,1,0:T(8,128)(2,1)S(1)} %all-to-all-done.1.rest_2_), custom_call_target="tpu_custom_call" | custom-call | flops 134217728 | bytes 2097152 | tf_op jit(solution)/shard_map/pallas_call | solution.py:541
  121.9 3.4 %collective-permute-start.25 = (bf16[64,1024]{1,0:T(8,128)(2,1)}, bf16[64,1024]{1,0:T(8,128)(2,1)}, u32[]{:S(2)}, u32[]{:S(2)}) collective-permute-start(bf16[64,1024]{1,0:T(8,128)(2,1)} %get-tuple-element.117), channel_id=1, source_target_pairs={{0,3},{1,2},{2,1},{3,0},{4,7},{5,6},{6,5},{7,4},{8,11},{9,10},{10,... | collective-permute-start | bytes 393224 | tf_op jit(solution)/shard_map/ppermute | solution.py:37
  125.3 2.0 %shard_map.107 = (bf16[64,1024]{1,0:T(8,128)(2,1)S(1)}, bf16[64,1024]{1,0:T(8,128)(2,1)}) custom-call(s32[3]{0:T(128)S(1)} %copy-done.7, bf16[256,4096]{1,0:T(8,128)(2,1)S(1)} %bitcast.13, bf16[256,512]{1,0:T(8,128)(2,1)} %bitcast.2.rest_0_, bf16[256,512]{1,0:T(8,128)(2,1)} %bitcast.3.rest_1_, bf16[8,2,32,128]{3,2,1,0:T(8,128)(2,1)S(1)} %all-to-all-done.1.rest_2_), custom_call_target="tpu_custom_call" | custom-call | flops 134217728 | bytes 2097152 | tf_op jit(solution)/shard_map/pallas_call | solution.py:541
  131.3 2.1 %collective-permute-start.22 = (bf16[64,1024]{1,0:T(8,128)(2,1)S(1)}, bf16[64,1024]{1,0:T(8,128)(2,1)S(1)}, u32[]{:S(2)}, u32[]{:S(2)}) collective-permute-start(bf16[64,1024]{1,0:T(8,128)(2,1)S(1)} %get-tuple-element.114), channel_id=1, source_target_pairs={{0,1},{1,0},{2,3},{3,2},{4,5},{5,4},{6,7},{7,6},{8,9},{9,8},{10,11... | collective-permute-start | bytes 393224 | tf_op jit(solution)/shard_map/ppermute | solution.py:37
  133.4 2.0 %collective-permute-start.21 = (bf16[64,1024]{1,0:T(8,128)(2,1)S(1)}, bf16[64,1024]{1,0:T(8,128)(2,1)S(1)}, u32[]{:S(2)}, u32[]{:S(2)}) collective-permute-start(bf16[64,1024]{1,0:T(8,128)(2,1)S(1)} %copy-done.15), channel_id=1, source_target_pairs={{0,2},{1,3},{2,0},{3,1},{4,6},{5,7},{6,4},{7,5},{8,10},{9,11},{10,... | collective-permute-start | bytes 393224 | tf_op jit(solution)/shard_map/ppermute | solution.py:37
  138.4 3.4 %collective-permute-done.23.rest_1_ = bf16[64,1024]{1,0:T(8,128)(2,1)S(1)} collective-permute-done((bf16[64,1024]{1,0:T(8,128)(2,1)S(1)}, bf16[64,1024]{1,0:T(8,128)(2,1)S(1)}, u32[]{:S(2)}, u32[]{:S(2)}) %collective-permute-start.23) | collective-permute-done | bytes 131104 | tf_op jit(solution)/shard_map/ppermute | solution.py:37
  141.8 2.6 %collective-permute-done.22.rest_0_ = bf16[64,1024]{1,0:T(8,128)(2,1)S(1)} collective-permute-done((bf16[64,1024]{1,0:T(8,128)(2,1)S(1)}, bf16[64,1024]{1,0:T(8,128)(2,1)S(1)}, u32[]{:S(2)}, u32[]{:S(2)}) %collective-permute-start.22) | collective-permute-done | bytes 131104 | tf_op jit(solution)/shard_map/ppermute | solution.py:37
  146.3 2.6 %collective-permute-done.20.rest_2_ = bf16[64,1024]{1,0:T(8,128)(2,1)S(1)} collective-permute-done((bf16[64,1024]{1,0:T(8,128)(2,1)S(1)}, bf16[64,1024]{1,0:T(8,128)(2,1)S(1)}, u32[]{:S(2)}, u32[]{:S(2)}) %collective-permute-start.20) | collective-permute-done | bytes 131104 | tf_op jit(solution)/shard_map/ppermute | solution.py:37
  (93 shorter events, 39.8 us)
Async XLA Ops:
  5.9 71.5 %collective-permute-start.12 = (bf16[8,32,2048]{2,1,0:T(8,128)(2,1)}, bf16[8,32,2048]{2,1,0:T(8,128)(2,1)S(1)}, u32[]{:S(2)}, u32[]{:S(2)}) collective-permute-start(bf16[8,32,2048]{2,1,0:T(8,128)(2,1)} %shard_map.100), channel_id=1, source_target_pairs={{0,1},{1,0},{2,3},{3,2},{4,5},{5,4},{6,7},{7,6},{8,9},{9,8},{10,11... | collective-permute-start | bytes 3145736 | tf_op jit(solution)/shard_map/ppermute | solution.py:37
  9.1 26.8 %collective-permute-start = (bf16[23,16,256]{2,1,0:T(8,128)(2,1)}, bf16[23,16,256]{2,1,0:T(8,128)(2,1)S(1)}, u32[]{:S(2)}, u32[]{:S(2)}) collective-permute-start(bf16[23,16,256]{2,1,0:T(8,128)(2,1)} %get-tuple-element.64), channel_id=1, source_target_pairs={{0,1},{1,2},{2,3},{4,5},{5,6},{6,7},{8,9},{9,10},{10,11},{12,13},{... | collective-permute-start | bytes 565256 | tf_op jit(solution)/shard_map/ppermute | solution.py:25
  11.0 25.5 %collective-permute-start.1 = (bf16[23,16,256]{2,1,0:T(8,128)(2,1)}, bf16[23,16,256]{2,1,0:T(8,128)(2,1)S(1)}, u32[]{:S(2)}, u32[]{:S(2)}) collective-permute-start(bf16[23,16,256]{2,1,0:T(8,128)(2,1)} %get-tuple-element.65), channel_id=1, source_target_pairs={{1,0},{2,1},{3,2},{5,4},{6,5},{7,6},{9,8},{10,9},{11,10},{13,12},{... | collective-permute-start | bytes 565256 | tf_op jit(solution)/shard_map/ppermute | solution.py:25
  36.9 4.3 %collective-permute-start.2 = (bf16[72,256]{1,0:T(8,128)(2,1)S(1)}, bf16[72,256]{1,0:T(8,128)(2,1)S(1)}, u32[]{:S(2)}, u32[]{:S(2)}) collective-permute-start(bf16[72,256]{1,0:T(8,128)(2,1)S(1)} %get-tuple-element.69), channel_id=1, source_target_pairs={{28,0},{0,4},{4,8},{8,12},{12,16},{16,20},{20,24},{24,28},{29,1},{... | collective-permute-start | bytes 110600 | tf_op jit(solution)/shard_map/ppermute | solution.py:33
  41.3 4.4 %collective-permute-start.4 = (bf16[72,256]{1,0:T(8,128)(2,1)S(1)}, bf16[72,256]{1,0:T(8,128)(2,1)S(1)}, u32[]{:S(2)}, u32[]{:S(2)}) collective-permute-start(bf16[72,256]{1,0:T(8,128)(2,1)S(1)} %get-tuple-element.78), channel_id=1, source_target_pairs={{28,0},{0,4},{4,8},{8,12},{12,16},{16,20},{20,24},{24,28},{29,1},{... | collective-permute-start | bytes 110600 | tf_op jit(solution)/shard_map/ppermute | solution.py:33
  50.2 5.3 %collective-permute-start.8 = (bf16[72,256]{1,0:T(8,128)(2,1)S(1)}, bf16[72,256]{1,0:T(8,128)(2,1)S(1)}, u32[]{:S(2)}, u32[]{:S(2)}) collective-permute-start(bf16[72,256]{1,0:T(8,128)(2,1)S(1)} %get-tuple-element.94), channel_id=1, source_target_pairs={{28,0},{0,4},{4,8},{8,12},{12,16},{16,20},{20,24},{24,28},{29,1},{... | collective-permute-start | bytes 110600 | tf_op jit(solution)/shard_map/ppermute | solution.py:33
  50.9 4.6 %collective-permute-start.9 = (bf16[72,256]{1,0:T(8,128)(2,1)S(1)}, bf16[72,256]{1,0:T(8,128)(2,1)S(1)}, u32[]{:S(2)}, u32[]{:S(2)}) collective-permute-start(bf16[72,256]{1,0:T(8,128)(2,1)S(1)} %get-tuple-element.95), channel_id=1, source_target_pairs={{4,0},{8,4},{12,8},{16,12},{20,16},{24,20},{28,24},{0,28},{5,1},{9... | collective-permute-start | bytes 110600 | tf_op jit(solution)/shard_map/ppermute | solution.py:33
  56.1 21.3 %collective-permute-start.17 = (bf16[64,2048]{1,0:T(8,128)(2,1)S(1)}, bf16[64,2048]{1,0:T(8,128)(2,1)S(1)}, u32[]{:S(2)}, u32[]{:S(2)}) collective-permute-start(bf16[64,2048]{1,0:T(8,128)(2,1)S(1)} %get-tuple-element.102.first), channel_id=1, source_target_pairs={{0,2},{1,3},{2,0},{3,1},{4,6},{5,7},{6,4},{7,5},{8,10},{9,11},{10,... | collective-permute-start | bytes 786440 | tf_op jit(solution)/shard_map/ppermute | solution.py:37
  58.9 18.5 %collective-permute-start.18 = (bf16[64,2048]{1,0:T(8,128)(2,1)S(1)}, bf16[64,2048]{1,0:T(8,128)(2,1)S(1)}, u32[]{:S(2)}, u32[]{:S(2)}) collective-permute-start(bf16[64,2048]{1,0:T(8,128)(2,1)S(1)} %get-tuple-element.103), channel_id=1, source_target_pairs={{0,3},{1,2},{2,1},{3,0},{4,7},{5,6},{6,5},{7,4},{8,11},{9,10},{10,... | collective-permute-start | bytes 786440 | tf_op jit(solution)/shard_map/ppermute | solution.py:37
  60.3 27.6 %collective-permute-start.13 = (bf16[64,2048]{1,0:T(8,128)(2,1)S(1)}, bf16[64,2048]{1,0:T(8,128)(2,1)S(1)}, u32[]{:S(2)}, u32[]{:S(2)}) collective-permute-start(bf16[64,2048]{1,0:T(8,128)(2,1)S(1)} %get-tuple-element.103), channel_id=1, source_target_pairs={{0,1},{1,0},{2,3},{3,2},{4,5},{5,4},{6,7},{7,6},{8,9},{9,8},{10,11... | collective-permute-start | bytes 786440 | tf_op jit(solution)/shard_map/ppermute | solution.py:37
  78.8 13.7 %collective-permute-start.19 = (bf16[2,256,128]{2,1,0:T(8,128)(2,1)S(1)}, bf16[2,256,128]{2,1,0:T(8,128)(2,1)S(1)}, u32[]{:S(2)}, u32[]{:S(2)}) collective-permute-start(bf16[2,256,128]{2,1,0:T(8,128)(2,1)S(1)} %get-tuple-element.111), channel_id=1, source_target_pairs={{0,1},{1,0},{2,3},{3,2},{4,5},{5,4},{6,7},{7,6},{8,9},{9,8},{10,11... | collective-permute-start | bytes 393224 | tf_op jit(solution)/shard_map/ppermute | solution.py:37
  85.7 33.5 %collective-permute-start.15 = (bf16[8,32,512]{2,1,0:T(8,128)(2,1)}, bf16[8,32,512]{2,1,0:T(8,128)(2,1)}, u32[]{:S(2)}, u32[]{:S(2)}) collective-permute-start(bf16[8,32,512]{2,1,0:T(8,128)(2,1)} %get-tuple-element.107), channel_id=1, source_target_pairs={{0,1},{1,0},{2,3},{3,2},{4,5},{5,4},{6,7},{7,6},{8,9},{9,8},{10,11... | collective-permute-start | bytes 786440 | tf_op jit(solution)/shard_map/ppermute | solution.py:37
  85.8 33.4 %collective-permute-start.16 = (bf16[8,32,512]{2,1,0:T(8,128)(2,1)}, bf16[8,32,512]{2,1,0:T(8,128)(2,1)}, u32[]{:S(2)}, u32[]{:S(2)}) collective-permute-start(bf16[8,32,512]{2,1,0:T(8,128)(2,1)} %get-tuple-element.108), channel_id=1, source_target_pairs={{0,1},{1,0},{2,3},{3,2},{4,5},{5,4},{6,7},{7,6},{8,9},{9,8},{10,11... | collective-permute-start | bytes 786440 | tf_op jit(solution)/shard_map/ppermute | solution.py:37
  87.8 37.5 %collective-permute-start.10 = (bf16[8,32,512]{2,1,0:T(8,128)(2,1)}, bf16[8,32,512]{2,1,0:T(8,128)(2,1)}, u32[]{:S(2)}, u32[]{:S(2)}) collective-permute-start(bf16[8,32,512]{2,1,0:T(8,128)(2,1)} %get-tuple-element.100), channel_id=1, source_target_pairs={{0,1},{1,0},{2,3},{3,2},{4,5},{5,4},{6,7},{7,6},{8,9},{9,8},{10,11... | collective-permute-start | bytes 786440 | tf_op jit(solution)/shard_map/ppermute | solution.py:37
  87.9 37.4 %collective-permute-start.11 = (bf16[8,32,512]{2,1,0:T(8,128)(2,1)}, bf16[8,32,512]{2,1,0:T(8,128)(2,1)}, u32[]{:S(2)}, u32[]{:S(2)}) collective-permute-start(bf16[8,32,512]{2,1,0:T(8,128)(2,1)} %get-tuple-element.101), channel_id=1, source_target_pairs={{0,1},{1,0},{2,3},{3,2},{4,5},{5,4},{6,7},{7,6},{8,9},{9,8},{10,11... | collective-permute-start | bytes 786440 | tf_op jit(solution)/shard_map/ppermute | solution.py:37
  92.5 21.1 %collective-permute-start.14 = (bf16[2,256,128]{2,1,0:T(8,128)(2,1)}, bf16[2,256,128]{2,1,0:T(8,128)(2,1)S(1)}, u32[]{:S(2)}, u32[]{:S(2)}) collective-permute-start(bf16[2,256,128]{2,1,0:T(8,128)(2,1)} %get-tuple-element.105), channel_id=1, source_target_pairs={{0,1},{1,0},{2,3},{3,2},{4,5},{5,4},{6,7},{7,6},{8,9},{9,8},{10,11... | collective-permute-start | bytes 393224 | tf_op jit(solution)/shard_map/ppermute | solution.py:37
  93.8 22.0 %all-to-all-start.1 = ((bf16[8,2,32,128]{3,2,1,0:T(8,128)(2,1)}), bf16[8,2,32,128]{3,2,1,0:T(8,128)(2,1)S(1)}, u32[]{:S(2)}, u32[]{:S(2)}) async-start(bf16[8,2,32,128]{3,2,1,0:T(8,128)(2,1)} %shard_map.106), calls=%async_computation.1 | async-start | bytes 262144 | tf_op jit(solution)/shard_map/all_to_all | solution.py:633
  115.8 12.6 %all-to-all-start = ((bf16[8,2,32,128]{3,2,1,0:T(8,128)(2,1)}), bf16[8,2,32,128]{3,2,1,0:T(8,128)(2,1)S(1)}, u32[]{:S(2)}, u32[]{:S(2)}) async-start(bf16[8,2,32,128]{3,2,1,0:T(8,128)(2,1)} %copy-done.4), calls=%async_computation | async-start | bytes 262144 | tf_op jit(solution)/shard_map/all_to_all | solution.py:633
  121.9 13.5 %collective-permute-start.25 = (bf16[64,1024]{1,0:T(8,128)(2,1)}, bf16[64,1024]{1,0:T(8,128)(2,1)}, u32[]{:S(2)}, u32[]{:S(2)}) collective-permute-start(bf16[64,1024]{1,0:T(8,128)(2,1)} %get-tuple-element.117), channel_id=1, source_target_pairs={{0,3},{1,2},{2,1},{3,0},{4,7},{5,6},{6,5},{7,4},{8,11},{9,10},{10,... | collective-permute-start | bytes 393224 | tf_op jit(solution)/shard_map/ppermute | solution.py:37
  128.0 10.4 %collective-permute-start.24 = (bf16[64,1024]{1,0:T(8,128)(2,1)}, bf16[64,1024]{1,0:T(8,128)(2,1)S(1)}, u32[]{:S(2)}, u32[]{:S(2)}) collective-permute-start(bf16[64,1024]{1,0:T(8,128)(2,1)} %get-tuple-element.116), channel_id=1, source_target_pairs={{0,3},{1,2},{2,1},{3,0},{4,7},{5,6},{6,5},{7,4},{8,11},{9,10},{10,... | collective-permute-start | bytes 393224 | tf_op jit(solution)/shard_map/ppermute | solution.py:37
  129.8 12.0 %collective-permute-start.23 = (bf16[64,1024]{1,0:T(8,128)(2,1)S(1)}, bf16[64,1024]{1,0:T(8,128)(2,1)S(1)}, u32[]{:S(2)}, u32[]{:S(2)}) collective-permute-start(bf16[64,1024]{1,0:T(8,128)(2,1)S(1)} %get-tuple-element.115), channel_id=1, source_target_pairs={{0,1},{1,0},{2,3},{3,2},{4,5},{5,4},{6,7},{7,6},{8,9},{9,8},{10,11... | collective-permute-start | bytes 393224 | tf_op jit(solution)/shard_map/ppermute | solution.py:37
  131.3 13.1 %collective-permute-start.22 = (bf16[64,1024]{1,0:T(8,128)(2,1)S(1)}, bf16[64,1024]{1,0:T(8,128)(2,1)S(1)}, u32[]{:S(2)}, u32[]{:S(2)}) collective-permute-start(bf16[64,1024]{1,0:T(8,128)(2,1)S(1)} %get-tuple-element.114), channel_id=1, source_target_pairs={{0,1},{1,0},{2,3},{3,2},{4,5},{5,4},{6,7},{7,6},{8,9},{9,8},{10,11... | collective-permute-start | bytes 393224 | tf_op jit(solution)/shard_map/ppermute | solution.py:37
  133.4 12.9 %collective-permute-start.21 = (bf16[64,1024]{1,0:T(8,128)(2,1)S(1)}, bf16[64,1024]{1,0:T(8,128)(2,1)S(1)}, u32[]{:S(2)}, u32[]{:S(2)}) collective-permute-start(bf16[64,1024]{1,0:T(8,128)(2,1)S(1)} %copy-done.15), channel_id=1, source_target_pairs={{0,2},{1,3},{2,0},{3,1},{4,6},{5,7},{6,4},{7,5},{8,10},{9,11},{10,... | collective-permute-start | bytes 393224 | tf_op jit(solution)/shard_map/ppermute | solution.py:37
  135.4 13.5 %collective-permute-start.20 = (bf16[64,1024]{1,0:T(8,128)(2,1)S(1)}, bf16[64,1024]{1,0:T(8,128)(2,1)S(1)}, u32[]{:S(2)}, u32[]{:S(2)}) collective-permute-start(bf16[64,1024]{1,0:T(8,128)(2,1)S(1)} %copy-done.17), channel_id=1, source_target_pairs={{0,2},{1,3},{2,0},{3,1},{4,6},{5,7},{6,4},{7,5},{8,10},{9,11},{10,... | collective-permute-start | bytes 393224 | tf_op jit(solution)/shard_map/ppermute | solution.py:37
  (22 other events, 203.2 us)

commit v7 on v5

--- a/solution.py
+++ b/solution.py
@@ -10,6 +10,7 @@
 LANES = 128
 PARTS = 4
 LOAD_GRANT = 40 << 20
+WIDE_GRANT = 60 << 20
 STAGES = 2
 LANE_TILES = 2
 HALVES = 2
@@ -54,14 +55,9 @@
     return ref[pl.ds(at, 1), :]
 
 
-def pack_kernel(table, axes, bricks, innov_lo, innov_hi, cour_lo, cour_hi, diff_lo, diff_hi, left, down, up, sea, place, left_other, rows, vmem, sems):
+def pack_kernel(table, axes, bricks, innov_lo, innov_hi, cour_lo, cour_hi, diff_lo, diff_hi, down, up, sea, place, rows):
     me = lax.axis_index(axes[1])
-    side = lax.rem(me, 2)
-    place[0], place[1], place[2] = me, side, lax.axis_index(axes[0])
-    half = left_other.shape[2]
-    window = pl.ds(pl.multiple_of((1 - side) * half, half), half)
-    load = pltpu.make_async_copy(left.at[0, :, :, window], vmem, sems.at[0])
-    load.start()
+    place[0], place[1], place[2] = me, lax.rem(me, 2), lax.axis_index(axes[0])
     depth = diff_lo.shape[0]
     levels, _, count = bricks.shape
     lat_cells = sea.shape[1]
@@ -100,11 +96,7 @@
             out[at] = value.astype(jnp.bfloat16)
 
     fill(down, innov_hi, cour_hi, diff_hi, sea_hi, lambda d: depth - d, -1.0)
-    load.wait()
-    store = pltpu.make_async_copy(vmem, left_other, sems.at[1])
-    store.start()
     fill(up, innov_lo, cour_lo, diff_lo, sea_lo, lambda d: d - 1, 1.0)
-    store.wait()
 
 
 def load_kernel(*refs):
@@ -348,7 +340,7 @@
     to_east[...] = (east_gain[...] * high_rows).astype(jnp.bfloat16)
 
 
-def pack(innovations, courant, diffusivity, bricks, left):
+def pack(innovations, courant, diffusivity, bricks):
     levels, lon_cells, lat_cells = diffusivity.shape
     steps = innovations.shape[0] - 1
     table, layers = halo_table(steps)
@@ -362,31 +354,25 @@
         return [pl.BlockSpec(tuple(block), at(index)) for index in (0, end)]
 
     message = jax.ShapeDtypeStruct((layers, lon_cells, lat_cells), bf16)
-    _, slots, width, cols = left.shape
-    other = jax.ShapeDtypeStruct((slots, width, cols // 2), bf16)
     return pl.pallas_call(
         functools.partial(pack_kernel, table, ("lon", "depth")),
         grid=(1,),
         in_specs=[VMEM]
         + edges(innovations.shape, 1)
         + edges(courant.shape, 1)
-        + edges(diffusivity.shape, 0)
-        + [ANY],
+        + edges(diffusivity.shape, 0),
         out_shape=[
             message,
             message,
             jax.ShapeDtypeStruct((levels, lat_cells), f32),
             jax.ShapeDtypeStruct((3,), jnp.int32),
-            other,
         ],
-        out_specs=[VMEM, VMEM, VMEM, SMEM, ANY],
+        out_specs=[VMEM, VMEM, VMEM, SMEM],
         scratch_shapes=[
             pltpu.VMEM((levels, bricks.shape[2]), f32),
-            pltpu.VMEM((slots, width, cols // 2), bf16),
-            pltpu.SemaphoreType.DMA((2,)),
         ],
         cost_estimate=pl.CostEstimate(flops=0, bytes_accessed=1 << 20, transcendentals=0),
-    )(bricks, innovations, innovations, courant, courant, diffusivity, diffusivity, left)
+    )(bricks, innovations, innovations, courant, courant, diffusivity, diffusivity)
 
 
 def sweep(inputs, sea, before, after, place):
@@ -528,30 +514,45 @@
         out[1][:, lanes] = total[levels:].astype(out[1].dtype)
 
 
-def join_kernel(flip, place, *rest):
-    ones, twos = rest[:HALVES], rest[HALVES : 2 * HALVES]
-    out, slab, sem, *rows = rest[-(3 + LANE_TILES) :]
-    levels, half, lat_cells = slab.shape
+def add_rows(place, own, arrived1, arrived2, arrived3, rows):
+    levels = own.shape[0]
+    each = rows[0].shape[0] // levels // 2
     f32 = jnp.float32
-    each = half // HALVES
-    for x in range(half):
+    wide = own.shape[1] // each
+    for x in range(each):
         for c, lanes in enumerate(rows):
-            at = (x % each) * lat_cells + c * LANES
-            cols = slice(at, at + LANES)
-            value = ones[x // each][:, cols].astype(f32) + twos[x // each][:, cols].astype(f32)
-            lanes[pl.ds(x, levels, stride=half), :] = value
-    side = 1 - place[1] if flip else place[1]
-    start = pl.multiple_of(side * half, half)
+            cols = slice(x * wide + c * LANES, x * wide + (c + 1) * LANES)
+            mine = own[:, cols] + arrived2[:, cols].astype(f32)
+            other = arrived1[:, cols].astype(f32) + arrived3[:, cols].astype(f32)
+            lanes[pl.ds(place[1] * each + x, levels, stride=2 * each), :] = mine
+            lanes[pl.ds((1 - place[1]) * each + x, levels, stride=2 * each), :] = other
+
+
+def early_kernel(place, own, arrived1, arrived2, arrived3, *rows):
+    add_rows(place, own, arrived1, arrived2, arrived3, rows)
+
+
+def join_kernel(place, own, arrived1, arrived2, arrived3, *rest):
+    early = rest[:LANE_TILES]
+    out, slab, sem, *rows = rest[LANE_TILES:]
+    add_rows(place, own, arrived1, arrived2, arrived3, rows)
+    levels, lon_cells, _ = slab.shape
+    half = lon_cells // 2
+    each = half // 2
+    lower = lax.broadcasted_iota(jnp.int32, (half, LANES), 0) < each
     parts = 4
     size = levels // parts
     copies = []
     for part in range(parts):
         for z in range(part * size, (part + 1) * size):
-            for c, lanes in enumerate(rows):
-                slab[z, :, c * LANES : (c + 1) * LANES] = lanes[z * half : (z + 1) * half, :]
+            for c in range(LANE_TILES):
+                a = early[c][z * half : (z + 1) * half, :]
+                b = rows[c][z * half : (z + 1) * half, :]
+                lanes = slice(c * LANES, (c + 1) * LANES)
+                slab[z, :half, lanes] = jnp.where(lower, a, pltpu.roll(b, each, 0))
+                slab[z, half:, lanes] = jnp.where(lower, pltpu.roll(a, each, 0), b)
         here = pl.ds(part * size, size)
-        target = out.at[here, pl.ds(start, half)]
-        copies.append(pltpu.make_async_copy(slab.at[here], target, sem.at[part]))
+        copies.append(pltpu.make_async_copy(slab.at[here], out.at[here], sem.at[part]))
         copies[-1].start()
     for copy in copies:
         copy.wait()
@@ -585,7 +586,16 @@
     width = left.shape[2]
     rows = slots * width
 
-    down, up, sea, place, left_other = pack(innovations, courant, diffusivity, sea_bricks, left)
+    down, up, sea, place = pack(innovations, courant, diffusivity, sea_bricks)
+    (left_other,) = call(
+        halves_kernel,
+        (place, left),
+        [SMEM, ANY],
+        [((slots, width, half), bf16, ANY)],
+        grant=WIDE_GRANT,
+        moved=2 << 20,
+        scratch=[pltpu.VMEM((1, slots, width, half), bf16), pltpu.SemaphoreType.DMA((2,))],
+    )
     before = from_behind(down, "depth", 1)
     after = from_behind(up, "depth", -1)
     inputs = (innovations, courant, diffusivity)
@@ -657,27 +667,23 @@
             if stage:
                 first = swapped(first, "depth", stage)
             arrived[stage].append(first)
-    scratch = [
-        pltpu.VMEM((levels, lon_cells // 2, lat_cells), f32),
-        pltpu.SemaphoreType.DMA((4,)),
-    ] + [pltpu.VMEM((levels * lon_cells // 2, LANES), f32)] * LANE_TILES
-    whole = [((levels, lon_cells, lat_cells), f32, ANY)]
+    rows_of = (levels * lon_cells // 2, LANES)
+    pieces = [[arrived[mask][part] for mask in range(count)] for part in range(HALVES)]
+    early = call(
+        early_kernel,
+        (place, *pieces[0]),
+        [SMEM] + [VMEM] * count,
+        [(rows_of, f32)] * LANE_TILES,
+        moved=2 << 20,
+    )
     (gradient,) = call(
-        functools.partial(join_kernel, True),
-        (place, *arrived[1], *arrived[3]),
-        [SMEM] + [VMEM] * (2 * HALVES),
-        whole,
-        scratch=scratch,
-        moved=2 << 20,
-    )
-    (gradient,) = call(
-        functools.partial(join_kernel, False),
-        (place, *arrived[0], *arrived[2], gradient),
-        [SMEM] + [VMEM] * (2 * HALVES) + [ANY],
-        whole,
-        scratch=scratch,
-        moved=2 << 20,
-        aliases={1 + 2 * HALVES: 0},
+        join_kernel,
+        (place, *pieces[1], *early),
+        [SMEM] + [VMEM] * (count + LANE_TILES),
+        [((levels, lon_cells, lat_cells), f32, ANY)],
+        scratch=[pltpu.VMEM((levels, lon_cells, lat_cells), f32), pltpu.SemaphoreType.DMA((4,))]
+        + [pltpu.VMEM(rows_of, f32)] * LANE_TILES,
+        moved=3 << 20,
     )
     return (lam, gradient)
 

time: 137 us -> 136 us (level)
  local copies, waits for them, and re-layouts: 1.97 us -> 4.6 us
  waiting for transfers between devices: 56.7 us -> 54.5 us
  starting transfers between devices: 47.3 us -> 45.6 us
    unnamed x28, local copies, waits for them, and re-layouts: 1.97 us -> 4.6 us
    pallas_call x14 -> x15, Pallas kernels: 18.6 us -> 21.1 us  [call(): pl.pallas_call(kernel, in_specs=in_specs, out_shape=[jax.ShapeDtypeStruct...]
    pallas_call x1, Pallas kernels: 4.35 us -> 2.14 us  [pack(): pl.pallas_call(functools.partial(pack_kernel, table, ('lon', 'depth')), g...]
    ppermute x16, waiting for transfers between devices: 35.7 us -> 34 us  [swapped(): lax.ppermute(block, axis, [(i, i ^ mask) for i in range(lax.axis_size(axi...]
    ppermute x16, starting transfers between devices: 29.7 us -> 28 us  [swapped(): lax.ppermute(block, axis, [(i, i ^ mask) for i in range(lax.axis_size(axi...]
  transfers between devices with their start and end apart: 27 -> 27, of which waited for: 16 -> 11; matrix products, arithmetic and copies ran while one was open for 0% -> 0% of each run, Pallas kernels for 17% -> 17%
where the time goes in v7:
time: 136 us
  waiting for transfers between devices  54.5 us (40%)
  starting transfers between devices  45.6 us (34%)
  Pallas kernels  30 us (22%)
  local copies, waits for them, and re-layouts  4.6 us (3%)
    ppermute x16, waiting for transfers between devices, swapped(): lax.ppermute(block, axis, [(i, i ^ mask) for i in range(lax.axis_size(axi...  34 us
    ppermute x16, starting transfers between devices, swapped(): lax.ppermute(block, axis, [(i, i ^ mask) for i in range(lax.axis_size(axi...  28 us
    pallas_call x15, Pallas kernels, call(): pl.pallas_call(kernel, in_specs=in_specs, out_shape=[jax.ShapeDtypeStruct...  21.1 us
    ppermute x2, waiting for transfers between devices, from_behind(): lax.ppermute(value, axis, [(source, source + steps) for source in range(i...  20.4 us
    ppermute x8, starting transfers between devices, shifted(): return lax.ppermute(block, axis, route)  11 us
    pallas_call x4, Pallas kernels, sweep(): pl.pallas_call(functools.partial(step_kernel, table, step), in_specs=[VME...  6.27 us
    unnamed x28, local copies, waits for them, and re-layouts  4.6 us
    all_to_all x1, starting transfers between devices, per_device(): received = [lax.all_to_all(coeff[0], 'lon', 0, 0, tiled=True)]  3.41 us
  transfers between devices with their start and end apart: 27, of which 11 were waited for; matrix products, arithmetic and copies ran while one was open for 0% of the time, Pallas kernels for 17%

profile of v7, /device:TPU:0, one launch (start us, length us, event | category | flops | bytes accessed | tf_op | source)
XLA Modules:
  0.0 135.7 jit_solution(3004491468341577072)
XLA Ops:
  0.6 2.1 %shard_map.87 = (bf16[23,16,256]{2,1,0:T(8,128)(2,1)}, bf16[23,16,256]{2,1,0:T(8,128)(2,1)}, f32[64,256]{1,0:T(8,128)}, s32[3]{0:T(128)}) custom-call(s32[64,1,128]{2,1,0:T(1,128)} %bricks.1, f32[5,64,16,256]{3,2,1,0:T(8,128)} %innov_hi.1, f32[5,64,16,256]{3,2,1,0:T(8,128)} %innov_hi.1, f32[3,64,16,256]{3,2,1,0:T(8,128)} %cour_hi.1, ...), custom_call_target="tpu_custom_call" | custom-call | bytes 1048576 | tf_op jit(solution)/shard_map/pallas_call | solution.py:357
  2.8 3.1 %shard_map.100 = bf16[8,32,2048]{2,1,0:T(8,128)(2,1)} custom-call(s32[3]{0:T(128)} %get-tuple-element.93.place, bf16[1,8,32,4096]{3,2,1,0:T(8,128)(2,1)} %bitcast.16), custom_call_target="tpu_custom_call" | custom-call | bytes 2097152 | tf_op jit(solution)/shard_map/pallas_call | solution.py:562
  5.9 3.1 %collective-permute-start.12 = (bf16[8,32,2048]{2,1,0:T(8,128)(2,1)}, bf16[8,32,2048]{2,1,0:T(8,128)(2,1)S(1)}, u32[]{:S(2)}, u32[]{:S(2)}) collective-permute-start(bf16[8,32,2048]{2,1,0:T(8,128)(2,1)} %shard_map.100), channel_id=1, source_target_pairs={{0,1},{1,0},{2,3},{3,2},{4,5},{5,4},{6,7},{7,6},{8,9},{9,8},{10,11... | collective-permute-start | bytes 3145736 | tf_op jit(solution)/shard_map/ppermute | solution.py:38
  9.1 1.9 %collective-permute-start = (bf16[23,16,256]{2,1,0:T(8,128)(2,1)}, bf16[23,16,256]{2,1,0:T(8,128)(2,1)S(1)}, u32[]{:S(2)}, u32[]{:S(2)}) collective-permute-start(bf16[23,16,256]{2,1,0:T(8,128)(2,1)} %get-tuple-element.66), channel_id=1, source_target_pairs={{0,1},{1,2},{2,3},{4,5},{5,6},{6,7},{8,9},{9,10},{10,11},{12,13},{... | collective-permute-start | bytes 565256 | tf_op jit(solution)/shard_map/ppermute | solution.py:26
  13.5 2.5 %shard_map.86 = (f32[5,64,16,256]{3,2,1,0:T(8,128)S(1)}, f32[3,64,16,256]{3,2,1,0:T(8,128)S(1)}, f32[64,16,256]{2,1,0:T(8,128)S(1)}) custom-call(f32[5,64,16,256]{3,2,1,0:T(8,128)} %innov_hi.1, f32[3,64,16,256]{3,2,1,0:T(8,128)S(1)} %copy-done.1, f32[64,16,256]{2,1,0:T(8,128)S(1)} %copy-done.3), custom_call_target="tpu_custom_call" | custom-call | bytes 18874368 | tf_op jit(solution)/shard_map/pallas_call | solution.py:562
  16.1 19.7 %collective-permute-done.before = bf16[23,16,256]{2,1,0:T(8,128)(2,1)S(1)} collective-permute-done((bf16[23,16,256]{2,1,0:T(8,128)(2,1)}, bf16[23,16,256]{2,1,0:T(8,128)(2,1)S(1)}, u32[]{:S(2)}, u32[]{:S(2)}) %collective-permute-start) | collective-permute-done | bytes 188448 | tf_op jit(solution)/shard_map/ppermute | solution.py:26
  37.0 2.6 %collective-permute-start.3 = (bf16[72,256]{1,0:T(8,128)(2,1)S(1)}, bf16[72,256]{1,0:T(8,128)(2,1)S(1)}, u32[]{:S(2)}, u32[]{:S(2)}) collective-permute-start(bf16[72,256]{1,0:T(8,128)(2,1)S(1)} %get-tuple-element.72), channel_id=1, source_target_pairs={{4,0},{8,4},{12,8},{16,12},{20,16},{24,20},{28,24},{0,28},{5,1},{9... | collective-permute-start | bytes 110600 | tf_op jit(solution)/shard_map/ppermute | solution.py:34
  42.2 1.8 %collective-permute-start.5 = (bf16[72,256]{1,0:T(8,128)(2,1)S(1)}, bf16[72,256]{1,0:T(8,128)(2,1)S(1)}, u32[]{:S(2)}, u32[]{:S(2)}) collective-permute-start(bf16[72,256]{1,0:T(8,128)(2,1)S(1)} %get-tuple-element.81), channel_id=1, source_target_pairs={{4,0},{8,4},{12,8},{16,12},{20,16},{24,20},{28,24},{0,28},{5,1},{9... | collective-permute-start | bytes 110600 | tf_op jit(solution)/shard_map/ppermute | solution.py:34
  44.1 1.6 %shard_map.91 = (f32[72,16,256]{2,1,0:T(8,128)S(1)}, f32[72,256]{1,0:T(8,128)S(1)}, f32[72,256]{1,0:T(8,128)S(1)}) custom-call(f32[5,64,16,256]{3,2,1,0:T(8,128)S(1)} %get-tuple-element.62.innov, f32[3,64,16,256]{3,2,1,0:T(8,128)S(1)} %get-tuple-element.63.cour, f32[64,16,256]{2,1,0:T(8,128)S(1)} %get-tuple-element.64.diff, ...), custom_call_target="tpu_custom_call" | custom-call | flops 10485760 | bytes 9437184 | tf_op jit(solution)/shard_map/pallas_call | solution.py:402
  46.5 2.0 %collective-permute-start.7 = (bf16[72,256]{1,0:T(8,128)(2,1)S(1)}, bf16[72,256]{1,0:T(8,128)(2,1)S(1)}, u32[]{:S(2)}, u32[]{:S(2)}) collective-permute-start(bf16[72,256]{1,0:T(8,128)(2,1)S(1)} %get-tuple-element.88), channel_id=1, source_target_pairs={{4,0},{8,4},{12,8},{16,12},{20,16},{24,20},{28,24},{0,28},{5,1},{9... | collective-permute-start | bytes 110600 | tf_op jit(solution)/shard_map/ppermute | solution.py:34
  50.9 2.0 %collective-permute-start.9 = (bf16[72,256]{1,0:T(8,128)(2,1)S(1)}, bf16[72,256]{1,0:T(8,128)(2,1)S(1)}, u32[]{:S(2)}, u32[]{:S(2)}) collective-permute-start(bf16[72,256]{1,0:T(8,128)(2,1)S(1)} %get-tuple-element.97), channel_id=1, source_target_pairs={{4,0},{8,4},{12,8},{16,12},{20,16},{24,20},{28,24},{0,28},{5,1},{9... | collective-permute-start | bytes 110600 | tf_op jit(solution)/shard_map/ppermute | solution.py:34
  57.3 2.8 %collective-permute-start.15 = (bf16[64,2048]{1,0:T(8,128)(2,1)S(1)}, bf16[64,2048]{1,0:T(8,128)(2,1)S(1)}, u32[]{:S(2)}, u32[]{:S(2)}) collective-permute-start(bf16[64,2048]{1,0:T(8,128)(2,1)S(1)} %get-tuple-element.104.first), channel_id=1, source_target_pairs={{0,2},{1,3},{2,0},{3,1},{4,6},{5,7},{6,4},{7,5},{8,10},{9,11},{10,... | collective-permute-start | bytes 786440 | tf_op jit(solution)/shard_map/ppermute | solution.py:38
  61.7 16.9 %collective-permute-done.15.first = bf16[64,2048]{1,0:T(8,128)(2,1)S(1)} collective-permute-done((bf16[64,2048]{1,0:T(8,128)(2,1)S(1)}, bf16[64,2048]{1,0:T(8,128)(2,1)S(1)}, u32[]{:S(2)}, u32[]{:S(2)}) %collective-permute-start.15) | collective-permute-done | bytes 262176 | tf_op jit(solution)/shard_map/ppermute | solution.py:38
  79.9 5.2 %collective-permute-start.17 = (bf16[2,256,128]{2,1,0:T(8,128)(2,1)S(1)}, bf16[2,256,128]{2,1,0:T(8,128)(2,1)S(1)}, u32[]{:S(2)}, u32[]{:S(2)}) collective-permute-start(bf16[2,256,128]{2,1,0:T(8,128)(2,1)S(1)} %get-tuple-element.109), channel_id=1, source_target_pairs={{0,1},{1,0},{2,3},{3,2},{4,5},{5,4},{6,7},{7,6},{8,9},{9,8},{10,11... | collective-permute-start | bytes 393224 | tf_op jit(solution)/shard_map/ppermute | solution.py:38
  89.5 2.0 %collective-permute-start.22 = (bf16[8,32,512]{2,1,0:T(8,128)(2,1)}, bf16[8,32,512]{2,1,0:T(8,128)(2,1)}, u32[]{:S(2)}, u32[]{:S(2)}) collective-permute-start(bf16[8,32,512]{2,1,0:T(8,128)(2,1)} %get-tuple-element.115), channel_id=1, source_target_pairs={{0,1},{1,0},{2,3},{3,2},{4,5},{5,4},{6,7},{7,6},{8,9},{9,8},{10,11... | collective-permute-start | bytes 786440 | tf_op jit(solution)/shard_map/ppermute | solution.py:38
  93.0 3.4 %all-to-all-start = ((bf16[8,2,32,256]{3,2,1,0:T(8,128)(2,1)}), bf16[8,2,32,256]{3,2,1,0:T(8,128)(2,1)S(1)}, u32[]{:S(2)}, u32[]{:S(2)}) async-start(bf16[8,2,32,256]{3,2,1,0:T(8,128)(2,1)} %copy-done.4), calls=%async_computation | async-start | bytes 524288 | tf_op jit(solution)/shard_map/all_to_all | solution.py:650
  96.4 1.9 %collective-permute-start.10 = (bf16[8,32,512]{2,1,0:T(8,128)(2,1)}, bf16[8,32,512]{2,1,0:T(8,128)(2,1)}, u32[]{:S(2)}, u32[]{:S(2)}) collective-permute-start(bf16[8,32,512]{2,1,0:T(8,128)(2,1)} %copy-done.13), channel_id=1, source_target_pairs={{0,1},{1,0},{2,3},{3,2},{4,5},{5,4},{6,7},{7,6},{8,9},{9,8},{10,11... | collective-permute-start | bytes 786440 | tf_op jit(solution)/shard_map/ppermute | solution.py:38
  99.0 5.6 %collective-permute-done.21 = bf16[8,32,512]{2,1,0:T(8,128)(2,1)} collective-permute-done((bf16[8,32,512]{2,1,0:T(8,128)(2,1)}, bf16[8,32,512]{2,1,0:T(8,128)(2,1)}, u32[]{:S(2)}, u32[]{:S(2)}) %collective-permute-start.21) | collective-permute-done | bytes 262176 | tf_op jit(solution)/shard_map/ppermute | solution.py:38
  106.0 4.0 %collective-permute-start.24 = (bf16[64,1024]{1,0:T(8,128)(2,1)S(1)}, bf16[64,1024]{1,0:T(8,128)(2,1)S(1)}, u32[]{:S(2)}, u32[]{:S(2)}) collective-permute-start(bf16[64,1024]{1,0:T(8,128)(2,1)S(1)} %get-tuple-element.118), channel_id=1, source_target_pairs={{0,2},{1,3},{2,0},{3,1},{4,6},{5,7},{6,4},{7,5},{8,10},{9,11},{10,... | collective-permute-start | bytes 393224 | tf_op jit(solution)/shard_map/ppermute | solution.py:38
  112.1 6.6 %collective-permute-done.11 = bf16[8,32,512]{2,1,0:T(8,128)(2,1)} collective-permute-done((bf16[8,32,512]{2,1,0:T(8,128)(2,1)}, bf16[8,32,512]{2,1,0:T(8,128)(2,1)}, u32[]{:S(2)}, u32[]{:S(2)}) %collective-permute-start.11) | collective-permute-done | bytes 262176 | tf_op jit(solution)/shard_map/ppermute | solution.py:38
  120.1 3.4 %collective-permute-start.19 = (bf16[64,1024]{1,0:T(8,128)(2,1)S(1)}, bf16[64,1024]{1,0:T(8,128)(2,1)S(1)}, u32[]{:S(2)}, u32[]{:S(2)}) collective-permute-start(bf16[64,1024]{1,0:T(8,128)(2,1)S(1)} %get-tuple-element.112), channel_id=1, source_target_pairs={{0,2},{1,3},{2,0},{3,1},{4,6},{5,7},{6,4},{7,5},{8,10},{9,11},{10,... | collective-permute-start | bytes 393224 | tf_op jit(solution)/shard_map/ppermute | solution.py:38
  123.5 2.5 %collective-permute-start.20 = (bf16[64,1024]{1,0:T(8,128)(2,1)S(1)}, bf16[64,1024]{1,0:T(8,128)(2,1)S(1)}, u32[]{:S(2)}, u32[]{:S(2)}) collective-permute-start(bf16[64,1024]{1,0:T(8,128)(2,1)S(1)} %get-tuple-element.113), channel_id=1, source_target_pairs={{0,3},{1,2},{2,1},{3,0},{4,7},{5,6},{6,5},{7,4},{8,11},{9,10},{10,... | collective-permute-start | bytes 393224 | tf_op jit(solution)/shard_map/ppermute | solution.py:38
  129.8 3.1 %collective-permute-done.19.arrived2 = bf16[64,1024]{1,0:T(8,128)(2,1)S(1)} collective-permute-done((bf16[64,1024]{1,0:T(8,128)(2,1)S(1)}, bf16[64,1024]{1,0:T(8,128)(2,1)S(1)}, u32[]{:S(2)}, u32[]{:S(2)}) %collective-permute-start.19) | collective-permute-done | bytes 131104 | tf_op jit(solution)/shard_map/ppermute | solution.py:38
  134.0 1.7 %shard_map.109 = f32[64,16,256]{2,1,0:T(8,128)} custom-call(s32[3]{0:T(128)S(1)} %copy-done.5, f32[64,1024]{1,0:T(8,128)S(1)} %get-tuple-element.110.own, bf16[64,1024]{1,0:T(8,128)(2,1)S(1)} %collective-permute-done.18.arrived1, bf16[64,1024]{1,0:T(8,128)(2,1)S(1)} %collective-permute-done.19.arrived2, ...), custom_call_target="tpu_custom_call" | custom-call | bytes 3145728 | tf_op jit(solution)/shard_map/pallas_call | solution.py:562
  (82 shorter events, 32.8 us)
Async XLA Ops:
  5.9 72.6 %collective-permute-start.12 = (bf16[8,32,2048]{2,1,0:T(8,128)(2,1)}, bf16[8,32,2048]{2,1,0:T(8,128)(2,1)S(1)}, u32[]{:S(2)}, u32[]{:S(2)}) collective-permute-start(bf16[8,32,2048]{2,1,0:T(8,128)(2,1)} %shard_map.100), channel_id=1, source_target_pairs={{0,1},{1,0},{2,3},{3,2},{4,5},{5,4},{6,7},{7,6},{8,9},{9,8},{10,11... | collective-permute-start | bytes 3145736 | tf_op jit(solution)/shard_map/ppermute | solution.py:38
  9.1 26.8 %collective-permute-start = (bf16[23,16,256]{2,1,0:T(8,128)(2,1)}, bf16[23,16,256]{2,1,0:T(8,128)(2,1)S(1)}, u32[]{:S(2)}, u32[]{:S(2)}) collective-permute-start(bf16[23,16,256]{2,1,0:T(8,128)(2,1)} %get-tuple-element.66), channel_id=1, source_target_pairs={{0,1},{1,2},{2,3},{4,5},{5,6},{6,7},{8,9},{9,10},{10,11},{12,13},{... | collective-permute-start | bytes 565256 | tf_op jit(solution)/shard_map/ppermute | solution.py:26
  11.0 25.5 %collective-permute-start.1 = (bf16[23,16,256]{2,1,0:T(8,128)(2,1)}, bf16[23,16,256]{2,1,0:T(8,128)(2,1)S(1)}, u32[]{:S(2)}, u32[]{:S(2)}) collective-permute-start(bf16[23,16,256]{2,1,0:T(8,128)(2,1)} %get-tuple-element.67), channel_id=1, source_target_pairs={{1,0},{2,1},{3,2},{5,4},{6,5},{7,6},{9,8},{10,9},{11,10},{13,12},{... | collective-permute-start | bytes 565256 | tf_op jit(solution)/shard_map/ppermute | solution.py:26
  36.9 4.3 %collective-permute-start.2 = (bf16[72,256]{1,0:T(8,128)(2,1)S(1)}, bf16[72,256]{1,0:T(8,128)(2,1)S(1)}, u32[]{:S(2)}, u32[]{:S(2)}) collective-permute-start(bf16[72,256]{1,0:T(8,128)(2,1)S(1)} %get-tuple-element.71), channel_id=1, source_target_pairs={{28,0},{0,4},{4,8},{8,12},{12,16},{16,20},{20,24},{24,28},{29,1},{... | collective-permute-start | bytes 110600 | tf_op jit(solution)/shard_map/ppermute | solution.py:34
  41.3 4.4 %collective-permute-start.4 = (bf16[72,256]{1,0:T(8,128)(2,1)S(1)}, bf16[72,256]{1,0:T(8,128)(2,1)S(1)}, u32[]{:S(2)}, u32[]{:S(2)}) collective-permute-start(bf16[72,256]{1,0:T(8,128)(2,1)S(1)} %get-tuple-element.80), channel_id=1, source_target_pairs={{28,0},{0,4},{4,8},{8,12},{12,16},{16,20},{20,24},{24,28},{29,1},{... | collective-permute-start | bytes 110600 | tf_op jit(solution)/shard_map/ppermute | solution.py:34
  45.8 4.3 %collective-permute-start.6 = (bf16[72,256]{1,0:T(8,128)(2,1)S(1)}, bf16[72,256]{1,0:T(8,128)(2,1)S(1)}, u32[]{:S(2)}, u32[]{:S(2)}) collective-permute-start(bf16[72,256]{1,0:T(8,128)(2,1)S(1)} %get-tuple-element.87), channel_id=1, source_target_pairs={{28,0},{0,4},{4,8},{8,12},{12,16},{16,20},{20,24},{24,28},{29,1},{... | collective-permute-start | bytes 110600 | tf_op jit(solution)/shard_map/ppermute | solution.py:34
  50.2 5.3 %collective-permute-start.8 = (bf16[72,256]{1,0:T(8,128)(2,1)S(1)}, bf16[72,256]{1,0:T(8,128)(2,1)S(1)}, u32[]{:S(2)}, u32[]{:S(2)}) collective-permute-start(bf16[72,256]{1,0:T(8,128)(2,1)S(1)} %get-tuple-element.96), channel_id=1, source_target_pairs={{28,0},{0,4},{4,8},{8,12},{12,16},{16,20},{20,24},{24,28},{29,1},{... | collective-permute-start | bytes 110600 | tf_op jit(solution)/shard_map/ppermute | solution.py:34
  50.9 4.6 %collective-permute-start.9 = (bf16[72,256]{1,0:T(8,128)(2,1)S(1)}, bf16[72,256]{1,0:T(8,128)(2,1)S(1)}, u32[]{:S(2)}, u32[]{:S(2)}) collective-permute-start(bf16[72,256]{1,0:T(8,128)(2,1)S(1)} %get-tuple-element.97), channel_id=1, source_target_pairs={{4,0},{8,4},{12,8},{16,12},{20,16},{24,20},{28,24},{0,28},{5,1},{9... | collective-permute-start | bytes 110600 | tf_op jit(solution)/shard_map/ppermute | solution.py:34
  57.3 21.2 %collective-permute-start.15 = (bf16[64,2048]{1,0:T(8,128)(2,1)S(1)}, bf16[64,2048]{1,0:T(8,128)(2,1)S(1)}, u32[]{:S(2)}, u32[]{:S(2)}) collective-permute-start(bf16[64,2048]{1,0:T(8,128)(2,1)S(1)} %get-tuple-element.104.first), channel_id=1, source_target_pairs={{0,2},{1,3},{2,0},{3,1},{4,6},{5,7},{6,4},{7,5},{8,10},{9,11},{10,... | collective-permute-start | bytes 786440 | tf_op jit(solution)/shard_map/ppermute | solution.py:38
  60.1 18.5 %collective-permute-start.16 = (bf16[64,2048]{1,0:T(8,128)(2,1)S(1)}, bf16[64,2048]{1,0:T(8,128)(2,1)S(1)}, u32[]{:S(2)}, u32[]{:S(2)}) collective-permute-start(bf16[64,2048]{1,0:T(8,128)(2,1)S(1)} %get-tuple-element.105), channel_id=1, source_target_pairs={{0,3},{1,2},{2,1},{3,0},{4,7},{5,6},{6,5},{7,4},{8,11},{9,10},{10,... | collective-permute-start | bytes 786440 | tf_op jit(solution)/shard_map/ppermute | solution.py:38
  61.5 23.7 %collective-permute-start.13 = (bf16[64,2048]{1,0:T(8,128)(2,1)S(1)}, bf16[64,2048]{1,0:T(8,128)(2,1)S(1)}, u32[]{:S(2)}, u32[]{:S(2)}) collective-permute-start(bf16[64,2048]{1,0:T(8,128)(2,1)S(1)} %get-tuple-element.105), channel_id=1, source_target_pairs={{0,1},{1,0},{2,3},{3,2},{4,5},{5,4},{6,7},{7,6},{8,9},{9,8},{10,11... | collective-permute-start | bytes 786440 | tf_op jit(solution)/shard_map/ppermute | solution.py:38
  79.9 11.6 %collective-permute-start.17 = (bf16[2,256,128]{2,1,0:T(8,128)(2,1)S(1)}, bf16[2,256,128]{2,1,0:T(8,128)(2,1)S(1)}, u32[]{:S(2)}, u32[]{:S(2)}) collective-permute-start(bf16[2,256,128]{2,1,0:T(8,128)(2,1)S(1)} %get-tuple-element.109), channel_id=1, source_target_pairs={{0,1},{1,0},{2,3},{3,2},{4,5},{5,4},{6,7},{7,6},{8,9},{9,8},{10,11... | collective-permute-start | bytes 393224 | tf_op jit(solution)/shard_map/ppermute | solution.py:38
  86.5 5.2 %collective-permute-start.14 = (bf16[2,256,128]{2,1,0:T(8,128)(2,1)S(1)}, bf16[2,256,128]{2,1,0:T(8,128)(2,1)S(1)}, u32[]{:S(2)}, u32[]{:S(2)}) collective-permute-start(bf16[2,256,128]{2,1,0:T(8,128)(2,1)S(1)} %get-tuple-element.107), channel_id=1, source_target_pairs={{0,1},{1,0},{2,3},{3,2},{4,5},{5,4},{6,7},{7,6},{8,9},{9,8},{10,11... | collective-permute-start | bytes 393224 | tf_op jit(solution)/shard_map/ppermute | solution.py:38
  89.5 9.5 %collective-permute-start.22 = (bf16[8,32,512]{2,1,0:T(8,128)(2,1)}, bf16[8,32,512]{2,1,0:T(8,128)(2,1)}, u32[]{:S(2)}, u32[]{:S(2)}) collective-permute-start(bf16[8,32,512]{2,1,0:T(8,128)(2,1)} %get-tuple-element.115), channel_id=1, source_target_pairs={{0,1},{1,0},{2,3},{3,2},{4,5},{5,4},{6,7},{7,6},{8,9},{9,8},{10,11... | collective-permute-start | bytes 786440 | tf_op jit(solution)/shard_map/ppermute | solution.py:38
  91.5 13.1 %collective-permute-start.21 = (bf16[8,32,512]{2,1,0:T(8,128)(2,1)}, bf16[8,32,512]{2,1,0:T(8,128)(2,1)}, u32[]{:S(2)}, u32[]{:S(2)}) collective-permute-start(bf16[8,32,512]{2,1,0:T(8,128)(2,1)} %get-tuple-element.114), channel_id=1, source_target_pairs={{0,1},{1,0},{2,3},{3,2},{4,5},{5,4},{6,7},{7,6},{8,9},{9,8},{10,11... | collective-permute-start | bytes 786440 | tf_op jit(solution)/shard_map/ppermute | solution.py:38
  93.0 11.6 %all-to-all-start = ((bf16[8,2,32,256]{3,2,1,0:T(8,128)(2,1)}), bf16[8,2,32,256]{3,2,1,0:T(8,128)(2,1)S(1)}, u32[]{:S(2)}, u32[]{:S(2)}) async-start(bf16[8,2,32,256]{3,2,1,0:T(8,128)(2,1)} %copy-done.4), calls=%async_computation | async-start | bytes 524288 | tf_op jit(solution)/shard_map/all_to_all | solution.py:650
  96.4 15.6 %collective-permute-start.10 = (bf16[8,32,512]{2,1,0:T(8,128)(2,1)}, bf16[8,32,512]{2,1,0:T(8,128)(2,1)}, u32[]{:S(2)}, u32[]{:S(2)}) collective-permute-start(bf16[8,32,512]{2,1,0:T(8,128)(2,1)} %copy-done.13), channel_id=1, source_target_pairs={{0,1},{1,0},{2,3},{3,2},{4,5},{5,4},{6,7},{7,6},{8,9},{9,8},{10,11... | collective-permute-start | bytes 786440 | tf_op jit(solution)/shard_map/ppermute | solution.py:38
  98.4 20.3 %collective-permute-start.11 = (bf16[8,32,512]{2,1,0:T(8,128)(2,1)}, bf16[8,32,512]{2,1,0:T(8,128)(2,1)}, u32[]{:S(2)}, u32[]{:S(2)}) collective-permute-start(bf16[8,32,512]{2,1,0:T(8,128)(2,1)} %copy-done.12), channel_id=1, source_target_pairs={{0,1},{1,0},{2,3},{3,2},{4,5},{5,4},{6,7},{7,6},{8,9},{9,8},{10,11... | collective-permute-start | bytes 786440 | tf_op jit(solution)/shard_map/ppermute | solution.py:38
  106.0 21.4 %collective-permute-start.24 = (bf16[64,1024]{1,0:T(8,128)(2,1)S(1)}, bf16[64,1024]{1,0:T(8,128)(2,1)S(1)}, u32[]{:S(2)}, u32[]{:S(2)}) collective-permute-start(bf16[64,1024]{1,0:T(8,128)(2,1)S(1)} %get-tuple-element.118), channel_id=1, source_target_pairs={{0,2},{1,3},{2,0},{3,1},{4,6},{5,7},{6,4},{7,5},{8,10},{9,11},{10,... | collective-permute-start | bytes 393224 | tf_op jit(solution)/shard_map/ppermute | solution.py:38
  110.0 19.1 %collective-permute-start.25 = (bf16[64,1024]{1,0:T(8,128)(2,1)S(1)}, bf16[64,1024]{1,0:T(8,128)(2,1)S(1)}, u32[]{:S(2)}, u32[]{:S(2)}) collective-permute-start(bf16[64,1024]{1,0:T(8,128)(2,1)S(1)} %get-tuple-element.119), channel_id=1, source_target_pairs={{0,3},{1,2},{2,1},{3,0},{4,7},{5,6},{6,5},{7,4},{8,11},{9,10},{10,... | collective-permute-start | bytes 393224 | tf_op jit(solution)/shard_map/ppermute | solution.py:38
  111.8 17.3 %collective-permute-start.23 = (bf16[64,1024]{1,0:T(8,128)(2,1)S(1)}, bf16[64,1024]{1,0:T(8,128)(2,1)S(1)}, u32[]{:S(2)}, u32[]{:S(2)}) collective-permute-start(bf16[64,1024]{1,0:T(8,128)(2,1)S(1)} %get-tuple-element.117), channel_id=1, source_target_pairs={{0,1},{1,0},{2,3},{3,2},{4,5},{5,4},{6,7},{7,6},{8,9},{9,8},{10,11... | collective-permute-start | bytes 393224 | tf_op jit(solution)/shard_map/ppermute | solution.py:38
  120.1 12.9 %collective-permute-start.19 = (bf16[64,1024]{1,0:T(8,128)(2,1)S(1)}, bf16[64,1024]{1,0:T(8,128)(2,1)S(1)}, u32[]{:S(2)}, u32[]{:S(2)}) collective-permute-start(bf16[64,1024]{1,0:T(8,128)(2,1)S(1)} %get-tuple-element.112), channel_id=1, source_target_pairs={{0,2},{1,3},{2,0},{3,1},{4,6},{5,7},{6,4},{7,5},{8,10},{9,11},{10,... | collective-permute-start | bytes 393224 | tf_op jit(solution)/shard_map/ppermute | solution.py:38
  123.5 9.6 %collective-permute-start.20 = (bf16[64,1024]{1,0:T(8,128)(2,1)S(1)}, bf16[64,1024]{1,0:T(8,128)(2,1)S(1)}, u32[]{:S(2)}, u32[]{:S(2)}) collective-permute-start(bf16[64,1024]{1,0:T(8,128)(2,1)S(1)} %get-tuple-element.113), channel_id=1, source_target_pairs={{0,3},{1,2},{2,1},{3,0},{4,7},{5,6},{6,5},{7,4},{8,11},{9,10},{10,... | collective-permute-start | bytes 393224 | tf_op jit(solution)/shard_map/ppermute | solution.py:38
  127.4 6.7 %collective-permute-start.18 = (bf16[64,1024]{1,0:T(8,128)(2,1)S(1)}, bf16[64,1024]{1,0:T(8,128)(2,1)S(1)}, u32[]{:S(2)}, u32[]{:S(2)}) collective-permute-start(bf16[64,1024]{1,0:T(8,128)(2,1)S(1)} %get-tuple-element.111), channel_id=1, source_target_pairs={{0,1},{1,0},{2,3},{3,2},{4,5},{5,4},{6,7},{7,6},{8,9},{9,8},{10,11... | collective-permute-start | bytes 393224 | tf_op jit(solution)/shard_map/ppermute | solution.py:38
  (17 other events, 109.8 us)

commit v8 on v7

--- a/solution.py
+++ b/solution.py
@@ -55,9 +55,7 @@
     return ref[pl.ds(at, 1), :]
 
 
-def pack_kernel(table, axes, bricks, innov_lo, innov_hi, cour_lo, cour_hi, diff_lo, diff_hi, down, up, sea, place, rows):
-    me = lax.axis_index(axes[1])
-    place[0], place[1], place[2] = me, lax.rem(me, 2), lax.axis_index(axes[0])
+def pack_kernel(table, bricks, innov_lo, innov_hi, cour_lo, cour_hi, diff_lo, diff_hi, down, up, sea, rows):
     depth = diff_lo.shape[0]
     levels, _, count = bricks.shape
     lat_cells = sea.shape[1]
@@ -355,7 +353,7 @@
 
     message = jax.ShapeDtypeStruct((layers, lon_cells, lat_cells), bf16)
     return pl.pallas_call(
-        functools.partial(pack_kernel, table, ("lon", "depth")),
+        functools.partial(pack_kernel, table),
         grid=(1,),
         in_specs=[VMEM]
         + edges(innovations.shape, 1)
@@ -365,9 +363,8 @@
             message,
             message,
             jax.ShapeDtypeStruct((levels, lat_cells), f32),
-            jax.ShapeDtypeStruct((3,), jnp.int32),
         ],
-        out_specs=[VMEM, VMEM, VMEM, SMEM],
+        out_specs=[VMEM, VMEM, VMEM],
         scratch_shapes=[
             pltpu.VMEM((levels, bricks.shape[2]), f32),
         ],
@@ -433,7 +430,7 @@
         (place, *edge, mine, other),
         [SMEM] + [VMEM] * 7,
         [(half, bf16)] * 2 + [(extended, f32)] * 2,
-        aliases={6: 0, 7: 1},
+        aliases={5: 0, 6: 1},
     )
     (lam,) = call(
         emit_kernel,
@@ -478,7 +475,7 @@
                 [kept[c, at, :] + arrived[c, at, :].astype(jnp.float32) for kept, arrived in stages], 1
             )
             row = lax.broadcasted_iota(jnp.int32, value.shape, 0) + owner * rows
-            value = jnp.where(row < ranks[0, k], value, 0.0).astype(jnp.bfloat16)
+            value = jnp.where(row < ranks[:1, k : k + 1], value, 0.0).astype(jnp.bfloat16)
             if len(out) > 1:
                 out[k][c] = value
             else:
@@ -558,7 +555,20 @@
         copy.wait()
 
 
+HERE = object()
+
+
+def located(kernel):
+    def run(*refs):
+        me = lax.axis_index("depth")
+        return kernel((me, lax.rem(me, 2), lax.axis_index("lon")), *refs)
+
+    return run
+
+
 def call(kernel, operands, in_specs, outs, grant=GRANT, flops=0, moved=1 << 20, scratch=(), aliases=None):
+    if operands[0] is HERE:
+        kernel, operands, in_specs = located(kernel), operands[1:], in_specs[1:]
     return pl.pallas_call(
         kernel,
         in_specs=in_specs,
@@ -586,7 +596,8 @@
     width = left.shape[2]
     rows = slots * width
 
-    down, up, sea, place = pack(innovations, courant, diffusivity, sea_bricks)
+    down, up, sea = pack(innovations, courant, diffusivity, sea_bricks)
+    place = HERE
     (left_other,) = call(
         halves_kernel,
         (place, left),
@@ -638,12 +649,12 @@
             moved=3 << 20,
         )
         sums += [kept, swapped(sent, "depth", 1)]
-    grouped = lon_count == slots
+    grouped = False
     slot = (2, width, count * levels)
     coeff = call(
         functools.partial(mask_kernel, slots),
         (place, tile_ranks, *sums),
-        [SMEM, SMEM] + [VMEM] * len(sums),
+        [SMEM, VMEM] + [VMEM] * len(sums),
         [((lon_count,) + slot, bf16)] if grouped else [(slot, bf16)] * slots,
     )
     if grouped:

time: 136 us -> 130 us (0.956)
  Pallas kernels: 30 us -> 22.1 us
  waiting for transfers between devices: 54.5 us -> 59.8 us
  local copies, waits for them, and re-layouts: 4.6 us -> 1.24 us
    pallas_call x15, Pallas kernels: 21.1 us -> 13.3 us  [call(): pl.pallas_call(kernel, in_specs=in_specs, out_shape=[jax.ShapeDtypeStruct...]
    ppermute x8 -> x15, waiting for transfers between devices: 0.15 us -> 5.95 us  [shifted(): return lax.ppermute(block, axis, route)]
    ppermute x8 -> x15, starting transfers between devices: 11 us -> 16.6 us  [shifted(): return lax.ppermute(block, axis, route)]
    all_to_all x1 -> x0, starting transfers between devices: 3.41 us -> none  [per_device(): received = [lax.all_to_all(coeff[0], 'lon', 0, 0, tiled=True)]]
    unnamed x28 -> x12, local copies, waits for them, and re-layouts: 4.6 us -> 1.24 us
    ppermute x16, starting transfers between devices: 28 us -> 25.4 us  [swapped(): lax.ppermute(block, axis, [(i, i ^ mask) for i in range(lax.axis_size(axi...]
    ppermute x2, waiting for transfers between devices: 20.4 us -> 18.1 us  [from_behind(): lax.ppermute(value, axis, [(source, source + steps) for source in range(i...]
    ppermute x16, waiting for transfers between devices: 34 us -> 35.7 us  [swapped(): lax.ppermute(block, axis, [(i, i ^ mask) for i in range(lax.axis_size(axi...]
  transfers between devices with their start and end apart: 27 -> 33, of which waited for: 11 -> 18; matrix products, arithmetic and copies ran while one was open for 0% -> 0% of each run, Pallas kernels for 17% -> 15%
where the time goes in v8:
time: 130 us; the launch traced here: 129 us
  waiting for transfers between devices  59.8 us (46%)
  starting transfers between devices  45.2 us (35%)
  Pallas kernels  22.1 us (17%)
    ppermute x16, waiting for transfers between devices, swapped(): lax.ppermute(block, axis, [(i, i ^ mask) for i in range(lax.axis_size(axi...  35.7 us
    ppermute x16, starting transfers between devices, swapped(): lax.ppermute(block, axis, [(i, i ^ mask) for i in range(lax.axis_size(axi...  25.4 us
    ppermute x2, waiting for transfers between devices, from_behind(): lax.ppermute(value, axis, [(source, source + steps) for source in range(i...  18.1 us
    ppermute x15, starting transfers between devices, shifted(): return lax.ppermute(block, axis, route)  16.6 us
    pallas_call x15, Pallas kernels, call(): pl.pallas_call(kernel, in_specs=in_specs, out_shape=[jax.ShapeDtypeStruct...  13.3 us
    pallas_call x4, Pallas kernels, sweep(): pl.pallas_call(functools.partial(step_kernel, table, step), in_specs=[VME...  5.99 us
    ppermute x15, waiting for transfers between devices, shifted(): return lax.ppermute(block, axis, route)  5.95 us
    ppermute x2, starting transfers between devices, from_behind(): lax.ppermute(value, axis, [(source, source + steps) for source in range(i...  3.23 us
  transfers between devices with their start and end apart: 33, of which 18 were waited for; matrix products, arithmetic and copies ran while one was open for 0% of the time, Pallas kernels for 15%

profile of v8, /device:TPU:0, one launch (start us, length us, event | category | flops | bytes accessed | tf_op | source)
XLA Modules:
  0.0 129.3 jit_solution(15256328435431093526)
XLA Ops:
  0.6 2.2 %shard_map.100 = bf16[8,32,2048]{2,1,0:T(8,128)(2,1)} custom-call(bf16[1,8,32,4096]{3,2,1,0:T(8,128)(2,1)} %bitcast.16), custom_call_target="tpu_custom_call" | custom-call | bytes 2097152 | tf_op jit(solution)/shard_map/pallas_call | solution.py:572
  2.9 3.1 %collective-permute-start.12 = (bf16[8,32,2048]{2,1,0:T(8,128)(2,1)}, bf16[8,32,2048]{2,1,0:T(8,128)(2,1)}, u32[]{:S(2)}, u32[]{:S(2)}) collective-permute-start(bf16[8,32,2048]{2,1,0:T(8,128)(2,1)} %shard_map.100), channel_id=1, source_target_pairs={{0,1},{1,0},{2,3},{3,2},{4,5},{5,4},{6,7},{7,6},{8,9},{9,8},{10,11... | collective-permute-start | bytes 3145736 | tf_op jit(solution)/shard_map/ppermute | solution.py:38
  6.0 2.3 %shard_map.87 = (bf16[23,16,256]{2,1,0:T(8,128)(2,1)}, bf16[23,16,256]{2,1,0:T(8,128)(2,1)}, f32[64,256]{1,0:T(8,128)}) custom-call(s32[64,1,128]{2,1,0:T(1,128)} %bricks.1, f32[5,64,16,256]{3,2,1,0:T(8,128)} %innov_hi.1, f32[5,64,16,256]{3,2,1,0:T(8,128)} %innov_hi.1, f32[3,64,16,256]{3,2,1,0:T(8,128)} %cour_hi.1, f32[3,64,16,256]{3,2,1,0:T(8,128)} %cour_hi.1, ...), custom_call_target="tpu_custom_call" | custom-call | bytes 1048576 | tf_op jit(solution)/shard_map/pallas_call | solution.py:355
  8.2 1.9 %collective-permute-start = (bf16[23,16,256]{2,1,0:T(8,128)(2,1)}, bf16[23,16,256]{2,1,0:T(8,128)(2,1)S(1)}, u32[]{:S(2)}, u32[]{:S(2)}) collective-permute-start(bf16[23,16,256]{2,1,0:T(8,128)(2,1)} %get-tuple-element.73), channel_id=1, source_target_pairs={{0,1},{1,2},{2,3},{4,5},{5,6},{6,7},{8,9},{9,10},{10,11},{12,13},{... | collective-permute-start | bytes 565256 | tf_op jit(solution)/shard_map/ppermute | solution.py:26
  12.7 2.5 %shard_map.86 = (f32[5,64,16,256]{3,2,1,0:T(8,128)S(1)}, f32[3,64,16,256]{3,2,1,0:T(8,128)S(1)}, f32[64,16,256]{2,1,0:T(8,128)S(1)}) custom-call(f32[5,64,16,256]{3,2,1,0:T(8,128)} %innov_hi.1, f32[3,64,16,256]{3,2,1,0:T(8,128)S(1)} %copy-done.1, f32[64,16,256]{2,1,0:T(8,128)S(1)} %copy-done.3), custom_call_target="tpu_custom_call" | custom-call | bytes 18874368 | tf_op jit(solution)/shard_map/pallas_call | solution.py:572
  15.3 17.5 %collective-permute-done.before = bf16[23,16,256]{2,1,0:T(8,128)(2,1)S(1)} collective-permute-done((bf16[23,16,256]{2,1,0:T(8,128)(2,1)}, bf16[23,16,256]{2,1,0:T(8,128)(2,1)S(1)}, u32[]{:S(2)}, u32[]{:S(2)}) %collective-permute-start) | collective-permute-done | bytes 188448 | tf_op jit(solution)/shard_map/ppermute | solution.py:26
  33.9 2.6 %collective-permute-start.3 = (bf16[72,256]{1,0:T(8,128)(2,1)S(1)}, bf16[72,256]{1,0:T(8,128)(2,1)S(1)}, u32[]{:S(2)}, u32[]{:S(2)}) collective-permute-start(bf16[72,256]{1,0:T(8,128)(2,1)S(1)} %get-tuple-element.79), channel_id=1, source_target_pairs={{4,0},{8,4},{12,8},{16,12},{20,16},{24,20},{28,24},{0,28},{5,1},{9... | collective-permute-start | bytes 110600 | tf_op jit(solution)/shard_map/ppermute | solution.py:34
  43.4 2.0 %collective-permute-start.7 = (bf16[72,256]{1,0:T(8,128)(2,1)S(1)}, bf16[72,256]{1,0:T(8,128)(2,1)S(1)}, u32[]{:S(2)}, u32[]{:S(2)}) collective-permute-start(bf16[72,256]{1,0:T(8,128)(2,1)S(1)} %get-tuple-element.95), channel_id=1, source_target_pairs={{4,0},{8,4},{12,8},{16,12},{20,16},{24,20},{28,24},{0,28},{5,1},{9... | collective-permute-start | bytes 110600 | tf_op jit(solution)/shard_map/ppermute | solution.py:34
  47.8 2.0 %collective-permute-start.9 = (bf16[72,256]{1,0:T(8,128)(2,1)S(1)}, bf16[72,256]{1,0:T(8,128)(2,1)S(1)}, u32[]{:S(2)}, u32[]{:S(2)}) collective-permute-start(bf16[72,256]{1,0:T(8,128)(2,1)S(1)} %get-tuple-element.103), channel_id=1, source_target_pairs={{4,0},{8,4},{12,8},{16,12},{20,16},{24,20},{28,24},{0,28},{5,1},{9... | collective-permute-start | bytes 110600 | tf_op jit(solution)/shard_map/ppermute | solution.py:34
  51.9 2.8 %collective-permute-start.15 = (bf16[64,2048]{1,0:T(8,128)(2,1)S(1)}, bf16[64,2048]{1,0:T(8,128)(2,1)S(1)}, u32[]{:S(2)}, u32[]{:S(2)}) collective-permute-start(bf16[64,2048]{1,0:T(8,128)(2,1)S(1)} %get-tuple-element.110.refs_2_), channel_id=1, source_target_pairs={{0,2},{1,3},{2,0},{3,1},{4,6},{5,7},{6,4},{7,5},{8,10},{9,11},{10,... | collective-permute-start | bytes 786440 | tf_op jit(solution)/shard_map/ppermute | solution.py:38
  56.5 1.9 %collective-permute-start.29 = (bf16[8,32,512]{2,1,0:T(8,128)(2,1)S(1)}, bf16[8,32,512]{2,1,0:T(8,128)(2,1)S(1)}, u32[]{:S(2)}, u32[]{:S(2)}) collective-permute-start(bf16[8,32,512]{2,1,0:T(8,128)(2,1)S(1)} %get-tuple-element.129), channel_id=1, source_target_pairs={{0,1},{1,0},{2,3},{3,2},{4,5},{5,4},{6,7},{7,6},{8,9},{9,8},{10,11... | collective-permute-start | bytes 786440 | tf_op jit(solution)/shard_map/ppermute | solution.py:38
  58.4 14.9 %collective-permute-done.15.refs_2_ = bf16[64,2048]{1,0:T(8,128)(2,1)S(1)} collective-permute-done((bf16[64,2048]{1,0:T(8,128)(2,1)S(1)}, bf16[64,2048]{1,0:T(8,128)(2,1)S(1)}, u32[]{:S(2)}, u32[]{:S(2)}) %collective-permute-start.15) | collective-permute-done | bytes 262176 | tf_op jit(solution)/shard_map/ppermute | solution.py:38
  73.4 2.0 %shard_map.102 = (f32[2,256,128]{2,1,0:T(8,128)S(1)}, bf16[2,256,128]{2,1,0:T(8,128)(2,1)S(1)}) custom-call(bf16[256,4096]{1,0:T(8,128)(2,1)S(1)} %bitcast.17, bf16[256,2048]{1,0:T(8,128)(2,1)} %bitcast.6.refs_1_, bf16[64,2048]{1,0:T(8,128)(2,1)S(1)} %collective-permute-done.15.refs_2_, bf16[64,2048]{1,0:T(8,128)(2,1)S(1)} %collective-permute-done.16.refs_3_), custom_call_target="tpu_custom_call" | custom-call | flops 268435456 | bytes 3145728 | tf_op jit(solution)/shard_map/pallas_call | solution.py:572
  75.4 5.6 %collective-permute-start.17 = (bf16[2,256,128]{2,1,0:T(8,128)(2,1)S(1)}, bf16[2,256,128]{2,1,0:T(8,128)(2,1)S(1)}, u32[]{:S(2)}, u32[]{:S(2)}) collective-permute-start(bf16[2,256,128]{2,1,0:T(8,128)(2,1)S(1)} %get-tuple-element.115), channel_id=1, source_target_pairs={{0,1},{1,0},{2,3},{3,2},{4,5},{5,4},{6,7},{7,6},{8,9},{9,8},{10,11... | collective-permute-start | bytes 393224 | tf_op jit(solution)/shard_map/ppermute | solution.py:38
  81.1 2.0 %shard_map.101 = (f32[2,256,128]{2,1,0:T(8,128)S(1)}, bf16[2,256,128]{2,1,0:T(8,128)(2,1)S(1)}) custom-call(bf16[256,4096]{1,0:T(8,128)(2,1)S(1)} %bitcast.18, bf16[256,2048]{1,0:T(8,128)(2,1)} %bitcast.6.refs_1_, bf16[64,2048]{1,0:T(8,128)(2,1)S(1)} %get-tuple-element.110.refs_2_, bf16[64,2048]{1,0:T(8,128)(2,1)S(1)} %collective-permute-done.13.refs_3_), custom_call_target="tpu_custom_call" | custom-call | flops 268435456 | bytes 3145728 | tf_op jit(solution)/shard_map/pallas_call | solution.py:572
  83.2 2.0 %collective-permute-start.10 = (bf16[8,32,512]{2,1,0:T(8,128)(2,1)S(1)}, bf16[8,32,512]{2,1,0:T(8,128)(2,1)S(1)}, u32[]{:S(2)}, u32[]{:S(2)}) collective-permute-start(bf16[8,32,512]{2,1,0:T(8,128)(2,1)S(1)} %get-tuple-element.108), channel_id=1, source_target_pairs={{0,1},{1,0},{2,3},{3,2},{4,5},{5,4},{6,7},{7,6},{8,9},{9,8},{10,11... | collective-permute-start | bytes 786440 | tf_op jit(solution)/shard_map/ppermute | solution.py:38
  85.2 4.2 %collective-permute-done.17.refs_4_ = bf16[2,256,128]{2,1,0:T(8,128)(2,1)S(1)} collective-permute-done((bf16[2,256,128]{2,1,0:T(8,128)(2,1)S(1)}, bf16[2,256,128]{2,1,0:T(8,128)(2,1)S(1)}, u32[]{:S(2)}, u32[]{:S(2)}) %collective-permute-start.17) | collective-permute-done | bytes 131104 | tf_op jit(solution)/shard_map/ppermute | solution.py:38
  89.4 2.8 %collective-permute-done.14.refs_2_ = bf16[2,256,128]{2,1,0:T(8,128)(2,1)S(1)} collective-permute-done((bf16[2,256,128]{2,1,0:T(8,128)(2,1)S(1)}, bf16[2,256,128]{2,1,0:T(8,128)(2,1)S(1)}, u32[]{:S(2)}, u32[]{:S(2)}) %collective-permute-start.14) | collective-permute-done | bytes 131104 | tf_op jit(solution)/shard_map/ppermute | solution.py:38
  97.9 2.3 %collective-permute-start.23 = (bf16[2,32,256]{2,1,0:T(8,128)(2,1)S(1)}, bf16[2,32,256]{2,1,0:T(8,128)(2,1)S(1)}, u32[]{:S(2)}, u32[]{:S(2)}) collective-permute-start(bf16[2,32,256]{2,1,0:T(8,128)(2,1)S(1)} %get-tuple-element.122), channel_id=1, source_target_pairs={{24,0},{28,4},{0,8},{4,12},{8,16},{12,20},{16,24},{20,28},{25,1},{... | collective-permute-start | bytes 98312 | tf_op jit(solution)/shard_map/ppermute | solution.py:34
  105.6 2.0 %collective-permute-start.32 = (bf16[64,1024]{1,0:T(8,128)(2,1)S(1)}, bf16[64,1024]{1,0:T(8,128)(2,1)S(1)}, u32[]{:S(2)}, u32[]{:S(2)}) collective-permute-start(bf16[64,1024]{1,0:T(8,128)(2,1)S(1)} %get-tuple-element.133), channel_id=1, source_target_pairs={{0,3},{1,2},{2,1},{3,0},{4,7},{5,6},{6,5},{7,4},{8,11},{9,10},{10,... | collective-permute-start | bytes 393224 | tf_op jit(solution)/shard_map/ppermute | solution.py:38
  108.8 2.0 %collective-permute-start.26 = (bf16[64,1024]{1,0:T(8,128)(2,1)S(1)}, bf16[64,1024]{1,0:T(8,128)(2,1)S(1)}, u32[]{:S(2)}, u32[]{:S(2)}) collective-permute-start(bf16[64,1024]{1,0:T(8,128)(2,1)S(1)} %get-tuple-element.126), channel_id=1, source_target_pairs={{0,2},{1,3},{2,0},{3,1},{4,6},{5,7},{6,4},{7,5},{8,10},{9,11},{10,... | collective-permute-start | bytes 393224 | tf_op jit(solution)/shard_map/ppermute | solution.py:38
  110.8 2.0 %collective-permute-start.27 = (bf16[64,1024]{1,0:T(8,128)(2,1)S(1)}, bf16[64,1024]{1,0:T(8,128)(2,1)S(1)}, u32[]{:S(2)}, u32[]{:S(2)}) collective-permute-start(bf16[64,1024]{1,0:T(8,128)(2,1)S(1)} %get-tuple-element.127), channel_id=1, source_target_pairs={{0,3},{1,2},{2,1},{3,0},{4,7},{5,6},{6,5},{7,4},{8,11},{9,10},{10,... | collective-permute-start | bytes 393224 | tf_op jit(solution)/shard_map/ppermute | solution.py:38
  113.1 3.8 %collective-permute-done.31.refs_2_ = bf16[64,1024]{1,0:T(8,128)(2,1)S(1)} collective-permute-done((bf16[64,1024]{1,0:T(8,128)(2,1)S(1)}, bf16[64,1024]{1,0:T(8,128)(2,1)S(1)}, u32[]{:S(2)}, u32[]{:S(2)}) %collective-permute-start.31) | collective-permute-done | bytes 131104 | tf_op jit(solution)/shard_map/ppermute | solution.py:38
  118.5 9.6 %collective-permute-done.26.refs_2_ = bf16[64,1024]{1,0:T(8,128)(2,1)S(1)} collective-permute-done((bf16[64,1024]{1,0:T(8,128)(2,1)S(1)}, bf16[64,1024]{1,0:T(8,128)(2,1)S(1)}, u32[]{:S(2)}, u32[]{:S(2)}) %collective-permute-start.26) | collective-permute-done | bytes 131104 | tf_op jit(solution)/shard_map/ppermute | solution.py:38
  (78 shorter events, 32.2 us)
Async XLA Ops:
  2.9 70.6 %collective-permute-start.12 = (bf16[8,32,2048]{2,1,0:T(8,128)(2,1)}, bf16[8,32,2048]{2,1,0:T(8,128)(2,1)}, u32[]{:S(2)}, u32[]{:S(2)}) collective-permute-start(bf16[8,32,2048]{2,1,0:T(8,128)(2,1)} %shard_map.100), channel_id=1, source_target_pairs={{0,1},{1,0},{2,3},{3,2},{4,5},{5,4},{6,7},{7,6},{8,9},{9,8},{10,11... | collective-permute-start | bytes 3145736 | tf_op jit(solution)/shard_map/ppermute | solution.py:38
  8.2 24.5 %collective-permute-start = (bf16[23,16,256]{2,1,0:T(8,128)(2,1)}, bf16[23,16,256]{2,1,0:T(8,128)(2,1)S(1)}, u32[]{:S(2)}, u32[]{:S(2)}) collective-permute-start(bf16[23,16,256]{2,1,0:T(8,128)(2,1)} %get-tuple-element.73), channel_id=1, source_target_pairs={{0,1},{1,2},{2,3},{4,5},{5,6},{6,7},{8,9},{9,10},{10,11},{12,13},{... | collective-permute-start | bytes 565256 | tf_op jit(solution)/shard_map/ppermute | solution.py:26
  10.2 23.2 %collective-permute-start.1 = (bf16[23,16,256]{2,1,0:T(8,128)(2,1)}, bf16[23,16,256]{2,1,0:T(8,128)(2,1)S(1)}, u32[]{:S(2)}, u32[]{:S(2)}) collective-permute-start(bf16[23,16,256]{2,1,0:T(8,128)(2,1)} %get-tuple-element.74), channel_id=1, source_target_pairs={{1,0},{2,1},{3,2},{5,4},{6,5},{7,6},{9,8},{10,9},{11,10},{13,12},{... | collective-permute-start | bytes 565256 | tf_op jit(solution)/shard_map/ppermute | solution.py:26
  33.9 4.3 %collective-permute-start.2 = (bf16[72,256]{1,0:T(8,128)(2,1)S(1)}, bf16[72,256]{1,0:T(8,128)(2,1)S(1)}, u32[]{:S(2)}, u32[]{:S(2)}) collective-permute-start(bf16[72,256]{1,0:T(8,128)(2,1)S(1)} %get-tuple-element.78), channel_id=1, source_target_pairs={{28,0},{0,4},{4,8},{8,12},{12,16},{16,20},{20,24},{24,28},{29,1},{... | collective-permute-start | bytes 110600 | tf_op jit(solution)/shard_map/ppermute | solution.py:34
  33.9 4.3 %collective-permute-start.3 = (bf16[72,256]{1,0:T(8,128)(2,1)S(1)}, bf16[72,256]{1,0:T(8,128)(2,1)S(1)}, u32[]{:S(2)}, u32[]{:S(2)}) collective-permute-start(bf16[72,256]{1,0:T(8,128)(2,1)S(1)} %get-tuple-element.79), channel_id=1, source_target_pairs={{4,0},{8,4},{12,8},{16,12},{20,16},{24,20},{28,24},{0,28},{5,1},{9... | collective-permute-start | bytes 110600 | tf_op jit(solution)/shard_map/ppermute | solution.py:34
  38.2 4.3 %collective-permute-start.4 = (bf16[72,256]{1,0:T(8,128)(2,1)S(1)}, bf16[72,256]{1,0:T(8,128)(2,1)S(1)}, u32[]{:S(2)}, u32[]{:S(2)}) collective-permute-start(bf16[72,256]{1,0:T(8,128)(2,1)S(1)} %get-tuple-element.87), channel_id=1, source_target_pairs={{28,0},{0,4},{4,8},{8,12},{12,16},{16,20},{20,24},{24,28},{29,1},{... | collective-permute-start | bytes 110600 | tf_op jit(solution)/shard_map/ppermute | solution.py:34
  42.7 4.3 %collective-permute-start.6 = (bf16[72,256]{1,0:T(8,128)(2,1)S(1)}, bf16[72,256]{1,0:T(8,128)(2,1)S(1)}, u32[]{:S(2)}, u32[]{:S(2)}) collective-permute-start(bf16[72,256]{1,0:T(8,128)(2,1)S(1)} %get-tuple-element.94), channel_id=1, source_target_pairs={{28,0},{0,4},{4,8},{8,12},{12,16},{16,20},{20,24},{24,28},{29,1},{... | collective-permute-start | bytes 110600 | tf_op jit(solution)/shard_map/ppermute | solution.py:34
  47.1 4.7 %collective-permute-start.8 = (bf16[72,256]{1,0:T(8,128)(2,1)S(1)}, bf16[72,256]{1,0:T(8,128)(2,1)S(1)}, u32[]{:S(2)}, u32[]{:S(2)}) collective-permute-start(bf16[72,256]{1,0:T(8,128)(2,1)S(1)} %get-tuple-element.102), channel_id=1, source_target_pairs={{28,0},{0,4},{4,8},{8,12},{12,16},{16,20},{20,24},{24,28},{29,1},{... | collective-permute-start | bytes 110600 | tf_op jit(solution)/shard_map/ppermute | solution.py:34
  51.9 21.4 %collective-permute-start.15 = (bf16[64,2048]{1,0:T(8,128)(2,1)S(1)}, bf16[64,2048]{1,0:T(8,128)(2,1)S(1)}, u32[]{:S(2)}, u32[]{:S(2)}) collective-permute-start(bf16[64,2048]{1,0:T(8,128)(2,1)S(1)} %get-tuple-element.110.refs_2_), channel_id=1, source_target_pairs={{0,2},{1,3},{2,0},{3,1},{4,6},{5,7},{6,4},{7,5},{8,10},{9,11},{10,... | collective-permute-start | bytes 786440 | tf_op jit(solution)/shard_map/ppermute | solution.py:38
  54.7 18.7 %collective-permute-start.16 = (bf16[64,2048]{1,0:T(8,128)(2,1)S(1)}, bf16[64,2048]{1,0:T(8,128)(2,1)S(1)}, u32[]{:S(2)}, u32[]{:S(2)}) collective-permute-start(bf16[64,2048]{1,0:T(8,128)(2,1)S(1)} %get-tuple-element.111), channel_id=1, source_target_pairs={{0,3},{1,2},{2,1},{3,0},{4,7},{5,6},{6,5},{7,4},{8,11},{9,10},{10,... | collective-permute-start | bytes 786440 | tf_op jit(solution)/shard_map/ppermute | solution.py:38
  56.1 25.0 %collective-permute-start.13 = (bf16[64,2048]{1,0:T(8,128)(2,1)S(1)}, bf16[64,2048]{1,0:T(8,128)(2,1)S(1)}, u32[]{:S(2)}, u32[]{:S(2)}) collective-permute-start(bf16[64,2048]{1,0:T(8,128)(2,1)S(1)} %get-tuple-element.111), channel_id=1, source_target_pairs={{0,1},{1,0},{2,3},{3,2},{4,5},{5,4},{6,7},{7,6},{8,9},{9,8},{10,11... | collective-permute-start | bytes 786440 | tf_op jit(solution)/shard_map/ppermute | solution.py:38
  56.5 37.3 %collective-permute-start.29 = (bf16[8,32,512]{2,1,0:T(8,128)(2,1)S(1)}, bf16[8,32,512]{2,1,0:T(8,128)(2,1)S(1)}, u32[]{:S(2)}, u32[]{:S(2)}) collective-permute-start(bf16[8,32,512]{2,1,0:T(8,128)(2,1)S(1)} %get-tuple-element.129), channel_id=1, source_target_pairs={{0,1},{1,0},{2,3},{3,2},{4,5},{5,4},{6,7},{7,6},{8,9},{9,8},{10,11... | collective-permute-start | bytes 786440 | tf_op jit(solution)/shard_map/ppermute | solution.py:38
  73.3 20.6 %collective-permute-start.28 = (bf16[8,32,512]{2,1,0:T(8,128)(2,1)S(1)}, bf16[8,32,512]{2,1,0:T(8,128)(2,1)S(1)}, u32[]{:S(2)}, u32[]{:S(2)}) collective-permute-start(bf16[8,32,512]{2,1,0:T(8,128)(2,1)S(1)} %get-tuple-element.128), channel_id=1, source_target_pairs={{0,1},{1,0},{2,3},{3,2},{4,5},{5,4},{6,7},{7,6},{8,9},{9,8},{10,11... | collective-permute-start | bytes 786440 | tf_op jit(solution)/shard_map/ppermute | solution.py:38
  75.4 13.9 %collective-permute-start.17 = (bf16[2,256,128]{2,1,0:T(8,128)(2,1)S(1)}, bf16[2,256,128]{2,1,0:T(8,128)(2,1)S(1)}, u32[]{:S(2)}, u32[]{:S(2)}) collective-permute-start(bf16[2,256,128]{2,1,0:T(8,128)(2,1)S(1)} %get-tuple-element.115), channel_id=1, source_target_pairs={{0,1},{1,0},{2,3},{3,2},{4,5},{5,4},{6,7},{7,6},{8,9},{9,8},{10,11... | collective-permute-start | bytes 393224 | tf_op jit(solution)/shard_map/ppermute | solution.py:38
  83.1 9.1 %collective-permute-start.14 = (bf16[2,256,128]{2,1,0:T(8,128)(2,1)S(1)}, bf16[2,256,128]{2,1,0:T(8,128)(2,1)S(1)}, u32[]{:S(2)}, u32[]{:S(2)}) collective-permute-start(bf16[2,256,128]{2,1,0:T(8,128)(2,1)S(1)} %get-tuple-element.113), channel_id=1, source_target_pairs={{0,1},{1,0},{2,3},{3,2},{4,5},{5,4},{6,7},{7,6},{8,9},{9,8},{10,11... | collective-permute-start | bytes 393224 | tf_op jit(solution)/shard_map/ppermute | solution.py:38
  83.2 25.3 %collective-permute-start.10 = (bf16[8,32,512]{2,1,0:T(8,128)(2,1)S(1)}, bf16[8,32,512]{2,1,0:T(8,128)(2,1)S(1)}, u32[]{:S(2)}, u32[]{:S(2)}) collective-permute-start(bf16[8,32,512]{2,1,0:T(8,128)(2,1)S(1)} %get-tuple-element.108), channel_id=1, source_target_pairs={{0,1},{1,0},{2,3},{3,2},{4,5},{5,4},{6,7},{7,6},{8,9},{9,8},{10,11... | collective-permute-start | bytes 786440 | tf_op jit(solution)/shard_map/ppermute | solution.py:38
  89.4 19.1 %collective-permute-start.11 = (bf16[8,32,512]{2,1,0:T(8,128)(2,1)S(1)}, bf16[8,32,512]{2,1,0:T(8,128)(2,1)S(1)}, u32[]{:S(2)}, u32[]{:S(2)}) collective-permute-start(bf16[8,32,512]{2,1,0:T(8,128)(2,1)S(1)} %get-tuple-element.109), channel_id=1, source_target_pairs={{0,1},{1,0},{2,3},{3,2},{4,5},{5,4},{6,7},{7,6},{8,9},{9,8},{10,11... | collective-permute-start | bytes 786440 | tf_op jit(solution)/shard_map/ppermute | solution.py:38
  97.9 4.8 %collective-permute-start.23 = (bf16[2,32,256]{2,1,0:T(8,128)(2,1)S(1)}, bf16[2,32,256]{2,1,0:T(8,128)(2,1)S(1)}, u32[]{:S(2)}, u32[]{:S(2)}) collective-permute-start(bf16[2,32,256]{2,1,0:T(8,128)(2,1)S(1)} %get-tuple-element.122), channel_id=1, source_target_pairs={{24,0},{28,4},{0,8},{4,12},{8,16},{12,20},{16,24},{20,28},{25,1},{... | collective-permute-start | bytes 98312 | tf_op jit(solution)/shard_map/ppermute | solution.py:34
  103.9 13.0 %collective-permute-start.31 = (bf16[64,1024]{1,0:T(8,128)(2,1)S(1)}, bf16[64,1024]{1,0:T(8,128)(2,1)S(1)}, u32[]{:S(2)}, u32[]{:S(2)}) collective-permute-start(bf16[64,1024]{1,0:T(8,128)(2,1)S(1)} %get-tuple-element.132), channel_id=1, source_target_pairs={{0,2},{1,3},{2,0},{3,1},{4,6},{5,7},{6,4},{7,5},{8,10},{9,11},{10,... | collective-permute-start | bytes 393224 | tf_op jit(solution)/shard_map/ppermute | solution.py:38
  105.6 12.5 %collective-permute-start.32 = (bf16[64,1024]{1,0:T(8,128)(2,1)S(1)}, bf16[64,1024]{1,0:T(8,128)(2,1)S(1)}, u32[]{:S(2)}, u32[]{:S(2)}) collective-permute-start(bf16[64,1024]{1,0:T(8,128)(2,1)S(1)} %get-tuple-element.133), channel_id=1, source_target_pairs={{0,3},{1,2},{2,1},{3,0},{4,7},{5,6},{6,5},{7,4},{8,11},{9,10},{10,... | collective-permute-start | bytes 393224 | tf_op jit(solution)/shard_map/ppermute | solution.py:38
  107.9 10.5 %collective-permute-start.30 = (bf16[64,1024]{1,0:T(8,128)(2,1)S(1)}, bf16[64,1024]{1,0:T(8,128)(2,1)S(1)}, u32[]{:S(2)}, u32[]{:S(2)}) collective-permute-start(bf16[64,1024]{1,0:T(8,128)(2,1)S(1)} %get-tuple-element.131), channel_id=1, source_target_pairs={{0,1},{1,0},{2,3},{3,2},{4,5},{5,4},{6,7},{7,6},{8,9},{9,8},{10,11... | collective-permute-start | bytes 393224 | tf_op jit(solution)/shard_map/ppermute | solution.py:38
  108.8 19.3 %collective-permute-start.26 = (bf16[64,1024]{1,0:T(8,128)(2,1)S(1)}, bf16[64,1024]{1,0:T(8,128)(2,1)S(1)}, u32[]{:S(2)}, u32[]{:S(2)}) collective-permute-start(bf16[64,1024]{1,0:T(8,128)(2,1)S(1)} %get-tuple-element.126), channel_id=1, source_target_pairs={{0,2},{1,3},{2,0},{3,1},{4,6},{5,7},{6,4},{7,5},{8,10},{9,11},{10,... | collective-permute-start | bytes 393224 | tf_op jit(solution)/shard_map/ppermute | solution.py:38
  110.8 17.4 %collective-permute-start.27 = (bf16[64,1024]{1,0:T(8,128)(2,1)S(1)}, bf16[64,1024]{1,0:T(8,128)(2,1)S(1)}, u32[]{:S(2)}, u32[]{:S(2)}) collective-permute-start(bf16[64,1024]{1,0:T(8,128)(2,1)S(1)} %get-tuple-element.127), channel_id=1, source_target_pairs={{0,3},{1,2},{2,1},{3,0},{4,7},{5,6},{6,5},{7,4},{8,11},{9,10},{10,... | collective-permute-start | bytes 393224 | tf_op jit(solution)/shard_map/ppermute | solution.py:38
  116.9 11.2 %collective-permute-start.25 = (bf16[64,1024]{1,0:T(8,128)(2,1)S(1)}, bf16[64,1024]{1,0:T(8,128)(2,1)S(1)}, u32[]{:S(2)}, u32[]{:S(2)}) collective-permute-start(bf16[64,1024]{1,0:T(8,128)(2,1)S(1)} %get-tuple-element.125), channel_id=1, source_target_pairs={{0,1},{1,0},{2,3},{3,2},{4,5},{5,4},{6,7},{7,6},{8,9},{9,8},{10,11... | collective-permute-start | bytes 393224 | tf_op jit(solution)/shard_map/ppermute | solution.py:38
  (15 other events, 106.7 us)

commit v9 on v8

--- a/solution.py
+++ b/solution.py
@@ -99,9 +99,12 @@
 
 def load_kernel(*refs):
     count = len(refs) // 2
-    copies = [pltpu.make_async_copy(refs[n], refs[count + n], refs[-1].at[n]) for n in range(count)]
-    for copy in copies:
-        copy.start()
+    copies = []
+    for source, target in zip(refs[:count], refs[count : 2 * count]):
+        leading = range(source.shape[0]) if len(source.shape) > 3 else (pl.ds(0, source.shape[0]),)
+        for n in leading:
+            copies.append(pltpu.make_async_copy(source.at[n], target.at[n], refs[-1].at[len(copies)]))
+            copies[-1].start()
     for copy in copies:
         copy.wait()
 
@@ -116,6 +119,25 @@
         loads.append(pltpu.make_async_copy(right.at[0, :, :, window], vmem.at[n], sems.at[n]))
         loads[-1].start()
         stores.append(pltpu.make_async_copy(vmem.at[n], target, sems.at[len(targets) + n]))
+    for load, store in zip(loads, stores):
+        load.wait()
+        store.start()
+    for store in stores:
+        store.wait()
+
+
+def left_kernel(place, right, *rest):
+    targets, (vmem, sems) = rest[:-2], rest[-2:]
+    wide = targets[0].shape[2]
+    start = (1 - place[1]) * wide * len(targets)
+    loads, stores = [], []
+    for n, target in enumerate(targets):
+        window = pl.ds(pl.multiple_of(start + n * wide, wide), wide)
+        for k in range(target.shape[0]):
+            at = len(loads)
+            loads.append(pltpu.make_async_copy(right.at[0, k, :, window], vmem.at[n, k], sems.at[0, at]))
+            loads[-1].start()
+            stores.append(pltpu.make_async_copy(vmem.at[n, k], target.at[k], sems.at[1, at]))
     for load, store in zip(loads, stores):
         load.wait()
         store.start()
@@ -599,13 +621,13 @@
     down, up, sea = pack(innovations, courant, diffusivity, sea_bricks)
     place = HERE
     (left_other,) = call(
-        halves_kernel,
+        left_kernel,
         (place, left),
         [SMEM, ANY],
         [((slots, width, half), bf16, ANY)],
         grant=WIDE_GRANT,
         moved=2 << 20,
-        scratch=[pltpu.VMEM((1, slots, width, half), bf16), pltpu.SemaphoreType.DMA((2,))],
+        scratch=[pltpu.VMEM((1, slots, width, half), bf16), pltpu.SemaphoreType.DMA((2, slots))],
     )
     before = from_behind(down, "depth", 1)
     after = from_behind(up, "depth", -1)
@@ -617,7 +639,7 @@
         [(a.shape, a.dtype) for a in inputs],
         grant=LOAD_GRANT,
         moved=18 << 20,
-        scratch=[pltpu.SemaphoreType.DMA((3,))],
+        scratch=[pltpu.SemaphoreType.DMA((sum(a.shape[0] if a.ndim > 3 else 1 for a in inputs),))],
     )
     right_other = call(
         halves_kernel,

time: 130 us -> 130 us (level)
  no operation moved by 1% of the time
where the time goes in v9:
time: 130 us; the launch traced here: 129 us
  waiting for transfers between devices  59.7 us (46%)
  starting transfers between devices  45.2 us (35%)
  Pallas kernels  22.1 us (17%)
    ppermute x16, waiting for transfers between devices, swapped(): lax.ppermute(block, axis, [(i, i ^ mask) for i in range(lax.axis_size(axi...  35.7 us
    ppermute x16, starting transfers between devices, swapped(): lax.ppermute(block, axis, [(i, i ^ mask) for i in range(lax.axis_size(axi...  25.4 us
    ppermute x2, waiting for transfers between devices, from_behind(): lax.ppermute(value, axis, [(source, source + steps) for source in range(i...  18 us
    ppermute x15, starting transfers between devices, shifted(): return lax.ppermute(block, axis, route)  16.6 us
    pallas_call x15, Pallas kernels, call(): pl.pallas_call(kernel, in_specs=in_specs, out_shape=[jax.ShapeDtypeStruct...  13.3 us
    pallas_call x4, Pallas kernels, sweep(): pl.pallas_call(functools.partial(step_kernel, table, step), in_specs=[VME...  5.99 us
    ppermute x15, waiting for transfers between devices, shifted(): return lax.ppermute(block, axis, route)  5.95 us
    ppermute x2, starting transfers between devices, from_behind(): lax.ppermute(value, axis, [(source, source + steps) for source in range(i...  3.23 us
  transfers between devices with their start and end apart: 33, of which 18 were waited for; matrix products, arithmetic and copies ran while one was open for 0% of the time, Pallas kernels for 15%

profile of v9, /device:TPU:0, one launch (start us, length us, event | category | flops | bytes accessed | tf_op | source)
XLA Modules:
  0.0 129.1 jit_solution(10604132392583405411)
XLA Ops:
  0.6 2.1 %shard_map.100 = bf16[8,32,2048]{2,1,0:T(8,128)(2,1)} custom-call(bf16[1,8,32,4096]{3,2,1,0:T(8,128)(2,1)} %bitcast.16), custom_call_target="tpu_custom_call" | custom-call | bytes 2097152 | tf_op jit(solution)/shard_map/pallas_call | solution.py:594
  2.7 3.1 %collective-permute-start.12 = (bf16[8,32,2048]{2,1,0:T(8,128)(2,1)}, bf16[8,32,2048]{2,1,0:T(8,128)(2,1)}, u32[]{:S(2)}, u32[]{:S(2)}) collective-permute-start(bf16[8,32,2048]{2,1,0:T(8,128)(2,1)} %shard_map.100), channel_id=1, source_target_pairs={{0,1},{1,0},{2,3},{3,2},{4,5},{5,4},{6,7},{7,6},{8,9},{9,8},{10,11... | collective-permute-start | bytes 3145736 | tf_op jit(solution)/shard_map/ppermute | solution.py:38
  5.9 2.3 %shard_map.87 = (bf16[23,16,256]{2,1,0:T(8,128)(2,1)}, bf16[23,16,256]{2,1,0:T(8,128)(2,1)}, f32[64,256]{1,0:T(8,128)}) custom-call(s32[64,1,128]{2,1,0:T(1,128)} %bricks.1, f32[5,64,16,256]{3,2,1,0:T(8,128)} %innov_hi.1, f32[5,64,16,256]{3,2,1,0:T(8,128)} %innov_hi.1, f32[3,64,16,256]{3,2,1,0:T(8,128)} %cour_hi.1, f32[3,64,16,256]{3,2,1,0:T(8,128)} %cour_hi.1, ...), custom_call_target="tpu_custom_call" | custom-call | bytes 1048576 | tf_op jit(solution)/shard_map/pallas_call | solution.py:377
  8.1 1.9 %collective-permute-start = (bf16[23,16,256]{2,1,0:T(8,128)(2,1)}, bf16[23,16,256]{2,1,0:T(8,128)(2,1)S(1)}, u32[]{:S(2)}, u32[]{:S(2)}) collective-permute-start(bf16[23,16,256]{2,1,0:T(8,128)(2,1)} %get-tuple-element.73), channel_id=1, source_target_pairs={{0,1},{1,2},{2,3},{4,5},{5,6},{6,7},{8,9},{9,10},{10,11},{12,13},{... | collective-permute-start | bytes 565256 | tf_op jit(solution)/shard_map/ppermute | solution.py:26
  12.6 2.6 %shard_map.86 = (f32[5,64,16,256]{3,2,1,0:T(8,128)S(1)}, f32[3,64,16,256]{3,2,1,0:T(8,128)S(1)}, f32[64,16,256]{2,1,0:T(8,128)S(1)}) custom-call(f32[5,64,16,256]{3,2,1,0:T(8,128)} %innov_hi.1, f32[3,64,16,256]{3,2,1,0:T(8,128)S(1)} %copy-done.1, f32[64,16,256]{2,1,0:T(8,128)S(1)} %copy-done.3), custom_call_target="tpu_custom_call" | custom-call | bytes 18874368 | tf_op jit(solution)/shard_map/pallas_call | solution.py:594
  15.2 17.4 %collective-permute-done.before = bf16[23,16,256]{2,1,0:T(8,128)(2,1)S(1)} collective-permute-done((bf16[23,16,256]{2,1,0:T(8,128)(2,1)}, bf16[23,16,256]{2,1,0:T(8,128)(2,1)S(1)}, u32[]{:S(2)}, u32[]{:S(2)}) %collective-permute-start) | collective-permute-done | bytes 188448 | tf_op jit(solution)/shard_map/ppermute | solution.py:26
  33.8 2.6 %collective-permute-start.3 = (bf16[72,256]{1,0:T(8,128)(2,1)S(1)}, bf16[72,256]{1,0:T(8,128)(2,1)S(1)}, u32[]{:S(2)}, u32[]{:S(2)}) collective-permute-start(bf16[72,256]{1,0:T(8,128)(2,1)S(1)} %get-tuple-element.79), channel_id=1, source_target_pairs={{4,0},{8,4},{12,8},{16,12},{20,16},{24,20},{28,24},{0,28},{5,1},{9... | collective-permute-start | bytes 110600 | tf_op jit(solution)/shard_map/ppermute | solution.py:34
  43.3 2.0 %collective-permute-start.7 = (bf16[72,256]{1,0:T(8,128)(2,1)S(1)}, bf16[72,256]{1,0:T(8,128)(2,1)S(1)}, u32[]{:S(2)}, u32[]{:S(2)}) collective-permute-start(bf16[72,256]{1,0:T(8,128)(2,1)S(1)} %get-tuple-element.95), channel_id=1, source_target_pairs={{4,0},{8,4},{12,8},{16,12},{20,16},{24,20},{28,24},{0,28},{5,1},{9... | collective-permute-start | bytes 110600 | tf_op jit(solution)/shard_map/ppermute | solution.py:34
  47.7 2.0 %collective-permute-start.9 = (bf16[72,256]{1,0:T(8,128)(2,1)S(1)}, bf16[72,256]{1,0:T(8,128)(2,1)S(1)}, u32[]{:S(2)}, u32[]{:S(2)}) collective-permute-start(bf16[72,256]{1,0:T(8,128)(2,1)S(1)} %get-tuple-element.103), channel_id=1, source_target_pairs={{4,0},{8,4},{12,8},{16,12},{20,16},{24,20},{28,24},{0,28},{5,1},{9... | collective-permute-start | bytes 110600 | tf_op jit(solution)/shard_map/ppermute | solution.py:34
  51.8 2.8 %collective-permute-start.15 = (bf16[64,2048]{1,0:T(8,128)(2,1)S(1)}, bf16[64,2048]{1,0:T(8,128)(2,1)S(1)}, u32[]{:S(2)}, u32[]{:S(2)}) collective-permute-start(bf16[64,2048]{1,0:T(8,128)(2,1)S(1)} %get-tuple-element.110.refs_2_), channel_id=1, source_target_pairs={{0,2},{1,3},{2,0},{3,1},{4,6},{5,7},{6,4},{7,5},{8,10},{9,11},{10,... | collective-permute-start | bytes 786440 | tf_op jit(solution)/shard_map/ppermute | solution.py:38
  56.4 1.9 %collective-permute-start.29 = (bf16[8,32,512]{2,1,0:T(8,128)(2,1)S(1)}, bf16[8,32,512]{2,1,0:T(8,128)(2,1)S(1)}, u32[]{:S(2)}, u32[]{:S(2)}) collective-permute-start(bf16[8,32,512]{2,1,0:T(8,128)(2,1)S(1)} %get-tuple-element.129), channel_id=1, source_target_pairs={{0,1},{1,0},{2,3},{3,2},{4,5},{5,4},{6,7},{7,6},{8,9},{9,8},{10,11... | collective-permute-start | bytes 786440 | tf_op jit(solution)/shard_map/ppermute | solution.py:38
  58.3 14.9 %collective-permute-done.15.refs_2_ = bf16[64,2048]{1,0:T(8,128)(2,1)S(1)} collective-permute-done((bf16[64,2048]{1,0:T(8,128)(2,1)S(1)}, bf16[64,2048]{1,0:T(8,128)(2,1)S(1)}, u32[]{:S(2)}, u32[]{:S(2)}) %collective-permute-start.15) | collective-permute-done | bytes 262176 | tf_op jit(solution)/shard_map/ppermute | solution.py:38
  73.3 2.0 %shard_map.102 = (f32[2,256,128]{2,1,0:T(8,128)S(1)}, bf16[2,256,128]{2,1,0:T(8,128)(2,1)S(1)}) custom-call(bf16[256,4096]{1,0:T(8,128)(2,1)S(1)} %bitcast.17, bf16[256,2048]{1,0:T(8,128)(2,1)} %bitcast.6.refs_1_, bf16[64,2048]{1,0:T(8,128)(2,1)S(1)} %collective-permute-done.15.refs_2_, bf16[64,2048]{1,0:T(8,128)(2,1)S(1)} %collective-permute-done.16.refs_3_), custom_call_target="tpu_custom_call" | custom-call | flops 268435456 | bytes 3145728 | tf_op jit(solution)/shard_map/pallas_call | solution.py:594
  75.3 5.6 %collective-permute-start.17 = (bf16[2,256,128]{2,1,0:T(8,128)(2,1)S(1)}, bf16[2,256,128]{2,1,0:T(8,128)(2,1)S(1)}, u32[]{:S(2)}, u32[]{:S(2)}) collective-permute-start(bf16[2,256,128]{2,1,0:T(8,128)(2,1)S(1)} %get-tuple-element.115), channel_id=1, source_target_pairs={{0,1},{1,0},{2,3},{3,2},{4,5},{5,4},{6,7},{7,6},{8,9},{9,8},{10,11... | collective-permute-start | bytes 393224 | tf_op jit(solution)/shard_map/ppermute | solution.py:38
  80.9 2.0 %shard_map.101 = (f32[2,256,128]{2,1,0:T(8,128)S(1)}, bf16[2,256,128]{2,1,0:T(8,128)(2,1)S(1)}) custom-call(bf16[256,4096]{1,0:T(8,128)(2,1)S(1)} %bitcast.18, bf16[256,2048]{1,0:T(8,128)(2,1)} %bitcast.6.refs_1_, bf16[64,2048]{1,0:T(8,128)(2,1)S(1)} %get-tuple-element.110.refs_2_, bf16[64,2048]{1,0:T(8,128)(2,1)S(1)} %collective-permute-done.13.refs_3_), custom_call_target="tpu_custom_call" | custom-call | flops 268435456 | bytes 3145728 | tf_op jit(solution)/shard_map/pallas_call | solution.py:594
  83.0 2.0 %collective-permute-start.10 = (bf16[8,32,512]{2,1,0:T(8,128)(2,1)S(1)}, bf16[8,32,512]{2,1,0:T(8,128)(2,1)S(1)}, u32[]{:S(2)}, u32[]{:S(2)}) collective-permute-start(bf16[8,32,512]{2,1,0:T(8,128)(2,1)S(1)} %get-tuple-element.108), channel_id=1, source_target_pairs={{0,1},{1,0},{2,3},{3,2},{4,5},{5,4},{6,7},{7,6},{8,9},{9,8},{10,11... | collective-permute-start | bytes 786440 | tf_op jit(solution)/shard_map/ppermute | solution.py:38
  85.0 4.2 %collective-permute-done.17.refs_4_ = bf16[2,256,128]{2,1,0:T(8,128)(2,1)S(1)} collective-permute-done((bf16[2,256,128]{2,1,0:T(8,128)(2,1)S(1)}, bf16[2,256,128]{2,1,0:T(8,128)(2,1)S(1)}, u32[]{:S(2)}, u32[]{:S(2)}) %collective-permute-start.17) | collective-permute-done | bytes 131104 | tf_op jit(solution)/shard_map/ppermute | solution.py:38
  89.3 2.8 %collective-permute-done.14.refs_2_ = bf16[2,256,128]{2,1,0:T(8,128)(2,1)S(1)} collective-permute-done((bf16[2,256,128]{2,1,0:T(8,128)(2,1)S(1)}, bf16[2,256,128]{2,1,0:T(8,128)(2,1)S(1)}, u32[]{:S(2)}, u32[]{:S(2)}) %collective-permute-start.14) | collective-permute-done | bytes 131104 | tf_op jit(solution)/shard_map/ppermute | solution.py:38
  97.8 2.3 %collective-permute-start.23 = (bf16[2,32,256]{2,1,0:T(8,128)(2,1)S(1)}, bf16[2,32,256]{2,1,0:T(8,128)(2,1)S(1)}, u32[]{:S(2)}, u32[]{:S(2)}) collective-permute-start(bf16[2,32,256]{2,1,0:T(8,128)(2,1)S(1)} %get-tuple-element.122), channel_id=1, source_target_pairs={{24,0},{28,4},{0,8},{4,12},{8,16},{12,20},{16,24},{20,28},{25,1},{... | collective-permute-start | bytes 98312 | tf_op jit(solution)/shard_map/ppermute | solution.py:34
  105.4 2.0 %collective-permute-start.32 = (bf16[64,1024]{1,0:T(8,128)(2,1)S(1)}, bf16[64,1024]{1,0:T(8,128)(2,1)S(1)}, u32[]{:S(2)}, u32[]{:S(2)}) collective-permute-start(bf16[64,1024]{1,0:T(8,128)(2,1)S(1)} %get-tuple-element.133), channel_id=1, source_target_pairs={{0,3},{1,2},{2,1},{3,0},{4,7},{5,6},{6,5},{7,4},{8,11},{9,10},{10,... | collective-permute-start | bytes 393224 | tf_op jit(solution)/shard_map/ppermute | solution.py:38
  108.7 2.0 %collective-permute-start.26 = (bf16[64,1024]{1,0:T(8,128)(2,1)S(1)}, bf16[64,1024]{1,0:T(8,128)(2,1)S(1)}, u32[]{:S(2)}, u32[]{:S(2)}) collective-permute-start(bf16[64,1024]{1,0:T(8,128)(2,1)S(1)} %get-tuple-element.126), channel_id=1, source_target_pairs={{0,2},{1,3},{2,0},{3,1},{4,6},{5,7},{6,4},{7,5},{8,10},{9,11},{10,... | collective-permute-start | bytes 393224 | tf_op jit(solution)/shard_map/ppermute | solution.py:38
  110.6 2.0 %collective-permute-start.27 = (bf16[64,1024]{1,0:T(8,128)(2,1)S(1)}, bf16[64,1024]{1,0:T(8,128)(2,1)S(1)}, u32[]{:S(2)}, u32[]{:S(2)}) collective-permute-start(bf16[64,1024]{1,0:T(8,128)(2,1)S(1)} %get-tuple-element.127), channel_id=1, source_target_pairs={{0,3},{1,2},{2,1},{3,0},{4,7},{5,6},{6,5},{7,4},{8,11},{9,10},{10,... | collective-permute-start | bytes 393224 | tf_op jit(solution)/shard_map/ppermute | solution.py:38
  113.0 3.8 %collective-permute-done.31.refs_2_ = bf16[64,1024]{1,0:T(8,128)(2,1)S(1)} collective-permute-done((bf16[64,1024]{1,0:T(8,128)(2,1)S(1)}, bf16[64,1024]{1,0:T(8,128)(2,1)S(1)}, u32[]{:S(2)}, u32[]{:S(2)}) %collective-permute-start.31) | collective-permute-done | bytes 131104 | tf_op jit(solution)/shard_map/ppermute | solution.py:38
  118.4 9.6 %collective-permute-done.26.refs_2_ = bf16[64,1024]{1,0:T(8,128)(2,1)S(1)} collective-permute-done((bf16[64,1024]{1,0:T(8,128)(2,1)S(1)}, bf16[64,1024]{1,0:T(8,128)(2,1)S(1)}, u32[]{:S(2)}, u32[]{:S(2)}) %collective-permute-start.26) | collective-permute-done | bytes 131104 | tf_op jit(solution)/shard_map/ppermute | solution.py:38
  (78 shorter events, 32.2 us)
Async XLA Ops:
  2.7 70.6 %collective-permute-start.12 = (bf16[8,32,2048]{2,1,0:T(8,128)(2,1)}, bf16[8,32,2048]{2,1,0:T(8,128)(2,1)}, u32[]{:S(2)}, u32[]{:S(2)}) collective-permute-start(bf16[8,32,2048]{2,1,0:T(8,128)(2,1)} %shard_map.100), channel_id=1, source_target_pairs={{0,1},{1,0},{2,3},{3,2},{4,5},{5,4},{6,7},{7,6},{8,9},{9,8},{10,11... | collective-permute-start | bytes 3145736 | tf_op jit(solution)/shard_map/ppermute | solution.py:38
  8.1 24.5 %collective-permute-start = (bf16[23,16,256]{2,1,0:T(8,128)(2,1)}, bf16[23,16,256]{2,1,0:T(8,128)(2,1)S(1)}, u32[]{:S(2)}, u32[]{:S(2)}) collective-permute-start(bf16[23,16,256]{2,1,0:T(8,128)(2,1)} %get-tuple-element.73), channel_id=1, source_target_pairs={{0,1},{1,2},{2,3},{4,5},{5,6},{6,7},{8,9},{9,10},{10,11},{12,13},{... | collective-permute-start | bytes 565256 | tf_op jit(solution)/shard_map/ppermute | solution.py:26
  10.1 23.2 %collective-permute-start.1 = (bf16[23,16,256]{2,1,0:T(8,128)(2,1)}, bf16[23,16,256]{2,1,0:T(8,128)(2,1)S(1)}, u32[]{:S(2)}, u32[]{:S(2)}) collective-permute-start(bf16[23,16,256]{2,1,0:T(8,128)(2,1)} %get-tuple-element.74), channel_id=1, source_target_pairs={{1,0},{2,1},{3,2},{5,4},{6,5},{7,6},{9,8},{10,9},{11,10},{13,12},{... | collective-permute-start | bytes 565256 | tf_op jit(solution)/shard_map/ppermute | solution.py:26
  33.7 4.3 %collective-permute-start.2 = (bf16[72,256]{1,0:T(8,128)(2,1)S(1)}, bf16[72,256]{1,0:T(8,128)(2,1)S(1)}, u32[]{:S(2)}, u32[]{:S(2)}) collective-permute-start(bf16[72,256]{1,0:T(8,128)(2,1)S(1)} %get-tuple-element.78), channel_id=1, source_target_pairs={{28,0},{0,4},{4,8},{8,12},{12,16},{16,20},{20,24},{24,28},{29,1},{... | collective-permute-start | bytes 110600 | tf_op jit(solution)/shard_map/ppermute | solution.py:34
  33.8 4.3 %collective-permute-start.3 = (bf16[72,256]{1,0:T(8,128)(2,1)S(1)}, bf16[72,256]{1,0:T(8,128)(2,1)S(1)}, u32[]{:S(2)}, u32[]{:S(2)}) collective-permute-start(bf16[72,256]{1,0:T(8,128)(2,1)S(1)} %get-tuple-element.79), channel_id=1, source_target_pairs={{4,0},{8,4},{12,8},{16,12},{20,16},{24,20},{28,24},{0,28},{5,1},{9... | collective-permute-start | bytes 110600 | tf_op jit(solution)/shard_map/ppermute | solution.py:34
  38.1 4.3 %collective-permute-start.4 = (bf16[72,256]{1,0:T(8,128)(2,1)S(1)}, bf16[72,256]{1,0:T(8,128)(2,1)S(1)}, u32[]{:S(2)}, u32[]{:S(2)}) collective-permute-start(bf16[72,256]{1,0:T(8,128)(2,1)S(1)} %get-tuple-element.87), channel_id=1, source_target_pairs={{28,0},{0,4},{4,8},{8,12},{12,16},{16,20},{20,24},{24,28},{29,1},{... | collective-permute-start | bytes 110600 | tf_op jit(solution)/shard_map/ppermute | solution.py:34
  42.5 4.3 %collective-permute-start.6 = (bf16[72,256]{1,0:T(8,128)(2,1)S(1)}, bf16[72,256]{1,0:T(8,128)(2,1)S(1)}, u32[]{:S(2)}, u32[]{:S(2)}) collective-permute-start(bf16[72,256]{1,0:T(8,128)(2,1)S(1)} %get-tuple-element.94), channel_id=1, source_target_pairs={{28,0},{0,4},{4,8},{8,12},{12,16},{16,20},{20,24},{24,28},{29,1},{... | collective-permute-start | bytes 110600 | tf_op jit(solution)/shard_map/ppermute | solution.py:34
  47.0 4.7 %collective-permute-start.8 = (bf16[72,256]{1,0:T(8,128)(2,1)S(1)}, bf16[72,256]{1,0:T(8,128)(2,1)S(1)}, u32[]{:S(2)}, u32[]{:S(2)}) collective-permute-start(bf16[72,256]{1,0:T(8,128)(2,1)S(1)} %get-tuple-element.102), channel_id=1, source_target_pairs={{28,0},{0,4},{4,8},{8,12},{12,16},{16,20},{20,24},{24,28},{29,1},{... | collective-permute-start | bytes 110600 | tf_op jit(solution)/shard_map/ppermute | solution.py:34
  51.8 21.4 %collective-permute-start.15 = (bf16[64,2048]{1,0:T(8,128)(2,1)S(1)}, bf16[64,2048]{1,0:T(8,128)(2,1)S(1)}, u32[]{:S(2)}, u32[]{:S(2)}) collective-permute-start(bf16[64,2048]{1,0:T(8,128)(2,1)S(1)} %get-tuple-element.110.refs_2_), channel_id=1, source_target_pairs={{0,2},{1,3},{2,0},{3,1},{4,6},{5,7},{6,4},{7,5},{8,10},{9,11},{10,... | collective-permute-start | bytes 786440 | tf_op jit(solution)/shard_map/ppermute | solution.py:38
  54.6 18.7 %collective-permute-start.16 = (bf16[64,2048]{1,0:T(8,128)(2,1)S(1)}, bf16[64,2048]{1,0:T(8,128)(2,1)S(1)}, u32[]{:S(2)}, u32[]{:S(2)}) collective-permute-start(bf16[64,2048]{1,0:T(8,128)(2,1)S(1)} %get-tuple-element.111), channel_id=1, source_target_pairs={{0,3},{1,2},{2,1},{3,0},{4,7},{5,6},{6,5},{7,4},{8,11},{9,10},{10,... | collective-permute-start | bytes 786440 | tf_op jit(solution)/shard_map/ppermute | solution.py:38
  55.9 25.0 %collective-permute-start.13 = (bf16[64,2048]{1,0:T(8,128)(2,1)S(1)}, bf16[64,2048]{1,0:T(8,128)(2,1)S(1)}, u32[]{:S(2)}, u32[]{:S(2)}) collective-permute-start(bf16[64,2048]{1,0:T(8,128)(2,1)S(1)} %get-tuple-element.111), channel_id=1, source_target_pairs={{0,1},{1,0},{2,3},{3,2},{4,5},{5,4},{6,7},{7,6},{8,9},{9,8},{10,11... | collective-permute-start | bytes 786440 | tf_op jit(solution)/shard_map/ppermute | solution.py:38
  56.4 37.3 %collective-permute-start.29 = (bf16[8,32,512]{2,1,0:T(8,128)(2,1)S(1)}, bf16[8,32,512]{2,1,0:T(8,128)(2,1)S(1)}, u32[]{:S(2)}, u32[]{:S(2)}) collective-permute-start(bf16[8,32,512]{2,1,0:T(8,128)(2,1)S(1)} %get-tuple-element.129), channel_id=1, source_target_pairs={{0,1},{1,0},{2,3},{3,2},{4,5},{5,4},{6,7},{7,6},{8,9},{9,8},{10,11... | collective-permute-start | bytes 786440 | tf_op jit(solution)/shard_map/ppermute | solution.py:38
  73.2 20.6 %collective-permute-start.28 = (bf16[8,32,512]{2,1,0:T(8,128)(2,1)S(1)}, bf16[8,32,512]{2,1,0:T(8,128)(2,1)S(1)}, u32[]{:S(2)}, u32[]{:S(2)}) collective-permute-start(bf16[8,32,512]{2,1,0:T(8,128)(2,1)S(1)} %get-tuple-element.128), channel_id=1, source_target_pairs={{0,1},{1,0},{2,3},{3,2},{4,5},{5,4},{6,7},{7,6},{8,9},{9,8},{10,11... | collective-permute-start | bytes 786440 | tf_op jit(solution)/shard_map/ppermute | solution.py:38
  75.3 13.9 %collective-permute-start.17 = (bf16[2,256,128]{2,1,0:T(8,128)(2,1)S(1)}, bf16[2,256,128]{2,1,0:T(8,128)(2,1)S(1)}, u32[]{:S(2)}, u32[]{:S(2)}) collective-permute-start(bf16[2,256,128]{2,1,0:T(8,128)(2,1)S(1)} %get-tuple-element.115), channel_id=1, source_target_pairs={{0,1},{1,0},{2,3},{3,2},{4,5},{5,4},{6,7},{7,6},{8,9},{9,8},{10,11... | collective-permute-start | bytes 393224 | tf_op jit(solution)/shard_map/ppermute | solution.py:38
  83.0 9.1 %collective-permute-start.14 = (bf16[2,256,128]{2,1,0:T(8,128)(2,1)S(1)}, bf16[2,256,128]{2,1,0:T(8,128)(2,1)S(1)}, u32[]{:S(2)}, u32[]{:S(2)}) collective-permute-start(bf16[2,256,128]{2,1,0:T(8,128)(2,1)S(1)} %get-tuple-element.113), channel_id=1, source_target_pairs={{0,1},{1,0},{2,3},{3,2},{4,5},{5,4},{6,7},{7,6},{8,9},{9,8},{10,11... | collective-permute-start | bytes 393224 | tf_op jit(solution)/shard_map/ppermute | solution.py:38
  83.0 25.3 %collective-permute-start.10 = (bf16[8,32,512]{2,1,0:T(8,128)(2,1)S(1)}, bf16[8,32,512]{2,1,0:T(8,128)(2,1)S(1)}, u32[]{:S(2)}, u32[]{:S(2)}) collective-permute-start(bf16[8,32,512]{2,1,0:T(8,128)(2,1)S(1)} %get-tuple-element.108), channel_id=1, source_target_pairs={{0,1},{1,0},{2,3},{3,2},{4,5},{5,4},{6,7},{7,6},{8,9},{9,8},{10,11... | collective-permute-start | bytes 786440 | tf_op jit(solution)/shard_map/ppermute | solution.py:38
  89.3 19.1 %collective-permute-start.11 = (bf16[8,32,512]{2,1,0:T(8,128)(2,1)S(1)}, bf16[8,32,512]{2,1,0:T(8,128)(2,1)S(1)}, u32[]{:S(2)}, u32[]{:S(2)}) collective-permute-start(bf16[8,32,512]{2,1,0:T(8,128)(2,1)S(1)} %get-tuple-element.109), channel_id=1, source_target_pairs={{0,1},{1,0},{2,3},{3,2},{4,5},{5,4},{6,7},{7,6},{8,9},{9,8},{10,11... | collective-permute-start | bytes 786440 | tf_op jit(solution)/shard_map/ppermute | solution.py:38
  97.8 4.8 %collective-permute-start.23 = (bf16[2,32,256]{2,1,0:T(8,128)(2,1)S(1)}, bf16[2,32,256]{2,1,0:T(8,128)(2,1)S(1)}, u32[]{:S(2)}, u32[]{:S(2)}) collective-permute-start(bf16[2,32,256]{2,1,0:T(8,128)(2,1)S(1)} %get-tuple-element.122), channel_id=1, source_target_pairs={{24,0},{28,4},{0,8},{4,12},{8,16},{12,20},{16,24},{20,28},{25,1},{... | collective-permute-start | bytes 98312 | tf_op jit(solution)/shard_map/ppermute | solution.py:34
  103.8 13.0 %collective-permute-start.31 = (bf16[64,1024]{1,0:T(8,128)(2,1)S(1)}, bf16[64,1024]{1,0:T(8,128)(2,1)S(1)}, u32[]{:S(2)}, u32[]{:S(2)}) collective-permute-start(bf16[64,1024]{1,0:T(8,128)(2,1)S(1)} %get-tuple-element.132), channel_id=1, source_target_pairs={{0,2},{1,3},{2,0},{3,1},{4,6},{5,7},{6,4},{7,5},{8,10},{9,11},{10,... | collective-permute-start | bytes 393224 | tf_op jit(solution)/shard_map/ppermute | solution.py:38
  105.4 12.5 %collective-permute-start.32 = (bf16[64,1024]{1,0:T(8,128)(2,1)S(1)}, bf16[64,1024]{1,0:T(8,128)(2,1)S(1)}, u32[]{:S(2)}, u32[]{:S(2)}) collective-permute-start(bf16[64,1024]{1,0:T(8,128)(2,1)S(1)} %get-tuple-element.133), channel_id=1, source_target_pairs={{0,3},{1,2},{2,1},{3,0},{4,7},{5,6},{6,5},{7,4},{8,11},{9,10},{10,... | collective-permute-start | bytes 393224 | tf_op jit(solution)/shard_map/ppermute | solution.py:38
  107.8 10.5 %collective-permute-start.30 = (bf16[64,1024]{1,0:T(8,128)(2,1)S(1)}, bf16[64,1024]{1,0:T(8,128)(2,1)S(1)}, u32[]{:S(2)}, u32[]{:S(2)}) collective-permute-start(bf16[64,1024]{1,0:T(8,128)(2,1)S(1)} %get-tuple-element.131), channel_id=1, source_target_pairs={{0,1},{1,0},{2,3},{3,2},{4,5},{5,4},{6,7},{7,6},{8,9},{9,8},{10,11... | collective-permute-start | bytes 393224 | tf_op jit(solution)/shard_map/ppermute | solution.py:38
  108.7 19.3 %collective-permute-start.26 = (bf16[64,1024]{1,0:T(8,128)(2,1)S(1)}, bf16[64,1024]{1,0:T(8,128)(2,1)S(1)}, u32[]{:S(2)}, u32[]{:S(2)}) collective-permute-start(bf16[64,1024]{1,0:T(8,128)(2,1)S(1)} %get-tuple-element.126), channel_id=1, source_target_pairs={{0,2},{1,3},{2,0},{3,1},{4,6},{5,7},{6,4},{7,5},{8,10},{9,11},{10,... | collective-permute-start | bytes 393224 | tf_op jit(solution)/shard_map/ppermute | solution.py:38
  110.6 17.4 %collective-permute-start.27 = (bf16[64,1024]{1,0:T(8,128)(2,1)S(1)}, bf16[64,1024]{1,0:T(8,128)(2,1)S(1)}, u32[]{:S(2)}, u32[]{:S(2)}) collective-permute-start(bf16[64,1024]{1,0:T(8,128)(2,1)S(1)} %get-tuple-element.127), channel_id=1, source_target_pairs={{0,3},{1,2},{2,1},{3,0},{4,7},{5,6},{6,5},{7,4},{8,11},{9,10},{10,... | collective-permute-start | bytes 393224 | tf_op jit(solution)/shard_map/ppermute | solution.py:38
  116.7 11.2 %collective-permute-start.25 = (bf16[64,1024]{1,0:T(8,128)(2,1)S(1)}, bf16[64,1024]{1,0:T(8,128)(2,1)S(1)}, u32[]{:S(2)}, u32[]{:S(2)}) collective-permute-start(bf16[64,1024]{1,0:T(8,128)(2,1)S(1)} %get-tuple-element.125), channel_id=1, source_target_pairs={{0,1},{1,0},{2,3},{3,2},{4,5},{5,4},{6,7},{7,6},{8,9},{9,8},{10,11... | collective-permute-start | bytes 393224 | tf_op jit(solution)/shard_map/ppermute | solution.py:38
  (15 other events, 106.7 us)
